TPU v7x, 32 devices: a whole 2x2x4 slice. The times are simulated.
32 devices in a mesh: dp: 8 (over y, x, core), tensor: 4 (over z).
Axes of the slice: x: 2, y: 2, z: 4, core: 2. Of those that a mesh axis runs over, the one named last changes fastest.
Arguments:
- tokens: bfloat16 [8192, 1536], P('dp'), may hold values from -6 to 6
- cotangent: bfloat16 [8192, 1536], P('dp'), may hold values from -6 to 6
- segment_ids: int32 [8, 1024], P('dp'), may hold values from 0 to 2, never falling along the last dimension, each value on 1 to 512 neighbouring positions
- routes: int32 [8192, 8], P('dp'), may hold values from 0 to 39, all different within a row; in each aligned block of 1024 rows (0 to 1023, 1024 to 2047, ...) at most 384 rows name the same one
- attn_gain: float32 [1536], replicated, may hold values from 0.5 to 1.5
- query_weight: bfloat16 [1536, 1536], P(None, 'tensor'), may hold values from -0.15625 to 0.15625
- key_weight: bfloat16 [1536, 512], P(None, 'tensor'), may hold values from -0.15625 to 0.15625
- value_weight: bfloat16 [1536, 512], P(None, 'tensor'), may hold values from -0.15625 to 0.15625
- out_weight: bfloat16 [1536, 1536], P('tensor'), may hold values from -3 to 3
- ffn_gain: float32 [1536], replicated, may hold values from 0.5 to 1.5
- router_weight: bfloat16 [1536, 40], replicated, may hold values from -0.15625 to 0.15625
- gate_weight: bfloat16 [40, 1536, 512], P('tensor'), may hold values from -0.15625 to 0.15625
- up_weight: bfloat16 [40, 1536, 512], P('tensor'), may hold values from -0.15625 to 0.15625
- down_weight: bfloat16 [40, 512, 1536], P('tensor'), may hold values from -2 to 2
Outputs:
- output: bfloat16 [8192, 1536], P('dp')
- grad_tokens: float32 [8192, 1536], P('dp')
- grad_attn_gain: float32 [1536], P('dp')
- grad_query: float32 [1536, 1536], P('dp', 'tensor')
- grad_key: float32 [1536, 512], P('dp', 'tensor')
- grad_value: float32 [1536, 512], P('dp', 'tensor')
- grad_out: float32 [1536, 1536], P('tensor', 'dp')
- grad_ffn_gain: float32 [1536], P('dp')
- grad_router: float32 [1536, 40], P('dp')
- grad_gate: float32 [40, 1536, 512], P('tensor', 'dp')
- grad_up: float32 [40, 1536, 512], P('tensor', 'dp')
- grad_down: float32 [40, 512, 1536], P('tensor', 'dp')
Inputs may be any that keep to these rules, and one draw needn't show every extreme that they name: `routes`: each token names 8 different experts, and every expert is named by some token; among the tokens of one packed sequence no expert is named more than 384 times, and in every draw some expert is named exactly 384 times within some sequence. `segment_ids`: ids never fall along a sequence; a document has 1 to 512 tokens, and one has exactly 512.
All inputs are finite; a program needn't handle non-finite values.
Results may differ from a plain program's by a relative error of at most 0.014.
Values sent between devices are 32-bit elements; how exact they have to be, the bound alone decides.
A program may use at most 448 MiB of HBM per device.

v0:
```python
import jax
import jax.numpy as jnp
from jax import lax
from jax.sharding import PartitionSpec as P

HEAD = 64
CAP = 384


EPSILON = 1e-06
RESIDUAL = 0.22
ATTN_SCALE = 0.015625
ROPE_BASE = 10000.0
MASKED = -1e30


def left_inner(first, second):
    return lax.dot_general(
        first, second, (((0,), (0,)), ((), ())), preferred_element_type=jnp.float32
    )


def right_inner(first, second):
    return lax.dot_general(
        first, second, (((1,), (1,)), ((), ())), preferred_element_type=jnp.float32
    )


def doc_positions(segment):
    places = jnp.arange(segment.shape[0], dtype=jnp.int32)
    starts_here = jnp.concatenate([jnp.ones((1,), dtype=jnp.bool_), segment[1:] != segment[:-1]])
    opening = lax.cummax(jnp.where(starts_here, places, jnp.zeros_like(places)), axis=0)
    return places - opening


def rope_tables(segment, head_size):
    halfway = head_size // 2
    spread = jnp.arange(halfway, dtype=jnp.float32) * (2.0 / head_size)
    inverse = jnp.power(ROPE_BASE, -spread)
    angles = doc_positions(segment).astype(jnp.float32)[:, None] * inverse[None, :]
    cosine = jnp.cos(angles)
    sine_table = jnp.sin(angles)
    return (
        jnp.concatenate([cosine, cosine], 1)[:, None, :],
        jnp.concatenate([sine_table, sine_table], 1)[:, None, :],
    )


def rotate_half(vector):
    halfway = vector.shape[-1] // 2
    return jnp.concatenate([-vector[..., halfway:], vector[..., :halfway]], -1)


def rotate_back(vector):
    halfway = vector.shape[-1] // 2
    return jnp.concatenate([vector[..., halfway:], -vector[..., :halfway]], -1)


def rope_apply(vector, cosine, sine_table):
    return vector * cosine + rotate_half(vector) * sine_table


def rope_undo(gradient, cosine, sine_table):
    return gradient * cosine + rotate_back(gradient * sine_table)


def rms_forward(hidden, gain):
    recip = lax.rsqrt(jnp.mean(hidden * hidden, axis=-1, keepdims=True) + EPSILON)
    unit = hidden * recip
    return (unit * gain, unit, recip)


def rms_backward(gradient, unit, recip, gain):
    gain_grad = jnp.sum(gradient * unit, axis=0)
    scaled = gradient * gain
    return (recip * (scaled - unit * jnp.mean(scaled * unit, axis=-1, keepdims=True)), gain_grad)


def route_slots(route_rows, expert_ids, capacity):
    length = route_rows.shape[0]
    count_experts = expert_ids.shape[0]
    picked = jnp.sum(
        (route_rows[:, :, None] == expert_ids[None, None, :]).astype(jnp.int32), axis=1
    )
    before = jnp.cumsum(picked, axis=0) - picked
    columns = jnp.arange(count_experts, dtype=jnp.int32)[None, :]
    target = jnp.where(picked > 0, columns * capacity + before, count_experts * capacity)
    places = jnp.broadcast_to(jnp.arange(length, dtype=jnp.int32)[:, None], target.shape)
    slots = (
        jnp.zeros((count_experts * capacity,), jnp.int32)
        .at[target.reshape(-1)]
        .set(places.reshape(-1), mode="drop")
    )
    filled = jnp.sum(picked, axis=0)
    valid = (jnp.arange(capacity, dtype=jnp.int32)[None, :] < filled[:, None]).astype(jnp.float32)
    return (slots.reshape(count_experts, capacity), valid, picked > 0)


def block_mask(segment, first_row, block_rows):
    rows = first_row + jnp.arange(block_rows, dtype=jnp.int32)
    row_segment = lax.dynamic_slice_in_dim(segment, first_row, block_rows)
    columns = jnp.arange(segment.shape[0], dtype=jnp.int32)
    return (row_segment[:, None] == segment[None, :]) & (rows[:, None] >= columns[None, :])


def attend_scores(queries, keys_wide, allowed):
    scores = ATTN_SCALE * jnp.einsum(
        "qhe,khe->hqk", queries, keys_wide, preferred_element_type=jnp.float32
    )
    return jnp.where(allowed[None], scores, MASKED)


def attend_forward(queries, keys_wide, values_wide, allowed):
    scores = attend_scores(queries, keys_wide, allowed)
    logsum = jnp.log(jnp.sum(jnp.exp(scores), axis=-1, keepdims=True))
    prob_b = jnp.exp(scores - logsum).astype(jnp.bfloat16)
    attended = jnp.einsum(
        "hqk,khe->qhe", prob_b, values_wide, preferred_element_type=jnp.float32
    ).astype(jnp.bfloat16)
    return (attended, logsum)


def attend_backward(queries, keys_wide, values_wide, allowed, logsum, attended, grad_attended):
    scores = attend_scores(queries, keys_wide, allowed)
    probs = jnp.exp(scores - logsum)
    prob_b = probs.astype(jnp.bfloat16)
    row_dot = jnp.transpose(
        jnp.sum(grad_attended.astype(jnp.float32) * attended.astype(jnp.float32), axis=-1)
    )[:, :, None]
    grad_values = jnp.einsum(
        "hqk,qhe->khe", prob_b, grad_attended, preferred_element_type=jnp.float32
    )
    grad_probs = jnp.einsum(
        "qhe,khe->hqk", grad_attended, values_wide, preferred_element_type=jnp.float32
    )
    grad_scores = (ATTN_SCALE * probs * (grad_probs - row_dot)).astype(jnp.bfloat16)
    grad_queries = jnp.einsum(
        "hqk,khe->qhe", grad_scores, keys_wide, preferred_element_type=jnp.float32
    )
    grad_keys = jnp.einsum("hqk,qhe->khe", grad_scores, queries, preferred_element_type=jnp.float32)
    return (grad_queries, grad_keys, grad_values)


def on_device(
    tokens,
    cotangent,
    segment_ids,
    routes,
    attn_gain,
    query_weight,
    key_weight,
    value_weight,
    out_weight,
    ffn_gain,
    router_weight,
    gate_weight,
    up_weight,
    down_weight,
):
    length = tokens.shape[0]
    width = tokens.shape[1]
    segment = segment_ids[0]
    heads_local = query_weight.shape[1] // HEAD
    kv_local = key_weight.shape[1] // HEAD
    group_size = heads_local // kv_local
    experts_all = router_weight.shape[1]
    experts_local = gate_weight.shape[0]
    cosine, sine_table = rope_tables(segment, HEAD)
    hidden_in = tokens.astype(jnp.float32)
    normed, unit_one, recip_one = rms_forward(hidden_in, attn_gain)
    normed_b = normed.astype(jnp.bfloat16)
    queries = rope_apply(
        jnp.dot(normed_b, query_weight, preferred_element_type=jnp.float32).reshape(
            length, heads_local, HEAD
        ),
        cosine,
        sine_table,
    ).astype(jnp.bfloat16)
    keys_rot = rope_apply(
        jnp.dot(normed_b, key_weight, preferred_element_type=jnp.float32).reshape(
            length, kv_local, HEAD
        ),
        cosine,
        sine_table,
    ).astype(jnp.bfloat16)
    values = (
        jnp.dot(normed_b, value_weight, preferred_element_type=jnp.float32)
        .astype(jnp.bfloat16)
        .reshape(length, kv_local, HEAD)
    )
    keys_wide = jnp.repeat(keys_rot, group_size, axis=1)
    values_wide = jnp.repeat(values, group_size, axis=1)
    block_rows = min(512, length)
    count_blocks = length // block_rows
    first_rows = jnp.arange(count_blocks, dtype=jnp.int32) * block_rows
    query_blocks = queries.reshape(count_blocks, block_rows, heads_local, HEAD)

    def forward_block(pieces):
        query_part, first_row = pieces
        return attend_forward(
            query_part, keys_wide, values_wide, block_mask(segment, first_row, block_rows)
        )

    attended, logsum = lax.map(forward_block, (query_blocks, first_rows))
    attended_flat = attended.reshape(length, heads_local * HEAD)
    attn_out = lax.psum(
        jnp.dot(attended_flat, out_weight, preferred_element_type=jnp.float32), "tensor"
    )
    middle = hidden_in + RESIDUAL * attn_out
    normed_two, unit_two, recip_two = rms_forward(middle, ffn_gain)
    normed_two_b = normed_two.astype(jnp.bfloat16)
    logits = jnp.dot(normed_two_b, router_weight, preferred_element_type=jnp.float32)
    all_ids = jnp.arange(experts_all, dtype=jnp.int32)
    chosen = jnp.sum((routes[:, :, None] == all_ids[None, None, :]).astype(jnp.int32), axis=1) > 0
    raised = jnp.where(chosen, jnp.exp(logits), 0.0)
    gate_probs = raised / jnp.sum(raised, axis=-1, keepdims=True)
    first_expert = lax.axis_index("tensor") * experts_local
    local_ids = first_expert + jnp.arange(experts_local, dtype=jnp.int32)
    slot_token, valid, unused = route_slots(routes, local_ids, CAP)
    gate_local = lax.dynamic_slice_in_dim(gate_probs, first_expert, experts_local, 1)
    gate_slots = jnp.take_along_axis(jnp.transpose(gate_local), slot_token, axis=1) * valid
    rows_in = normed_two_b[slot_token]

    def expert_inputs(expert_rows_in):
        gate_input = jnp.einsum(
            "ecd,edf->ecf", expert_rows_in, gate_weight, preferred_element_type=jnp.float32
        )
        up_input = jnp.einsum(
            "ecd,edf->ecf", expert_rows_in, up_weight, preferred_element_type=jnp.float32
        )
        return (gate_input, up_input)

    gate_input, up_input = expert_inputs(rows_in)
    activation = (
        gate_input * jax.nn.sigmoid(gate_input) * up_input * gate_slots[:, :, None]
    ).astype(jnp.bfloat16)
    expert_rows = jnp.einsum(
        "ecf,efd->ecd", activation, down_weight, preferred_element_type=jnp.float32
    )
    moe_part = jax.ops.segment_sum(
        expert_rows.reshape(-1, width), slot_token.reshape(-1), num_segments=length
    )
    moe_out = lax.psum(moe_part, "tensor")
    output = (middle + RESIDUAL * moe_out).astype(jnp.bfloat16)
    grad_moe_b = (RESIDUAL * cotangent.astype(jnp.float32)).astype(jnp.bfloat16)
    normed_again, grad_moe_b = lax.optimization_barrier((normed_two_b, grad_moe_b))
    rows_back = normed_again[slot_token]
    back_gate, back_up = expert_inputs(rows_back)
    grad_rows = grad_moe_b[slot_token]
    sigmoid_val = jax.nn.sigmoid(back_gate)
    silu_out = back_gate * sigmoid_val
    hidden = silu_out * back_up
    activation_back = (hidden * gate_slots[:, :, None]).astype(jnp.bfloat16)
    grad_down = jnp.einsum(
        "ecf,ecd->efd", activation_back, grad_rows, preferred_element_type=jnp.float32
    )
    grad_act = jnp.einsum(
        "ecd,efd->ecf", grad_rows, down_weight, preferred_element_type=jnp.float32
    )
    grad_column = jnp.sum(grad_act * hidden, axis=-1) * valid
    grad_hidden = grad_act * gate_slots[:, :, None]
    grad_gate_in = (
        grad_hidden * back_up * sigmoid_val * (1.0 + back_gate * (1.0 - sigmoid_val))
    ).astype(jnp.bfloat16)
    grad_up_in = (grad_hidden * silu_out).astype(jnp.bfloat16)
    grad_gate = jnp.einsum(
        "ecd,ecf->edf", rows_back, grad_gate_in, preferred_element_type=jnp.float32
    )
    grad_up = jnp.einsum("ecd,ecf->edf", rows_back, grad_up_in, preferred_element_type=jnp.float32)
    grad_rows_in = jnp.einsum(
        "ecf,edf->ecd", grad_gate_in, gate_weight, preferred_element_type=jnp.float32
    ) + jnp.einsum("ecf,edf->ecd", grad_up_in, up_weight, preferred_element_type=jnp.float32)
    expert_grads = (grad_gate, grad_up, grad_down)
    grad_normed_part = jax.ops.segment_sum(
        grad_rows_in.reshape(-1, width), slot_token.reshape(-1), num_segments=length
    )
    grad_gates_local = (
        jnp.zeros((length, experts_local), jnp.float32)
        .at[slot_token, jnp.arange(experts_local, dtype=jnp.int32)[:, None]]
        .add(grad_column)
    )
    grad_gates_part = lax.dynamic_update_slice_in_dim(
        jnp.zeros((length, experts_all), jnp.float32), grad_gates_local, first_expert, 1
    )
    grad_normed_sum, grad_gates = lax.psum((grad_normed_part, grad_gates_part), "tensor")
    weighted = jnp.sum(gate_probs * grad_gates, axis=-1, keepdims=True)
    grad_logits_b = (gate_probs * (grad_gates - weighted)).astype(jnp.bfloat16)
    grad_router = left_inner(normed_two_b, grad_logits_b)
    grad_normed_two = grad_normed_sum + right_inner(grad_logits_b, router_weight)
    grad_from_norm, grad_ffn_gain = rms_backward(grad_normed_two, unit_two, recip_two, ffn_gain)
    grad_middle = cotangent.astype(jnp.float32) + grad_from_norm
    grad_branch_b = (RESIDUAL * grad_middle).astype(jnp.bfloat16)
    grad_out = left_inner(attended_flat, grad_branch_b)
    grad_attended = (
        right_inner(grad_branch_b, out_weight)
        .astype(jnp.bfloat16)
        .reshape(count_blocks, block_rows, heads_local, HEAD)
    )

    def backward_block(running, pieces):
        query_part, first_row, logsum_part, attended_part, grad_part = pieces
        grad_queries, grad_keys, grad_values = attend_backward(
            query_part,
            keys_wide,
            values_wide,
            block_mask(segment, first_row, block_rows),
            logsum_part,
            attended_part,
            grad_part,
        )
        return ((running[0] + grad_keys, running[1] + grad_values), grad_queries)

    wide_zero = jnp.zeros((length, heads_local, HEAD), jnp.float32)
    (grad_keys_wide, grad_values_wide), grad_query_blocks = lax.scan(
        backward_block,
        (wide_zero, wide_zero),
        (query_blocks, first_rows, logsum, attended, grad_attended),
    )
    grad_queries_b = (
        rope_undo(grad_query_blocks.reshape(length, heads_local, HEAD), cosine, sine_table)
        .astype(jnp.bfloat16)
        .reshape(length, heads_local * HEAD)
    )
    grad_keys_b = (
        rope_undo(
            jnp.sum(grad_keys_wide.reshape(length, kv_local, group_size, HEAD), axis=2),
            cosine,
            sine_table,
        )
        .astype(jnp.bfloat16)
        .reshape(length, kv_local * HEAD)
    )
    grad_values_b = (
        jnp.sum(grad_values_wide.reshape(length, kv_local, group_size, HEAD), axis=2)
        .astype(jnp.bfloat16)
        .reshape(length, kv_local * HEAD)
    )
    grad_query = left_inner(normed_b, grad_queries_b)
    grad_key = left_inner(normed_b, grad_keys_b)
    grad_value = left_inner(normed_b, grad_values_b)
    grad_normed_local = (
        right_inner(grad_queries_b, query_weight)
        + right_inner(grad_keys_b, key_weight)
        + right_inner(grad_values_b, value_weight)
    )
    grad_normed = lax.psum(grad_normed_local, "tensor")
    grad_from_first, grad_attn_gain = rms_backward(grad_normed, unit_one, recip_one, attn_gain)
    grad_tokens = grad_middle + grad_from_first
    summed = tuple(
        (
            lax.psum_scatter(grad_attn_gain, "dp", scatter_dimension=0, tiled=True),
            lax.psum_scatter(grad_query, "dp", scatter_dimension=0, tiled=True),
            lax.psum_scatter(grad_key, "dp", scatter_dimension=0, tiled=True),
            lax.psum_scatter(grad_value, "dp", scatter_dimension=0, tiled=True),
            lax.psum_scatter(grad_out, "dp", scatter_dimension=1, tiled=True),
            lax.psum_scatter(grad_ffn_gain, "dp", scatter_dimension=0, tiled=True),
            lax.psum_scatter(grad_router, "dp", scatter_dimension=0, tiled=True),
            lax.psum_scatter(expert_grads[0], "dp", scatter_dimension=1, tiled=True),
            lax.psum_scatter(expert_grads[1], "dp", scatter_dimension=1, tiled=True),
            lax.psum_scatter(expert_grads[2], "dp", scatter_dimension=1, tiled=True),
        )
    )
    return (output, grad_tokens) + summed


def solution(mesh):
    return jax.shard_map(
        on_device,
        mesh=mesh,
        in_specs=(
            P("dp", None),
            P("dp", None),
            P("dp", None),
            P("dp", None),
            P(),
            P(None, "tensor"),
            P(None, "tensor"),
            P(None, "tensor"),
            P("tensor", None),
            P(),
            P(),
            P("tensor", None, None),
            P("tensor", None, None),
            P("tensor", None, None),
        ),
        out_specs=(
            P("dp", None),
            P("dp", None),
            P("dp"),
            P("dp", "tensor"),
            P("dp", "tensor"),
            P("dp", "tensor"),
            P("tensor", "dp"),
            P("dp"),
            P("dp", None),
            P("tensor", "dp", None),
            P("tensor", "dp", None),
            P("tensor", "dp", None),
        ),
        check_vma=False,
    )
```

profile of v0, /device:TPU:8, one launch (start us, length us, event | category | flops | bytes accessed | tf_op | source)
XLA Modules:
  0.0 2153.1 jit_solution(11519907561322758243)
XLA Ops:
  41.5 38.2 %while.28 = (s32[]{:T(128)}, bf16[2,512,6,64]{1,3,2,0:T(8,128)(2,1)S(1)}, f32[2,6,512,1]{2,1,3,0:T(8,128)}, s32[2]{0:T(128)S(1)}, s32[1024]{0:T(1024)S(1)}, /*in...) while((s32[]{:T(128)}, ...), condition=%wide.region_5.6_spmd.clone, body=%wide.region_3.5_spmd.clone.sunk | while | flops 829093376 | bytes 31492336 | solution.py:204
  91.1 37.9 %scatter_custom_fusion = s32[3840]{0:T(1024)S(1)} fusion(s32[10240]{0:T(1024)S(1)} %bitcast.285, s32[10240]{0:T(1024)S(1)} %reshape.517, s32[]{:T(128)} %constant.39.clone.1), kind=kCustom, calls=%fused_computation.161 | custom fusion | bytes 15364 | tf_op jit(solution)/shard_map/scatter | solution.py:92
  134.8 173.3 %all-reduce.9.cloned.1.call-done = f32[1024,1536]{1,0:T(8,128)} async-done(((f32[1024,1536]{1,0:T(8,128)}), f32[1024,1536]{1,0:T(8,128)}) %all-reduce.9.cloned.1.call-update) | async-done | bytes 6291472 | tf_op jit(solution)/shard_map/psum | solution.py:206
  320.6 26.6 %gather_fusion.2 = bf16[3840,1536]{1,0:T(8,128)(2,1)} fusion(bf16[1024,1536]{1,0:T(8,128)(2,1)} %multiply_convert_fusion.6, s32[4096]{0:T(1024)S(1)} %pad_clamp_fusion), kind=kCustom, calls=%fused_computation.2 | custom fusion | bytes 23608320 | tf_op jit(solution)/shard_map/gather | solution.py:247
  379.1 29.3 %gather_fusion.3 = f32[3840]{0:T(1024)S(1)} fusion(f32[10,1024]{1,0:T(8,128)S(1)} %dynamic-slice_bitcast_fusion.1, s32[3840]{0:T(1024)S(1)} %reshape.507), kind=kCustom, calls=%fused_computation.3 | custom fusion | bytes 61440 | tf_op jit(solution)/shard_map/jit(take_along_axis)/gather | solution.py:221
  408.5 26.2 %gather_fusion.1 = bf16[3840,1536]{1,0:T(8,128)(2,1)} fusion(bf16[1024,1536]{1,0:T(8,128)(2,1)} %fusion.48, s32[4096]{0:T(1024)S(1)} %pad_clamp_fusion), kind=kCustom, calls=%fused_computation.1 | custom fusion | bytes 23608320 | tf_op jit(solution)/shard_map/gather | solution.py:249
  434.7 19.7 multiply_reduce_fusion
  469.6 24.8 %convolution_add_fusion = f32[10,384,1536]{2,1,0:T(8,128)} fusion(f32[10,384,1536]{2,1,0:T(8,128)} %fusion.99, bf16[10,384,512]{2,1,0:T(8,128)(2,1)} %get-tuple-element.350, bf16[10,1536,512]{2,1,0:T(8,128)(2,1)} %param.30), kind=kOutput, calls=%fused_computation.59 | convolution fusion | flops 6045696000 | bytes 66846720 | tf_op jit(solution)/shard_map/ecf,edf->ecd/dot_general | solution.py:272
  494.4 44.0 %scatter_custom_fusion.2 = f32[1024,1536]{1,0:T(8,128)} fusion(s32[3840]{0:T(1024)} %copy-done.45, f32[3840,1536]{1,0:T(8,128)} %bitcast.250, f32[]{:T(128)} %constant.53.clone.1), kind=kCustom, calls=%fused_computation.99 | custom fusion | flops 5898240 | bytes 6291968 | tf_op jit(solution)/shard_map/scatter-add | solution.py:274
  538.4 27.2 %scatter_custom_fusion.3 = f32[10240]{0:T(1024)S(1)} fusion(s32[3840]{0:T(1024)} %reshape.537, f32[3840]{0:T(1024)S(1)} %reshape.539, f32[]{:T(128)} %constant.53.clone.1), kind=kCustom, calls=%fused_computation.155 | custom fusion | flops 3840 | bytes 41472
  567.2 26.1 %gather_fusion = bf16[3840,1536]{1,0:T(8,128)(2,1)} fusion(bf16[1024,1536]{1,0:T(8,128)(2,1)} %multiply_convert_fusion.6, s32[4096]{0:T(1024)S(1)} %pad_clamp_fusion), kind=kCustom, calls=%fused_computation | custom fusion | bytes 23608320 | tf_op jit(solution)/shard_map/gather | solution.py:222
  608.3 31.0 %fusion.56 = f32[10,384,1536]{2,1,0:T(8,128)} fusion(bf16[10,512,1536]{2,1,0:T(8,128)(2,1)} %param.31, f32[10,384,512]{2,1,0:T(8,128)} %fusion.96, f32[10,384]{1,0:T(8,128)S(1)} %select_select_fusion, bf16[10,384,1536]{2,1,0:T(8,128)(2,1)} %bitcast.257, bf16[10,1536,512]{2,1,0:T(8,128)(2,1)} %param.30), kind=kOutput, calls=%fused_computation.92 | convolution fusion | flops 12093358080 | bytes 74726400 | tf_op jit(solution)/shard_map/ecf,efd->ecd/dot_general | solution.py:237
  639.4 44.4 %scatter_custom_fusion.1 = f32[1024,1536]{1,0:T(8,128)} fusion(s32[3840]{0:T(1024)} %copy-done.45, f32[3840,1536]{1,0:T(8,128)} %bitcast.287, f32[]{:T(128)} %constant.53.clone.1), kind=kCustom, calls=%fused_computation.101 | custom fusion | flops 5898240 | bytes 6291968 | tf_op jit(solution)/shard_map/scatter-add | solution.py:240
  683.8 110.6 %all-reduce.13.cloned.1.call-done = (f32[1024,1536]{1,0:T(8,128)}, f32[1024,40]{0,1:T(8,128)}) async-done(((f32[1024,1536]{1,0:T(8,128)}, f32[1024,40]{0,1:T(8,128)}), (f32[1024,1536]{1,0:T(8,128)}, f32[1024,40]{0,1:T(8,128)})) %all-reduce.13.cloned.1.call-update) | async-done | bytes 6455312 | tf_op jit(solution)/shard_map/psum | solution.py:285
  820.8 91.8 %while.29 = (s32[]{:T(128)}, f32[1024,6,64]{0,2,1:T(8,128)S(1)}, f32[1024,6,64]{0,2,1:T(8,128)}, f32[2,512,6,64]{1,0,3,2:T(2,128)}, bf16[2,512,6,64]{1,3,2,0:T(8...) while((s32[]{:T(128)}, f32[1024,6,64]{0,2,1:T(8,128)S(1)}, ...), condition=%wide.region_26.27_spmd.clone, body=%wide.region_24.26_spmd.clone.sunk | while | flops 2051798528 | bytes 209649584 | solution.py:314
  955.3 23.3 %fusion.57 = f32[10,512,1536]{2,1,0:T(8,128)} fusion(bf16[10,384,1536]{2,1,0:T(8,128)(2,1)} %bitcast.255, f32[10,384]{1,0:T(8,128)S(1)} %copy-done.58, f32[10,384,512]{2,1,0:T(8,128)} %fusion.97, f32[10,384,512]{2,1,0:T(8,128)} %fusion.98), kind=kOutput, calls=%fused_computation.93 | convolution fusion | flops 6053560320 | bytes 58997760 | tf_op jit(solution)/shard_map/ecf,ecd->efd/dot_general | solution.py:254
  1019.3 371.4 %all-reduce.11.cloned.1.call-done = (f32[1024,1536]{1,0:T(8,128)}, f32[1024,1536]{1,0:T(8,128)}) async-done(((f32[1024,1536]{1,0:T(8,128)}, f32[1024,1536]{1,0:T(8,128)}), (f32[1024,1536]{1,0:T(8,128)}, f32[1024,1536]{1,0:T(8,128)})) %all-reduce.11.cloned.1.call-update) | async-done | bytes 12582928 | tf_op jit(solution)/shard_map/psum | solution.py:243
  1395.5 24.4 %all-reduce.2 = (f32[1536]{0:T(1024)S(1)}, f32[1536]{0:T(1024)S(1)}) all-reduce(f32[1536]{0:T(1024)S(1)} %get-tuple-element.290, f32[1536]{0:T(1024)S(1)} %copy-done.56), channel_id=2, replica_groups=mesh['dp'=8,'tensor'=4] {'dp'}, use_global_device_ids=true, to_apply=%region_32.33.clone | all-reduce | flops 3072 | bytes 24576
  1434.5 35.2 %reduce-scatter.15.cloned.1.call-done = f32[192,128]{1,0:T(8,128)} async-done(((f32[1536,128]{1,0:T(8,128)}), f32[192,128]{1,0:T(8,128)}) %reduce-scatter.15.cloned.1.call-update) | async-done | bytes 98320 | tf_op jit(solution)/shard_map/reduce_scatter | solution.py:354
  1469.7 46.8 %reduce-scatter.11.cloned.1.call-done = f32[192,384]{1,0:T(8,128)} async-done(((f32[1536,384]{1,0:T(8,128)}), f32[192,384]{1,0:T(8,128)}) %reduce-scatter.11.cloned.1.call-update) | async-done | bytes 294928 | tf_op jit(solution)/shard_map/reduce_scatter | solution.py:352
  1516.6 46.4 %reduce-scatter.17.cloned.1.call-done = f32[384,192]{0,1:T(8,128)} async-done(((f32[384,1536]{0,1:T(8,128)}), f32[384,192]{0,1:T(8,128)}) %reduce-scatter.17.cloned.1.call-update) | async-done | bytes 294928 | tf_op jit(solution)/shard_map/reduce_scatter | solution.py:355
  1563.0 194.5 %reduce-scatter.23.cloned.1.call-done = f32[10,64,1536]{2,1,0:T(8,128)} async-done(((f32[10,512,1536]{2,1,0:T(8,128)}), f32[10,64,1536]{2,1,0:T(8,128)}) %reduce-scatter.23.cloned.1.call-update) | async-done | bytes 3932176 | tf_op jit(solution)/shard_map/reduce_scatter | solution.py:360
  1757.5 194.3 %reduce-scatter.19.cloned.1.call-done = f32[10,192,512]{2,1,0:T(8,128)} async-done(((f32[10,1536,512]{2,1,0:T(8,128)}), f32[10,192,512]{2,1,0:T(8,128)}) %reduce-scatter.19.cloned.1.call-update) | async-done | bytes 3932176 | tf_op jit(solution)/shard_map/reduce_scatter | solution.py:358
  1951.8 194.5 %reduce-scatter.21.cloned.1.call-done = f32[10,192,512]{2,1,0:T(8,128)} async-done(((f32[10,1536,512]{2,1,0:T(8,128)}), f32[10,192,512]{2,1,0:T(8,128)}) %reduce-scatter.21.cloned.1.call-update) | async-done | bytes 3932176 | tf_op jit(solution)/shard_map/reduce_scatter | solution.py:359
  (352 shorter events, 376.6 us)
Async XLA Ops:
  7.2 300.9 %all-reduce.9.cloned.1.call-start = ((), (), s32[]{:S(2)}) async-start(), calls=%async_computation.8 | async-start | bytes 12582912 | tf_op jit(solution)/shard_map/psum | solution.py:206
  86.2 708.1 %all-reduce.13.cloned.1.call-start = ((), (), s32[]{:S(2)}) async-start(), calls=%async_computation.18 | async-start | bytes 12910592 | tf_op jit(solution)/shard_map/psum | solution.py:285
  134.8 180.7 %copy-start.47 = (f32[1536]{0:T(1024)S(1)}, f32[1536]{0:T(1024)}, u32[]{:S(2)}) copy-start(f32[1536]{0:T(1024)} %param.27) | copy-start | bytes 18436
  434.7 173.6 %copy-start.57 = (f32[10,384]{1,0:T(8,128)}, f32[10,384]{1,0:T(8,128)S(1)}, u32[]{:S(2)}) copy-start(f32[10,384]{1,0:T(8,128)S(1)} %select_select_fusion) | copy-start | bytes 46084
  566.9 450.8 %reduce-scatter.25.cloned.1.call-start = ((), (), s32[]{:S(2)}) async-start(), calls=%async_computation.16 | async-start | bytes 884736
  639.3 155.1 %copy-start.30 = (f32[1024,40]{0,1:T(8,128)S(1)}, f32[1024,40]{0,1:T(8,128)}, u32[]{:S(2)}) copy-start(f32[1024,40]{0,1:T(8,128)} %copy-done.29) | copy-start | bytes 491524
  639.3 155.1 %copy-start.53 = (f32[1024]{0:T(1024)S(1)}, f32[1024]{0:T(1024)}, u32[]{:S(2)}) copy-start(f32[1024]{0:T(1024)} %copy-done.52) | copy-start | bytes 12292
  639.3 160.8 %copy-start.41 = (bf16[1536,40]{0,1:T(8,128)(2,1)S(1)}, bf16[1536,40]{0,1:T(8,128)(2,1)}, u32[]{:S(2)}) copy-start(bf16[1536,40]{0,1:T(8,128)(2,1)} %param.28) | copy-start | bytes 368644
  639.3 160.8 %copy-start.48 = (f32[1536]{0:T(1024)S(1)}, f32[1536]{0:T(1024)}, u32[]{:S(2)}) copy-start(f32[1536]{0:T(1024)} %param.27) | copy-start | bytes 18436
  639.4 160.8 %copy-start.51 = (f32[1024]{0:T(1024)S(1)}, f32[1024]{0:T(1024)}, u32[]{:S(2)}) copy-start(f32[1024]{0:T(1024)} %copy-done.50) | copy-start | bytes 12292
  820.8 92.0 %copy-start.28 = (f32[1024,64]{0,1:T(8,128)S(1)}, f32[1024,64]{0,1:T(8,128)}, u32[]{:S(2)}) copy-start(f32[1024,64]{0,1:T(8,128)} %copy-done.27) | copy-start | bytes 786436
  820.8 92.1 %copy-start.26 = (f32[1024,64]{0,1:T(8,128)S(1)}, f32[1024,64]{0,1:T(8,128)}, u32[]{:S(2)}) copy-start(f32[1024,64]{0,1:T(8,128)} %copy-done.25) | copy-start | bytes 786436
  927.2 463.5 %all-reduce.11.cloned.1.call-start = ((), (), s32[]{:S(2)}) async-start(), calls=%async_computation.17 | async-start | bytes 25165824 | tf_op jit(solution)/shard_map/psum | solution.py:243
  935.5 499.0 %reduce-scatter.13.cloned.1.call-start = ((), (), s32[]{:S(2)}) async-start(), calls=%async_computation.10 | async-start | bytes 884736 | tf_op jit(solution)/shard_map/reduce_scatter | solution.py:353
  939.5 530.2 %reduce-scatter.15.cloned.1.call-start = ((), (), s32[]{:S(2)}) async-start(), calls=%async_computation.11 | async-start | bytes 884736 | tf_op jit(solution)/shard_map/reduce_scatter | solution.py:354
  943.4 573.2 %reduce-scatter.11.cloned.1.call-start = ((), (), s32[]{:S(2)}) async-start(), calls=%async_computation.9 | async-start | bytes 2654208 | tf_op jit(solution)/shard_map/reduce_scatter | solution.py:352
  948.7 614.3 %reduce-scatter.17.cloned.1.call-start = ((), (), s32[]{:S(2)}) async-start(), calls=%async_computation.12 | async-start | bytes 2654208 | tf_op jit(solution)/shard_map/reduce_scatter | solution.py:355
  955.3 802.3 %reduce-scatter.23.cloned.1.call-start = ((), (), s32[]{:S(2)}) async-start(), calls=%async_computation.15 | async-start | bytes 35389440 | tf_op jit(solution)/shard_map/reduce_scatter | solution.py:360
  978.6 973.2 %reduce-scatter.19.cloned.1.call-start = ((), (), s32[]{:S(2)}) async-start(), calls=%async_computation.13 | async-start | bytes 35389440 | tf_op jit(solution)/shard_map/reduce_scatter | solution.py:358
  997.0 1149.4 %reduce-scatter.21.cloned.1.call-start = ((), (), s32[]{:S(2)}) async-start(), calls=%async_computation.14 | async-start | bytes 35389440 | tf_op jit(solution)/shard_map/reduce_scatter | solution.py:359
  1015.8 374.9 %copy-start.49 = (f32[1536]{0:T(1024)S(1)}, f32[1536]{0:T(1024)}, u32[]{:S(2)}) copy-start(f32[1536]{0:T(1024)} %param.22) | copy-start | bytes 18436
  1015.8 374.9 %copy-start.55 = (f32[1024]{0:T(1024)S(1)}, f32[1024]{0:T(1024)}, u32[]{:S(2)}) copy-start(f32[1024]{0:T(1024)} %copy-done.54) | copy-start | bytes 12292
  1015.8 379.7 %copy-start.56 = (f32[1536]{0:T(1024)S(1)}, f32[1536]{0:T(1024)}, u32[]{:S(2)}) copy-start(f32[1536]{0:T(1024)} %get-tuple-element.288) | copy-start | bytes 18436
  1421.2 725.2 %copy-start.1 = (bf16[384,1536]{1,0:T(8,128)(2,1)S(1)}, bf16[384,1536]{1,0:T(8,128)(2,1)}, u32[]{:S(2)}) copy-start(bf16[384,1536]{1,0:T(8,128)(2,1)} %param.26) | copy-start | bytes 3538948
  (62 other events, 547.4 us)
Sparse Core Ops, SparseCore 0:
  86.3 221.7 all-reduce.8
  567.0 227.3 all-reduce.12
  927.4 36.1 reduce-scatter.24
  966.1 424.5 all-reduce.10
  1394.6 36.2 reduce-scatter.12
  1434.8 34.9 reduce-scatter.14
  1474.0 42.4 reduce-scatter.10
  1520.5 42.4 reduce-scatter.16
  1567.7 189.8 reduce-scatter.22
  1762.0 189.8 reduce-scatter.18
  1956.5 189.8 reduce-scatter.20
where the time goes:
time: 2170 us; the launch traced here: 2150 us
  waiting for transfers between devices  1370 us (63%)
  matrix products  326 us (15%)
  local copies, waits for them, and re-layouts  225 us (10%)
  other arithmetic  185 us (9%)
  blocking collectives  24.4 us (1%)
    psum x1, waiting for transfers between devices, on_device(): moe_out = lax.psum(moe_part, 'tensor')  371 us
    reduce_scatter x1, waiting for transfers between devices, on_device(): lax.psum_scatter(expert_grads[1], 'dp', scatter_dimension=1, tiled=True)  194 us
    reduce_scatter x1, waiting for transfers between devices, on_device(): lax.psum_scatter(expert_grads[2], 'dp', scatter_dimension=1, tiled=True)  194 us
    reduce_scatter x1, waiting for transfers between devices, on_device(): lax.psum_scatter(expert_grads[0], 'dp', scatter_dimension=1, tiled=True)  194 us
    psum x1, waiting for transfers between devices, on_device(): lax.psum(jnp.dot(attended_flat, out_weight, preferred_element_type=jnp.fl...  173 us
    psum x1, waiting for transfers between devices, on_device(): lax.psum((grad_normed_part, grad_gates_part), 'tensor')  111 us
    reduce_scatter x1, waiting for transfers between devices, on_device(): lax.psum_scatter(grad_query, 'dp', scatter_dimension=0, tiled=True)  46.8 us
    reduce_scatter x1, waiting for transfers between devices, on_device(): lax.psum_scatter(grad_out, 'dp', scatter_dimension=1, tiled=True)  46.4 us
  transfers between devices with their start and end apart: 11, of which 9 were waited for; matrix products, arithmetic and copies ran while one was open for 13% of the time, Pallas kernels for 0%

commit v1 on v0

--- a/solution.py
+++ b/solution.py
@@ -1,7 +1,13 @@
+import functools
+
 import jax
 import jax.numpy as jnp
 from jax import lax
+from jax.experimental import pallas as pl
+from jax.experimental.pallas import tpu as pltpu
 from jax.sharding import PartitionSpec as P
+
+MESH = pl.DeviceIdType.MESH
 
 HEAD = 64
 CAP = 384
@@ -28,8 +34,7 @@
 
 def doc_positions(segment):
     places = jnp.arange(segment.shape[0], dtype=jnp.int32)
-    starts_here = jnp.concatenate([jnp.ones((1,), dtype=jnp.bool_), segment[1:] != segment[:-1]])
-    opening = lax.cummax(jnp.where(starts_here, places, jnp.zeros_like(places)), axis=0)
+    opening = jnp.sum((segment[None, :] < segment[:, None]).astype(jnp.int32), axis=1)
     return places - opening
 
 
@@ -76,24 +81,12 @@
     return (recip * (scaled - unit * jnp.mean(scaled * unit, axis=-1, keepdims=True)), gain_grad)
 
 
-def route_slots(route_rows, expert_ids, capacity):
-    length = route_rows.shape[0]
-    count_experts = expert_ids.shape[0]
-    picked = jnp.sum(
-        (route_rows[:, :, None] == expert_ids[None, None, :]).astype(jnp.int32), axis=1
-    )
-    before = jnp.cumsum(picked, axis=0) - picked
-    columns = jnp.arange(count_experts, dtype=jnp.int32)[None, :]
-    target = jnp.where(picked > 0, columns * capacity + before, count_experts * capacity)
-    places = jnp.broadcast_to(jnp.arange(length, dtype=jnp.int32)[:, None], target.shape)
-    slots = (
-        jnp.zeros((count_experts * capacity,), jnp.int32)
-        .at[target.reshape(-1)]
-        .set(places.reshape(-1), mode="drop")
-    )
-    filled = jnp.sum(picked, axis=0)
-    valid = (jnp.arange(capacity, dtype=jnp.int32)[None, :] < filled[:, None]).astype(jnp.float32)
-    return (slots.reshape(count_experts, capacity), valid, picked > 0)
+def slot_places(picked):
+    length = picked.shape[1]
+    tokens = jnp.arange(length, dtype=jnp.int32)
+    earlier = (tokens[:, None] < tokens[None, :]).astype(jnp.bfloat16)
+    before = jnp.dot(picked.astype(jnp.bfloat16), earlier, preferred_element_type=jnp.float32)
+    return jnp.where(picked > 0, before.astype(jnp.int32), -1)
 
 
 def block_mask(segment, first_row, block_rows):
@@ -141,7 +134,338 @@
     return (grad_queries, grad_keys, grad_values)
 
 
+STEPS = 32
+LAG = 2
+GATE_ROWS = 512
+
+
+def line_sum_kernel(n, count, *refs):
+    xs, outs = refs[:count], refs[count : 2 * count]
+    lows, highs = refs[2 * count : 3 * count], refs[3 * count : 4 * count]
+    low_recv, high_recv, total_recv, up_send, low_send, high_send = refs[4 * count :]
+    me = lax.axis_index("tensor")
+    root = n // 2
+    has_low, has_high = me > 0, me < n - 1
+    barrier = pltpu.get_barrier_semaphore()
+
+    @pl.when(has_low)
+    def _():
+        pl.semaphore_signal(barrier, inc=1, device_id={"tensor": me - 1}, device_id_type=MESH)
+
+    @pl.when(has_high)
+    def _():
+        pl.semaphore_signal(barrier, inc=1, device_id={"tensor": me + 1}, device_id_type=MESH)
+
+    pl.semaphore_wait(barrier, has_low.astype(jnp.int32) + has_high.astype(jnp.int32))
+
+    def piece(ref, c):
+        rows = ref.shape[0] // STEPS
+        return ref.at[pl.ds(pl.multiple_of(c * rows, rows), rows), :]
+
+    def copies(sources, targets, c, send, recv, to):
+        return [
+            pltpu.make_async_remote_copy(
+                src_ref=piece(source, c),
+                dst_ref=piece(target, c),
+                send_sem=send.at[i, c],
+                recv_sem=recv.at[i, c],
+                device_id={"tensor": to},
+                device_id_type=MESH,
+            )
+            for i, (source, target) in enumerate(zip(sources, targets))
+        ]
+
+    def start(sources, targets, c, send, recv, to):
+        for copy in copies(sources, targets, c, send, recv, to):
+            copy.start()
+
+    def arrived(targets, c, send, recv):
+        for copy in copies(targets, targets, c, send, recv, me):
+            copy.wait_recv()
+
+    def reduce_step(c):
+        for side, inner, held, recv, to in (
+            (me < root, has_low, lows, low_recv, me + 1),
+            (me > root, has_high, highs, high_recv, me - 1),
+        ):
+
+            @pl.when(side & inner)
+            def _():
+                arrived(held, c, up_send, recv)
+                for x, h in zip(xs, held):
+                    piece(h, c)[...] += piece(x, c)[...]
+                start(held, held, c, up_send, recv, to)
+
+            @pl.when(side & jnp.logical_not(inner))
+            def _():
+                start(xs, held, c, up_send, recv, to)
+
+        @pl.when(me == root)
+        def _():
+            arrived(lows, c, up_send, low_recv)
+            if root < n - 1:
+                arrived(highs, c, up_send, high_recv)
+            for x, low, high, out in zip(xs, lows, highs, outs):
+                total = piece(x, c)[...] + piece(low, c)[...]
+                if root < n - 1:
+                    total += piece(high, c)[...]
+                piece(out, c)[...] = total
+            start(outs, outs, c, low_send, total_recv, me - 1)
+            if root < n - 1:
+                start(outs, outs, c, high_send, total_recv, me + 1)
+
+    def total_step(c):
+        @pl.when(me != root)
+        def _():
+            arrived(outs, c, low_send, total_recv)
+
+        @pl.when((me < root) & has_low)
+        def _():
+            start(outs, outs, c, low_send, total_recv, me - 1)
+
+        @pl.when((me > root) & has_high)
+        def _():
+            start(outs, outs, c, high_send, total_recv, me + 1)
+
+    lag = jnp.where(has_low & has_high, LAG, STEPS)
+
+    def step(t, carry):
+        @pl.when(t < STEPS)
+        def _():
+            reduce_step(t)
+
+        @pl.when((t >= lag) & (t - lag < STEPS))
+        def _():
+            total_step(t - lag)
+
+        return carry
+
+    lax.fori_loop(0, 2 * STEPS, step, 0)
+
+    def drain(c, carry):
+        for condition, send in (
+            (me != root, up_send),
+            ((me <= root) & has_low, low_send),
+            ((me >= root) & has_high, high_send),
+        ):
+
+            @pl.when(condition)
+            def _():
+                for copy in copies(xs, lows, c, send, low_recv, me):
+                    copy.wait_send()
+
+        return carry
+
+    lax.fori_loop(0, STEPS, drain, 0)
+
+
+def line_sum(x, extra, n, name):
+    arrays = [x] if extra is None else [x, extra]
+    count = len(arrays)
+    shapes = [jax.ShapeDtypeStruct(array.shape, jnp.float32) for array in arrays]
+    size = sum(array.size for array in arrays)
+    results = pl.pallas_call(
+        functools.partial(line_sum_kernel, n, count),
+        out_shape=shapes,
+        in_specs=[pl.BlockSpec(memory_space=pltpu.VMEM)] * count,
+        out_specs=[pl.BlockSpec(memory_space=pltpu.VMEM)] * count,
+        scratch_shapes=[pltpu.VMEM(array.shape, jnp.float32) for array in arrays * 2]
+        + [pltpu.SemaphoreType.DMA((count, STEPS))] * 6,
+        compiler_params=pltpu.CompilerParams(
+            collective_id=name, has_side_effects=True, vmem_limit_bytes=40 << 20
+        ),
+        cost_estimate=pl.CostEstimate(
+            flops=3 * size, bytes_accessed=8 * size, transcendentals=0
+        ),
+    )(*arrays)
+    return (results[0], None) if extra is None else tuple(results)
+
+
+def expert_kernel(
+    first,
+    chained,
+    count_ref,
+    place_ref,
+    gate_ref,
+    normed_ref,
+    grad_ref,
+    gate_w,
+    up_w,
+    down_w,
+    *refs,
+):
+    if chained:
+        moe_in, back_in = refs[:2]
+        refs = refs[2:]
+    both_out, down_out, moe_out, back_out, gates_out = refs[:5]
+    rows_ref, grads_ref, moe_rows, back_rows, slot_gate, slot_grad, sems = refs[5:]
+    expert, half = pl.program_id(0), pl.program_id(1)
+    halves = pl.num_programs(1)
+    filled = count_ref[first + expert]
+    length = normed_ref.shape[0]
+    block = gate_w.shape[2]
+    started = (expert == 0) & (half == 0)
+
+    if chained:
+        copy_moe = pltpu.make_async_copy(moe_in, moe_out, sems.at[0])
+        copy_back = pltpu.make_async_copy(back_in, back_out, sems.at[1])
+
+        @pl.when(started)
+        def _():
+            copy_moe.start()
+            copy_back.start()
+
+        @pl.when((expert == 0) & (half == halves - 1))
+        def _():
+            copy_moe.wait()
+            copy_back.wait()
+
+    else:
+
+        @pl.when(started)
+        def _():
+            moe_out[...] = jnp.zeros_like(moe_out)
+            back_out[...] = jnp.zeros_like(back_out)
+
+    def run(rows):
+        mask = lax.broadcasted_iota(jnp.int32, (rows, length), 0) == place_ref[0]
+
+        @pl.when(half == 0)
+        def _():
+            picks = jnp.where(mask, 1.0, 0.0).astype(jnp.bfloat16)
+            rows_ref[:rows] = jnp.dot(
+                picks, normed_ref[...], preferred_element_type=jnp.float32
+            ).astype(jnp.bfloat16)
+            grads_ref[:rows] = jnp.dot(
+                picks, grad_ref[...], preferred_element_type=jnp.float32
+            ).astype(jnp.bfloat16)
+            slot_gate[:rows] = jnp.broadcast_to(
+                jnp.sum(jnp.where(mask, gate_ref[0], 0.0), axis=1, keepdims=True), (rows, 128)
+            )
+
+        rows_in = rows_ref[:rows]
+        grad_rows = grads_ref[:rows]
+        gate = slot_gate[:rows, :1]
+        gate_input = jnp.dot(rows_in, gate_w[0], preferred_element_type=jnp.float32)
+        up_input = jnp.dot(rows_in, up_w[0], preferred_element_type=jnp.float32)
+        grad_act = right_inner(grad_rows, down_w[0])
+        sigmoid_val = jax.nn.sigmoid(gate_input)
+        silu_out = gate_input * sigmoid_val
+        hidden = silu_out * up_input
+        activation = (hidden * gate).astype(jnp.bfloat16)
+        column = jnp.sum(grad_act * hidden, axis=1, keepdims=True)
+        grad_hidden = grad_act * gate
+        grad_gate_in = (
+            grad_hidden * up_input * sigmoid_val * (1.0 + gate_input * (1.0 - sigmoid_val))
+        ).astype(jnp.bfloat16)
+        grad_up_in = (grad_hidden * silu_out).astype(jnp.bfloat16)
+        down_out[0] = left_inner(activation, grad_rows)
+        grads = left_inner(rows_in, jnp.concatenate([grad_gate_in, grad_up_in], 1))
+        both_out[0, 0] = grads[:, :block]
+        both_out[0, 1] = grads[:, block:]
+        moe = jnp.dot(activation, down_w[0], preferred_element_type=jnp.float32)
+        back = right_inner(grad_gate_in, gate_w[0]) + right_inner(grad_up_in, up_w[0])
+
+        @pl.when(half == 0)
+        def _():
+            moe_rows[:rows] = moe
+            back_rows[:rows] = back
+            slot_grad[:rows] = jnp.broadcast_to(column, (rows, 128))
+
+        @pl.when((half > 0) & (half < halves - 1))
+        def _():
+            moe_rows[:rows] += moe
+            back_rows[:rows] += back
+            slot_grad[:rows] += jnp.broadcast_to(column, (rows, 128))
+
+        @pl.when(half == halves - 1)
+        def _():
+            picks = jnp.where(mask, 1.0, 0.0).astype(jnp.bfloat16)
+            moe_out[...] += left_inner(picks, (moe_rows[:rows] + moe).astype(jnp.bfloat16))
+            back_out[...] += left_inner(picks, (back_rows[:rows] + back).astype(jnp.bfloat16))
+            total = slot_grad[:rows, :1] + column
+            gates_out[0] = jnp.sum(jnp.where(mask, total, 0.0), axis=0, keepdims=True)
+
+    sizes = (128, 256, CAP)
+    for low, rows in zip((-1,) + sizes[:-1], sizes):
+        pl.when((filled > low) & (filled <= rows))(functools.partial(run, rows))
+
+
+def expert_stage(first, last, counts, places, gate_rows, normed_b, grad_b, gate_w, up_w, down_w, sums):
+    number = last - first
+    length, width = normed_b.shape
+    hidden = gate_w.shape[2]
+    block = 256
+    halves = hidden // block
+    experts = places.shape[0]
+    chained = sums is not None
+    whole = lambda e, h, c: (0, 0)
+    row_spec = pl.BlockSpec((1, 1, length), lambda e, h, c: (first + e, 0, 0))
+    once = pl.Buffered(1)
+    in_specs = [
+        row_spec,
+        row_spec,
+        pl.BlockSpec((length, width), whole, pipeline_mode=once),
+        pl.BlockSpec((length, width), whole, pipeline_mode=once),
+        pl.BlockSpec((1, width, block), lambda e, h, c: (first + e, 0, h)),
+        pl.BlockSpec((1, width, block), lambda e, h, c: (first + e, 0, h)),
+        pl.BlockSpec((1, block, width), lambda e, h, c: (first + e, h, 0)),
+    ]
+    args = [
+        counts,
+        places.reshape(experts, 1, length),
+        gate_rows.reshape(experts, 1, length),
+        normed_b,
+        grad_b,
+        gate_w,
+        up_w,
+        down_w,
+    ]
+    if chained:
+        in_specs += [pl.BlockSpec(memory_space=pl.ANY)] * 2
+        args += [sums[0], sums[1]]
+    both, down, moe, back, gates = pl.pallas_call(
+        functools.partial(expert_kernel, first, chained),
+        out_shape=[
+            jax.ShapeDtypeStruct((number, 2, width, hidden), jnp.float32),
+            jax.ShapeDtypeStruct((number, hidden, width), jnp.float32),
+            jax.ShapeDtypeStruct((length, width), jnp.float32),
+            jax.ShapeDtypeStruct((length, width), jnp.float32),
+            jax.ShapeDtypeStruct((number, 1, length), jnp.float32),
+        ],
+        grid_spec=pltpu.PrefetchScalarGridSpec(
+            num_scalar_prefetch=1,
+            grid=(number, halves),
+            in_specs=in_specs,
+            out_specs=[
+                pl.BlockSpec((1, 2, width, block), lambda e, h, c: (e, 0, 0, h)),
+                pl.BlockSpec((1, block, width), lambda e, h, c: (e, h, 0)),
+                pl.BlockSpec((length, width), whole, pipeline_mode=once),
+                pl.BlockSpec((length, width), whole, pipeline_mode=once),
+                pl.BlockSpec((1, 1, length), lambda e, h, c: (e, 0, 0)),
+            ],
+            scratch_shapes=[
+                pltpu.VMEM((CAP, width), jnp.bfloat16),
+                pltpu.VMEM((CAP, width), jnp.bfloat16),
+                pltpu.VMEM((CAP, width), jnp.float32),
+                pltpu.VMEM((CAP, width), jnp.float32),
+                pltpu.VMEM((CAP, 128), jnp.float32),
+                pltpu.VMEM((CAP, 128), jnp.float32),
+                pltpu.SemaphoreType.DMA((2,)),
+            ],
+        ),
+        compiler_params=pltpu.CompilerParams(
+            dimension_semantics=("arbitrary", "arbitrary"), vmem_limit_bytes=60 << 20
+        ),
+        cost_estimate=pl.CostEstimate(
+            flops=number * 8 * 10**9, bytes_accessed=number * 14 * 10**6, transcendentals=0
+        ),
+    )(*args)
+    return ((both, down), (moe, back, gates))
+
+
 def on_device(
+    ring,
     tokens,
     cotangent,
     segment_ids,
@@ -203,8 +527,8 @@
 
     attended, logsum = lax.map(forward_block, (query_blocks, first_rows))
     attended_flat = attended.reshape(length, heads_local * HEAD)
-    attn_out = lax.psum(
-        jnp.dot(attended_flat, out_weight, preferred_element_type=jnp.float32), "tensor"
+    attn_out, unused = line_sum(
+        jnp.dot(attended_flat, out_weight, preferred_element_type=jnp.float32), None, ring, 1
     )
     middle = hidden_in + RESIDUAL * attn_out
     normed_two, unit_two, recip_two = rms_forward(middle, ffn_gain)
@@ -216,73 +540,40 @@
     gate_probs = raised / jnp.sum(raised, axis=-1, keepdims=True)
     first_expert = lax.axis_index("tensor") * experts_local
     local_ids = first_expert + jnp.arange(experts_local, dtype=jnp.int32)
-    slot_token, valid, unused = route_slots(routes, local_ids, CAP)
-    gate_local = lax.dynamic_slice_in_dim(gate_probs, first_expert, experts_local, 1)
-    gate_slots = jnp.take_along_axis(jnp.transpose(gate_local), slot_token, axis=1) * valid
-    rows_in = normed_two_b[slot_token]
-
-    def expert_inputs(expert_rows_in):
-        gate_input = jnp.einsum(
-            "ecd,edf->ecf", expert_rows_in, gate_weight, preferred_element_type=jnp.float32
+    picked = jnp.sum((routes[None, :, :] == local_ids[:, None, None]).astype(jnp.int32), axis=2)
+    places = slot_places(picked)
+    counts = jnp.sum(picked, axis=1)
+    gate_rows = jnp.transpose(lax.dynamic_slice_in_dim(gate_probs, first_expert, experts_local, 1))
+    grad_moe_b = (RESIDUAL * cotangent.astype(jnp.float32)).astype(jnp.bfloat16)
+    middle_expert = experts_local // 2
+    grads_first, sums = expert_stage(
+        0, middle_expert, counts, places, gate_rows, normed_two_b, grad_moe_b,
+        gate_weight, up_weight, down_weight, None,
+    )
+    grads_last, sums_last = expert_stage(
+        middle_expert, experts_local, counts, places, gate_rows, normed_two_b, grad_moe_b,
+        gate_weight, up_weight, down_weight, sums,
+    )
+    moe_part, grad_normed_part, unused = sums_last
+    grad_gates_local = jnp.concatenate([sums[2], sums_last[2]], 0)
+    shard_up_down = [
+        (
+            lax.psum_scatter(both, "dp", scatter_dimension=2, tiled=True),
+            lax.psum_scatter(down, "dp", scatter_dimension=1, tiled=True),
         )
-        up_input = jnp.einsum(
-            "ecd,edf->ecf", expert_rows_in, up_weight, preferred_element_type=jnp.float32
-        )
-        return (gate_input, up_input)
-
-    gate_input, up_input = expert_inputs(rows_in)
-    activation = (
-        gate_input * jax.nn.sigmoid(gate_input) * up_input * gate_slots[:, :, None]
-    ).astype(jnp.bfloat16)
-    expert_rows = jnp.einsum(
-        "ecf,efd->ecd", activation, down_weight, preferred_element_type=jnp.float32
-    )
-    moe_part = jax.ops.segment_sum(
-        expert_rows.reshape(-1, width), slot_token.reshape(-1), num_segments=length
-    )
-    moe_out = lax.psum(moe_part, "tensor")
-    output = (middle + RESIDUAL * moe_out).astype(jnp.bfloat16)
-    grad_moe_b = (RESIDUAL * cotangent.astype(jnp.float32)).astype(jnp.bfloat16)
-    normed_again, grad_moe_b = lax.optimization_barrier((normed_two_b, grad_moe_b))
-    rows_back = normed_again[slot_token]
-    back_gate, back_up = expert_inputs(rows_back)
-    grad_rows = grad_moe_b[slot_token]
-    sigmoid_val = jax.nn.sigmoid(back_gate)
-    silu_out = back_gate * sigmoid_val
-    hidden = silu_out * back_up
-    activation_back = (hidden * gate_slots[:, :, None]).astype(jnp.bfloat16)
-    grad_down = jnp.einsum(
-        "ecf,ecd->efd", activation_back, grad_rows, preferred_element_type=jnp.float32
-    )
-    grad_act = jnp.einsum(
-        "ecd,efd->ecf", grad_rows, down_weight, preferred_element_type=jnp.float32
-    )
-    grad_column = jnp.sum(grad_act * hidden, axis=-1) * valid
-    grad_hidden = grad_act * gate_slots[:, :, None]
-    grad_gate_in = (
-        grad_hidden * back_up * sigmoid_val * (1.0 + back_gate * (1.0 - sigmoid_val))
-    ).astype(jnp.bfloat16)
-    grad_up_in = (grad_hidden * silu_out).astype(jnp.bfloat16)
-    grad_gate = jnp.einsum(
-        "ecd,ecf->edf", rows_back, grad_gate_in, preferred_element_type=jnp.float32
-    )
-    grad_up = jnp.einsum("ecd,ecf->edf", rows_back, grad_up_in, preferred_element_type=jnp.float32)
-    grad_rows_in = jnp.einsum(
-        "ecf,edf->ecd", grad_gate_in, gate_weight, preferred_element_type=jnp.float32
-    ) + jnp.einsum("ecf,edf->ecd", grad_up_in, up_weight, preferred_element_type=jnp.float32)
-    expert_grads = (grad_gate, grad_up, grad_down)
-    grad_normed_part = jax.ops.segment_sum(
-        grad_rows_in.reshape(-1, width), slot_token.reshape(-1), num_segments=length
-    )
-    grad_gates_local = (
-        jnp.zeros((length, experts_local), jnp.float32)
-        .at[slot_token, jnp.arange(experts_local, dtype=jnp.int32)[:, None]]
-        .add(grad_column)
-    )
+        for both, down in (grads_first, grads_last)
+    ]
     grad_gates_part = lax.dynamic_update_slice_in_dim(
-        jnp.zeros((length, experts_all), jnp.float32), grad_gates_local, first_expert, 1
-    )
-    grad_normed_sum, grad_gates = lax.psum((grad_normed_part, grad_gates_part), "tensor")
+        jnp.zeros((experts_all, length), jnp.float32),
+        grad_gates_local.reshape(experts_local, length),
+        first_expert,
+        0,
+    ).reshape(-1, 128)
+    grad_gates_part = jnp.pad(grad_gates_part, ((0, GATE_ROWS - grad_gates_part.shape[0]), (0, 0)))
+    grad_normed_sum, gates_sum = line_sum(grad_normed_part, grad_gates_part, ring, 2)
+    grad_gates = jnp.transpose(
+        gates_sum[: experts_all * length // 128].reshape(experts_all, length)
+    )
     weighted = jnp.sum(gate_probs * grad_gates, axis=-1, keepdims=True)
     grad_logits_b = (gate_probs * (grad_gates - weighted)).astype(jnp.bfloat16)
     grad_router = left_inner(normed_two_b, grad_logits_b)
@@ -335,37 +626,51 @@
         .astype(jnp.bfloat16)
         .reshape(length, kv_local * HEAD)
     )
-    grad_query = left_inner(normed_b, grad_queries_b)
-    grad_key = left_inner(normed_b, grad_keys_b)
-    grad_value = left_inner(normed_b, grad_values_b)
+    grads_wide = jnp.concatenate([grad_queries_b, grad_keys_b, grad_values_b], 1)
+    grad_projections = left_inner(normed_b, grads_wide)
     grad_normed_local = (
         right_inner(grad_queries_b, query_weight)
         + right_inner(grad_keys_b, key_weight)
         + right_inner(grad_values_b, value_weight)
     )
-    grad_normed = lax.psum(grad_normed_local, "tensor")
+    grad_normed, unused = line_sum(grad_normed_local, None, ring, 3)
     grad_from_first, grad_attn_gain = rms_backward(grad_normed, unit_one, recip_one, attn_gain)
     grad_tokens = grad_middle + grad_from_first
-    summed = tuple(
-        (
-            lax.psum_scatter(grad_attn_gain, "dp", scatter_dimension=0, tiled=True),
-            lax.psum_scatter(grad_query, "dp", scatter_dimension=0, tiled=True),
-            lax.psum_scatter(grad_key, "dp", scatter_dimension=0, tiled=True),
-            lax.psum_scatter(grad_value, "dp", scatter_dimension=0, tiled=True),
-            lax.psum_scatter(grad_out, "dp", scatter_dimension=1, tiled=True),
-            lax.psum_scatter(grad_ffn_gain, "dp", scatter_dimension=0, tiled=True),
-            lax.psum_scatter(grad_router, "dp", scatter_dimension=0, tiled=True),
-            lax.psum_scatter(expert_grads[0], "dp", scatter_dimension=1, tiled=True),
-            lax.psum_scatter(expert_grads[1], "dp", scatter_dimension=1, tiled=True),
-            lax.psum_scatter(expert_grads[2], "dp", scatter_dimension=1, tiled=True),
-        )
-    )
-    return (output, grad_tokens) + summed
+    moe_out, unused = line_sum(moe_part, None, ring, 4)
+    output = (middle + RESIDUAL * moe_out).astype(jnp.bfloat16)
+    small = jnp.concatenate(
+        [
+            grad_projections,
+            left_inner(grad_branch_b, attended_flat),
+            grad_router,
+            grad_ffn_gain[:, None],
+            grad_attn_gain[:, None],
+        ],
+        1,
+    )
+    small = lax.psum_scatter(small, "dp", scatter_dimension=0, tiled=True)
+    wide_q, wide_k = heads_local * HEAD, kv_local * HEAD
+    at = [0, wide_q, wide_q + wide_k, wide_q + 2 * wide_k]
+    at += [at[3] + wide_q, at[3] + wide_q + experts_all]
+    return (
+        output,
+        grad_tokens,
+        small[:, at[5] + 1],
+        small[:, at[0] : at[1]],
+        small[:, at[1] : at[2]],
+        small[:, at[2] : at[3]],
+        jnp.transpose(small[:, at[3] : at[4]]),
+        small[:, at[5]],
+        small[:, at[4] : at[5]],
+        jnp.concatenate([both[:, 0] for both, down in shard_up_down], 0),
+        jnp.concatenate([both[:, 1] for both, down in shard_up_down], 0),
+        jnp.concatenate([down for both, down in shard_up_down], 0),
+    )
 
 
 def solution(mesh):
     return jax.shard_map(
-        on_device,
+        functools.partial(on_device, mesh.shape["tensor"]),
         mesh=mesh,
         in_specs=(
             P("dp", None),

time: 2170 us -> 1750 us (0.81)
  Pallas kernels: 0 us -> 758 us
  waiting for transfers between devices: 1370 us -> 639 us
  matrix products: 326 us -> 101 us
  other arithmetic: 185 us -> 70.8 us
  local copies, waits for them, and re-layouts: 225 us -> 137 us
  blocking collectives: 24.4 us -> 0 us
    pallas_call x0 -> x6, Pallas kernels: none -> 758 us  [the longest x4 605 us: line_sum(): pl.pallas_call(functools.partial(line_sum_kernel, n, count), out_shape=sh...]
    psum x3 -> x0, waiting for transfers between devices: 655 us -> none  [the longest x1 371 us: on_device(): moe_out = lax.psum(moe_part, 'tensor')]
    dot_general x10 -> x1, matrix products: 196 us -> 0.32 us  [slot_places(): jnp.dot(picked.astype(jnp.bfloat16), earlier, preferred_element_type=jnp....]
    reduce_scatter x7 -> x4, waiting for transfers between devices: 712 us -> 598 us  [the longest x2 379 us: on_device(): lax.psum_scatter(both, 'dp', scatter_dimension=2, tiled=True)]
    gather x6 -> x0, local copies, waits for them, and re-layouts: 108 us -> none  [the longest x3 29.3 us: on_device(): jnp.take_along_axis(jnp.transpose(gate_local), slot_token, axis=1) * valid]
    scatter-add x2 -> x0, other arithmetic: 88.4 us -> none  [the longest x1 44.4 us: on_device(): jax.ops.segment_sum(expert_rows.reshape(-1, width), slot_token.reshape(-1...]
    unnamed x12 -> x6, waiting for transfers between devices: 0.2 us -> 41.5 us
    scatter x1 -> x0, local copies, waits for them, and re-layouts: 37.9 us -> none  [route_slots(): slots = jnp.zeros((count_experts * capacity,), jnp.int32).at[target.resha...]
  transfers between devices with their start and end apart: 11 -> 5, of which waited for: 9 -> 5; matrix products, arithmetic and copies ran while one was open for 13% -> 3% of each run, Pallas kernels for 0% -> 0%
where the time goes in v1:
time: 1750 us; the launch traced here: 1730 us
  Pallas kernels  758 us (43%)
  waiting for transfers between devices  639 us (37%)
  local copies, waits for them, and re-layouts  137 us (8%)
  matrix products  101 us (6%)
  other arithmetic  70.8 us (4%)
    pallas_call x4, Pallas kernels, line_sum(): pl.pallas_call(functools.partial(line_sum_kernel, n, count), out_shape=sh...  605 us
    reduce_scatter x2, waiting for transfers between devices, on_device(): lax.psum_scatter(both, 'dp', scatter_dimension=2, tiled=True)  379 us
    reduce_scatter x2, waiting for transfers between devices, on_device(): lax.psum_scatter(down, 'dp', scatter_dimension=1, tiled=True)  219 us
    pallas_call x2, Pallas kernels, expert_stage(): pl.pallas_call(functools.partial(expert_kernel, first, chained), out_shap...  153 us
    unnamed x6, waiting for transfers between devices  41.5 us
  transfers between devices with their start and end apart: 5, of which 5 were waited for; matrix products, arithmetic and copies ran while one was open for 3% of the time, Pallas kernels for 0%

profile of v1, /device:TPU:8, one launch (start us, length us, event | category | flops | bytes accessed | tf_op | source)
XLA Modules:
  0.0 1731.0 jit_solution(4673919086997539347)
XLA Ops:
  45.8 39.9 %while.28 = (s32[]{:T(128)}, bf16[2,512,6,64]{1,3,2,0:T(8,128)(2,1)}, f32[2,6,512,1]{2,1,3,0:T(8,128)}, s32[2]{0:T(128)S(1)}, s32[1024]{0:T(1024)S(1)}, /*index=...) while((s32[]{:T(128)}, ...), condition=%wide.region_4.5_spmd.clone, body=%wide.region_2.4_spmd.clone.sunk | while | flops 829093376 | bytes 31488248 | solution.py:528
  50.1 6.6 exponential_reduce_fusion.2
  56.7 8.5 fusion.140
  69.9 6.6 exponential_reduce_fusion.2
  76.5 8.5 fusion.140
  94.3 154.8 %shard_map.229 = f32[1024,1536]{1,0:T(8,128)S(1)} custom-call(f32[1024,1536]{1,0:T(8,128)S(1)} %fusion.90.refs_0_), custom_call_target="tpu_custom_call" | custom-call | flops 4718592 | bytes 12582912 | tf_op jit(solution)/shard_map/pallas_call | solution.py:267
  259.7 86.8 %shard_map.230 = (f32[5,2,1536,512]{3,2,1,0:T(8,128)}, f32[5,512,1536]{2,1,0:T(8,128)}, f32[1024,1536]{1,0:T(8,128)}, f32[1024,1536]{1,0:T(8,128)}, f32[5,1,1024]{2,1,0:T(1,128)}) custom-call(s32[10]{0:T(128)} %get-tuple-element.361.count_ref, s32[10,1,1024]{2,1,0:T(1,128)} %reshape.312.place_ref, f32[10,1,1024]{2,1,0:T(1,128)} %reshape.313.gate_ref, ...), custom_call_target="tpu_custom_call" | custom-call | flops 40000000000 | bytes 70000000 | tf_op jit(solution)/shard_map/pallas_call | solution.py:427
  346.6 66.1 %shard_map.231 = (f32[5,2,1536,512]{3,2,1,0:T(8,128)}, f32[5,512,1536]{2,1,0:T(8,128)}, f32[1024,1536]{1,0:T(8,128)}, f32[1024,1536]{1,0:T(8,128)}, f32[5,1,1024]{2,1,0:T(1,128)}) custom-call(s32[10]{0:T(128)} %get-tuple-element.361.count_ref, s32[10,1,1024]{2,1,0:T(1,128)} %reshape.312.place_ref, f32[10,1,1024]{2,1,0:T(1,128)} %reshape.313.gate_ref, ...), custom_call_target="tpu_custom_call" | custom-call | flops 40000000000 | bytes 70000000 | tf_op jit(solution)/shard_map/pallas_call | solution.py:427
  415.5 148.1 %shard_map.232 = f32[1024,1536]{1,0:T(8,128)S(1)} custom-call(f32[1024,1536]{1,0:T(8,128)S(1)} %copy-done.5), custom_call_target="tpu_custom_call" | custom-call | flops 4718592 | bytes 12582912 | tf_op jit(solution)/shard_map/pallas_call | solution.py:267
  569.7 156.2 %shard_map.233 = (f32[1024,1536]{1,0:T(8,128)S(1)}, f32[512,128]{1,0:T(8,128)S(1)}) custom-call(f32[1024,1536]{1,0:T(8,128)S(1)} %copy-done.4, f32[512,128]{1,0:T(8,128)S(1)} %pad.4.refs_1_), custom_call_target="tpu_custom_call" | custom-call | flops 4915200 | bytes 13107200 | tf_op jit(solution)/shard_map/pallas_call | solution.py:267
  732.2 7.5 multiply_reduce_fusion
  758.5 78.3 %while.29 = (s32[]{:T(128)}, f32[1024,6,64]{0,2,1:T(8,128)S(1)}, f32[1024,6,64]{0,2,1:T(8,128)}, f32[2,512,6,64]{1,0,3,2:T(2,128)}, bf16[2,512,6,64]{1,3,2,0:T(8...) while((s32[]{:T(128)}, f32[1024,6,64]{0,2,1:T(8,128)S(1)}, ...), condition=%wide.region_14.15_spmd.clone, body=%wide.region_12.14_spmd.clone.sunk | while | flops 2051798528 | bytes 78469400 | solution.py:605
  782.5 14.9 dynamic_update_slice.26
  821.7 14.9 dynamic_update_slice.26
  854.2 146.1 %shard_map.234 = f32[1024,1536]{1,0:T(8,128)S(1)} custom-call(f32[1024,1536]{1,0:T(8,128)S(1)} %add_add_fusion.refs_0_), custom_call_target="tpu_custom_call" | custom-call | flops 4718592 | bytes 12582912 | tf_op jit(solution)/shard_map/pallas_call | solution.py:267
  1005.0 14.9 concatenate.62
  1019.9 7.6 copy.82
  1029.0 24.0 %copy.76 = f32[5,2,1536,512]{3,2,0,1:T(8,128)} copy(f32[5,2,1536,512]{3,2,1,0:T(8,128)} %get-tuple-element.154) | data formatting | bytes 62914560 | tf_op jit(solution)/shard_map/pallas_call | solution.py:427
  1053.6 9.5 fusion.52
  1063.1 39.5 %reduce-scatter.16.cloned.1.call-done = f32[192,1066]{1,0:T(8,128)} async-done(((f32[1536,1066]{1,0:T(8,128)}), f32[192,1066]{1,0:T(8,128)}) %reduce-scatter.16.cloned.1.call-update) | async-done | bytes 818704
  1110.1 105.6 %reduce-scatter.12.cloned.1.call-done = f32[5,64,1536]{2,1,0:T(8,128)} async-done(((f32[5,512,1536]{2,1,0:T(8,128)}), f32[5,64,1536]{2,1,0:T(8,128)}) %reduce-scatter.12.cloned.1.call-update) | async-done | bytes 1966096 | tf_op jit(solution)/shard_map/reduce_scatter | solution.py:562
  1215.7 113.1 %reduce-scatter.14.cloned.1.call-done = f32[5,64,1536]{2,1,0:T(8,128)} async-done(((f32[5,512,1536]{2,1,0:T(8,128)}), f32[5,64,1536]{2,1,0:T(8,128)}) %reduce-scatter.14.cloned.1.call-update) | async-done | bytes 1966096 | tf_op jit(solution)/shard_map/reduce_scatter | solution.py:562
  1333.2 189.4 %reduce-scatter.8.cloned.1.call-done = f32[5,2,192,512]{3,2,0,1:T(8,128)} async-done(((f32[5,2,1536,512]{3,2,0,1:T(8,128)}), f32[5,2,192,512]{3,2,0,1:T(8,128)}) %reduce-scatter.8.cloned.1.call-update) | async-done | bytes 3932176 | tf_op jit(solution)/shard_map/reduce_scatter | solution.py:561
  1526.6 189.8 %reduce-scatter.10.cloned.1.call-done = f32[5,2,192,512]{3,2,1,0:T(8,128)} async-done(((f32[5,2,1536,512]{3,2,1,0:T(8,128)}), f32[5,2,192,512]{3,2,1,0:T(8,128)}) %reduce-scatter.10.cloned.1.call-update) | async-done | bytes 3932176 | tf_op jit(solution)/shard_map/reduce_scatter | solution.py:561
  (255 shorter events, 188.2 us)
Async XLA Ops:
  7.2 85.3 %copy-start = (bf16[384,1536]{1,0:T(8,128)(2,1)S(1)}, bf16[384,1536]{1,0:T(8,128)(2,1)}, u32[]{:S(2)}) copy-start(bf16[384,1536]{1,0:T(8,128)(2,1)} %param.26) | copy-start | bytes 3538948
  7.2 15.9 copy-start.41
  7.2 15.9 copy-start.32
  7.2 1095.4 %reduce-scatter.16.cloned.1.call-start = ((), (), s32[]{:S(2)}) async-start(), calls=%async_computation.9 | async-start | bytes 7962624
  8.8 14.3 copy-start.9
  11.5 14.4 copy-start.39
  34.0 11.7 copy-start.27
  56.7 8.5 copy-start.35
  76.5 8.6 copy-start.35
  85.7 8.6 copy-start.13
  94.3 154.8 %copy-start.10 = (bf16[1024,1536]{1,0:T(8,128)(2,1)S(1)}, bf16[1024,1536]{1,0:T(8,128)(2,1)}, u32[]{:S(2)}) copy-start(bf16[1024,1536]{1,0:T(8,128)(2,1)} %param.18) | copy-start | bytes 9437188
  415.5 150.8 %copy-start.44 = (f32[5,1,1024]{2,1,0:T(1,128)S(1)}, f32[5,1,1024]{2,1,0:T(1,128)}, u32[]{:S(2)}) copy-start(f32[5,1,1024]{2,1,0:T(1,128)} %get-tuple-element.146) | copy-start | bytes 61444
  415.5 150.8 %copy-start.45 = (f32[5,1,1024]{2,1,0:T(1,128)S(1)}, f32[5,1,1024]{2,1,0:T(1,128)}, u32[]{:S(2)}) copy-start(f32[5,1,1024]{2,1,0:T(1,128)} %get-tuple-element.147) | copy-start | bytes 61444
  728.9 10.8 slice-start
  728.9 10.8 slice-start.2
  732.2 8.1 slice-start.3
  732.2 9.4 copy-start.16
  750.0 8.5 copy-start.7
  750.0 8.5 copy-start.37
  758.5 80.2 %copy-start.24 = (f32[1024,64]{0,1:T(8,128)S(1)}, f32[1024,64]{0,1:T(8,128)}, u32[]{:S(2)}) copy-start(f32[1024,64]{0,1:T(8,128)} %copy-done.23) | copy-start | bytes 786436
  1027.5 188.2 %reduce-scatter.12.cloned.1.call-start = ((), (), s32[]{:S(2)}) async-start(), calls=%async_computation.7 | async-start | bytes 17694720 | tf_op jit(solution)/shard_map/reduce_scatter | solution.py:562
  1028.3 300.6 %reduce-scatter.14.cloned.1.call-start = ((), (), s32[]{:S(2)}) async-start(), calls=%async_computation.8 | async-start | bytes 17694720 | tf_op jit(solution)/shard_map/reduce_scatter | solution.py:562
  1029.0 493.6 %reduce-scatter.8.cloned.1.call-start = ((), (), s32[]{:S(2)}) async-start(), calls=%async_computation.5 | async-start | bytes 35389440 | tf_op jit(solution)/shard_map/reduce_scatter | solution.py:561
  1053.0 663.3 %reduce-scatter.10.cloned.1.call-start = ((), (), s32[]{:S(2)}) async-start(), calls=%async_computation.6 | async-start | bytes 35389440 | tf_op jit(solution)/shard_map/reduce_scatter | solution.py:561
  (34 other events, 99.9 us)
Sparse Core Ops, SparseCore 0:
  1027.6 74.9 reduce-scatter.15
  1106.5 109.1 reduce-scatter.11
  1219.7 109.1 reduce-scatter.13
  1332.8 189.7 reduce-scatter.7
  1526.5 189.8 reduce-scatter.9

commit v2 on v1

v2 whole, which is shorter than its diff:
```python
import functools

import jax
import jax.numpy as jnp
from jax import lax
from jax.experimental import pallas as pl
from jax.experimental.pallas import tpu as pltpu
from jax.sharding import PartitionSpec as P

MESH = pl.DeviceIdType.MESH

HEAD = 64
CAP = 384


EPSILON = 1e-06
RESIDUAL = 0.22
ATTN_SCALE = 0.015625
ROPE_BASE = 10000.0


def left_inner(first, second):
    return lax.dot_general(
        first, second, (((0,), (0,)), ((), ())), preferred_element_type=jnp.float32
    )


def right_inner(first, second):
    return lax.dot_general(
        first, second, (((1,), (1,)), ((), ())), preferred_element_type=jnp.float32
    )


def doc_openings(segment):
    return jnp.sum((segment[None, :] < segment[:, None]).astype(jnp.int32), axis=1)


def rope_tables(opening, head_size):
    halfway = head_size // 2
    spread = jnp.arange(halfway, dtype=jnp.float32) * (2.0 / head_size)
    inverse = jnp.power(ROPE_BASE, -spread)
    places = jnp.arange(opening.shape[0], dtype=jnp.int32)
    angles = (places - opening).astype(jnp.float32)[:, None] * inverse[None, :]
    cosine, sine = jnp.cos(angles), jnp.sin(angles)
    none = jnp.zeros_like(sine)
    return (
        jnp.concatenate([cosine] * 4, 1),
        jnp.concatenate([-sine, none] * 2, 1),
        jnp.concatenate([none, sine] * 2, 1),
    )


def pad_columns(weight):
    missing = -weight.shape[1] % 128
    return weight if missing == 0 else jnp.pad(weight, ((0, 0), (0, missing)))


def rms_forward(hidden, gain):
    recip = lax.rsqrt(jnp.mean(hidden * hidden, axis=-1, keepdims=True) + EPSILON)
    unit = hidden * recip
    return (unit * gain, unit, recip)


def rms_backward(gradient, unit, recip, gain):
    gain_grad = jnp.sum(gradient * unit, axis=0)
    scaled = gradient * gain
    return (recip * (scaled - unit * jnp.mean(scaled * unit, axis=-1, keepdims=True)), gain_grad)


def slot_places(picked):
    length = picked.shape[1]
    tokens = jnp.arange(length, dtype=jnp.int32)
    earlier = (tokens[:, None] < tokens[None, :]).astype(jnp.bfloat16)
    before = jnp.dot(picked.astype(jnp.bfloat16), earlier, preferred_element_type=jnp.float32)
    return jnp.where(picked > 0, before.astype(jnp.int32), -1)


STEPS = 32
LAG = 2
GATE_ROWS = 512


def line_stages(n, xs, outs, scratch):
    count = len(xs)
    lows, highs = scratch[:count], scratch[count : 2 * count]
    low_recv, high_recv, total_recv, up_send, low_send, high_send = scratch[2 * count :]
    me = lax.axis_index("tensor")
    root = n // 2
    has_low, has_high = me > 0, me < n - 1

    def begin(others=()):
        barrier = pltpu.get_barrier_semaphore()
        for other in others:
            pl.semaphore_signal(barrier, inc=1, device_id=other, device_id_type=MESH)

        @pl.when(has_low)
        def _():
            pl.semaphore_signal(barrier, inc=1, device_id={"tensor": me - 1}, device_id_type=MESH)

        @pl.when(has_high)
        def _():
            pl.semaphore_signal(barrier, inc=1, device_id={"tensor": me + 1}, device_id_type=MESH)

        pl.semaphore_wait(
            barrier, len(others) + has_low.astype(jnp.int32) + has_high.astype(jnp.int32)
        )

    def piece(ref, c):
        rows = ref.shape[0] // STEPS
        return ref.at[pl.ds(pl.multiple_of(c * rows, rows), rows), :]

    def copies(sources, targets, c, send, recv, to):
        return [
            pltpu.make_async_remote_copy(
                src_ref=piece(source, c),
                dst_ref=piece(target, c),
                send_sem=send.at[i, c],
                recv_sem=recv.at[i, c],
                device_id={"tensor": to},
                device_id_type=MESH,
            )
            for i, (source, target) in enumerate(zip(sources, targets))
        ]

    def start(sources, targets, c, send, recv, to):
        for copy in copies(sources, targets, c, send, recv, to):
            copy.start()

    def arrived(targets, c, send, recv):
        for copy in copies(targets, targets, c, send, recv, me):
            copy.wait_recv()

    def reduce_step(c):
        for side, inner, held, recv, to in (
            (me < root, has_low, lows, low_recv, me + 1),
            (me > root, has_high, highs, high_recv, me - 1),
        ):

            @pl.when(side & inner)
            def _():
                arrived(held, c, up_send, recv)
                for x, h in zip(xs, held):
                    piece(h, c)[...] += piece(x, c)[...]
                start(held, held, c, up_send, recv, to)

            @pl.when(side & jnp.logical_not(inner))
            def _():
                start(xs, held, c, up_send, recv, to)

        @pl.when(me == root)
        def _():
            arrived(lows, c, up_send, low_recv)
            if root < n - 1:
                arrived(highs, c, up_send, high_recv)
            for x, low, high, out in zip(xs, lows, highs, outs):
                total = piece(x, c)[...] + piece(low, c)[...]
                if root < n - 1:
                    total += piece(high, c)[...]
                piece(out, c)[...] = total
            start(outs, outs, c, low_send, total_recv, me - 1)
            if root < n - 1:
                start(outs, outs, c, high_send, total_recv, me + 1)

    def total_step(c):
        @pl.when(me != root)
        def _():
            arrived(outs, c, low_send, total_recv)

        @pl.when((me < root) & has_low)
        def _():
            start(outs, outs, c, low_send, total_recv, me - 1)

        @pl.when((me > root) & has_high)
        def _():
            start(outs, outs, c, high_send, total_recv, me + 1)

    lag = jnp.where(has_low & has_high, LAG, STEPS)

    def step(t, carry):
        @pl.when(t < STEPS)
        def _():
            reduce_step(t)

        @pl.when((t >= lag) & (t - lag < STEPS))
        def _():
            total_step(t - lag)

        return carry

    def finish():
        def drain(c, carry):
            for condition, send in (
                (me != root, up_send),
                ((me <= root) & has_low, low_send),
                ((me >= root) & has_high, high_send),
            ):

                @pl.when(condition)
                def _():
                    for copy in copies(xs, lows, c, send, low_recv, me):
                        copy.wait_send()

            return carry

        lax.fori_loop(0, STEPS, drain, 0)

    return begin, step, finish


def line_scratch(arrays):
    return [pltpu.VMEM(array.shape, jnp.float32) for array in arrays * 2] + [
        pltpu.SemaphoreType.DMA((len(arrays), STEPS))
    ] * 6


def line_sum_kernel(n, count, *refs):
    begin, step, finish = line_stages(n, refs[:count], refs[count : 2 * count], refs[2 * count :])
    begin()
    lax.fori_loop(0, 2 * STEPS, step, 0)
    finish()


def line_sum(x, extra, n, name):
    arrays = [x] if extra is None else [x, extra]
    count = len(arrays)
    shapes = [jax.ShapeDtypeStruct(array.shape, jnp.float32) for array in arrays]
    size = sum(array.size for array in arrays)
    results = pl.pallas_call(
        functools.partial(line_sum_kernel, n, count),
        out_shape=shapes,
        in_specs=[pl.BlockSpec(memory_space=pltpu.VMEM)] * count,
        out_specs=[pl.BlockSpec(memory_space=pltpu.VMEM)] * count,
        scratch_shapes=line_scratch(arrays),
        compiler_params=pltpu.CompilerParams(
            collective_id=name, has_side_effects=True, vmem_limit_bytes=40 << 20
        ),
        cost_estimate=pl.CostEstimate(
            flops=3 * size, bytes_accessed=8 * size, transcendentals=0
        ),
    )(*arrays)
    return (results[0], None) if extra is None else tuple(results)


def expert_kernel(
    parts,
    first,
    chained,
    count_ref,
    place_ref,
    gate_ref,
    normed_ref,
    grad_ref,
    gate_w,
    up_w,
    down_w,
    *refs,
):
    if chained:
        moe_in, back_in = refs[:2]
        refs = refs[2:]
    grads_out, moe_out, back_out, gates_out = refs[:4]
    rows_ref, grads_ref, moe_rows, back_rows, slot_gate, slot_grad, sems = refs[4:]
    expert, half = pl.program_id(0), pl.program_id(1)
    halves = pl.num_programs(1)
    filled = count_ref[first + expert]
    length = normed_ref.shape[0]
    block = gate_w.shape[2]
    started = (expert == 0) & (half == 0)

    if chained:
        copy_moe = pltpu.make_async_copy(moe_in, moe_out, sems.at[0])
        copy_back = pltpu.make_async_copy(back_in, back_out, sems.at[1])

        @pl.when(started)
        def _():
            copy_moe.start()
            copy_back.start()

        @pl.when((expert == 0) & (half == halves - 1))
        def _():
            copy_moe.wait()
            copy_back.wait()

    else:

        @pl.when(started)
        def _():
            moe_out[...] = jnp.zeros_like(moe_out)
            back_out[...] = jnp.zeros_like(back_out)

    def run(rows):
        mask = lax.broadcasted_iota(jnp.int32, (rows, length), 0) == place_ref[0]

        @pl.when(half == 0)
        def _():
            picks = jnp.where(mask, 1.0, 0.0).astype(jnp.bfloat16)
            rows_ref[:rows] = jnp.dot(
                picks, normed_ref[...], preferred_element_type=jnp.float32
            ).astype(jnp.bfloat16)
            grads_ref[:rows] = jnp.dot(
                picks, grad_ref[...], preferred_element_type=jnp.float32
            ).astype(jnp.bfloat16)
            slot_gate[:rows] = jnp.broadcast_to(
                jnp.sum(jnp.where(mask, gate_ref[0], 0.0), axis=1, keepdims=True), (rows, 128)
            )

        rows_in = rows_ref[:rows]
        grad_rows = grads_ref[:rows]
        gate = slot_gate[:rows, :1]
        gate_input = jnp.dot(rows_in, gate_w[0], preferred_element_type=jnp.float32)
        up_input = jnp.dot(rows_in, up_w[0], preferred_element_type=jnp.float32)
        grad_act = right_inner(grad_rows, down_w[0])
        sigmoid_val = jax.nn.sigmoid(gate_input)
        silu_out = gate_input * sigmoid_val
        hidden = silu_out * up_input
        activation = (hidden * gate).astype(jnp.bfloat16)
        column = jnp.sum(grad_act * hidden, axis=1, keepdims=True)
        grad_hidden = grad_act * gate
        grad_gate_in = (
            grad_hidden * up_input * sigmoid_val * (1.0 + gate_input * (1.0 - sigmoid_val))
        ).astype(jnp.bfloat16)
        grad_up_in = (grad_hidden * silu_out).astype(jnp.bfloat16)
        lanes = pl.ds(pl.multiple_of(half * block, block), block)
        grads = left_inner(rows_in, jnp.concatenate([grad_gate_in, grad_up_in], 1))
        grads_out[0, 0, :, lanes] = grads[:, :block]
        grads_out[0, 1, :, lanes] = grads[:, block:]
        grad_down = left_inner(activation, grad_rows)
        hidden_all, width = grads_out.shape[3], grads_out.shape[2]
        own = hidden_all // parts
        blocks = width // hidden_all
        for part in range(block // own):
            for piece in range(blocks):
                at = half * (block // own) * blocks * own + (part * blocks + piece) * own
                grads_out[0, 2, pl.ds(pl.multiple_of(at, own), own), :] = grad_down[
                    part * own : (part + 1) * own, piece * hidden_all : (piece + 1) * hidden_all
                ]
        moe = jnp.dot(activation, down_w[0], preferred_element_type=jnp.float32)
        back = right_inner(grad_gate_in, gate_w[0]) + right_inner(grad_up_in, up_w[0])

        @pl.when(half == 0)
        def _():
            moe_rows[:rows] = moe
            back_rows[:rows] = back
            slot_grad[:rows] = jnp.broadcast_to(column, (rows, 128))

        @pl.when((half > 0) & (half < halves - 1))
        def _():
            moe_rows[:rows] += moe
            back_rows[:rows] += back
            slot_grad[:rows] += jnp.broadcast_to(column, (rows, 128))

        @pl.when(half == halves - 1)
        def _():
            picks = jnp.where(mask, 1.0, 0.0).astype(jnp.bfloat16)
            moe_out[...] += left_inner(picks, (moe_rows[:rows] + moe).astype(jnp.bfloat16))
            back_out[...] += left_inner(picks, (back_rows[:rows] + back).astype(jnp.bfloat16))
            total = slot_grad[:rows, :1] + column
            gates_out[0] = jnp.sum(jnp.where(mask, total, 0.0), axis=0, keepdims=True)

    sizes = (128, 256, CAP)
    for low, rows in zip((-1,) + sizes[:-1], sizes):
        pl.when((filled > low) & (filled <= rows))(functools.partial(run, rows))


def expert_stage(parts, first, last, counts, places, gate_rows, normed_b, grad_b, gate_w, up_w, down_w, sums):
    number = last - first
    length, width = normed_b.shape
    hidden = gate_w.shape[2]
    block = 256
    halves = hidden // block
    experts = places.shape[0]
    chained = sums is not None
    whole = lambda e, h, c: (0, 0)
    row_spec = pl.BlockSpec((1, 1, length), lambda e, h, c: (first + e, 0, 0))
    once = pl.Buffered(1)
    in_specs = [
        row_spec,
        row_spec,
        pl.BlockSpec((length, width), whole, pipeline_mode=once),
        pl.BlockSpec((length, width), whole, pipeline_mode=once),
        pl.BlockSpec((1, width, block), lambda e, h, c: (first + e, 0, h)),
        pl.BlockSpec((1, width, block), lambda e, h, c: (first + e, 0, h)),
        pl.BlockSpec((1, block, width), lambda e, h, c: (first + e, h, 0)),
    ]
    args = [
        counts,
        places.reshape(experts, 1, length),
        gate_rows.reshape(experts, 1, length),
        normed_b,
        grad_b,
        gate_w,
        up_w,
        down_w,
    ]
    if chained:
        in_specs += [pl.BlockSpec(memory_space=pl.ANY)] * 2
        args += [sums[0], sums[1]]
    grads, moe, back, gates = pl.pallas_call(
        functools.partial(expert_kernel, parts, first, chained),
        out_shape=[
            jax.ShapeDtypeStruct((number, 3, width, hidden), jnp.float32),
            jax.ShapeDtypeStruct((length, width), jnp.float32),
            jax.ShapeDtypeStruct((length, width), jnp.float32),
            jax.ShapeDtypeStruct((number, 1, length), jnp.float32),
        ],
        grid_spec=pltpu.PrefetchScalarGridSpec(
            num_scalar_prefetch=1,
            grid=(number, halves),
            in_specs=in_specs,
            out_specs=[
                pl.BlockSpec((1, 3, width, hidden), lambda e, h, c: (e, 0, 0, 0)),
                pl.BlockSpec((length, width), whole, pipeline_mode=once),
                pl.BlockSpec((length, width), whole, pipeline_mode=once),
                pl.BlockSpec((1, 1, length), lambda e, h, c: (e, 0, 0)),
            ],
            scratch_shapes=[
                pltpu.VMEM((CAP, width), jnp.bfloat16),
                pltpu.VMEM((CAP, width), jnp.bfloat16),
                pltpu.VMEM((CAP, width), jnp.float32),
                pltpu.VMEM((CAP, width), jnp.float32),
                pltpu.VMEM((CAP, 128), jnp.float32),
                pltpu.VMEM((CAP, 128), jnp.float32),
                pltpu.SemaphoreType.DMA((2,)),
            ],
        ),
        compiler_params=pltpu.CompilerParams(
            dimension_semantics=("arbitrary", "arbitrary"), vmem_limit_bytes=63 << 20
        ),
        cost_estimate=pl.CostEstimate(
            flops=number * 8 * 10**9, bytes_accessed=number * 14 * 10**6, transcendentals=0
        ),
    )(*args)
    return (grads, (moe, back, gates))


SPAN = 768
ROWS = 256


def lane_halves(shape):
    return lax.broadcasted_iota(jnp.int32, shape, len(shape) - 1) // HEAD


def select_halves(tile, source, half):
    kept = jnp.where(lane_halves(tile.shape) == source, tile, 0.0)
    return kept if source == half else pltpu.roll(kept, HEAD, 1)


def spread_pairs(tile, target):
    for source in range(2):
        for half in range(2):
            target[2 * source + half] = select_halves(tile, source, half).astype(jnp.bfloat16)


def rope_tile(tile, cosine, sine_low, sine_high):
    return tile * cosine + pltpu.roll(tile, 128 - HEAD // 2, 1) * sine_low + pltpu.roll(
        tile, HEAD // 2, 1
    ) * sine_high


def rope_back_tile(tile, cosine, sine_low, sine_high):
    return (
        tile * cosine
        + pltpu.roll(tile * sine_low, HEAD // 2, 1)
        + pltpu.roll(tile * sine_high, 128 - HEAD // 2, 1)
    )


def window(block):
    first = block * ROWS
    return first, jnp.maximum(first + ROWS - SPAN, 0)


def attend_forward_kernel(
    heads,
    group,
    tokens_ref,
    gain_ref,
    query_w,
    key_w,
    value_w,
    cosine_ref,
    sine_low_ref,
    sine_high_ref,
    opening_ref,
    normed_out,
    query_out,
    key_out,
    value_out,
    attended_out,
    logsum_out,
    key_pairs,
    value_pairs,
    tiles_ref,
):
    tiles, length, unused = query_out.shape
    hidden = tokens_ref[...].astype(jnp.float32)
    recip = lax.rsqrt(jnp.mean(hidden * hidden, axis=1, keepdims=True) + EPSILON)
    normed_out[...] = (hidden * recip * gain_ref[...]).astype(jnp.bfloat16)
    cosine, sine_low, sine_high = cosine_ref[...], sine_low_ref[...], sine_high_ref[...]
    for tile in range(tiles):
        query = jnp.dot(
            normed_out[...],
            query_w[:, tile * 128 : (tile + 1) * 128],
            preferred_element_type=jnp.float32,
        )
        query_out[tile] = rope_tile(query, cosine, sine_low, sine_high).astype(jnp.bfloat16)
    key = rope_tile(
        jnp.dot(normed_out[...], key_w[...], preferred_element_type=jnp.float32),
        cosine,
        sine_low,
        sine_high,
    )
    value = jnp.dot(normed_out[...], value_w[...], preferred_element_type=jnp.float32)
    key_out[...] = key.astype(jnp.bfloat16)
    value_out[...] = value.astype(jnp.bfloat16)
    spread_pairs(key, key_pairs)
    spread_pairs(value, value_pairs)
    blocks = length // ROWS
    tiles_ref[...] = jnp.zeros_like(tiles_ref)

    def unit(step, carry):
        head, block = step // blocks, step % blocks
        tile, half = head // 2, head % 2
        pair = 2 * (head // group) + half
        first, low = window(block)
        rows = pl.ds(pl.multiple_of(first, ROWS), ROWS)
        span = pl.ds(pl.multiple_of(low, ROWS), SPAN)
        scores = right_inner(query_out[tile, rows, :], key_pairs[pair, span, :])
        columns = low + lax.broadcasted_iota(jnp.int32, (ROWS, SPAN), 1)
        own = first + lax.broadcasted_iota(jnp.int32, (ROWS, SPAN), 0)
        allowed = (columns >= opening_ref[rows, :]) & (columns <= own)
        raised = jnp.where(allowed, jnp.exp(ATTN_SCALE * scores), 0.0)
        total = jnp.sum(raised, axis=1, keepdims=True)
        product = jnp.dot(
            raised.astype(jnp.bfloat16), value_pairs[pair, span, :], preferred_element_type=jnp.float32
        )
        tiles_ref[tile, rows, :] += product / total
        wide = jnp.broadcast_to(jnp.log(total), (ROWS, 128))
        logsum_out[head, :, rows] = jnp.transpose(wide)[:1]
        return carry

    lax.fori_loop(0, heads * blocks, unit, 0)
    for tile in range(tiles):
        attended_out[:, tile * 128 : (tile + 1) * 128] = tiles_ref[tile].astype(jnp.bfloat16)


def attend_forward(tokens, gain, query_w, key_w, value_w, tables, opening, heads, group):
    length, width = tokens.shape
    wide = query_w.shape[1]
    tiles = wide // 128
    bf16, f32 = jnp.bfloat16, jnp.float32
    full = pl.BlockSpec(memory_space=pltpu.VMEM)
    return pl.pallas_call(
        functools.partial(attend_forward_kernel, heads, group),
        out_shape=[
            jax.ShapeDtypeStruct((length, width), bf16),
            jax.ShapeDtypeStruct((tiles, length, 128), bf16),
            jax.ShapeDtypeStruct((length, 128), bf16),
            jax.ShapeDtypeStruct((length, 128), bf16),
            jax.ShapeDtypeStruct((length, wide), bf16),
            jax.ShapeDtypeStruct((heads, 1, length), f32),
        ],
        in_specs=[full] * 9,
        out_specs=[full] * 6,
        scratch_shapes=[
            pltpu.VMEM((4, length, 128), bf16),
            pltpu.VMEM((4, length, 128), bf16),
            pltpu.VMEM((tiles, length, 128), f32),
        ],
        compiler_params=pltpu.CompilerParams(vmem_limit_bytes=48 << 20),
        cost_estimate=pl.CostEstimate(
            flops=8 * 10**9, bytes_accessed=12 * 10**6, transcendentals=5 * 10**6
        ),
    )(tokens, gain.reshape(1, width), query_w, key_w, value_w, *tables, opening.reshape(length, 1))


def attend_backward_kernel(
    n,
    heads,
    group,
    branch_ref,
    out_w,
    query_ref,
    key_ref,
    value_ref,
    attended_ref,
    logsum_ref,
    query_w,
    key_w,
    value_w,
    cosine_ref,
    sine_low_ref,
    sine_high_ref,
    opening_ref,
    moe_ref,
    grads_out,
    normed_out,
    moe_out,
    key_pairs,
    value_pairs,
    attend_grads,
    query_grads,
    key_grads,
    value_grads,
    delta_ref,
    *line,
):
    tiles, length, unused = query_ref.shape
    line_start, line_step, line_end = line_stages(n, [moe_ref], [moe_out], line)
    line_start()
    spread_pairs(key_ref[...].astype(jnp.float32), key_pairs)
    spread_pairs(value_ref[...].astype(jnp.float32), value_pairs)
    halves = (
        lax.broadcasted_iota(jnp.int32, (8, 128), 0) == lane_halves((8, 128))
    ).astype(jnp.float32)
    for tile in range(tiles):
        lanes = slice(tile * 128, (tile + 1) * 128)
        grad = right_inner(branch_ref[...], out_w[lanes, :]).astype(jnp.bfloat16)
        attend_grads[tile] = grad
        products = grad.astype(jnp.float32) * attended_ref[:, lanes].astype(jnp.float32)
        sums = lax.dot_general(
            halves,
            products,
            (((1,), (1,)), ((), ())),
            precision=lax.Precision.HIGHEST,
            preferred_element_type=jnp.float32,
        )
        delta_ref[2 * tile] = sums[0:1]
        delta_ref[2 * tile + 1] = sums[1:2]
    query_grads[...] = jnp.zeros_like(query_grads)
    key_grads[...] = jnp.zeros_like(key_grads)
    value_grads[...] = jnp.zeros_like(value_grads)
    blocks = length // ROWS
    units = heads * blocks
    each = -(-2 * STEPS // units)

    def unit(step, carry):
        lax.fori_loop(step * each, step * each + each, line_step, 0)
        head, block = step // blocks, step % blocks
        tile, half = head // 2, head % 2
        pair = 2 * (head // group) + half
        first, low = window(block)
        rows = pl.ds(pl.multiple_of(first, ROWS), ROWS)
        span = pl.ds(pl.multiple_of(low, ROWS), SPAN)
        keys = key_pairs[pair, span, :]
        query = query_ref[tile, rows, :]
        grad = attend_grads[tile, rows, :]
        scores = right_inner(keys, query)
        columns = low + lax.broadcasted_iota(jnp.int32, (SPAN, ROWS), 0)
        own = first + lax.broadcasted_iota(jnp.int32, (SPAN, ROWS), 1)
        allowed = (columns >= opening_ref[:, rows]) & (columns <= own)
        probs = jnp.where(
            allowed, jnp.exp(ATTN_SCALE * scores - logsum_ref[head, :, rows]), 0.0
        )
        grad_probs = right_inner(value_pairs[pair, span, :], grad)
        grad_scores = (probs * (grad_probs - delta_ref[head, :, rows])).astype(jnp.bfloat16)
        value_grads[pair, span, :] += jnp.dot(
            probs.astype(jnp.bfloat16), grad, preferred_element_type=jnp.float32
        )
        key_grads[pair, span, :] += jnp.dot(
            grad_scores, query, preferred_element_type=jnp.float32
        )
        query_grads[tile, rows, :] += left_inner(grad_scores, keys)
        return carry

    lax.fori_loop(0, units, unit, 0)
    cosine, sine_low, sine_high = cosine_ref[...], sine_low_ref[...], sine_high_ref[...]
    wide = tiles * 128
    for tile in range(tiles):
        grads_out[:, tile * 128 : (tile + 1) * 128] = rope_back_tile(
            ATTN_SCALE * query_grads[tile], cosine, sine_low, sine_high
        ).astype(jnp.bfloat16)
    totals = []
    for grads in (key_grads, value_grads):
        totals.append(
            sum(
                select_halves(grads[2 * source + half], half, source)
                for source in range(2)
                for half in range(2)
            )
        )
    grads_out[:, wide : wide + 128] = rope_back_tile(
        ATTN_SCALE * totals[0], cosine, sine_low, sine_high
    ).astype(jnp.bfloat16)
    grads_out[:, wide + 128 : wide + 256] = totals[1].astype(jnp.bfloat16)
    normed_out[...] = (
        right_inner(grads_out[:, :wide], query_w[...])
        + right_inner(grads_out[:, wide : wide + 128], key_w[...])
        + right_inner(grads_out[:, wide + 128 :], value_w[...])
    )
    line_end()


def attend_backward(
    n, branch, out_w, query, key, value, attended, logsum, query_w, key_w, value_w, tables, opening, moe,
    heads, group, name,
):
    length, width = branch.shape
    tiles = query.shape[0]
    wide = tiles * 128
    bf16, f32 = jnp.bfloat16, jnp.float32
    full = pl.BlockSpec(memory_space=pltpu.VMEM)
    return pl.pallas_call(
        functools.partial(attend_backward_kernel, n, heads, group),
        out_shape=[
            jax.ShapeDtypeStruct((length, wide + 256), bf16),
            jax.ShapeDtypeStruct((length, width), f32),
            jax.ShapeDtypeStruct((length, width), f32),
        ],
        in_specs=[full] * 15,
        out_specs=[full] * 3,
        scratch_shapes=[
            pltpu.VMEM((4, length, 128), bf16),
            pltpu.VMEM((4, length, 128), bf16),
            pltpu.VMEM((tiles, length, 128), bf16),
            pltpu.VMEM((tiles, length, 128), f32),
            pltpu.VMEM((4, length, 128), f32),
            pltpu.VMEM((4, length, 128), f32),
            pltpu.VMEM((2 * tiles, 1, length), f32),
        ]
        + line_scratch([moe]),
        compiler_params=pltpu.CompilerParams(
            collective_id=name, has_side_effects=True, vmem_limit_bytes=60 << 20
        ),
        cost_estimate=pl.CostEstimate(
            flops=12 * 10**9, bytes_accessed=30 * 10**6, transcendentals=5 * 10**6
        ),
    )(
        branch, out_w, query, key, value, attended, logsum, query_w, key_w, value_w, *tables,
        opening.reshape(1, length), moe,
    )


def finish_kernel(
    n,
    parts,
    local_ref,
    normed_ref,
    grads_ref,
    branch_ref,
    attended_ref,
    normed_two_ref,
    logits_ref,
    gain_ref,
    normed_out,
    shard_out,
    weights_ref,
    *scratch,
):
    levels = parts.bit_length() - 1
    held = scratch[:levels]
    sends, recvs = scratch[levels : levels + 2]
    line_start, line_step, line_end = line_stages(n, [local_ref], [normed_out], scratch[levels + 2 :])
    me = lax.axis_index("dp")
    width = normed_ref.shape[1]
    own = width // parts
    wide, attended_wide = grads_ref.shape[1], attended_ref.shape[1]
    line_start([{"dp": jnp.bitwise_xor(me, 1 << level)} for level in range(levels)])

    def run_line(first, last):
        lax.fori_loop(first, last, line_step, 0)

    run_line(0, 2)
    pieces = 4
    block = width // pieces
    for piece in range(pieces):
        rows = slice(piece * block, (piece + 1) * block)
        weights_ref[rows, :wide] = left_inner(normed_ref[:, rows], grads_ref[...])
        weights_ref[rows, wide : wide + attended_wide] = left_inner(
            branch_ref[:, rows], attended_ref[...]
        )
        gain = jnp.transpose(jnp.broadcast_to(gain_ref[:, rows], (128, block)))
        lanes = lax.broadcasted_iota(jnp.int32, (block, 128), 1)
        weights_ref[rows, wide + attended_wide :] = jnp.where(
            lanes == 127, gain, left_inner(normed_two_ref[:, rows], logits_ref[...])
        )
        run_line(2 + 2 * piece, 4 + 2 * piece)
    done = 2 + 2 * pieces

    def shard(number):
        return weights_ref.at[pl.ds(pl.multiple_of(number * own, own), own), :]

    def copies(level):
        peer = jnp.bitwise_xor(me, 1 << level)
        low = jnp.bitwise_and(peer, (2 << level) - 1)
        return [
            pltpu.make_async_remote_copy(
                src_ref=shard(low + (i << (level + 1))),
                dst_ref=held[level].at[i],
                send_sem=sends.at[level, i],
                recv_sem=recvs.at[level, i],
                device_id={"dp": peer},
                device_id_type=MESH,
            )
            for i in range(parts >> (level + 1))
        ]

    stops = [10, 12, 14, 10]
    for level in range(levels):
        for copy in copies(level):
            copy.start()
        until = done + stops[level]
        run_line(done, until)
        done = until
        kept = jnp.bitwise_and(me, (2 << level) - 1)
        for i, copy in enumerate(copies(level)):
            copy.wait_recv()
            target = shard(kept + (i << (level + 1)))
            target[...] += held[level][i]
    run_line(done, 2 * STEPS)
    shard_out[...] = shard(me)[...]
    for level in range(levels):
        for copy in copies(level):
            copy.wait_send()
    line_end()


def finish(n, parts, grad_local, normed_b, grads_wide, branch_b, attended, normed_two_b, grad_logits_b, ffn_gain_grad, name):
    length, width = normed_b.shape
    columns = grads_wide.shape[1] + attended.shape[1] + 128
    logits = jnp.pad(grad_logits_b, ((0, 0), (0, 128 - grad_logits_b.shape[1])))
    full = pl.BlockSpec(memory_space=pltpu.VMEM)
    levels = parts.bit_length() - 1
    own = width // parts
    f32 = jnp.float32
    return pl.pallas_call(
        functools.partial(finish_kernel, n, parts),
        out_shape=[
            jax.ShapeDtypeStruct((length, width), f32),
            jax.ShapeDtypeStruct((own, columns), f32),
        ],
        in_specs=[full] * 8,
        out_specs=[full] * 2,
        scratch_shapes=[pltpu.VMEM((width, columns), f32)]
        + [pltpu.VMEM((parts >> (level + 1), own, columns), f32) for level in range(levels)]
        + [pltpu.SemaphoreType.DMA((levels, parts // 2))] * 2
        + line_scratch([grad_local]),
        compiler_params=pltpu.CompilerParams(
            collective_id=name, has_side_effects=True, vmem_limit_bytes=60 << 20
        ),
        cost_estimate=pl.CostEstimate(
            flops=2 * length * width * columns, bytes_accessed=50 * 10**6, transcendentals=0
        ),
    )(
        grad_local, normed_b, grads_wide, branch_b, attended, normed_two_b, logits,
        ffn_gain_grad.reshape(1, width),
    )


def place_kernel(shards_ref, *refs):
    gate_out, up_out, down_out = refs[-3:]
    gate_out[0] = shards_ref[0, 0]
    up_out[0] = shards_ref[0, 1]
    rows, hidden = down_out.shape[1], shards_ref.shape[3]
    for piece in range(down_out.shape[2] // hidden):
        down_out[0, :, piece * hidden : (piece + 1) * hidden] = shards_ref[
            0, 2, piece * rows : (piece + 1) * rows, :
        ]


def place_shards(parts, shards, first, experts, before):
    number, unused, rows, hidden = shards.shape
    down_rows = hidden // parts
    width = rows * parts
    shapes = [(experts, rows, hidden), (experts, rows, hidden), (experts, down_rows, width)]
    spec = lambda shape: pl.BlockSpec((1,) + shape[1:], lambda e: (first + e, 0, 0))
    args, extra, aliases = [shards], [], {}
    if before is not None:
        args += list(before)
        extra = [pl.BlockSpec(memory_space=pl.ANY)] * 3
        aliases = {1: 0, 2: 1, 3: 2}
    return pl.pallas_call(
        place_kernel,
        out_shape=[jax.ShapeDtypeStruct(shape, jnp.float32) for shape in shapes],
        grid=(number,),
        in_specs=[pl.BlockSpec((1, 3, rows, hidden), lambda e: (e, 0, 0, 0))] + extra,
        out_specs=[spec(shape) for shape in shapes],
        input_output_aliases=aliases,
        cost_estimate=pl.CostEstimate(
            flops=0, bytes_accessed=8 * shards.size, transcendentals=0
        ),
    )(*args)


def on_device(
    ring,
    tokens,
    cotangent,
    segment_ids,
    routes,
    attn_gain,
    query_weight,
    key_weight,
    value_weight,
    out_weight,
    ffn_gain,
    router_weight,
    gate_weight,
    up_weight,
    down_weight,
):
    length = tokens.shape[0]
    width = tokens.shape[1]
    segment = segment_ids[0]
    heads_local = query_weight.shape[1] // HEAD
    kv_local = key_weight.shape[1] // HEAD
    group_size = heads_local // kv_local
    experts_all = router_weight.shape[1]
    experts_local = gate_weight.shape[0]
    parts = lax.axis_size("dp")
    opening = doc_openings(segment)
    tables = rope_tables(opening, HEAD)
    query_w, key_w, value_w = (pad_columns(w) for w in (query_weight, key_weight, value_weight))
    out_w = jnp.transpose(pad_columns(jnp.transpose(out_weight)))
    hidden_in = tokens.astype(jnp.float32)
    normed_b, queries, keys, values, attended, logsum = attend_forward(
        tokens, attn_gain, query_w, key_w, value_w, tables, opening, heads_local, group_size
    )
    all_ids = jnp.arange(experts_all, dtype=jnp.int32)
    chosen = jnp.sum((routes[:, :, None] == all_ids[None, None, :]).astype(jnp.int32), axis=1) > 0
    first_expert = lax.axis_index("tensor") * experts_local
    local_ids = first_expert + jnp.arange(experts_local, dtype=jnp.int32)
    picked = jnp.sum((routes[None, :, :] == local_ids[:, None, None]).astype(jnp.int32), axis=2)
    places_in = slot_places(picked)
    counts = jnp.sum(picked, axis=1)
    grad_moe_b = (RESIDUAL * cotangent.astype(jnp.float32)).astype(jnp.bfloat16)
    attn_out, unused = line_sum(
        jnp.dot(attended, out_w, preferred_element_type=jnp.float32), None, ring, 1
    )
    middle = hidden_in + RESIDUAL * attn_out
    normed_two, unit_two, recip_two = rms_forward(middle, ffn_gain)
    normed_two_b = normed_two.astype(jnp.bfloat16)
    logits = jnp.dot(normed_two_b, router_weight, preferred_element_type=jnp.float32)
    raised = jnp.where(chosen, jnp.exp(logits), 0.0)
    gate_probs = raised / jnp.sum(raised, axis=-1, keepdims=True)
    gate_rows = jnp.transpose(lax.dynamic_slice_in_dim(gate_probs, first_expert, experts_local, 1))
    early = 2 * experts_local // 5
    grads_first, sums = expert_stage(
        parts, 0, early, counts, places_in, gate_rows, normed_two_b, grad_moe_b,
        gate_weight, up_weight, down_weight, None,
    )
    shards_first = lax.psum_scatter(grads_first, "dp", scatter_dimension=2, tiled=True)
    grads_last, sums_last = expert_stage(
        parts, early, experts_local, counts, places_in, gate_rows, normed_two_b, grad_moe_b,
        gate_weight, up_weight, down_weight, sums,
    )
    moe_part, grad_normed_part, unused = sums_last
    grad_gates_local = jnp.concatenate([sums[2], sums_last[2]], 0)
    grad_gates_part = lax.dynamic_update_slice_in_dim(
        jnp.zeros((experts_all, length), jnp.float32),
        grad_gates_local.reshape(experts_local, length),
        first_expert,
        0,
    ).reshape(-1, 128)
    grad_gates_part = jnp.pad(grad_gates_part, ((0, GATE_ROWS - grad_gates_part.shape[0]), (0, 0)))
    grad_normed_sum, gates_sum = line_sum(grad_normed_part, grad_gates_part, ring, 2)
    grad_gates = jnp.transpose(
        gates_sum[: experts_all * length // 128].reshape(experts_all, length)
    )
    weighted = jnp.sum(gate_probs * grad_gates, axis=-1, keepdims=True)
    grad_logits_b = (gate_probs * (grad_gates - weighted)).astype(jnp.bfloat16)
    grad_normed_two = grad_normed_sum + right_inner(grad_logits_b, router_weight)
    grad_from_norm, grad_ffn_gain = rms_backward(grad_normed_two, unit_two, recip_two, ffn_gain)
    grad_middle = cotangent.astype(jnp.float32) + grad_from_norm
    grad_branch_b = (RESIDUAL * grad_middle).astype(jnp.bfloat16)
    shards_first, grads_last, grad_branch_b = lax.optimization_barrier(
        (shards_first, grads_last, grad_branch_b)
    )
    shards_last = lax.psum_scatter(grads_last, "dp", scatter_dimension=2, tiled=True)
    grads_wide, grad_normed_local, moe_out = attend_backward(
        ring, grad_branch_b, out_w, queries, keys, values, attended, logsum,
        query_w, key_w, value_w, tables, opening, moe_part, heads_local, group_size, 3,
    )
    output = (middle + RESIDUAL * moe_out).astype(jnp.bfloat16)
    grad_normed, small = finish(
        ring, parts, grad_normed_local, normed_b, grads_wide, grad_branch_b, attended, normed_two_b,
        grad_logits_b, grad_ffn_gain, 4,
    )
    recip_one = lax.rsqrt(jnp.mean(hidden_in * hidden_in, axis=-1, keepdims=True) + EPSILON)
    unit_one = hidden_in * recip_one
    grad_from_first, grad_attn_gain = rms_backward(grad_normed, unit_one, recip_one, attn_gain)
    grad_tokens = grad_middle + grad_from_first
    grad_attn_gain = lax.psum_scatter(grad_attn_gain, "dp", scatter_dimension=0, tiled=True)
    shards_last, grad_attn_gain = lax.optimization_barrier((shards_last, grad_attn_gain))
    tiled_q = query_w.shape[1]
    wide_q, wide_k = heads_local * HEAD, kv_local * HEAD
    at_out = tiled_q + 256
    at_router = at_out + tiled_q
    grads_placed = place_shards(parts, shards_first, 0, experts_local, None)
    grad_gate, grad_up, grad_down = place_shards(parts, shards_last, early, experts_local, grads_placed)
    return (
        output,
        grad_tokens,
        grad_attn_gain,
        small[:, :wide_q],
        small[:, tiled_q : tiled_q + wide_k],
        small[:, tiled_q + 128 : tiled_q + 128 + wide_k],
        jnp.transpose(small[:, at_out : at_out + wide_q]),
        small[:, at_router + 127],
        small[:, at_router : at_router + experts_all],
        grad_gate,
        grad_up,
        grad_down,
    )


def solution(mesh):
    return jax.shard_map(
        functools.partial(on_device, mesh.shape["tensor"]),
        mesh=mesh,
        in_specs=(
            P("dp", None),
            P("dp", None),
            P("dp", None),
            P("dp", None),
            P(),
            P(None, "tensor"),
            P(None, "tensor"),
            P(None, "tensor"),
            P("tensor", None),
            P(),
            P(),
            P("tensor", None, None),
            P("tensor", None, None),
            P("tensor", None, None),
        ),
        out_specs=(
            P("dp", None),
            P("dp", None),
            P("dp"),
            P("dp", "tensor"),
            P("dp", "tensor"),
            P("dp", "tensor"),
            P("tensor", "dp"),
            P("dp"),
            P("dp", None),
            P("tensor", "dp", None),
            P("tensor", "dp", None),
            P("tensor", "dp", None),
        ),
        check_vma=False,
    )
```

time: 1750 us -> 1020 us (0.58)
  waiting for transfers between devices: 639 us -> 0.04 us
  Pallas kernels: 758 us -> 906 us
  local copies, waits for them, and re-layouts: 137 us -> 26.4 us
  matrix products: 101 us -> 8.99 us
  other arithmetic: 70.8 us -> 44.8 us
    reduce_scatter x4 -> x2, waiting for transfers between devices: 598 us -> 0.01 us  [the longest x1 0.01 us: on_device(): lax.psum_scatter(grads_first, 'dp', scatter_dimension=2, tiled=True)]
    pallas_call x2 -> x7, Pallas kernels: 153 us -> 590 us  [the longest x1 214 us: finish(): pl.pallas_call(functools.partial(finish_kernel, n, parts), out_shape=[jax...]
    pallas_call x4 -> x2, Pallas kernels: 605 us -> 316 us  [line_sum(): pl.pallas_call(functools.partial(line_sum_kernel, n, count), out_shape=sh...]
    dot_general x21 -> x1, matrix products: 85.6 us -> 1.78 us  [on_device(): jnp.dot(attended, out_w, preferred_element_type=jnp.float32)]
    unnamed x6 -> x2, waiting for transfers between devices: 41.5 us -> 0.03 us
    dynamic_update_slice x6 -> x0, local copies, waits for them, and re-layouts: 31.5 us -> none  [the longest x4 31.4 us: on_device(): lax.scan(backward_block, (wide_zero, wide_zero), (query_blocks, first_row...]
    pallas_call x1 -> x0, local copies, waits for them, and re-layouts: 24 us -> none  [expert_stage(): pl.pallas_call(functools.partial(expert_kernel, first, chained), out_shap...]
    concatenate x3 -> x0, local copies, waits for them, and re-layouts: 20.3 us -> none  [the longest x1 14.9 us: on_device(): jnp.concatenate([grad_projections, left_inner(grad_branch_b, attended_fla...]
  transfers between devices with their start and end apart: 5 -> 2, of which waited for: 5 -> 0; matrix products, arithmetic and copies ran while one was open for 3% -> 4% of each run, Pallas kernels for 0% -> 64%
where the time goes in v2:
time: 1020 us
  Pallas kernels  906 us (89%)
  other arithmetic  44.8 us (4%)
  local copies, waits for them, and re-layouts  26.4 us (3%)
  between operations  15.4 us (2%)
  blocking collectives  15.2 us (1%)
    pallas_call x2, Pallas kernels, line_sum(): pl.pallas_call(functools.partial(line_sum_kernel, n, count), out_shape=sh...  316 us
    pallas_call x1, Pallas kernels, finish(): pl.pallas_call(functools.partial(finish_kernel, n, parts), out_shape=[jax...  214 us
    pallas_call x1, Pallas kernels, attend_backward(): pl.pallas_call(functools.partial(attend_backward_kernel, n, heads, group)...  185 us
    pallas_call x2, Pallas kernels, expert_stage(): pl.pallas_call(functools.partial(expert_kernel, parts, first, chained), o...  157 us
    pallas_call x1, Pallas kernels, attend_forward(): pl.pallas_call(functools.partial(attend_forward_kernel, heads, group), ou...  21.6 us
  transfers between devices with their start and end apart: 2, of which 0 were waited for; matrix products, arithmetic and copies ran while one was open for 4% of the time, Pallas kernels for 64%

profile of v2, /device:TPU:8, one launch (start us, length us, event | category | flops | bytes accessed | tf_op | source)
XLA Modules:
  0.0 1016.8 jit_solution(5765404125746709711)
XLA Ops:
  14.1 4.3 fusion.3.grad_ref
  18.3 1.9 multiply_sine_fusion
  21.6 21.6 %shard_map.229 = (bf16[1024,1536]{1,0:T(8,128)(2,1)}, bf16[3,1024,128]{2,1,0:T(8,128)(2,1)S(1)}, bf16[1024,128]{1,0:T(8,128)(2,1)S(1)}, bf16[1024,128]{1,0:T(8,1...) custom-call(bf16[1024,1536]{1,0:T(8,128)(2,1)} %tokens_ref.1, f32[1,1536]{1,0:T(1,128)S(1)} %reshape.99.gain_ref, ...), custom_call_target="tpu_custom_call" | custom-call | flops 8000000000 | bytes 12000000 | tf_op jit(solution)/shard_map/pallas_call | solution.py:554
  44.7 1.8 fusion.21.refs_0_
  46.5 154.7 %shard_map.230 = f32[1024,1536]{1,0:T(8,128)S(1)} custom-call(f32[1024,1536]{1,0:T(8,128)S(1)} %fusion.21.refs_0_), custom_call_target="tpu_custom_call" | custom-call | flops 4718592 | bytes 12582912 | tf_op jit(solution)/shard_map/pallas_call | solution.py:228
  201.3 3.8 multiply_reduce_fusion.2
  205.2 3.4 multiply_convert_fusion.1.normed_ref.normed_two_ref
  208.6 1.7 copy-done.15
  212.5 68.9 %shard_map.231 = (f32[4,3,1536,512]{3,2,1,0:T(8,128)}, f32[1024,1536]{1,0:T(8,128)}, f32[1024,1536]{1,0:T(8,128)}, f32[4,1,1024]{2,1,0:T(1,128)}) custom-call(s32[10]{0:T(128)} %get-tuple-element.129.count_ref, s32[10,1,1024]{2,1,0:T(1,128)} %reshape.100.place_ref, f32[10,1,1024]{2,1,0:T(1,128)} %copy.54.gate_ref, bf16[1024,1536]{1,0:T(8,128)(2,1)} %copy-done.15, ...), custom_call_target="tpu_custom_call" | custom-call | flops 32000000000 | bytes 56000000 | tf_op jit(solution)/shard_map/pallas_call | solution.py:398
  281.5 87.7 %shard_map.232 = (f32[6,3,1536,512]{3,2,1,0:T(8,128)}, f32[1024,1536]{1,0:T(8,128)}, f32[1024,1536]{1,0:T(8,128)}, f32[6,1,1024]{2,1,0:T(1,128)}) custom-call(s32[10]{0:T(128)} %get-tuple-element.129.count_ref, s32[10,1,1024]{2,1,0:T(1,128)} %reshape.100.place_ref, f32[10,1,1024]{2,1,0:T(1,128)} %copy.54.gate_ref, bf16[1024,1536]{1,0:T(8,128)(2,1)} %copy-done.15, ...), custom_call_target="tpu_custom_call" | custom-call | flops 48000000000 | bytes 84000000 | tf_op jit(solution)/shard_map/pallas_call | solution.py:398
  370.7 3.1 copy-done.1
  373.8 161.6 %shard_map.233 = (f32[1024,1536]{1,0:T(8,128)S(1)}, f32[512,128]{1,0:T(8,128)S(1)}) custom-call(f32[1024,1536]{1,0:T(8,128)S(1)} %copy-done.1, f32[512,128]{1,0:T(8,128)S(1)} %pad.8.refs_1_), custom_call_target="tpu_custom_call" | custom-call | flops 4915200 | bytes 13107200 | tf_op jit(solution)/shard_map/pallas_call | solution.py:228
  535.4 2.7 copy-done.2
  542.0 5.9 multiply_reduce_fusion
  547.9 2.7 copy-done.14
  550.5 3.3 multiply_convert_fusion.branch_ref
  556.5 184.6 %shard_map.234 = (bf16[1024,640]{1,0:T(8,128)(2,1)}, f32[1024,1536]{1,0:T(8,128)}, f32[1024,1536]{1,0:T(8,128)}) custom-call(bf16[1024,1536]{1,0:T(8,128)(2,1)} %multiply_convert_fusion.branch_ref, bf16[384,1536]{1,0:T(8,128)(2,1)} %out_w.1, bf16[3,1024,128]{2,1,0:T(8,128)(2,1)} %copy-done.10, bf16[1024,128]{1,0:T(8,128)(2,1)} %copy-done.11, ...), custom_call_target="tpu_custom_call" | custom-call | flops 12000000000 | bytes 30000000 | tf_op jit(solution)/shard_map/pallas_call | solution.py:704
  741.1 214.4 %shard_map.235 = (f32[1024,1536]{1,0:T(8,128)}, f32[192,1152]{1,0:T(8,128)}) custom-call(f32[1024,1536]{1,0:T(8,128)} %get-tuple-element.61.local_ref, bf16[1024,1536]{1,0:T(8,128)(2,1)} %get-tuple-element.62.normed_ref, bf16[1024,640]{1,0:T(8,128)(2,1)} %get-tuple-element.63.grads_ref, bf16[1024,1536]{1,0:T(8,128)(2,1)} %multiply_convert_fusion.branch_ref, ...), custom_call_target="tpu_custom_call" | custom-call | flops 3623878656 | bytes 50000000 | tf_op jit(solution)/shard_map/pallas_call | solution.py:827
  957.3 5.0 shard_map.236
  962.3 4.0 fusion.8
  966.3 15.2 %all-reduce.2 = f32[1536]{0:T(1024)S(1)} all-reduce(f32[1536]{0:T(1024)S(1)} %get-tuple-element.126), channel_id=4, replica_groups=mesh['dp'=8,'tensor'=4] {'dp'}, use_global_device_ids=true, to_apply=%region_14.15.clone | all-reduce | flops 1536 | bytes 12288
  985.4 1.9 slice_bitcast_fusion
  987.3 15.1 %fusion.7 = (f32[1024,1536]{1,0:T(8,128)}, bf16[1024,1536]{1,0:T(8,128)(2,1)}) fusion(bf16[1024,1536]{1,0:T(8,128)(2,1)S(1)} %copy-done.17, f32[1024,1536]{1,0:T(8,128)} %get-tuple-element.64, f32[1024]{0:T(1024)S(1)} %broadcast_multiply_fusion, f32[1536]{0:T(1024)S(1)} %copy-done.22, f32[1024]{0:T(1024)S(1)} %add_rsqrt_fusion, ...), kind=kLoop, calls=%fused_computation.12 | loop fusion | flops 26738688 | bytes 40923136 | tf_op jit(solution)/shard_map/add | solution.py:983
  1002.4 7.3 shard_map.237
  (99 shorter events, 24.9 us)
Async XLA Ops:
  7.2 203.1 %copy-start = (bf16[1536,40]{0,1:T(8,128)(2,1)S(1)}, bf16[1536,40]{0,1:T(8,128)(2,1)}, u32[]{:S(2)}) copy-start(bf16[1536,40]{0,1:T(8,128)(2,1)} %param.24) | copy-start | bytes 368644
  7.2 546.6 %reduce-scatter.3.cloned.1.call-start = ((), (), s32[]{:S(2)}) async-start(), calls=%async_computation.2 | async-start | bytes 42467328 | tf_op jit(solution)/shard_map/reduce_scatter | solution.py:943
  8.6 13.0 %copy-start.23 = (s32[1024]{0:T(1024)}, s32[1024]{0:T(1024)S(1)}, u32[]{:S(2)}) copy-start(s32[1024]{0:T(1024)S(1)} %convert_reduce_fusion) | copy-start | bytes 12292
  13.8 7.8 copy-start.7
  13.8 7.8 copy-start.8
  13.8 7.8 copy-start.9
  21.6 21.7 %copy-start.4 = (f32[1024,128]{1,0:T(8,128)}, f32[1024,128]{1,0:T(8,128)S(1)}, u32[]{:S(2)}) copy-start(f32[1024,128]{1,0:T(8,128)S(1)} %get-tuple-element.139.sine_high_ref) | copy-start | bytes 1572868
  21.6 21.7 %copy-start.5 = (f32[1024,128]{1,0:T(8,128)}, f32[1024,128]{1,0:T(8,128)S(1)}, u32[]{:S(2)}) copy-start(f32[1024,128]{1,0:T(8,128)S(1)} %get-tuple-element.140.sine_low_ref) | copy-start | bytes 1572868
  21.6 21.7 %copy-start.6 = (f32[1024,128]{1,0:T(8,128)}, f32[1024,128]{1,0:T(8,128)S(1)}, u32[]{:S(2)}) copy-start(f32[1024,128]{1,0:T(8,128)S(1)} %get-tuple-element.147.cosine_ref) | copy-start | bytes 1572868
  21.6 23.1 %copy-start.20 = (bf16[384,1536]{1,0:T(8,128)(2,1)S(1)}, bf16[384,1536]{1,0:T(8,128)(2,1)}, u32[]{:S(2)}) copy-start(bf16[384,1536]{1,0:T(8,128)(2,1)} %out_w.1) | copy-start | bytes 3538948
  44.7 156.6 %copy-start.3 = (bf16[1024,384]{1,0:T(8,128)(2,1)}, bf16[1024,384]{1,0:T(8,128)(2,1)S(1)}, u32[]{:S(2)}) copy-start(bf16[1024,384]{1,0:T(8,128)(2,1)S(1)} %get-tuple-element.44.attended_ref) | copy-start | bytes 2359300
  44.7 156.6 %copy-start.10 = (bf16[3,1024,128]{2,1,0:T(8,128)(2,1)}, bf16[3,1024,128]{2,1,0:T(8,128)(2,1)S(1)}, u32[]{:S(2)}) copy-start(bf16[3,1024,128]{2,1,0:T(8,128)(2,1)S(1)} %get-tuple-element.55.query_ref) | copy-start | bytes 2359300
  44.7 156.6 %copy-start.13 = (f32[6,1,1024]{2,1,0:T(1,128)}, f32[6,1,1024]{2,1,0:T(1,128)S(1)}, u32[]{:S(2)}) copy-start(f32[6,1,1024]{2,1,0:T(1,128)S(1)} %get-tuple-element.58.logsum_ref) | copy-start | bytes 73732
  46.5 154.8 %copy-start.16 = (bf16[1024,1536]{1,0:T(8,128)(2,1)S(1)}, bf16[1024,1536]{1,0:T(8,128)(2,1)}, u32[]{:S(2)}) copy-start(bf16[1024,1536]{1,0:T(8,128)(2,1)} %tokens_ref.1) | copy-start | bytes 9437188
  201.3 3.8 copy-start.21
  205.1 5.1 copy-start.19
  281.4 721.0 %reduce-scatter.5.cloned.1.call-start = ((), (), s32[]{:S(2)}) async-start(), calls=%async_computation.3 | async-start | bytes 63700992 | tf_op jit(solution)/shard_map/reduce_scatter | solution.py:970
  281.5 87.8 %copy-start.24 = (f32[4,1,1024]{2,1,0:T(1,128)S(1)}, f32[4,1,1024]{2,1,0:T(1,128)}, u32[]{:S(2)}) copy-start(f32[4,1,1024]{2,1,0:T(1,128)} %get-tuple-element.50) | copy-start | bytes 49156
  370.7 3.1 copy-start.1
  373.8 176.7 %slice-start = ((s8[6291456]{0:T(1024)(128)(4,1)}), s8[2097152]{0:T(1024)(128)(4,1)S(1)}, s32[]{:S(2)}) async-start(s8[6291456]{0:T(1024)(128)(4,1)} %bitcast.28), calls=%async_computation.4 | async-start | bytes 4194304
  541.9 8.6 slice-start.1
  542.0 8.6 copy-start.18
  741.1 221.2 %copy-start.22 = (f32[1536]{0:T(1024)S(1)}, f32[1536]{0:T(1024)}, u32[]{:S(2)}) copy-start(f32[1536]{0:T(1024)} %param.18) | copy-start | bytes 18436
  955.6 6.8 copy-start.17
  (6 other events, 9.8 us)
Sparse Core Ops, SparseCore 0:
  281.6 231.7 reduce-scatter.2
  554.0 394.8 reduce-scatter.4

commit v3 on v2

--- a/solution.py
+++ b/solution.py
@@ -244,6 +244,7 @@
 def expert_kernel(
     parts,
     first,
+    numbers,
     chained,
     count_ref,
     place_ref,
@@ -258,129 +259,145 @@
     if chained:
         moe_in, back_in = refs[:2]
         refs = refs[2:]
-    grads_out, moe_out, back_out, gates_out = refs[:4]
-    rows_ref, grads_ref, moe_rows, back_rows, slot_gate, slot_grad, sems = refs[4:]
-    expert, half = pl.program_id(0), pl.program_id(1)
-    halves = pl.num_programs(1)
+    grads_out, refs = refs[: len(numbers)], refs[len(numbers) :]
+    moe_out, back_out, gates_out = refs[:3]
+    rows_ref, grads_ref, active_ref, gate_in_ref, up_in_ref, weights_ref, sems, out_sems = refs[3:]
+    expert = pl.program_id(0)
     filled = count_ref[first + expert]
-    length = normed_ref.shape[0]
-    block = gate_w.shape[2]
-    started = (expert == 0) & (half == 0)
+    length, width = normed_ref.shape
+    hidden_size = gate_w.shape[2]
+    sizes = (128, 256, CAP)
+
+    def by_size(run):
+        low = None
+        for rows in sizes:
+            fits = filled <= rows if low is None else filled > low
+            if low is not None and rows != sizes[-1]:
+                fits = fits & (filled <= rows)
+            pl.when(fits)(functools.partial(run, rows))
+            low = rows
 
     if chained:
         copy_moe = pltpu.make_async_copy(moe_in, moe_out, sems.at[0])
         copy_back = pltpu.make_async_copy(back_in, back_out, sems.at[1])
 
-        @pl.when(started)
+        @pl.when(expert == 0)
         def _():
             copy_moe.start()
             copy_back.start()
 
-        @pl.when((expert == 0) & (half == halves - 1))
-        def _():
-            copy_moe.wait()
-            copy_back.wait()
-
     else:
 
-        @pl.when(started)
+        @pl.when(expert == 0)
         def _():
             moe_out[...] = jnp.zeros_like(moe_out)
             back_out[...] = jnp.zeros_like(back_out)
 
-    def run(rows):
+    def slots(rows):
         mask = lax.broadcasted_iota(jnp.int32, (rows, length), 0) == place_ref[0]
-
-        @pl.when(half == 0)
-        def _():
-            picks = jnp.where(mask, 1.0, 0.0).astype(jnp.bfloat16)
-            rows_ref[:rows] = jnp.dot(
-                picks, normed_ref[...], preferred_element_type=jnp.float32
-            ).astype(jnp.bfloat16)
-            grads_ref[:rows] = jnp.dot(
-                picks, grad_ref[...], preferred_element_type=jnp.float32
-            ).astype(jnp.bfloat16)
-            slot_gate[:rows] = jnp.broadcast_to(
-                jnp.sum(jnp.where(mask, gate_ref[0], 0.0), axis=1, keepdims=True), (rows, 128)
-            )
-
-        rows_in = rows_ref[:rows]
-        grad_rows = grads_ref[:rows]
-        gate = slot_gate[:rows, :1]
+        return mask, jnp.where(mask, 1.0, 0.0).astype(jnp.bfloat16)
+
+    def enter(rows):
+        mask, picks = slots(rows)
+        rows_in = jnp.dot(picks, normed_ref[...], preferred_element_type=jnp.float32).astype(jnp.bfloat16)
+        grad_rows = jnp.dot(picks, grad_ref[...], preferred_element_type=jnp.float32).astype(jnp.bfloat16)
+        rows_ref[:rows] = rows_in
+        grads_ref[:rows] = grad_rows
+        gate = jnp.sum(jnp.where(mask, gate_ref[0], 0.0), axis=1, keepdims=True)
         gate_input = jnp.dot(rows_in, gate_w[0], preferred_element_type=jnp.float32)
         up_input = jnp.dot(rows_in, up_w[0], preferred_element_type=jnp.float32)
         grad_act = right_inner(grad_rows, down_w[0])
         sigmoid_val = jax.nn.sigmoid(gate_input)
         silu_out = gate_input * sigmoid_val
         hidden = silu_out * up_input
-        activation = (hidden * gate).astype(jnp.bfloat16)
+        active_ref[:rows] = (hidden * gate).astype(jnp.bfloat16)
         column = jnp.sum(grad_act * hidden, axis=1, keepdims=True)
+        gates_out[0] = jnp.sum(jnp.where(mask, column, 0.0), axis=0, keepdims=True)
         grad_hidden = grad_act * gate
-        grad_gate_in = (
+        gate_in_ref[:rows] = (
             grad_hidden * up_input * sigmoid_val * (1.0 + gate_input * (1.0 - sigmoid_val))
         ).astype(jnp.bfloat16)
-        grad_up_in = (grad_hidden * silu_out).astype(jnp.bfloat16)
-        lanes = pl.ds(pl.multiple_of(half * block, block), block)
-        grads = left_inner(rows_in, jnp.concatenate([grad_gate_in, grad_up_in], 1))
-        grads_out[0, 0, :, lanes] = grads[:, :block]
-        grads_out[0, 1, :, lanes] = grads[:, block:]
-        grad_down = left_inner(activation, grad_rows)
-        hidden_all, width = grads_out.shape[3], grads_out.shape[2]
-        own = hidden_all // parts
-        blocks = width // hidden_all
-        for part in range(block // own):
+        up_in_ref[:rows] = (grad_hidden * silu_out).astype(jnp.bfloat16)
+
+    by_size(enter)
+    if chained:
+
+        @pl.when(expert == 0)
+        def _():
+            copy_moe.wait()
+            copy_back.wait()
+
+    def leave(rows):
+        mask, picks = slots(rows)
+        moe = jnp.dot(active_ref[:rows], down_w[0], preferred_element_type=jnp.float32)
+        moe_out[...] += left_inner(picks, moe.astype(jnp.bfloat16))
+        back = right_inner(gate_in_ref[:rows], gate_w[0]) + right_inner(up_in_ref[:rows], up_w[0])
+        back_out[...] += left_inner(picks, back.astype(jnp.bfloat16))
+
+    by_size(leave)
+
+    def copies(target, number):
+        return [
+            pltpu.make_async_copy(weights_ref.at[kind], target.at[number, kind], out_sems.at[kind])
+            for kind in range(3)
+        ]
+
+    @pl.when(expert > 0)
+    def _():
+        for copy in copies(grads_out[0], 0):
+            copy.wait()
+
+    def weigh(rows):
+        grads = left_inner(
+            rows_ref[:rows], jnp.concatenate([gate_in_ref[:rows], up_in_ref[:rows]], 1)
+        )
+        weights_ref[0] = grads[:, :hidden_size]
+        weights_ref[1] = grads[:, hidden_size:]
+        grad_down = left_inner(active_ref[:rows], grads_ref[:rows])
+        own = hidden_size // parts
+        blocks = width // hidden_size
+        for part in range(parts):
             for piece in range(blocks):
-                at = half * (block // own) * blocks * own + (part * blocks + piece) * own
-                grads_out[0, 2, pl.ds(pl.multiple_of(at, own), own), :] = grad_down[
-                    part * own : (part + 1) * own, piece * hidden_all : (piece + 1) * hidden_all
+                at = (part * blocks + piece) * own
+                weights_ref[2, at : at + own, :] = grad_down[
+                    part * own : (part + 1) * own, piece * hidden_size : (piece + 1) * hidden_size
                 ]
-        moe = jnp.dot(activation, down_w[0], preferred_element_type=jnp.float32)
-        back = right_inner(grad_gate_in, gate_w[0]) + right_inner(grad_up_in, up_w[0])
-
-        @pl.when(half == 0)
+
+    by_size(weigh)
+    start = 0
+    for target, number in zip(grads_out, numbers):
+
+        @pl.when((expert >= start) & (expert < start + number))
         def _():
-            moe_rows[:rows] = moe
-            back_rows[:rows] = back
-            slot_grad[:rows] = jnp.broadcast_to(column, (rows, 128))
-
-        @pl.when((half > 0) & (half < halves - 1))
-        def _():
-            moe_rows[:rows] += moe
-            back_rows[:rows] += back
-            slot_grad[:rows] += jnp.broadcast_to(column, (rows, 128))
-
-        @pl.when(half == halves - 1)
-        def _():
-            picks = jnp.where(mask, 1.0, 0.0).astype(jnp.bfloat16)
-            moe_out[...] += left_inner(picks, (moe_rows[:rows] + moe).astype(jnp.bfloat16))
-            back_out[...] += left_inner(picks, (back_rows[:rows] + back).astype(jnp.bfloat16))
-            total = slot_grad[:rows, :1] + column
-            gates_out[0] = jnp.sum(jnp.where(mask, total, 0.0), axis=0, keepdims=True)
-
-    sizes = (128, 256, CAP)
-    for low, rows in zip((-1,) + sizes[:-1], sizes):
-        pl.when((filled > low) & (filled <= rows))(functools.partial(run, rows))
-
-
-def expert_stage(parts, first, last, counts, places, gate_rows, normed_b, grad_b, gate_w, up_w, down_w, sums):
-    number = last - first
+            for copy in copies(target, expert - start):
+                copy.start()
+
+        start += number
+
+    @pl.when(expert == pl.num_programs(0) - 1)
+    def _():
+        for copy in copies(grads_out[0], 0):
+            copy.wait()
+
+
+def expert_stage(parts, first, numbers, counts, places, gate_rows, normed_b, grad_b, gate_w, up_w, down_w, sums):
+    number = sum(numbers)
     length, width = normed_b.shape
     hidden = gate_w.shape[2]
-    block = 256
-    halves = hidden // block
     experts = places.shape[0]
     chained = sums is not None
-    whole = lambda e, h, c: (0, 0)
-    row_spec = pl.BlockSpec((1, 1, length), lambda e, h, c: (first + e, 0, 0))
+    whole = lambda e, c: (0, 0)
+    row_spec = pl.BlockSpec((1, 1, length), lambda e, c: (first + e, 0, 0))
     once = pl.Buffered(1)
+    f32, bf16 = jnp.float32, jnp.bfloat16
     in_specs = [
         row_spec,
         row_spec,
         pl.BlockSpec((length, width), whole, pipeline_mode=once),
         pl.BlockSpec((length, width), whole, pipeline_mode=once),
-        pl.BlockSpec((1, width, block), lambda e, h, c: (first + e, 0, h)),
-        pl.BlockSpec((1, width, block), lambda e, h, c: (first + e, 0, h)),
-        pl.BlockSpec((1, block, width), lambda e, h, c: (first + e, h, 0)),
+        pl.BlockSpec((1, width, hidden), lambda e, c: (first + e, 0, 0)),
+        pl.BlockSpec((1, width, hidden), lambda e, c: (first + e, 0, 0)),
+        pl.BlockSpec((1, hidden, width), lambda e, c: (first + e, 0, 0)),
     ]
     args = [
         counts,
@@ -395,42 +412,251 @@
     if chained:
         in_specs += [pl.BlockSpec(memory_space=pl.ANY)] * 2
         args += [sums[0], sums[1]]
-    grads, moe, back, gates = pl.pallas_call(
-        functools.partial(expert_kernel, parts, first, chained),
-        out_shape=[
-            jax.ShapeDtypeStruct((number, 3, width, hidden), jnp.float32),
-            jax.ShapeDtypeStruct((length, width), jnp.float32),
-            jax.ShapeDtypeStruct((length, width), jnp.float32),
-            jax.ShapeDtypeStruct((number, 1, length), jnp.float32),
+    results = pl.pallas_call(
+        functools.partial(expert_kernel, parts, first, numbers, chained),
+        out_shape=[jax.ShapeDtypeStruct((some, 3, width, hidden), f32) for some in numbers]
+        + [
+            jax.ShapeDtypeStruct((length, width), f32),
+            jax.ShapeDtypeStruct((length, width), f32),
+            jax.ShapeDtypeStruct((number, 1, length), f32),
         ],
         grid_spec=pltpu.PrefetchScalarGridSpec(
             num_scalar_prefetch=1,
-            grid=(number, halves),
+            grid=(number,),
             in_specs=in_specs,
-            out_specs=[
-                pl.BlockSpec((1, 3, width, hidden), lambda e, h, c: (e, 0, 0, 0)),
+            out_specs=[pl.BlockSpec(memory_space=pl.ANY)] * len(numbers)
+            + [
                 pl.BlockSpec((length, width), whole, pipeline_mode=once),
                 pl.BlockSpec((length, width), whole, pipeline_mode=once),
-                pl.BlockSpec((1, 1, length), lambda e, h, c: (e, 0, 0)),
+                pl.BlockSpec((1, 1, length), lambda e, c: (e, 0, 0)),
             ],
             scratch_shapes=[
-                pltpu.VMEM((CAP, width), jnp.bfloat16),
-                pltpu.VMEM((CAP, width), jnp.bfloat16),
-                pltpu.VMEM((CAP, width), jnp.float32),
-                pltpu.VMEM((CAP, width), jnp.float32),
-                pltpu.VMEM((CAP, 128), jnp.float32),
-                pltpu.VMEM((CAP, 128), jnp.float32),
+                pltpu.VMEM((CAP, width), bf16),
+                pltpu.VMEM((CAP, width), bf16),
+                pltpu.VMEM((CAP, hidden), bf16),
+                pltpu.VMEM((CAP, hidden), bf16),
+                pltpu.VMEM((CAP, hidden), bf16),
+                pltpu.VMEM((3, width, hidden), f32),
                 pltpu.SemaphoreType.DMA((2,)),
+                pltpu.SemaphoreType.DMA((3,)),
             ],
         ),
         compiler_params=pltpu.CompilerParams(
-            dimension_semantics=("arbitrary", "arbitrary"), vmem_limit_bytes=63 << 20
+            dimension_semantics=("arbitrary",), vmem_limit_bytes=63 << 20
         ),
         cost_estimate=pl.CostEstimate(
             flops=number * 8 * 10**9, bytes_accessed=number * 14 * 10**6, transcendentals=0
         ),
     )(*args)
-    return (grads, (moe, back, gates))
+    return results[: len(numbers)], results[len(numbers) :]
+
+
+PIECES = 16
+
+
+def line_gather_kernel(n, x_ref, out_ref, blocks_ref, recv, up_send, down_send):
+    me = lax.axis_index("tensor")
+    has_low, has_high = me > 0, me < n - 1
+    barrier = pltpu.get_barrier_semaphore()
+
+    @pl.when(has_low)
+    def _():
+        pl.semaphore_signal(barrier, inc=1, device_id={"tensor": me - 1}, device_id_type=MESH)
+
+    @pl.when(has_high)
+    def _():
+        pl.semaphore_signal(barrier, inc=1, device_id={"tensor": me + 1}, device_id_type=MESH)
+
+    blocks_ref[me] = x_ref[...].astype(jnp.float32)
+    pl.semaphore_wait(barrier, has_low.astype(jnp.int32) + has_high.astype(jnp.int32))
+    rows = x_ref.shape[0] // PIECES
+
+    def copy(block, c, send, to):
+        piece = blocks_ref.at[block, pl.ds(pl.multiple_of(c * rows, rows), rows), :]
+        return pltpu.make_async_remote_copy(
+            src_ref=piece,
+            dst_ref=piece,
+            send_sem=send.at[block, c],
+            recv_sem=recv.at[block, c],
+            device_id={"tensor": to},
+            device_id_type=MESH,
+        )
+
+    for hop in range(n):
+        low, high = me - hop, me + hop
+
+        def step(c, carry):
+            @pl.when(low >= 0)
+            def _():
+                if hop > 0:
+                    copy(low, c, up_send, me).wait_recv()
+
+                @pl.when(has_high)
+                def _():
+                    copy(low, c, up_send, me + 1).start()
+
+            @pl.when(high < n)
+            def _():
+                if hop > 0:
+                    copy(high, c, down_send, me).wait_recv()
+
+                @pl.when(has_low)
+                def _():
+                    copy(high, c, down_send, me - 1).start()
+
+            return carry
+
+        lax.fori_loop(0, PIECES, step, 0)
+    wide = x_ref.shape[1]
+    for block in range(n):
+        out_ref[:, block * wide : (block + 1) * wide] = blocks_ref[block].astype(jnp.bfloat16)
+    for hop in range(n):
+        low, high = me - hop, me + hop
+
+        def drain(c, carry):
+            @pl.when((low >= 0) & has_high)
+            def _():
+                copy(low, c, up_send, me).wait_send()
+
+            @pl.when((high < n) & has_low)
+            def _():
+                copy(high, c, down_send, me).wait_send()
+
+            return carry
+
+        lax.fori_loop(0, PIECES, drain, 0)
+
+
+def line_gather(x, n, name):
+    length, wide = x.shape
+    full = pl.BlockSpec(memory_space=pltpu.VMEM)
+    return pl.pallas_call(
+        functools.partial(line_gather_kernel, n),
+        out_shape=jax.ShapeDtypeStruct((length, n * wide), jnp.bfloat16),
+        in_specs=[full],
+        out_specs=full,
+        scratch_shapes=[pltpu.VMEM((n, length, wide), jnp.float32)]
+        + [pltpu.SemaphoreType.DMA((n, PIECES))] * 3,
+        compiler_params=pltpu.CompilerParams(
+            collective_id=name, has_side_effects=True, vmem_limit_bytes=32 << 20
+        ),
+        cost_estimate=pl.CostEstimate(
+            flops=0, bytes_accessed=16 * n * x.size, transcendentals=0
+        ),
+    )(x)
+
+
+BLOCK = 256
+
+
+def own_rows_kernel(parts, weight_ref, out_ref):
+    rows = out_ref.shape[0]
+    first = lax.axis_index("dp") * rows if parts > 1 else 0
+    out_ref[...] = weight_ref[pl.ds(pl.multiple_of(first, 16), rows), :].astype(jnp.float32)
+
+
+def gather_out_weight(out_weight, parts):
+    rows, width = out_weight.shape
+    ways = parts if rows % (16 * parts) == 0 else 1
+    full = pl.BlockSpec(memory_space=pltpu.VMEM)
+    own = pl.pallas_call(
+        functools.partial(own_rows_kernel, ways),
+        out_shape=jax.ShapeDtypeStruct((rows // ways, width), jnp.float32),
+        in_specs=[full],
+        out_specs=full,
+    )(out_weight)
+    gathered = lax.all_gather(own, "tensor")
+    return lax.all_gather(gathered, "dp") if ways > 1 else gathered[None]
+
+
+def middle_kernel(
+    attended_ref, weight_all_ref, tokens_ref, gain_ref, router_ref, chosen_ref, middle_out, normed_out, gates_out, weight_ref
+):
+    ways, n, rows, unused = weight_all_ref.shape
+    for way in range(ways):
+        for block in range(n):
+            at = (block * ways + way) * rows
+            weight_ref[at : at + rows, :] = weight_all_ref[way, block].astype(jnp.bfloat16)
+    for first in range(0, tokens_ref.shape[0], BLOCK):
+        own = slice(first, first + BLOCK)
+        branch = jnp.dot(attended_ref[own, :], weight_ref[...], preferred_element_type=jnp.float32)
+        middle = tokens_ref[own, :].astype(jnp.float32) + RESIDUAL * branch
+        middle_out[own, :] = middle
+        recip = lax.rsqrt(jnp.mean(middle * middle, axis=1, keepdims=True) + EPSILON)
+        normed = (middle * recip * gain_ref[...]).astype(jnp.bfloat16)
+        normed_out[own, :] = normed
+        logits = jnp.dot(normed, router_ref[...], preferred_element_type=jnp.float32)
+        raised = jnp.where(chosen_ref[own, :] > 0.0, jnp.exp(logits), 0.0)
+        gates_out[own, :] = raised / jnp.sum(raised, axis=1, keepdims=True)
+
+
+def enter_middle(attended, weight_all, tokens, gain, router, chosen):
+    length, width = tokens.shape
+    full = pl.BlockSpec(memory_space=pltpu.VMEM)
+    return pl.pallas_call(
+        middle_kernel,
+        out_shape=[
+            jax.ShapeDtypeStruct((length, width), jnp.float32),
+            jax.ShapeDtypeStruct((length, width), jnp.bfloat16),
+            jax.ShapeDtypeStruct((length, router.shape[1]), jnp.float32),
+        ],
+        in_specs=[full] * 6,
+        out_specs=[full] * 3,
+        scratch_shapes=[pltpu.VMEM((attended.shape[1], width), jnp.bfloat16)],
+        compiler_params=pltpu.CompilerParams(vmem_limit_bytes=56 << 20),
+        cost_estimate=pl.CostEstimate(
+            flops=2 * length * width * width, bytes_accessed=25 * 10**6, transcendentals=0
+        ),
+    )(attended, weight_all, tokens, gain.reshape(1, width), router, chosen)
+
+
+def turn_kernel(
+    summed_ref, grad_gates_ref, gates_ref, middle_ref, cotangent_ref, gain_ref, router_ref, grad_out, branch_out, logits_out, gain_out
+):
+    length, width = summed_ref.shape
+    experts = grad_gates_ref.shape[0]
+    gates_rows = jnp.concatenate(
+        [grad_gates_ref[...], jnp.zeros((128 - experts, length), jnp.float32)], 0
+    )
+    gain_sum = jnp.zeros((1, width), jnp.float32)
+    for first in range(0, length, BLOCK):
+        own = slice(first, first + BLOCK)
+        grad_gates = jnp.transpose(gates_rows[:, own])
+        gates = gates_ref[own, :]
+        weighted = jnp.sum(gates * grad_gates, axis=1, keepdims=True)
+        grad_logits = (gates * (grad_gates - weighted)).astype(jnp.bfloat16)
+        logits_out[own, :] = grad_logits
+        grad = summed_ref[own, :] + right_inner(grad_logits, router_ref[...])
+        middle = middle_ref[own, :]
+        recip = lax.rsqrt(jnp.mean(middle * middle, axis=1, keepdims=True) + EPSILON)
+        unit = middle * recip
+        gain_sum += jnp.sum(grad * unit, axis=0, keepdims=True)
+        scaled = grad * gain_ref[...]
+        back = recip * (scaled - unit * jnp.mean(scaled * unit, axis=1, keepdims=True))
+        total = cotangent_ref[own, :].astype(jnp.float32) + back
+        grad_out[own, :] = total
+        branch_out[own, :] = (RESIDUAL * total).astype(jnp.bfloat16)
+    gain_out[...] = gain_sum
+
+
+def turn_middle(summed, grad_gates, gates, middle, cotangent, gain, router):
+    length, width = summed.shape
+    full = pl.BlockSpec(memory_space=pltpu.VMEM)
+    return pl.pallas_call(
+        turn_kernel,
+        out_shape=[
+            jax.ShapeDtypeStruct((length, width), jnp.float32),
+            jax.ShapeDtypeStruct((length, width), jnp.bfloat16),
+            jax.ShapeDtypeStruct((length, gates.shape[1]), jnp.bfloat16),
+            jax.ShapeDtypeStruct((1, width), jnp.float32),
+        ],
+        in_specs=[full] * 7,
+        out_specs=[full] * 4,
+        compiler_params=pltpu.CompilerParams(vmem_limit_bytes=48 << 20),
+        cost_estimate=pl.CostEstimate(
+            flops=40 * length * width, bytes_accessed=25 * 10**6, transcendentals=0
+        ),
+    )(summed, grad_gates, gates, middle, cotangent, gain.reshape(1, width), router)
 
 
 SPAN = 768
@@ -796,7 +1022,7 @@
             for i in range(parts >> (level + 1))
         ]
 
-    stops = [10, 12, 14, 10]
+    stops = [6, 26, 16, 4]
     for level in range(levels):
         for copy in copies(level):
             copy.start()
@@ -819,7 +1045,6 @@
 def finish(n, parts, grad_local, normed_b, grads_wide, branch_b, attended, normed_two_b, grad_logits_b, ffn_gain_grad, name):
     length, width = normed_b.shape
     columns = grads_wide.shape[1] + attended.shape[1] + 128
-    logits = jnp.pad(grad_logits_b, ((0, 0), (0, 128 - grad_logits_b.shape[1])))
     full = pl.BlockSpec(memory_space=pltpu.VMEM)
     levels = parts.bit_length() - 1
     own = width // parts
@@ -843,8 +1068,8 @@
             flops=2 * length * width * columns, bytes_accessed=50 * 10**6, transcendentals=0
         ),
     )(
-        grad_local, normed_b, grads_wide, branch_b, attended, normed_two_b, logits,
-        ffn_gain_grad.reshape(1, width),
+        grad_local, normed_b, grads_wide, branch_b, attended, normed_two_b, grad_logits_b,
+        ffn_gain_grad,
     )
 
 
@@ -914,6 +1139,7 @@
     query_w, key_w, value_w = (pad_columns(w) for w in (query_weight, key_weight, value_weight))
     out_w = jnp.transpose(pad_columns(jnp.transpose(out_weight)))
     hidden_in = tokens.astype(jnp.float32)
+    out_all = gather_out_weight(out_weight, parts)
     normed_b, queries, keys, values, attended, logsum = attend_forward(
         tokens, attn_gain, query_w, key_w, value_w, tables, opening, heads_local, group_size
     )
@@ -925,26 +1151,27 @@
     places_in = slot_places(picked)
     counts = jnp.sum(picked, axis=1)
     grad_moe_b = (RESIDUAL * cotangent.astype(jnp.float32)).astype(jnp.bfloat16)
-    attn_out, unused = line_sum(
-        jnp.dot(attended, out_w, preferred_element_type=jnp.float32), None, ring, 1
-    )
-    middle = hidden_in + RESIDUAL * attn_out
-    normed_two, unit_two, recip_two = rms_forward(middle, ffn_gain)
-    normed_two_b = normed_two.astype(jnp.bfloat16)
-    logits = jnp.dot(normed_two_b, router_weight, preferred_element_type=jnp.float32)
-    raised = jnp.where(chosen, jnp.exp(logits), 0.0)
-    gate_probs = raised / jnp.sum(raised, axis=-1, keepdims=True)
+    attended_all = line_gather(attended, ring, 1)
+    attended_all = attended_all.reshape(length, ring, attended.shape[1])
+    attended_all = attended_all[:, :, : heads_local * HEAD].reshape(length, -1)
+    router_w = pad_columns(router_weight)
+    middle, normed_two_b, gate_probs = enter_middle(
+        attended_all, out_all, tokens, ffn_gain, router_w, pad_columns(chosen.astype(jnp.float32))
+    )
     gate_rows = jnp.transpose(lax.dynamic_slice_in_dim(gate_probs, first_expert, experts_local, 1))
-    early = 2 * experts_local // 5
-    grads_first, sums = expert_stage(
-        parts, 0, early, counts, places_in, gate_rows, normed_two_b, grad_moe_b,
+    numbers = (max(1, experts_local // 5), max(1, 3 * experts_local // 10))
+    numbers += (experts_local - sum(numbers),)
+    (grads_first,), sums = expert_stage(
+        parts, 0, numbers[:1], counts, places_in, gate_rows, normed_two_b, grad_moe_b,
         gate_weight, up_weight, down_weight, None,
     )
     shards_first = lax.psum_scatter(grads_first, "dp", scatter_dimension=2, tiled=True)
-    grads_last, sums_last = expert_stage(
-        parts, early, experts_local, counts, places_in, gate_rows, normed_two_b, grad_moe_b,
+    (grads_middle, grads_last), sums_last = expert_stage(
+        parts, numbers[0], numbers[1:], counts, places_in, gate_rows, normed_two_b, grad_moe_b,
         gate_weight, up_weight, down_weight, sums,
     )
+    shards_first, grads_middle = lax.optimization_barrier((shards_first, grads_middle))
+    shards_middle = lax.psum_scatter(grads_middle, "dp", scatter_dimension=2, tiled=True)
     moe_part, grad_normed_part, unused = sums_last
     grad_gates_local = jnp.concatenate([sums[2], sums_last[2]], 0)
     grad_gates_part = lax.dynamic_update_slice_in_dim(
@@ -954,18 +1181,14 @@
         0,
     ).reshape(-1, 128)
     grad_gates_part = jnp.pad(grad_gates_part, ((0, GATE_ROWS - grad_gates_part.shape[0]), (0, 0)))
+    shards_first, grad_normed_part = lax.optimization_barrier((shards_first, grad_normed_part))
     grad_normed_sum, gates_sum = line_sum(grad_normed_part, grad_gates_part, ring, 2)
-    grad_gates = jnp.transpose(
-        gates_sum[: experts_all * length // 128].reshape(experts_all, length)
-    )
-    weighted = jnp.sum(gate_probs * grad_gates, axis=-1, keepdims=True)
-    grad_logits_b = (gate_probs * (grad_gates - weighted)).astype(jnp.bfloat16)
-    grad_normed_two = grad_normed_sum + right_inner(grad_logits_b, router_weight)
-    grad_from_norm, grad_ffn_gain = rms_backward(grad_normed_two, unit_two, recip_two, ffn_gain)
-    grad_middle = cotangent.astype(jnp.float32) + grad_from_norm
-    grad_branch_b = (RESIDUAL * grad_middle).astype(jnp.bfloat16)
-    shards_first, grads_last, grad_branch_b = lax.optimization_barrier(
-        (shards_first, grads_last, grad_branch_b)
+    grad_gates = gates_sum[: experts_all * length // 128].reshape(experts_all, length)
+    grad_middle, grad_branch_b, grad_logits_b, grad_ffn_gain = turn_middle(
+        grad_normed_sum, grad_gates, gate_probs, middle, cotangent, ffn_gain, router_w
+    )
+    shards_middle, grads_last, grad_branch_b = lax.optimization_barrier(
+        (shards_middle, grads_last, grad_branch_b)
     )
     shards_last = lax.psum_scatter(grads_last, "dp", scatter_dimension=2, tiled=True)
     grads_wide, grad_normed_local, moe_out = attend_backward(
@@ -988,7 +1211,10 @@
     at_out = tiled_q + 256
     at_router = at_out + tiled_q
     grads_placed = place_shards(parts, shards_first, 0, experts_local, None)
-    grad_gate, grad_up, grad_down = place_shards(parts, shards_last, early, experts_local, grads_placed)
+    grads_placed = place_shards(parts, shards_middle, numbers[0], experts_local, grads_placed)
+    grad_gate, grad_up, grad_down = place_shards(
+        parts, shards_last, numbers[0] + numbers[1], experts_local, grads_placed
+    )
     return (
         output,
         grad_tokens,

time: 1020 us -> 996 us (0.976)
  Pallas kernels: 906 us -> 828 us
  waiting for transfers between devices: 0.04 us -> 77.1 us
  other arithmetic: 44.8 us -> 28.7 us
    pallas_call x2 -> x1, Pallas kernels: 316 us -> 162 us  [line_sum(): pl.pallas_call(functools.partial(line_sum_kernel, n, count), out_shape=sh...]
    pallas_call x2 -> x6, Pallas kernels: 157 us -> 266 us  [the longest x2 131 us: expert_stage(): pl.pallas_call(functools.partial(expert_kernel, parts, first, numbers, ch...]
    reduce_scatter x1, waiting for transfers between devices: 0.01 us -> 45.2 us  [on_device(): lax.psum_scatter(grads_first, 'dp', scatter_dimension=2, tiled=True)]
    pallas_call x1, Pallas kernels: 214 us -> 174 us  [finish(): pl.pallas_call(functools.partial(finish_kernel, n, parts), out_shape=[jax...]
    all_gather x0 -> x2, waiting for transfers between devices: none -> 31.9 us  [the longest x1 31.9 us: gather_out_weight(): gathered = lax.all_gather(own, 'tensor')]
  transfers between devices with their start and end apart: 2 -> 5, of which waited for: 0 -> 2; matrix products, arithmetic and copies ran while one was open for 4% -> 4% of each run, Pallas kernels for 64% -> 77%
where the time goes in v3:
time: 996 us; the launch traced here: 988 us
  Pallas kernels  828 us (83%)
  waiting for transfers between devices  77.1 us (8%)
  other arithmetic  28.7 us (3%)
  local copies, waits for them, and re-layouts  25.6 us (3%)
  between operations  15.1 us (2%)
  blocking collectives  12 us (1%)
    pallas_call x1, Pallas kernels, attend_backward(): pl.pallas_call(functools.partial(attend_backward_kernel, n, heads, group)...  190 us
    pallas_call x1, Pallas kernels, finish(): pl.pallas_call(functools.partial(finish_kernel, n, parts), out_shape=[jax...  174 us
    pallas_call x1, Pallas kernels, line_sum(): pl.pallas_call(functools.partial(line_sum_kernel, n, count), out_shape=sh...  162 us
    pallas_call x2, Pallas kernels, expert_stage(): pl.pallas_call(functools.partial(expert_kernel, parts, first, numbers, ch...  131 us
    pallas_call x1, Pallas kernels, line_gather(): pl.pallas_call(functools.partial(line_gather_kernel, n), out_shape=jax.Sh...  104 us
    reduce_scatter x1, waiting for transfers between devices, on_device(): lax.psum_scatter(grads_first, 'dp', scatter_dimension=2, tiled=True)  45.2 us
    all_gather x1, waiting for transfers between devices, gather_out_weight(): gathered = lax.all_gather(own, 'tensor')  31.9 us
    pallas_call x1, Pallas kernels, attend_forward(): pl.pallas_call(functools.partial(attend_forward_kernel, heads, group), ou...  21.6 us
  transfers between devices with their start and end apart: 5, of which 2 were waited for; matrix products, arithmetic and copies ran while one was open for 4% of the time, Pallas kernels for 77%

profile of v3, /device:TPU:8, one launch (start us, length us, event | category | flops | bytes accessed | tf_op | source)
XLA Modules:
  0.0 987.5 jit_solution(4616951727136684812)
XLA Ops:
  7.3 2.1 shard_map.231
  9.5 31.9 %all-gather.5.cloned.1.call-done = f32[192,1536]{1,0:T(8,128)} async-done(((f32[48,1536]{1,0:T(8,128)}), f32[192,1536]{1,0:T(8,128)}) %all-gather.5.cloned.1.call-update) | async-done | bytes 1179664 | tf_op jit(solution)/shard_map/all_gather | solution.py:568
  43.7 1.9 multiply_sine_fusion
  47.0 21.6 %shard_map.229 = (bf16[1024,1536]{1,0:T(8,128)(2,1)}, bf16[3,1024,128]{2,1,0:T(8,128)(2,1)S(1)}, bf16[1024,128]{1,0:T(8,128)(2,1)S(1)}, bf16[1024,128]{1,0:T(8,1...) custom-call(bf16[1024,1536]{1,0:T(8,128)(2,1)} %tokens_ref.3, f32[1,1536]{1,0:T(1,128)S(1)} %reshape.85.gain_ref, ...), custom_call_target="tpu_custom_call" | custom-call | flops 8000000000 | bytes 12000000 | tf_op jit(solution)/shard_map/pallas_call | solution.py:780
  68.7 103.9 %shard_map.230.attended_ref = bf16[1024,1536]{1,0:T(8,128)(2,1)S(1)} custom-call(bf16[1024,384]{1,0:T(8,128)(2,1)S(1)} %get-tuple-element.59.x_ref.attended_ref), custom_call_target="tpu_custom_call" | custom-call | bytes 25165824 | tf_op jit(solution)/shard_map/pallas_call | solution.py:533
  179.2 4.1 multiply_convert_fusion.grad_ref
  183.3 15.8 %shard_map.232 = (f32[1024,1536]{1,0:T(8,128)}, bf16[1024,1536]{1,0:T(8,128)(2,1)}, f32[1024,128]{1,0:T(8,128)}) custom-call(bf16[1024,1536]{1,0:T(8,128)(2,1)} %copy-done.2, f32[8,4,48,1536]{3,2,1,0:T(8,128)} %bitcast.20, bf16[1024,1536]{1,0:T(8,128)(2,1)} %tokens_ref.3, f32[1,1536]{1,0:T(1,128)} %reshape.86.gain_ref, bf16[1536,128]{1,0:T(8,128)(2,1)} %pad.14.router_ref, ...), custom_call_target="tpu_custom_call" | custom-call | flops 4831838208 | bytes 25000000 | tf_op jit(solution)/shard_map/pallas_call | solution.py:596
  201.1 42.2 %shard_map.233 = (f32[2,3,1536,512]{3,2,1,0:T(8,128)}, f32[1024,1536]{1,0:T(8,128)}, f32[1024,1536]{1,0:T(8,128)}, f32[2,1,1024]{2,1,0:T(1,128)}) custom-call(s32[10]{0:T(128)} %get-tuple-element.169.count_ref, s32[10,1,1024]{2,1,0:T(1,128)} %reshape.87.place_ref, f32[10,1,1024]{2,1,0:T(1,128)} %reshape.88.gate_ref, ...), custom_call_target="tpu_custom_call" | custom-call | flops 16000000000 | bytes 28000000 | tf_op jit(solution)/shard_map/pallas_call | solution.py:415
  243.4 89.0 %shard_map.234 = (f32[3,3,1536,512]{3,2,1,0:T(8,128)}, f32[5,3,1536,512]{3,2,1,0:T(8,128)}, f32[1024,1536]{1,0:T(8,128)}, f32[1024,1536]{1,0:T(8,128)}, f32[8,1,1024]{2,1,0:T(1,128)}) custom-call(s32[10]{0:T(128)} %get-tuple-element.169.count_ref, s32[10,1,1024]{2,1,0:T(1,128)} %reshape.87.place_ref, f32[10,1,1024]{2,1,0:T(1,128)} %reshape.88.gate_ref, ...), custom_call_target="tpu_custom_call" | custom-call | flops 64000000000 | bytes 112000000 | tf_op jit(solution)/shard_map/pallas_call | solution.py:415
  332.4 45.2 %reduce-scatter.4.cloned.1.call-done.shards_ref = f32[2,3,192,512]{3,2,1,0:T(8,128)} async-done(((f32[2,3,1536,512]{3,2,1,0:T(8,128)}), f32[2,3,192,512]{3,2,1,0:T(8,128)}) %reduce-scatter.4.cloned.1.call-update) | async-done | bytes 2359312 | tf_op jit(solution)/shard_map/reduce_scatter | solution.py:1168
  379.0 2.8 copy-done.1
  381.8 162.4 %shard_map.235 = (f32[1024,1536]{1,0:T(8,128)S(1)}, f32[512,128]{1,0:T(8,128)S(1)}) custom-call(f32[1024,1536]{1,0:T(8,128)S(1)} %copy-done.1, f32[512,128]{1,0:T(8,128)S(1)} %pad.17.refs_1_), custom_call_target="tpu_custom_call" | custom-call | flops 4915200 | bytes 13107200 | tf_op jit(solution)/shard_map/pallas_call | solution.py:228
  544.2 2.6 copy-done
  546.9 13.0 %shard_map.236 = (f32[1024,1536]{1,0:T(8,128)}, bf16[1024,1536]{1,0:T(8,128)(2,1)S(1)}, bf16[1024,128]{1,0:T(8,128)(2,1)S(1)}, f32[1,1536]{1,0:T(1,128)S(1)}) custom-call(f32[1024,1536]{1,0:T(8,128)} %copy-done, f32[40,1024]{1,0:T(8,128)S(1)} %reshape.91.grad_gates_ref, f32[1024,128]{1,0:T(8,128)S(1)} %copy-done.5, ...), custom_call_target="tpu_custom_call" | custom-call | flops 62914560 | bytes 25000000 | tf_op jit(solution)/shard_map/pallas_call | solution.py:645
  565.4 2.8 shard_map.239
  568.2 190.0 %shard_map.237 = (bf16[1024,640]{1,0:T(8,128)(2,1)}, f32[1024,1536]{1,0:T(8,128)}, f32[1024,1536]{1,0:T(8,128)}) custom-call(bf16[1024,1536]{1,0:T(8,128)(2,1)} %copy-done.3, bf16[384,1536]{1,0:T(8,128)(2,1)} %out_w.1, bf16[3,1024,128]{2,1,0:T(8,128)(2,1)} %copy-done.16, bf16[1024,128]{1,0:T(8,128)(2,1)} %copy-done.17, bf16[1024,128]{1,0:T(8,128)(2,1)} %copy-done.18, ...), custom_call_target="tpu_custom_call" | custom-call | flops 12000000000 | bytes 30000000 | tf_op jit(solution)/shard_map/pallas_call | solution.py:930
  758.2 174.0 %shard_map.238 = (f32[1024,1536]{1,0:T(8,128)}, f32[192,1152]{1,0:T(8,128)}) custom-call(f32[1024,1536]{1,0:T(8,128)} %get-tuple-element.85.local_ref, bf16[1024,1536]{1,0:T(8,128)(2,1)} %get-tuple-element.86.normed_ref, bf16[1024,640]{1,0:T(8,128)(2,1)} %get-tuple-element.87.grads_ref, bf16[1024,1536]{1,0:T(8,128)(2,1)} %copy-done.3, ...), custom_call_target="tpu_custom_call" | custom-call | flops 3623878656 | bytes 50000000 | tf_op jit(solution)/shard_map/pallas_call | solution.py:1052
  933.9 3.9 fusion.7
  937.7 12.0 %all-reduce.3 = f32[1536]{0:T(1024)S(1)} all-reduce(f32[1536]{0:T(1024)S(1)} %get-tuple-element.166), channel_id=7, replica_groups=mesh['dp'=8,'tensor'=4] {'dp'}, use_global_device_ids=true, to_apply=%region_10.11.clone | all-reduce | flops 1536 | bytes 12288
  950.4 4.6 shard_map.240
  958.3 2.1 slice_bitcast_fusion
  960.4 8.0 add_convert_fusion
  968.4 5.5 fusion.6
  973.9 6.9 shard_map.241
  (112 shorter events, 24.0 us)
Async XLA Ops:
  7.2 39.8 %copy-start.13 = (bf16[1536,384]{1,0:T(8,128)(2,1)S(1)}, bf16[1536,384]{1,0:T(8,128)(2,1)}, u32[]{:S(2)}) copy-start(bf16[1536,384]{1,0:T(8,128)(2,1)} %query_w.3) | copy-start | bytes 3538948
  7.2 39.8 %copy-start.14 = (bf16[1536,128]{1,0:T(8,128)(2,1)S(1)}, bf16[1536,128]{1,0:T(8,128)(2,1)}, u32[]{:S(2)}) copy-start(bf16[1536,128]{1,0:T(8,128)(2,1)} %key_w.3) | copy-start | bytes 1179652
  7.2 39.8 %copy-start.15 = (bf16[1536,128]{1,0:T(8,128)(2,1)S(1)}, bf16[1536,128]{1,0:T(8,128)(2,1)}, u32[]{:S(2)}) copy-start(bf16[1536,128]{1,0:T(8,128)(2,1)} %value_w.3) | copy-start | bytes 1179652
  7.2 34.1 %all-gather.5.cloned.1.call-start = ((), (), s32[]{:S(2)}) async-start(), calls=%async_computation.6 | async-start | bytes 1474560 | tf_op jit(solution)/shard_map/all_gather | solution.py:568
  9.4 173.9 %all-gather.7.cloned.1.call-start = ((), (), s32[]{:S(2)}) async-start(), calls=%async_computation.7 | async-start | bytes 10616832 | tf_op jit(solution)/shard_map/all_gather | solution.py:569
  41.3 336.2 %reduce-scatter.4.cloned.1.call-start = ((), (), s32[]{:S(2)}) async-start(), calls=%async_computation.3 | async-start | bytes 21233664 | tf_op jit(solution)/shard_map/reduce_scatter | solution.py:1168
  43.4 25.2 %copy-start.24 = (s32[1024]{0:T(1024)}, s32[1024]{0:T(1024)S(1)}, u32[]{:S(2)}) copy-start(s32[1024]{0:T(1024)S(1)} %convert_reduce_fusion) | copy-start | bytes 12292
  46.9 21.7 %copy-start.7 = (f32[1024,128]{1,0:T(8,128)}, f32[1024,128]{1,0:T(8,128)S(1)}, u32[]{:S(2)}) copy-start(f32[1024,128]{1,0:T(8,128)S(1)} %get-tuple-element.174.sine_high_ref) | copy-start | bytes 1572868
  46.9 21.7 %copy-start.8 = (f32[1024,128]{1,0:T(8,128)}, f32[1024,128]{1,0:T(8,128)S(1)}, u32[]{:S(2)}) copy-start(f32[1024,128]{1,0:T(8,128)S(1)} %get-tuple-element.175.sine_low_ref) | copy-start | bytes 1572868
  46.9 21.7 %copy-start.9 = (f32[1024,128]{1,0:T(8,128)}, f32[1024,128]{1,0:T(8,128)S(1)}, u32[]{:S(2)}) copy-start(f32[1024,128]{1,0:T(8,128)S(1)} %get-tuple-element.179.cosine_ref) | copy-start | bytes 1572868
  47.0 127.4 %copy-start.27 = (f32[1536]{0:T(1024)S(1)}, f32[1536]{0:T(1024)}, u32[]{:S(2)}) copy-start(f32[1536]{0:T(1024)} %param.23) | copy-start | bytes 18436
  47.0 128.0 %copy-start.22 = (bf16[1536,40]{0,1:T(8,128)(2,1)S(1)}, bf16[1536,40]{0,1:T(8,128)(2,1)}, u32[]{:S(2)}) copy-start(bf16[1536,40]{0,1:T(8,128)(2,1)} %param.24) | copy-start | bytes 368644
  47.0 128.2 %copy-start.21 = (s32[1024,8]{0,1:T(8,128)S(1)}, s32[1024,8]{0,1:T(8,128)}, u32[]{:S(2)}) copy-start(s32[1024,8]{0,1:T(8,128)} %param.17) | copy-start | bytes 98308
  68.7 104.0 %copy-start.16 = (bf16[3,1024,128]{2,1,0:T(8,128)(2,1)}, bf16[3,1024,128]{2,1,0:T(8,128)(2,1)S(1)}, u32[]{:S(2)}) copy-start(bf16[3,1024,128]{2,1,0:T(8,128)(2,1)S(1)} %get-tuple-element.78.query_ref) | copy-start | bytes 2359300
  68.7 104.0 %copy-start.17 = (bf16[1024,128]{1,0:T(8,128)(2,1)}, bf16[1024,128]{1,0:T(8,128)(2,1)S(1)}, u32[]{:S(2)}) copy-start(bf16[1024,128]{1,0:T(8,128)(2,1)S(1)} %get-tuple-element.79.key_ref) | copy-start | bytes 786436
  68.7 104.0 %copy-start.18 = (bf16[1024,128]{1,0:T(8,128)(2,1)}, bf16[1024,128]{1,0:T(8,128)(2,1)S(1)}, u32[]{:S(2)}) copy-start(bf16[1024,128]{1,0:T(8,128)(2,1)S(1)} %get-tuple-element.80.value_ref) | copy-start | bytes 786436
  68.7 114.6 %copy-start.4 = (bf16[1024,384]{1,0:T(8,128)(2,1)}, bf16[1024,384]{1,0:T(8,128)(2,1)S(1)}, u32[]{:S(2)}) copy-start(bf16[1024,384]{1,0:T(8,128)(2,1)S(1)} %get-tuple-element.59.x_ref.attended_ref) | copy-start | bytes 2359300
  68.7 114.6 %copy-start.19 = (f32[6,1,1024]{2,1,0:T(1,128)}, f32[6,1,1024]{2,1,0:T(1,128)S(1)}, u32[]{:S(2)}) copy-start(f32[6,1,1024]{2,1,0:T(1,128)S(1)} %get-tuple-element.81.logsum_ref) | copy-start | bytes 73732
  243.3 319.5 %reduce-scatter.6.cloned.1.call-start = ((), (), s32[]{:S(2)}) async-start(), calls=%async_computation.4 | async-start | bytes 31850496 | tf_op jit(solution)/shard_map/reduce_scatter | solution.py:1174
  377.6 169.3 %copy-start.5 = (f32[1024,128]{1,0:T(8,128)S(1)}, f32[1024,128]{1,0:T(8,128)}, u32[]{:S(2)}) copy-start(f32[1024,128]{1,0:T(8,128)} %get-tuple-element.61.gates_ref) | copy-start | bytes 1572868
  377.6 169.3 %copy-start.6 = (bf16[1536,128]{1,0:T(8,128)(2,1)S(1)}, bf16[1536,128]{1,0:T(8,128)(2,1)}, u32[]{:S(2)}) copy-start(bf16[1536,128]{1,0:T(8,128)(2,1)} %pad.14.router_ref) | copy-start | bytes 1179652
  377.6 169.3 %copy-start.11 = (f32[1,1536]{1,0:T(1,128)S(1)}, f32[1,1536]{1,0:T(1,128)}, u32[]{:S(2)}) copy-start(f32[1,1536]{1,0:T(1,128)} %reshape.86.gain_ref) | copy-start | bytes 18436
  377.6 596.3 %reduce-scatter.8.cloned.1.call-start = ((), (), s32[]{:S(2)}) async-start(), calls=%async_computation.5 | async-start | bytes 53084160 | tf_op jit(solution)/shard_map/reduce_scatter | solution.py:1193
  758.2 175.7 %copy-start.23 = (f32[1536]{0:T(1024)S(1)}, f32[1536]{0:T(1024)}, u32[]{:S(2)}) copy-start(f32[1536]{0:T(1024)} %param.18) | copy-start | bytes 18436
  (12 other events, 32.2 us)
Sparse Core Ops, SparseCore 0:
  10.2 31.0 all-gather.4
  43.2 58.4 all-gather.6
  243.4 134.0 reduce-scatter.3
  381.1 173.2 reduce-scatter.5
  563.0 271.0 reduce-scatter.7

commit v4 on v3

--- a/solution.py
+++ b/solution.py
@@ -266,7 +266,7 @@
     filled = count_ref[first + expert]
     length, width = normed_ref.shape
     hidden_size = gate_w.shape[2]
-    sizes = (128, 256, CAP)
+    sizes = (128, 192, 256, 320, CAP)
 
     def by_size(run):
         low = None
@@ -300,7 +300,9 @@
     def enter(rows):
         mask, picks = slots(rows)
         rows_in = jnp.dot(picks, normed_ref[...], preferred_element_type=jnp.float32).astype(jnp.bfloat16)
-        grad_rows = jnp.dot(picks, grad_ref[...], preferred_element_type=jnp.float32).astype(jnp.bfloat16)
+        grad_rows = (
+            RESIDUAL * jnp.dot(picks, grad_ref[...], preferred_element_type=jnp.float32)
+        ).astype(jnp.bfloat16)
         rows_ref[:rows] = rows_in
         grads_ref[:rows] = grad_rows
         gate = jnp.sum(jnp.where(mask, gate_ref[0], 0.0), axis=1, keepdims=True)
@@ -565,8 +567,7 @@
         in_specs=[full],
         out_specs=full,
     )(out_weight)
-    gathered = lax.all_gather(own, "tensor")
-    return lax.all_gather(gathered, "dp") if ways > 1 else gathered[None]
+    return ways, lax.all_gather(own, "tensor")
 
 
 def middle_kernel(
@@ -819,9 +820,11 @@
     sine_low_ref,
     sine_high_ref,
     opening_ref,
+    tokens_ref,
     moe_ref,
     grads_out,
     normed_out,
+    gain_out,
     moe_out,
     key_pairs,
     value_pairs,
@@ -835,6 +838,17 @@
     tiles, length, unused = query_ref.shape
     line_start, line_step, line_end = line_stages(n, [moe_ref], [moe_out], line)
     line_start()
+    blocks = length // ROWS
+    units = heads * blocks
+    taken = 0
+
+    def run_line(steps):
+        nonlocal taken
+        until = min(taken + steps, 2 * STEPS)
+        lax.fori_loop(taken, until, line_step, 0)
+        taken = until
+
+    run_line(2)
     spread_pairs(key_ref[...].astype(jnp.float32), key_pairs)
     spread_pairs(value_ref[...].astype(jnp.float32), value_pairs)
     halves = (
@@ -854,15 +868,15 @@
         )
         delta_ref[2 * tile] = sums[0:1]
         delta_ref[2 * tile + 1] = sums[1:2]
+        run_line(2)
     query_grads[...] = jnp.zeros_like(query_grads)
     key_grads[...] = jnp.zeros_like(key_grads)
     value_grads[...] = jnp.zeros_like(value_grads)
-    blocks = length // ROWS
-    units = heads * blocks
-    each = -(-2 * STEPS // units)
+    before, each = taken, (2 * STEPS - 8 - taken) // units
+    taken += units * each
 
     def unit(step, carry):
-        lax.fori_loop(step * each, step * each + each, line_step, 0)
+        lax.fori_loop(before + step * each, before + step * each + each, line_step, 0)
         head, block = step // blocks, step % blocks
         tile, half = head // 2, head % 2
         pair = 2 * (head // group) + half
@@ -910,16 +924,26 @@
         ATTN_SCALE * totals[0], cosine, sine_low, sine_high
     ).astype(jnp.bfloat16)
     grads_out[:, wide + 128 : wide + 256] = totals[1].astype(jnp.bfloat16)
-    normed_out[...] = (
-        right_inner(grads_out[:, :wide], query_w[...])
-        + right_inner(grads_out[:, wide : wide + 128], key_w[...])
-        + right_inner(grads_out[:, wide + 128 :], value_w[...])
-    )
+    gain_sum = jnp.zeros((1, normed_out.shape[1]), jnp.float32)
+    for block in range(blocks):
+        rows = slice(block * ROWS, (block + 1) * ROWS)
+        normed = (
+            right_inner(grads_out[rows, :wide], query_w[...])
+            + right_inner(grads_out[rows, wide : wide + 128], key_w[...])
+            + right_inner(grads_out[rows, wide + 128 :], value_w[...])
+        )
+        normed_out[rows, :] = normed
+        hidden = tokens_ref[rows, :].astype(jnp.float32)
+        recip = lax.rsqrt(jnp.mean(hidden * hidden, axis=1, keepdims=True) + EPSILON)
+        gain_sum += jnp.sum(normed * (hidden * recip), axis=0, keepdims=True)
+        run_line(2)
+    gain_out[...] = gain_sum
+    run_line(2 * STEPS)
     line_end()
 
 
 def attend_backward(
-    n, branch, out_w, query, key, value, attended, logsum, query_w, key_w, value_w, tables, opening, moe,
+    n, branch, out_w, query, key, value, attended, logsum, query_w, key_w, value_w, tables, opening, tokens, moe,
     heads, group, name,
 ):
     length, width = branch.shape
@@ -932,10 +956,11 @@
         out_shape=[
             jax.ShapeDtypeStruct((length, wide + 256), bf16),
             jax.ShapeDtypeStruct((length, width), f32),
+            jax.ShapeDtypeStruct((1, width), f32),
             jax.ShapeDtypeStruct((length, width), f32),
         ],
-        in_specs=[full] * 15,
-        out_specs=[full] * 3,
+        in_specs=[full] * 16,
+        out_specs=[full] * 4,
         scratch_shapes=[
             pltpu.VMEM((4, length, 128), bf16),
             pltpu.VMEM((4, length, 128), bf16),
@@ -947,14 +972,14 @@
         ]
         + line_scratch([moe]),
         compiler_params=pltpu.CompilerParams(
-            collective_id=name, has_side_effects=True, vmem_limit_bytes=60 << 20
+            collective_id=name, has_side_effects=True, vmem_limit_bytes=62 << 20
         ),
         cost_estimate=pl.CostEstimate(
             flops=12 * 10**9, bytes_accessed=30 * 10**6, transcendentals=5 * 10**6
         ),
     )(
         branch, out_w, query, key, value, attended, logsum, query_w, key_w, value_w, *tables,
-        opening.reshape(1, length), moe,
+        opening.reshape(1, length), tokens, moe,
     )
 
 
@@ -969,9 +994,19 @@
     normed_two_ref,
     logits_ref,
     gain_ref,
+    first_gain_ref,
     normed_out,
-    shard_out,
+    query_out,
+    key_out,
+    value_out,
+    branch_out,
+    router_out,
+    gain_out,
+    first_gain_out,
     weights_ref,
+    gains_ref,
+    gain_send,
+    gain_recv,
     *scratch,
 ):
     levels = parts.bit_length() - 1
@@ -982,7 +1017,11 @@
     width = normed_ref.shape[1]
     own = width // parts
     wide, attended_wide = grads_ref.shape[1], attended_ref.shape[1]
-    line_start([{"dp": jnp.bitwise_xor(me, 1 << level)} for level in range(levels)])
+    mine = lax.axis_index("tensor")
+    line_start(
+        [{"dp": jnp.bitwise_xor(me, 1 << level)} for level in range(levels)]
+        + [{"tensor": lax.rem(mine + ahead, n)} for ahead in range(1, n)]
+    )
 
     def run_line(first, last):
         lax.fori_loop(first, last, line_step, 0)
@@ -997,9 +1036,14 @@
             branch_ref[:, rows], attended_ref[...]
         )
         gain = jnp.transpose(jnp.broadcast_to(gain_ref[:, rows], (128, block)))
+        first_gain = jnp.transpose(jnp.broadcast_to(first_gain_ref[:, rows], (128, block)))
         lanes = lax.broadcasted_iota(jnp.int32, (block, 128), 1)
         weights_ref[rows, wide + attended_wide :] = jnp.where(
-            lanes == 127, gain, left_inner(normed_two_ref[:, rows], logits_ref[...])
+            lanes == 127,
+            gain,
+            jnp.where(
+                lanes == 126, first_gain, left_inner(normed_two_ref[:, rows], logits_ref[...])
+            ),
         )
         run_line(2 + 2 * piece, 4 + 2 * piece)
     done = 2 + 2 * pieces
@@ -1022,7 +1066,7 @@
             for i in range(parts >> (level + 1))
         ]
 
-    stops = [6, 26, 16, 4]
+    stops = [6, 24, 16, 2]
     for level in range(levels):
         for copy in copies(level):
             copy.start()
@@ -1034,42 +1078,76 @@
             copy.wait_recv()
             target = shard(kept + (i << (level + 1)))
             target[...] += held[level][i]
+    gains_ref[0] = shard(me)[:, wide + attended_wide :]
+    gain_copies = [
+        pltpu.make_async_remote_copy(
+            src_ref=gains_ref.at[0],
+            dst_ref=gains_ref.at[ahead],
+            send_sem=gain_send.at[ahead],
+            recv_sem=gain_recv.at[ahead],
+            device_id={"tensor": lax.rem(mine + ahead, n)},
+            device_id_type=MESH,
+        )
+        for ahead in range(1, n)
+    ]
+    for copy in gain_copies:
+        copy.start()
+    kept = shard(me)
+    query_out[...] = kept[:, : query_out.shape[1]]
+    key_out[...] = kept[:, wide - 256 : wide - 256 + key_out.shape[1]]
+    value_out[...] = kept[:, wide - 128 : wide - 128 + value_out.shape[1]]
+    branch_out[...] = jnp.transpose(kept[:, wide : wide + attended_wide])[: branch_out.shape[0]]
+    router_out[...] = gains_ref[0][:, : router_out.shape[1]]
     run_line(done, 2 * STEPS)
-    shard_out[...] = shard(me)[...]
+    total = gains_ref[0]
+    for ahead, copy in enumerate(gain_copies, 1):
+        copy.wait_recv()
+        total = total + gains_ref[ahead]
+    gain_out[...] = jnp.transpose(gains_ref[0])[127:]
+    first_gain_out[...] = jnp.transpose(total)[126:127]
     for level in range(levels):
         for copy in copies(level):
             copy.wait_send()
+    for copy in gain_copies:
+        copy.wait_send()
     line_end()
 
 
-def finish(n, parts, grad_local, normed_b, grads_wide, branch_b, attended, normed_two_b, grad_logits_b, ffn_gain_grad, name):
+def finish(
+    n, parts, grad_local, normed_b, grads_wide, branch_b, attended, normed_two_b, grad_logits_b, gain_grad, first_gain_grad,
+    wide_q, wide_k, experts, name,
+):
     length, width = normed_b.shape
     columns = grads_wide.shape[1] + attended.shape[1] + 128
     full = pl.BlockSpec(memory_space=pltpu.VMEM)
     levels = parts.bit_length() - 1
     own = width // parts
     f32 = jnp.float32
+    shapes = [(length, width), (own, wide_q), (own, wide_k), (own, wide_k), (wide_q, own)]
+    shapes += [(own, experts), (1, own), (1, own)]
     return pl.pallas_call(
         functools.partial(finish_kernel, n, parts),
-        out_shape=[
-            jax.ShapeDtypeStruct((length, width), f32),
-            jax.ShapeDtypeStruct((own, columns), f32),
-        ],
-        in_specs=[full] * 8,
-        out_specs=[full] * 2,
-        scratch_shapes=[pltpu.VMEM((width, columns), f32)]
+        out_shape=[jax.ShapeDtypeStruct(shape, f32) for shape in shapes],
+        in_specs=[full] * 9,
+        out_specs=[full] * 8,
+        scratch_shapes=[
+            pltpu.VMEM((width, columns), f32),
+            pltpu.VMEM((n, own, 128), f32),
+            pltpu.SemaphoreType.DMA((n,)),
+            pltpu.SemaphoreType.DMA((n,)),
+        ]
         + [pltpu.VMEM((parts >> (level + 1), own, columns), f32) for level in range(levels)]
         + [pltpu.SemaphoreType.DMA((levels, parts // 2))] * 2
         + line_scratch([grad_local]),
         compiler_params=pltpu.CompilerParams(
-            collective_id=name, has_side_effects=True, vmem_limit_bytes=60 << 20
+            collective_id=name, has_side_effects=True, vmem_limit_bytes=62 << 20
         ),
         cost_estimate=pl.CostEstimate(
             flops=2 * length * width * columns, bytes_accessed=50 * 10**6, transcendentals=0
         ),
     )(
-        grad_local, normed_b, grads_wide, branch_b, attended, normed_two_b, grad_logits_b,
-        ffn_gain_grad,
+        grad_local, normed_b, grads_wide, branch_b, attended, normed_two_b, grad_logits_b, gain_grad,
+        first_gain_grad,
     )
 
 
@@ -1139,7 +1217,7 @@
     query_w, key_w, value_w = (pad_columns(w) for w in (query_weight, key_weight, value_weight))
     out_w = jnp.transpose(pad_columns(jnp.transpose(out_weight)))
     hidden_in = tokens.astype(jnp.float32)
-    out_all = gather_out_weight(out_weight, parts)
+    ways, out_rows = gather_out_weight(out_weight, parts)
     normed_b, queries, keys, values, attended, logsum = attend_forward(
         tokens, attn_gain, query_w, key_w, value_w, tables, opening, heads_local, group_size
     )
@@ -1150,7 +1228,8 @@
     picked = jnp.sum((routes[None, :, :] == local_ids[:, None, None]).astype(jnp.int32), axis=2)
     places_in = slot_places(picked)
     counts = jnp.sum(picked, axis=1)
-    grad_moe_b = (RESIDUAL * cotangent.astype(jnp.float32)).astype(jnp.bfloat16)
+    out_rows, attended = lax.optimization_barrier((out_rows, attended))
+    out_all = lax.all_gather(out_rows, "dp") if ways > 1 else out_rows[None]
     attended_all = line_gather(attended, ring, 1)
     attended_all = attended_all.reshape(length, ring, attended.shape[1])
     attended_all = attended_all[:, :, : heads_local * HEAD].reshape(length, -1)
@@ -1159,15 +1238,15 @@
         attended_all, out_all, tokens, ffn_gain, router_w, pad_columns(chosen.astype(jnp.float32))
     )
     gate_rows = jnp.transpose(lax.dynamic_slice_in_dim(gate_probs, first_expert, experts_local, 1))
-    numbers = (max(1, experts_local // 5), max(1, 3 * experts_local // 10))
+    numbers = (max(1, experts_local // 10), max(1, 3 * experts_local // 10))
     numbers += (experts_local - sum(numbers),)
     (grads_first,), sums = expert_stage(
-        parts, 0, numbers[:1], counts, places_in, gate_rows, normed_two_b, grad_moe_b,
+        parts, 0, numbers[:1], counts, places_in, gate_rows, normed_two_b, cotangent,
         gate_weight, up_weight, down_weight, None,
     )
     shards_first = lax.psum_scatter(grads_first, "dp", scatter_dimension=2, tiled=True)
     (grads_middle, grads_last), sums_last = expert_stage(
-        parts, numbers[0], numbers[1:], counts, places_in, gate_rows, normed_two_b, grad_moe_b,
+        parts, numbers[0], numbers[1:], counts, places_in, gate_rows, normed_two_b, cotangent,
         gate_weight, up_weight, down_weight, sums,
     )
     shards_first, grads_middle = lax.optimization_barrier((shards_first, grads_middle))
@@ -1191,25 +1270,23 @@
         (shards_middle, grads_last, grad_branch_b)
     )
     shards_last = lax.psum_scatter(grads_last, "dp", scatter_dimension=2, tiled=True)
-    grads_wide, grad_normed_local, moe_out = attend_backward(
+    grads_wide, grad_normed_local, first_gain, moe_out = attend_backward(
         ring, grad_branch_b, out_w, queries, keys, values, attended, logsum,
-        query_w, key_w, value_w, tables, opening, moe_part, heads_local, group_size, 3,
+        query_w, key_w, value_w, tables, opening, tokens, moe_part, heads_local, group_size, 3,
     )
     output = (middle + RESIDUAL * moe_out).astype(jnp.bfloat16)
-    grad_normed, small = finish(
+    wide_q, wide_k = heads_local * HEAD, kv_local * HEAD
+    grad_normed, *small = finish(
         ring, parts, grad_normed_local, normed_b, grads_wide, grad_branch_b, attended, normed_two_b,
-        grad_logits_b, grad_ffn_gain, 4,
-    )
+        grad_logits_b, grad_ffn_gain, first_gain, wide_q, wide_k, experts_all, 4,
+    )
+    grad_query, grad_key, grad_value, grad_out, grad_router, grad_ffn_gain, grad_attn_gain = small
     recip_one = lax.rsqrt(jnp.mean(hidden_in * hidden_in, axis=-1, keepdims=True) + EPSILON)
     unit_one = hidden_in * recip_one
-    grad_from_first, grad_attn_gain = rms_backward(grad_normed, unit_one, recip_one, attn_gain)
-    grad_tokens = grad_middle + grad_from_first
-    grad_attn_gain = lax.psum_scatter(grad_attn_gain, "dp", scatter_dimension=0, tiled=True)
-    shards_last, grad_attn_gain = lax.optimization_barrier((shards_last, grad_attn_gain))
-    tiled_q = query_w.shape[1]
-    wide_q, wide_k = heads_local * HEAD, kv_local * HEAD
-    at_out = tiled_q + 256
-    at_router = at_out + tiled_q
+    scaled = grad_normed * attn_gain
+    inner = jnp.mean(scaled * unit_one, axis=-1, keepdims=True)
+    grad_tokens = grad_middle + recip_one * (scaled - unit_one * inner)
+    shards_last, grad_tokens = lax.optimization_barrier((shards_last, grad_tokens))
     grads_placed = place_shards(parts, shards_first, 0, experts_local, None)
     grads_placed = place_shards(parts, shards_middle, numbers[0], experts_local, grads_placed)
     grad_gate, grad_up, grad_down = place_shards(
@@ -1218,13 +1295,13 @@
     return (
         output,
         grad_tokens,
-        grad_attn_gain,
-        small[:, :wide_q],
-        small[:, tiled_q : tiled_q + wide_k],
-        small[:, tiled_q + 128 : tiled_q + 128 + wide_k],
-        jnp.transpose(small[:, at_out : at_out + wide_q]),
-        small[:, at_router + 127],
-        small[:, at_router : at_router + experts_all],
+        grad_attn_gain.reshape(-1),
+        grad_query,
+        grad_key,
+        grad_value,
+        grad_out,
+        grad_ffn_gain.reshape(-1),
+        grad_router,
         grad_gate,
         grad_up,
         grad_down,

time: 996 us -> 957 us (0.961)
  waiting for transfers between devices: 77.1 us -> 0.52 us
  Pallas kernels: 828 us -> 880 us
  blocking collectives: 12 us -> 0 us
    reduce_scatter x1, waiting for transfers between devices: 45.2 us -> 0.02 us  [on_device(): lax.psum_scatter(grads_first, 'dp', scatter_dimension=2, tiled=True)]
    all_gather x2, waiting for transfers between devices: 31.9 us -> 0.41 us  [the longest x1 0.41 us: gather_out_weight(): return (ways, lax.all_gather(own, 'tensor'))]
    pallas_call x1, Pallas kernels: 174 us -> 204 us  [finish(): pl.pallas_call(functools.partial(finish_kernel, n, parts), out_shape=[jax...]
    pallas_call x2, Pallas kernels: 131 us -> 161 us  [expert_stage(): pl.pallas_call(functools.partial(expert_kernel, parts, first, numbers, ch...]
    unnamed x1 -> x0, blocking collectives: 12 us -> none
    unnamed x66 -> x85, local copies, waits for them, and re-layouts: 12.9 us -> 24.2 us
  transfers between devices with their start and end apart: 5 -> 5, of which waited for: 2 -> 1; matrix products, arithmetic and copies ran while one was open for 4% -> 3% of each run, Pallas kernels for 77% -> 87%
where the time goes in v4:
time: 957 us; the launch traced here: 949 us
  Pallas kernels  880 us (92%)
  local copies, waits for them, and re-layouts  30 us (3%)
  other arithmetic  23 us (2%)
  between operations  14.7 us (2%)
    pallas_call x1, Pallas kernels, finish(): pl.pallas_call(functools.partial(finish_kernel, n, parts), out_shape=[jax...  204 us
    pallas_call x1, Pallas kernels, attend_backward(): pl.pallas_call(functools.partial(attend_backward_kernel, n, heads, group)...  181 us
    pallas_call x1, Pallas kernels, line_sum(): pl.pallas_call(functools.partial(line_sum_kernel, n, count), out_shape=sh...  164 us
    pallas_call x2, Pallas kernels, expert_stage(): pl.pallas_call(functools.partial(expert_kernel, parts, first, numbers, ch...  161 us
    pallas_call x1, Pallas kernels, line_gather(): pl.pallas_call(functools.partial(line_gather_kernel, n), out_shape=jax.Sh...  104 us
    unnamed x85, local copies, waits for them, and re-layouts  24.2 us
    pallas_call x1, Pallas kernels, attend_forward(): pl.pallas_call(functools.partial(attend_forward_kernel, heads, group), ou...  21.1 us
  transfers between devices with their start and end apart: 5, of which 1 were waited for; matrix products, arithmetic and copies ran while one was open for 3% of the time, Pallas kernels for 87%

profile of v4, /device:TPU:8, one launch (start us, length us, event | category | flops | bytes accessed | tf_op | source)
XLA Modules:
  0.0 948.5 jit_solution(9404775189290107871)
XLA Ops:
  7.3 2.1 shard_map.229
  11.8 1.9 multiply_sine_fusion
  15.1 21.1 %shard_map.230 = (bf16[1024,1536]{1,0:T(8,128)(2,1)}, bf16[3,1024,128]{2,1,0:T(8,128)(2,1)S(1)}, bf16[1024,128]{1,0:T(8,128)(2,1)S(1)}, bf16[1024,128]{1,0:T(8,1...) custom-call(bf16[1024,1536]{1,0:T(8,128)(2,1)} %tokens_ref.5, f32[1,1536]{1,0:T(1,128)S(1)} %reshape.91.gain_ref, ...), custom_call_target="tpu_custom_call" | custom-call | flops 8000000000 | bytes 12000000 | tf_op jit(solution)/shard_map/pallas_call | solution.py:781
  46.2 104.0 %shard_map.231.attended_ref = bf16[1024,1536]{1,0:T(8,128)(2,1)S(1)} custom-call(bf16[1024,384]{1,0:T(8,128)(2,1)S(1)} %get-tuple-element.69.x_ref.attended_ref), custom_call_target="tpu_custom_call" | custom-call | bytes 25165824 | tf_op jit(solution)/shard_map/pallas_call | solution.py:535
  150.3 1.7 copy-done.4
  151.9 15.8 %shard_map.232 = (f32[1024,1536]{1,0:T(8,128)}, bf16[1024,1536]{1,0:T(8,128)(2,1)}, f32[1024,128]{1,0:T(8,128)}) custom-call(bf16[1024,1536]{1,0:T(8,128)(2,1)} %copy-done.4, f32[8,4,48,1536]{3,2,1,0:T(8,128)} %bitcast.23, bf16[1024,1536]{1,0:T(8,128)(2,1)} %tokens_ref.5, f32[1,1536]{1,0:T(1,128)} %reshape.92.gain_ref, bf16[1536,128]{1,0:T(8,128)(2,1)} %pad.14.router_ref, ...), custom_call_target="tpu_custom_call" | custom-call | flops 4831838208 | bytes 25000000 | tf_op jit(solution)/shard_map/pallas_call | solution.py:597
  169.7 33.7 %shard_map.233 = (f32[1,3,1536,512]{3,2,1,0:T(8,128)}, f32[1024,1536]{1,0:T(8,128)}, f32[1024,1536]{1,0:T(8,128)}, f32[1,1,1024]{2,1,0:T(1,128)}) custom-call(s32[10]{0:T(128)} %get-tuple-element.185.count_ref, s32[10,1,1024]{2,1,0:T(1,128)} %reshape.93.place_ref, f32[10,1,1024]{2,1,0:T(1,128)} %reshape.94.gate_ref, ...), custom_call_target="tpu_custom_call" | custom-call | flops 8000000000 | bytes 14000000 | tf_op jit(solution)/shard_map/pallas_call | solution.py:417
  203.4 126.9 %shard_map.234 = (f32[3,3,1536,512]{3,2,1,0:T(8,128)}, f32[6,3,1536,512]{3,2,1,0:T(8,128)}, f32[1024,1536]{1,0:T(8,128)}, f32[1024,1536]{1,0:T(8,128)}, f32[9,1,1024]{2,1,0:T(1,128)}) custom-call(s32[10]{0:T(128)} %get-tuple-element.185.count_ref, s32[10,1,1024]{2,1,0:T(1,128)} %reshape.93.place_ref, f32[10,1,1024]{2,1,0:T(1,128)} %reshape.94.gate_ref, ...), custom_call_target="tpu_custom_call" | custom-call | flops 71999995904 | bytes 126000000 | tf_op jit(solution)/shard_map/pallas_call | solution.py:417
  331.9 2.8 copy-done.1
  334.6 163.7 %shard_map.235 = (f32[1024,1536]{1,0:T(8,128)S(1)}, f32[512,128]{1,0:T(8,128)S(1)}) custom-call(f32[1024,1536]{1,0:T(8,128)S(1)} %copy-done.1, f32[512,128]{1,0:T(8,128)S(1)} %pad.17.refs_1_), custom_call_target="tpu_custom_call" | custom-call | flops 4915200 | bytes 13107200 | tf_op jit(solution)/shard_map/pallas_call | solution.py:228
  498.3 2.6 copy-done
  501.0 12.9 %shard_map.236 = (f32[1024,1536]{1,0:T(8,128)}, bf16[1024,1536]{1,0:T(8,128)(2,1)S(1)}, bf16[1024,128]{1,0:T(8,128)(2,1)S(1)}, f32[1,1536]{1,0:T(1,128)S(1)}) custom-call(f32[1024,1536]{1,0:T(8,128)} %copy-done, f32[40,1024]{1,0:T(8,128)S(1)} %reshape.97.grad_gates_ref, f32[1024,128]{1,0:T(8,128)S(1)} %copy-done.5, ...), custom_call_target="tpu_custom_call" | custom-call | flops 62914560 | bytes 25000000 | tf_op jit(solution)/shard_map/pallas_call | solution.py:646
  513.9 1.7 copy-done.3
  516.9 1.9 copy-done.20
  519.4 2.3 shard_map.239
  521.7 180.8 %shard_map.237 = (bf16[1024,640]{1,0:T(8,128)(2,1)}, f32[1024,1536]{1,0:T(8,128)}, f32[1,1536]{1,0:T(1,128)}, f32[1024,1536]{1,0:T(8,128)}) custom-call(bf16[1024,1536]{1,0:T(8,128)(2,1)} %copy-done.3, bf16[384,1536]{1,0:T(8,128)(2,1)} %out_w.1, bf16[3,1024,128]{2,1,0:T(8,128)(2,1)} %copy-done.16, bf16[1024,128]{1,0:T(8,128)(2,1)} %copy-done.17, ...), custom_call_target="tpu_custom_call" | custom-call | flops 12000000000 | bytes 30000000 | tf_op jit(solution)/shard_map/pallas_call | solution.py:954
  702.5 204.3 %shard_map.238 = (f32[1024,1536]{1,0:T(8,128)}, f32[192,384]{1,0:T(8,128)}, f32[192,128]{1,0:T(8,128)}, f32[192,128]{1,0:T(8,128)}, f32[384,192]{1,0:T(8,128)}, ...) custom-call(f32[1024,1536]{1,0:T(8,128)} %get-tuple-element.97.local_ref, ...), custom_call_target="tpu_custom_call" | custom-call | flops 3623878656 | bytes 50000000 | tf_op jit(solution)/shard_map/pallas_call | solution.py:1128
  906.8 1.9 copy.63
  908.7 1.6 copy.64
  910.3 4.9 shard_map.240
  915.2 4.1 fusion.2
  919.3 8.1 add_convert_fusion
  927.4 3.6 fusion.5
  931.1 7.4 shard_map.241
  (125 shorter events, 22.3 us)
Async XLA Ops:
  7.2 7.8 copy-start.13
  7.2 7.8 copy-start.14
  7.2 34.1 %all-gather.5.cloned.1.call-start = ((), (), s32[]{:S(2)}) async-start(), calls=%async_computation.6 | async-start | bytes 1474560 | tf_op jit(solution)/shard_map/all_gather | solution.py:570
  9.4 142.5 %all-gather.7.cloned.1.call-start = ((), (), s32[]{:S(2)}) async-start(), calls=%async_computation.7 | async-start | bytes 10616832 | tf_op jit(solution)/shard_map/all_gather | solution.py:1232
  11.5 24.7 %copy-start.28 = (s32[1024]{0:T(1024)}, s32[1024]{0:T(1024)S(1)}, u32[]{:S(2)}) copy-start(s32[1024]{0:T(1024)S(1)} %convert_reduce_fusion) | copy-start | bytes 12292
  15.0 26.4 %copy-start.30 = (f32[1536]{0:T(1024)S(1)}, f32[1536]{0:T(1024)}, u32[]{:S(2)}) copy-start(f32[1536]{0:T(1024)} %param.23) | copy-start | bytes 18436
  15.0 27.0 %copy-start.24 = (bf16[1536,40]{0,1:T(8,128)(2,1)S(1)}, bf16[1536,40]{0,1:T(8,128)(2,1)}, u32[]{:S(2)}) copy-start(bf16[1536,40]{0,1:T(8,128)(2,1)} %param.24) | copy-start | bytes 368644
  15.0 27.2 %copy-start.23 = (s32[1024,8]{0,1:T(8,128)S(1)}, s32[1024,8]{0,1:T(8,128)}, u32[]{:S(2)}) copy-start(s32[1024,8]{0,1:T(8,128)} %param.17) | copy-start | bytes 98308
  40.9 126.8 %copy-start.2 = (bf16[1024,384]{1,0:T(8,128)(2,1)}, bf16[1024,384]{1,0:T(8,128)(2,1)S(1)}, u32[]{:S(2)}) copy-start(bf16[1024,384]{1,0:T(8,128)(2,1)S(1)} %get-tuple-element.69.x_ref.attended_ref) | copy-start | bytes 2359300
  40.9 126.8 %copy-start.19 = (f32[6,1,1024]{2,1,0:T(1,128)}, f32[6,1,1024]{2,1,0:T(1,128)S(1)}, u32[]{:S(2)}) copy-start(f32[6,1,1024]{2,1,0:T(1,128)S(1)} %get-tuple-element.92.logsum_ref) | copy-start | bytes 73732
  41.4 289.0 %reduce-scatter.4.cloned.1.call-start = ((), (), s32[]{:S(2)}) async-start(), calls=%async_computation.3 | async-start | bytes 10616832 | tf_op jit(solution)/shard_map/reduce_scatter | solution.py:1247
  203.3 313.5 %reduce-scatter.6.cloned.1.call-start = ((), (), s32[]{:S(2)}) async-start(), calls=%async_computation.4 | async-start | bytes 31850496 | tf_op jit(solution)/shard_map/reduce_scatter | solution.py:1253
  330.4 170.6 %copy-start.5 = (f32[1024,128]{1,0:T(8,128)S(1)}, f32[1024,128]{1,0:T(8,128)}, u32[]{:S(2)}) copy-start(f32[1024,128]{1,0:T(8,128)} %get-tuple-element.72.gates_ref) | copy-start | bytes 1572868
  330.4 170.6 %copy-start.6 = (bf16[1536,128]{1,0:T(8,128)(2,1)S(1)}, bf16[1536,128]{1,0:T(8,128)(2,1)}, u32[]{:S(2)}) copy-start(bf16[1536,128]{1,0:T(8,128)(2,1)} %pad.14.router_ref) | copy-start | bytes 1179652
  330.4 170.6 %copy-start.11 = (f32[1,1536]{1,0:T(1,128)S(1)}, f32[1,1536]{1,0:T(1,128)}, u32[]{:S(2)}) copy-start(f32[1,1536]{1,0:T(1,128)} %reshape.92.gain_ref) | copy-start | bytes 18436
  330.4 600.6 %reduce-scatter.8.cloned.1.call-start = ((), (), s32[]{:S(2)}) async-start(), calls=%async_computation.5 | async-start | bytes 63700992 | tf_op jit(solution)/shard_map/reduce_scatter | solution.py:1272
  915.2 12.2 %slice-start = ((s8[6291456]{0:T(1024)(128)(4,1)}), s8[4194304]{0:T(1024)(128)(4,1)S(1)}, s32[]{:S(2)}) async-start(s8[6291456]{0:T(1024)(128)(4,1)} %bitcast.12), calls=%async_computation.8 | async-start | bytes 8388608
  915.2 12.2 %slice-start.2 = ((s8[6291456]{0:T(1024)(128)(4,1)}), s8[4194304]{0:T(1024)(128)(4,1)S(1)}, s32[]{:S(2)}) async-start(s8[6291456]{0:T(1024)(128)(4,1)} %bitcast.14), calls=%async_computation.10 | async-start | bytes 8388608
  919.3 8.1 slice-start.1
  919.3 8.1 slice-start.3
  931.1 7.9 copy-start.22
  931.1 8.7 copy-start.26
  931.1 9.3 copy-start.25
  931.1 9.9 %copy-start.32 = (f32[1,192]{1,0:T(1,128)S(1)}, f32[1,192]{1,0:T(1,128)}, u32[]{:S(2)}) copy-start(f32[1,192]{1,0:T(1,128)} %get-tuple-element.110) | copy-start | bytes 2308
  (19 other events, 43.3 us)
Sparse Core Ops, SparseCore 0:
  10.2 31.0 all-gather.4
  43.2 58.4 all-gather.6
  203.5 78.1 reduce-scatter.3
  330.5 178.7 reduce-scatter.5
  517.0 378.7 reduce-scatter.7

commit v5 on v4

--- a/solution.py
+++ b/solution.py
@@ -266,7 +266,7 @@
     filled = count_ref[first + expert]
     length, width = normed_ref.shape
     hidden_size = gate_w.shape[2]
-    sizes = (128, 192, 256, 320, CAP)
+    sizes = (128, 256, CAP)
 
     def by_size(run):
         low = None
@@ -330,11 +330,18 @@
             copy_back.wait()
 
     def leave(rows):
-        mask, picks = slots(rows)
+        column = jnp.transpose(jnp.broadcast_to(place_ref[0], (128, length)))
+        column = jnp.concatenate([column] * (rows // 128), 1)
+        own = lax.broadcasted_iota(jnp.int32, (length, rows), 1)
+        picks = jnp.where(own == column, 1.0, 0.0).astype(jnp.bfloat16)
         moe = jnp.dot(active_ref[:rows], down_w[0], preferred_element_type=jnp.float32)
-        moe_out[...] += left_inner(picks, moe.astype(jnp.bfloat16))
+        moe_out[...] += jnp.dot(
+            picks, moe.astype(jnp.bfloat16), preferred_element_type=jnp.float32
+        )
         back = right_inner(gate_in_ref[:rows], gate_w[0]) + right_inner(up_in_ref[:rows], up_w[0])
-        back_out[...] += left_inner(picks, back.astype(jnp.bfloat16))
+        back_out[...] += jnp.dot(
+            picks, back.astype(jnp.bfloat16), preferred_element_type=jnp.float32
+        )
 
     by_size(leave)
 
@@ -1048,37 +1055,57 @@
         run_line(2 + 2 * piece, 4 + 2 * piece)
     done = 2 + 2 * pieces
 
-    def shard(number):
-        return weights_ref.at[pl.ds(pl.multiple_of(number * own, own), own), :]
+    columns = weights_ref.shape[1]
+    middle = columns // 256 * 128
+    orders = (
+        (slice(0, middle), list(range(levels))),
+        (slice(middle, columns), [0] + list(range(levels - 1, 0, -1))),
+    )
+
+    def shard(number, lanes):
+        return weights_ref.at[pl.ds(pl.multiple_of(number * own, own), own), lanes]
+
+    def numbers(order, level, peer):
+        fixed = sum(1 << bit for bit in order[: level + 1])
+        base = jnp.bitwise_and(peer, fixed)
+        free = order[level + 1 :]
+        return [
+            base + sum(((i >> place) & 1) << bit for place, bit in enumerate(free))
+            for i in range(1 << len(free))
+        ]
 
     def copies(level):
-        peer = jnp.bitwise_xor(me, 1 << level)
-        low = jnp.bitwise_and(peer, (2 << level) - 1)
-        return [
-            pltpu.make_async_remote_copy(
-                src_ref=shard(low + (i << (level + 1))),
-                dst_ref=held[level].at[i],
-                send_sem=sends.at[level, i],
-                recv_sem=recvs.at[level, i],
-                device_id={"dp": peer},
-                device_id_type=MESH,
-            )
-            for i in range(parts >> (level + 1))
-        ]
-
-    stops = [6, 24, 16, 2]
+        made = []
+        for side, (lanes, order) in enumerate(orders):
+            peer = jnp.bitwise_xor(me, 1 << order[level])
+            for i, number in enumerate(numbers(order, level, peer)):
+                made.append(
+                    pltpu.make_async_remote_copy(
+                        src_ref=shard(number, lanes),
+                        dst_ref=held[level].at[i, :, lanes],
+                        send_sem=sends.at[side, level, i],
+                        recv_sem=recvs.at[side, level, i],
+                        device_id={"dp": peer},
+                        device_id_type=MESH,
+                    )
+                )
+        return made
+
+    stops = [6, 28, 18, 2]
     for level in range(levels):
         for copy in copies(level):
             copy.start()
         until = done + stops[level]
         run_line(done, until)
         done = until
-        kept = jnp.bitwise_and(me, (2 << level) - 1)
-        for i, copy in enumerate(copies(level)):
+        for copy in copies(level):
             copy.wait_recv()
-            target = shard(kept + (i << (level + 1)))
-            target[...] += held[level][i]
-    gains_ref[0] = shard(me)[:, wide + attended_wide :]
+        for lanes, order in orders:
+            for i, number in enumerate(numbers(order, level, me)):
+                target = shard(number, lanes)
+                target[...] += held[level][i, :, lanes]
+    everything = slice(0, columns)
+    gains_ref[0] = shard(me, slice(wide + attended_wide, columns))[...]
     gain_copies = [
         pltpu.make_async_remote_copy(
             src_ref=gains_ref.at[0],
@@ -1092,7 +1119,7 @@
     ]
     for copy in gain_copies:
         copy.start()
-    kept = shard(me)
+    kept = shard(me, everything)
     query_out[...] = kept[:, : query_out.shape[1]]
     key_out[...] = kept[:, wide - 256 : wide - 256 + key_out.shape[1]]
     value_out[...] = kept[:, wide - 128 : wide - 128 + value_out.shape[1]]
@@ -1137,7 +1164,7 @@
             pltpu.SemaphoreType.DMA((n,)),
         ]
         + [pltpu.VMEM((parts >> (level + 1), own, columns), f32) for level in range(levels)]
-        + [pltpu.SemaphoreType.DMA((levels, parts // 2))] * 2
+        + [pltpu.SemaphoreType.DMA((2, levels, parts // 2))] * 2
         + line_scratch([grad_local]),
         compiler_params=pltpu.CompilerParams(
             collective_id=name, has_side_effects=True, vmem_limit_bytes=62 << 20

time: 957 us -> 919 us (0.960)
  Pallas kernels: 880 us -> 837 us
    pallas_call x2, Pallas kernels: 161 us -> 136 us  [expert_stage(): pl.pallas_call(functools.partial(expert_kernel, parts, first, numbers, ch...]
    pallas_call x1, Pallas kernels: 204 us -> 188 us  [finish(): pl.pallas_call(functools.partial(finish_kernel, n, parts), out_shape=[jax...]
where the time goes in v5:
time: 919 us; the launch traced here: 906 us
  Pallas kernels  837 us (91%)
  local copies, waits for them, and re-layouts  30 us (3%)
  other arithmetic  23 us (3%)
  between operations  14.7 us (2%)
    pallas_call x1, Pallas kernels, finish(): pl.pallas_call(functools.partial(finish_kernel, n, parts), out_shape=[jax...  188 us
    pallas_call x1, Pallas kernels, attend_backward(): pl.pallas_call(functools.partial(attend_backward_kernel, n, heads, group)...  186 us
    pallas_call x1, Pallas kernels, line_sum(): pl.pallas_call(functools.partial(line_sum_kernel, n, count), out_shape=sh...  157 us
    pallas_call x2, Pallas kernels, expert_stage(): pl.pallas_call(functools.partial(expert_kernel, parts, first, numbers, ch...  136 us
    pallas_call x1, Pallas kernels, line_gather(): pl.pallas_call(functools.partial(line_gather_kernel, n), out_shape=jax.Sh...  104 us
    unnamed x85, local copies, waits for them, and re-layouts  24.2 us
    pallas_call x1, Pallas kernels, attend_forward(): pl.pallas_call(functools.partial(attend_forward_kernel, heads, group), ou...  21.1 us
  transfers between devices with their start and end apart: 5, of which 1 were waited for; matrix products, arithmetic and copies ran while one was open for 3% of the time, Pallas kernels for 87%

profile of v5, /device:TPU:8, one launch (start us, length us, event | category | flops | bytes accessed | tf_op | source)
XLA Modules:
  0.0 905.9 jit_solution(12930733613805025191)
XLA Ops:
  7.3 2.1 shard_map.229
  11.8 1.9 multiply_sine_fusion
  15.1 21.1 %shard_map.230 = (bf16[1024,1536]{1,0:T(8,128)(2,1)}, bf16[3,1024,128]{2,1,0:T(8,128)(2,1)S(1)}, bf16[1024,128]{1,0:T(8,128)(2,1)S(1)}, bf16[1024,128]{1,0:T(8,1...) custom-call(bf16[1024,1536]{1,0:T(8,128)(2,1)} %tokens_ref.5, f32[1,1536]{1,0:T(1,128)S(1)} %reshape.91.gain_ref, ...), custom_call_target="tpu_custom_call" | custom-call | flops 8000000000 | bytes 12000000 | tf_op jit(solution)/shard_map/pallas_call | solution.py:788
  46.2 104.0 %shard_map.231.attended_ref = bf16[1024,1536]{1,0:T(8,128)(2,1)S(1)} custom-call(bf16[1024,384]{1,0:T(8,128)(2,1)S(1)} %get-tuple-element.69.x_ref.attended_ref), custom_call_target="tpu_custom_call" | custom-call | bytes 25165824 | tf_op jit(solution)/shard_map/pallas_call | solution.py:542
  150.3 1.7 copy-done.4
  151.9 15.8 %shard_map.232 = (f32[1024,1536]{1,0:T(8,128)}, bf16[1024,1536]{1,0:T(8,128)(2,1)}, f32[1024,128]{1,0:T(8,128)}) custom-call(bf16[1024,1536]{1,0:T(8,128)(2,1)} %copy-done.4, f32[8,4,48,1536]{3,2,1,0:T(8,128)} %bitcast.23, bf16[1024,1536]{1,0:T(8,128)(2,1)} %tokens_ref.5, f32[1,1536]{1,0:T(1,128)} %reshape.92.gain_ref, bf16[1536,128]{1,0:T(8,128)(2,1)} %pad.14.router_ref, ...), custom_call_target="tpu_custom_call" | custom-call | flops 4831838208 | bytes 25000000 | tf_op jit(solution)/shard_map/pallas_call | solution.py:604
  169.7 22.4 %shard_map.233 = (f32[1,3,1536,512]{3,2,1,0:T(8,128)}, f32[1024,1536]{1,0:T(8,128)}, f32[1024,1536]{1,0:T(8,128)}, f32[1,1,1024]{2,1,0:T(1,128)}) custom-call(s32[10]{0:T(128)} %get-tuple-element.185.count_ref, s32[10,1,1024]{2,1,0:T(1,128)} %reshape.93.place_ref, f32[10,1,1024]{2,1,0:T(1,128)} %reshape.94.gate_ref, ...), custom_call_target="tpu_custom_call" | custom-call | flops 8000000000 | bytes 14000000 | tf_op jit(solution)/shard_map/pallas_call | solution.py:424
  192.1 113.2 %shard_map.234 = (f32[3,3,1536,512]{3,2,1,0:T(8,128)}, f32[6,3,1536,512]{3,2,1,0:T(8,128)}, f32[1024,1536]{1,0:T(8,128)}, f32[1024,1536]{1,0:T(8,128)}, f32[9,1,1024]{2,1,0:T(1,128)}) custom-call(s32[10]{0:T(128)} %get-tuple-element.185.count_ref, s32[10,1,1024]{2,1,0:T(1,128)} %reshape.93.place_ref, f32[10,1,1024]{2,1,0:T(1,128)} %reshape.94.gate_ref, ...), custom_call_target="tpu_custom_call" | custom-call | flops 71999995904 | bytes 126000000 | tf_op jit(solution)/shard_map/pallas_call | solution.py:424
  306.9 2.8 copy-done.1
  309.7 157.3 %shard_map.235 = (f32[1024,1536]{1,0:T(8,128)S(1)}, f32[512,128]{1,0:T(8,128)S(1)}) custom-call(f32[1024,1536]{1,0:T(8,128)S(1)} %copy-done.1, f32[512,128]{1,0:T(8,128)S(1)} %pad.17.refs_1_), custom_call_target="tpu_custom_call" | custom-call | flops 4915200 | bytes 13107200 | tf_op jit(solution)/shard_map/pallas_call | solution.py:228
  467.0 2.6 copy-done
  469.7 12.9 %shard_map.236 = (f32[1024,1536]{1,0:T(8,128)}, bf16[1024,1536]{1,0:T(8,128)(2,1)S(1)}, bf16[1024,128]{1,0:T(8,128)(2,1)S(1)}, f32[1,1536]{1,0:T(1,128)S(1)}) custom-call(f32[1024,1536]{1,0:T(8,128)} %copy-done, f32[40,1024]{1,0:T(8,128)S(1)} %reshape.97.grad_gates_ref, f32[1024,128]{1,0:T(8,128)S(1)} %copy-done.5, ...), custom_call_target="tpu_custom_call" | custom-call | flops 62914560 | bytes 25000000 | tf_op jit(solution)/shard_map/pallas_call | solution.py:653
  482.5 1.7 copy-done.3
  485.5 1.9 copy-done.20
  488.1 2.3 shard_map.239
  490.4 185.6 %shard_map.237 = (bf16[1024,640]{1,0:T(8,128)(2,1)}, f32[1024,1536]{1,0:T(8,128)}, f32[1,1536]{1,0:T(1,128)}, f32[1024,1536]{1,0:T(8,128)}) custom-call(bf16[1024,1536]{1,0:T(8,128)(2,1)} %copy-done.3, bf16[384,1536]{1,0:T(8,128)(2,1)} %out_w.1, bf16[3,1024,128]{2,1,0:T(8,128)(2,1)} %copy-done.16, bf16[1024,128]{1,0:T(8,128)(2,1)} %copy-done.17, ...), custom_call_target="tpu_custom_call" | custom-call | flops 12000000000 | bytes 30000000 | tf_op jit(solution)/shard_map/pallas_call | solution.py:961
  676.0 188.2 %shard_map.238 = (f32[1024,1536]{1,0:T(8,128)}, f32[192,384]{1,0:T(8,128)}, f32[192,128]{1,0:T(8,128)}, f32[192,128]{1,0:T(8,128)}, f32[384,192]{1,0:T(8,128)}, ...) custom-call(f32[1024,1536]{1,0:T(8,128)} %get-tuple-element.97.local_ref, ...), custom_call_target="tpu_custom_call" | custom-call | flops 3623878656 | bytes 50000000 | tf_op jit(solution)/shard_map/pallas_call | solution.py:1155
  864.2 1.9 copy.63
  866.0 1.6 copy.64
  867.6 4.9 shard_map.240
  872.6 4.1 fusion.2
  876.7 8.1 add_convert_fusion
  884.8 3.6 fusion.5
  888.4 7.4 shard_map.241
  (125 shorter events, 22.3 us)
Async XLA Ops:
  7.2 7.8 copy-start.13
  7.2 7.8 copy-start.14
  7.2 34.1 %all-gather.5.cloned.1.call-start = ((), (), s32[]{:S(2)}) async-start(), calls=%async_computation.6 | async-start | bytes 1474560 | tf_op jit(solution)/shard_map/all_gather | solution.py:577
  9.4 142.5 %all-gather.7.cloned.1.call-start = ((), (), s32[]{:S(2)}) async-start(), calls=%async_computation.7 | async-start | bytes 10616832 | tf_op jit(solution)/shard_map/all_gather | solution.py:1259
  11.5 24.7 %copy-start.28 = (s32[1024]{0:T(1024)}, s32[1024]{0:T(1024)S(1)}, u32[]{:S(2)}) copy-start(s32[1024]{0:T(1024)S(1)} %convert_reduce_fusion) | copy-start | bytes 12292
  15.0 26.4 %copy-start.30 = (f32[1536]{0:T(1024)S(1)}, f32[1536]{0:T(1024)}, u32[]{:S(2)}) copy-start(f32[1536]{0:T(1024)} %param.23) | copy-start | bytes 18436
  15.0 27.0 %copy-start.24 = (bf16[1536,40]{0,1:T(8,128)(2,1)S(1)}, bf16[1536,40]{0,1:T(8,128)(2,1)}, u32[]{:S(2)}) copy-start(bf16[1536,40]{0,1:T(8,128)(2,1)} %param.24) | copy-start | bytes 368644
  15.0 27.2 %copy-start.23 = (s32[1024,8]{0,1:T(8,128)S(1)}, s32[1024,8]{0,1:T(8,128)}, u32[]{:S(2)}) copy-start(s32[1024,8]{0,1:T(8,128)} %param.17) | copy-start | bytes 98308
  40.9 126.8 %copy-start.2 = (bf16[1024,384]{1,0:T(8,128)(2,1)}, bf16[1024,384]{1,0:T(8,128)(2,1)S(1)}, u32[]{:S(2)}) copy-start(bf16[1024,384]{1,0:T(8,128)(2,1)S(1)} %get-tuple-element.69.x_ref.attended_ref) | copy-start | bytes 2359300
  40.9 126.8 %copy-start.19 = (f32[6,1,1024]{2,1,0:T(1,128)}, f32[6,1,1024]{2,1,0:T(1,128)S(1)}, u32[]{:S(2)}) copy-start(f32[6,1,1024]{2,1,0:T(1,128)S(1)} %get-tuple-element.92.logsum_ref) | copy-start | bytes 73732
  41.4 264.1 %reduce-scatter.4.cloned.1.call-start = ((), (), s32[]{:S(2)}) async-start(), calls=%async_computation.3 | async-start | bytes 10616832 | tf_op jit(solution)/shard_map/reduce_scatter | solution.py:1274
  192.1 293.4 %reduce-scatter.6.cloned.1.call-start = ((), (), s32[]{:S(2)}) async-start(), calls=%async_computation.4 | async-start | bytes 31850496 | tf_op jit(solution)/shard_map/reduce_scatter | solution.py:1280
  305.5 164.2 %copy-start.5 = (f32[1024,128]{1,0:T(8,128)S(1)}, f32[1024,128]{1,0:T(8,128)}, u32[]{:S(2)}) copy-start(f32[1024,128]{1,0:T(8,128)} %get-tuple-element.72.gates_ref) | copy-start | bytes 1572868
  305.5 164.2 %copy-start.6 = (bf16[1536,128]{1,0:T(8,128)(2,1)S(1)}, bf16[1536,128]{1,0:T(8,128)(2,1)}, u32[]{:S(2)}) copy-start(bf16[1536,128]{1,0:T(8,128)(2,1)} %pad.14.router_ref) | copy-start | bytes 1179652
  305.5 164.2 %copy-start.11 = (f32[1,1536]{1,0:T(1,128)S(1)}, f32[1,1536]{1,0:T(1,128)}, u32[]{:S(2)}) copy-start(f32[1,1536]{1,0:T(1,128)} %reshape.92.gain_ref) | copy-start | bytes 18436
  305.5 582.9 %reduce-scatter.8.cloned.1.call-start = ((), (), s32[]{:S(2)}) async-start(), calls=%async_computation.5 | async-start | bytes 63700992 | tf_op jit(solution)/shard_map/reduce_scatter | solution.py:1299
  872.5 12.2 %slice-start = ((s8[6291456]{0:T(1024)(128)(4,1)}), s8[4194304]{0:T(1024)(128)(4,1)S(1)}, s32[]{:S(2)}) async-start(s8[6291456]{0:T(1024)(128)(4,1)} %bitcast.12), calls=%async_computation.8 | async-start | bytes 8388608
  872.6 12.2 %slice-start.2 = ((s8[6291456]{0:T(1024)(128)(4,1)}), s8[4194304]{0:T(1024)(128)(4,1)S(1)}, s32[]{:S(2)}) async-start(s8[6291456]{0:T(1024)(128)(4,1)} %bitcast.14), calls=%async_computation.10 | async-start | bytes 8388608
  876.7 8.1 slice-start.1
  876.7 8.1 slice-start.3
  888.4 7.9 copy-start.22
  888.4 8.7 copy-start.26
  888.4 9.3 %copy-start.25 = (f32[192,128]{1,0:T(8,128)S(1)}, f32[192,128]{1,0:T(8,128)}, u32[]{:S(2)}) copy-start(f32[192,128]{1,0:T(8,128)} %get-tuple-element.209) | copy-start | bytes 294916
  888.4 9.9 %copy-start.32 = (f32[1,192]{1,0:T(1,128)S(1)}, f32[1,192]{1,0:T(1,128)}, u32[]{:S(2)}) copy-start(f32[1,192]{1,0:T(1,128)} %get-tuple-element.110) | copy-start | bytes 2308
  (19 other events, 43.3 us)
Sparse Core Ops, SparseCore 0:
  10.2 31.0 all-gather.4
  43.2 58.4 all-gather.6
  192.2 83.8 reduce-scatter.3
  305.6 171.9 reduce-scatter.5
  485.7 370.8 reduce-scatter.7

commit v6 on v5

--- a/solution.py
+++ b/solution.py
@@ -77,10 +77,9 @@
 
 STEPS = 32
 LAG = 2
-GATE_ROWS = 512
-
-
-def line_stages(n, xs, outs, scratch):
+
+
+def line_stages(n, xs, outs, scratch, done=None):
     count = len(xs)
     lows, highs = scratch[:count], scratch[count : 2 * count]
     low_recv, high_recv, total_recv, up_send, low_send, high_send = scratch[2 * count :]
@@ -160,6 +159,8 @@
             start(outs, outs, c, low_send, total_recv, me - 1)
             if root < n - 1:
                 start(outs, outs, c, high_send, total_recv, me + 1)
+            if done is not None:
+                done(c)
 
     def total_step(c):
         @pl.when(me != root)
@@ -173,6 +174,12 @@
         @pl.when((me > root) & has_high)
         def _():
             start(outs, outs, c, high_send, total_recv, me + 1)
+
+        if done is not None:
+
+            @pl.when(me != root)
+            def _():
+                done(c)
 
     lag = jnp.where(has_low & has_high, LAG, STEPS)
 
@@ -211,34 +218,6 @@
     return [pltpu.VMEM(array.shape, jnp.float32) for array in arrays * 2] + [
         pltpu.SemaphoreType.DMA((len(arrays), STEPS))
     ] * 6
-
-
-def line_sum_kernel(n, count, *refs):
-    begin, step, finish = line_stages(n, refs[:count], refs[count : 2 * count], refs[2 * count :])
-    begin()
-    lax.fori_loop(0, 2 * STEPS, step, 0)
-    finish()
-
-
-def line_sum(x, extra, n, name):
-    arrays = [x] if extra is None else [x, extra]
-    count = len(arrays)
-    shapes = [jax.ShapeDtypeStruct(array.shape, jnp.float32) for array in arrays]
-    size = sum(array.size for array in arrays)
-    results = pl.pallas_call(
-        functools.partial(line_sum_kernel, n, count),
-        out_shape=shapes,
-        in_specs=[pl.BlockSpec(memory_space=pltpu.VMEM)] * count,
-        out_specs=[pl.BlockSpec(memory_space=pltpu.VMEM)] * count,
-        scratch_shapes=line_scratch(arrays),
-        compiler_params=pltpu.CompilerParams(
-            collective_id=name, has_side_effects=True, vmem_limit_bytes=40 << 20
-        ),
-        cost_estimate=pl.CostEstimate(
-            flops=3 * size, bytes_accessed=8 * size, transcendentals=0
-        ),
-    )(*arrays)
-    return (results[0], None) if extra is None else tuple(results)
 
 
 def expert_kernel(
@@ -581,37 +560,53 @@
     attended_ref, weight_all_ref, tokens_ref, gain_ref, router_ref, chosen_ref, middle_out, normed_out, gates_out, weight_ref
 ):
     ways, n, rows, unused = weight_all_ref.shape
-    for way in range(ways):
-        for block in range(n):
-            at = (block * ways + way) * rows
-            weight_ref[at : at + rows, :] = weight_all_ref[way, block].astype(jnp.bfloat16)
-    for first in range(0, tokens_ref.shape[0], BLOCK):
-        own = slice(first, first + BLOCK)
-        branch = jnp.dot(attended_ref[own, :], weight_ref[...], preferred_element_type=jnp.float32)
-        middle = tokens_ref[own, :].astype(jnp.float32) + RESIDUAL * branch
-        middle_out[own, :] = middle
-        recip = lax.rsqrt(jnp.mean(middle * middle, axis=1, keepdims=True) + EPSILON)
-        normed = (middle * recip * gain_ref[...]).astype(jnp.bfloat16)
-        normed_out[own, :] = normed
-        logits = jnp.dot(normed, router_ref[...], preferred_element_type=jnp.float32)
-        raised = jnp.where(chosen_ref[own, :] > 0.0, jnp.exp(logits), 0.0)
-        gates_out[own, :] = raised / jnp.sum(raised, axis=1, keepdims=True)
+
+    @pl.when(pl.program_id(0) == 0)
+    def _():
+        for way in range(ways):
+            for block in range(n):
+                at = (block * ways + way) * rows
+                weight_ref[at : at + rows, :] = weight_all_ref[way, block].astype(jnp.bfloat16)
+
+    branch = jnp.dot(attended_ref[...], weight_ref[...], preferred_element_type=jnp.float32)
+    middle = tokens_ref[...].astype(jnp.float32) + RESIDUAL * branch
+    middle_out[...] = middle
+    recip = lax.rsqrt(jnp.mean(middle * middle, axis=1, keepdims=True) + EPSILON)
+    normed = (middle * recip * gain_ref[...]).astype(jnp.bfloat16)
+    normed_out[...] = normed
+    logits = jnp.dot(normed, router_ref[...], preferred_element_type=jnp.float32)
+    raised = jnp.where(chosen_ref[...] > 0.0, jnp.exp(logits), 0.0)
+    gates_out[...] = raised / jnp.sum(raised, axis=1, keepdims=True)
 
 
 def enter_middle(attended, weight_all, tokens, gain, router, chosen):
     length, width = tokens.shape
-    full = pl.BlockSpec(memory_space=pltpu.VMEM)
+    rows = lambda columns: pl.BlockSpec((BLOCK, columns), lambda i: (i, 0))
+    whole = lambda shape: pl.BlockSpec(
+        shape, lambda i: (0,) * len(shape), pipeline_mode=pl.Buffered(1)
+    )
+    experts = router.shape[1]
     return pl.pallas_call(
         middle_kernel,
         out_shape=[
             jax.ShapeDtypeStruct((length, width), jnp.float32),
             jax.ShapeDtypeStruct((length, width), jnp.bfloat16),
-            jax.ShapeDtypeStruct((length, router.shape[1]), jnp.float32),
+            jax.ShapeDtypeStruct((length, experts), jnp.float32),
         ],
-        in_specs=[full] * 6,
-        out_specs=[full] * 3,
+        grid=(length // BLOCK,),
+        in_specs=[
+            rows(attended.shape[1]),
+            whole(weight_all.shape),
+            rows(width),
+            whole((1, width)),
+            whole(router.shape),
+            rows(experts),
+        ],
+        out_specs=[rows(width), rows(width), rows(experts)],
         scratch_shapes=[pltpu.VMEM((attended.shape[1], width), jnp.bfloat16)],
-        compiler_params=pltpu.CompilerParams(vmem_limit_bytes=56 << 20),
+        compiler_params=pltpu.CompilerParams(
+            dimension_semantics=("arbitrary",), vmem_limit_bytes=48 << 20
+        ),
         cost_estimate=pl.CostEstimate(
             flops=2 * length * width * width, bytes_accessed=25 * 10**6, transcendentals=0
         ),
@@ -619,18 +614,27 @@
 
 
 def turn_kernel(
-    summed_ref, grad_gates_ref, gates_ref, middle_ref, cotangent_ref, gain_ref, router_ref, grad_out, branch_out, logits_out, gain_out
+    n,
+    part_ref,
+    gates_part_ref,
+    gates_ref,
+    middle_ref,
+    cotangent_ref,
+    gain_ref,
+    router_ref,
+    grad_out,
+    branch_out,
+    logits_out,
+    gain_out,
+    summed_ref,
+    grad_gates_ref,
+    *line,
 ):
-    length, width = summed_ref.shape
-    experts = grad_gates_ref.shape[0]
-    gates_rows = jnp.concatenate(
-        [grad_gates_ref[...], jnp.zeros((128 - experts, length), jnp.float32)], 0
-    )
-    gain_sum = jnp.zeros((1, width), jnp.float32)
-    for first in range(0, length, BLOCK):
-        own = slice(first, first + BLOCK)
-        grad_gates = jnp.transpose(gates_rows[:, own])
-        gates = gates_ref[own, :]
+    rows = part_ref.shape[0] // STEPS
+
+    def done(c):
+        own = pl.ds(pl.multiple_of(c * rows, rows), rows)
+        gates, grad_gates = gates_ref[own, :], grad_gates_ref[own, :]
         weighted = jnp.sum(gates * grad_gates, axis=1, keepdims=True)
         grad_logits = (gates * (grad_gates - weighted)).astype(jnp.bfloat16)
         logits_out[own, :] = grad_logits
@@ -638,33 +642,45 @@
         middle = middle_ref[own, :]
         recip = lax.rsqrt(jnp.mean(middle * middle, axis=1, keepdims=True) + EPSILON)
         unit = middle * recip
-        gain_sum += jnp.sum(grad * unit, axis=0, keepdims=True)
+        gain_out[...] += jnp.sum(grad * unit, axis=0, keepdims=True)
         scaled = grad * gain_ref[...]
         back = recip * (scaled - unit * jnp.mean(scaled * unit, axis=1, keepdims=True))
         total = cotangent_ref[own, :].astype(jnp.float32) + back
         grad_out[own, :] = total
         branch_out[own, :] = (RESIDUAL * total).astype(jnp.bfloat16)
-    gain_out[...] = gain_sum
-
-
-def turn_middle(summed, grad_gates, gates, middle, cotangent, gain, router):
-    length, width = summed.shape
+
+    begin, step, finish = line_stages(
+        n, [part_ref, gates_part_ref], [summed_ref, grad_gates_ref], line, done
+    )
+    begin()
+    gain_out[...] = jnp.zeros_like(gain_out)
+    lax.fori_loop(0, 2 * STEPS, step, 0)
+    finish()
+
+
+def turn_middle(n, part, gates_part, gates, middle, cotangent, gain, router, name):
+    length, width = part.shape
     full = pl.BlockSpec(memory_space=pltpu.VMEM)
+    f32 = jnp.float32
     return pl.pallas_call(
-        turn_kernel,
+        functools.partial(turn_kernel, n),
         out_shape=[
-            jax.ShapeDtypeStruct((length, width), jnp.float32),
+            jax.ShapeDtypeStruct((length, width), f32),
             jax.ShapeDtypeStruct((length, width), jnp.bfloat16),
-            jax.ShapeDtypeStruct((length, gates.shape[1]), jnp.bfloat16),
-            jax.ShapeDtypeStruct((1, width), jnp.float32),
+            jax.ShapeDtypeStruct(gates.shape, jnp.bfloat16),
+            jax.ShapeDtypeStruct((1, width), f32),
         ],
         in_specs=[full] * 7,
         out_specs=[full] * 4,
-        compiler_params=pltpu.CompilerParams(vmem_limit_bytes=48 << 20),
+        scratch_shapes=[pltpu.VMEM(part.shape, f32), pltpu.VMEM(gates.shape, f32)]
+        + line_scratch([part, gates_part]),
+        compiler_params=pltpu.CompilerParams(
+            collective_id=name, has_side_effects=True, vmem_limit_bytes=58 << 20
+        ),
         cost_estimate=pl.CostEstimate(
-            flops=40 * length * width, bytes_accessed=25 * 10**6, transcendentals=0
-        ),
-    )(summed, grad_gates, gates, middle, cotangent, gain.reshape(1, width), router)
+            flops=40 * length * width, bytes_accessed=60 * 10**6, transcendentals=0
+        ),
+    )(part, gates_part, gates, middle, cotangent, gain.reshape(1, width), router)
 
 
 SPAN = 768
@@ -829,10 +845,14 @@
     opening_ref,
     tokens_ref,
     moe_ref,
+    middle_ref,
     grads_out,
     normed_out,
     gain_out,
-    moe_out,
+    output_ref,
+    moe_sum,
+    middle_rows,
+    middle_sems,
     key_pairs,
     value_pairs,
     attend_grads,
@@ -843,8 +863,30 @@
     *line,
 ):
     tiles, length, unused = query_ref.shape
-    line_start, line_step, line_end = line_stages(n, [moe_ref], [moe_out], line)
+    share = length // STEPS
+
+    def share_rows(c):
+        return pl.ds(pl.multiple_of(c * share, share), share)
+
+    def fetch(c):
+        slot = lax.rem(c, 2)
+        return pltpu.make_async_copy(
+            middle_ref.at[share_rows(c), :], middle_rows.at[slot], middle_sems.at[slot]
+        )
+
+    def done(c):
+        fetch(c).wait()
+
+        @pl.when(c + 1 < STEPS)
+        def _():
+            fetch(c + 1).start()
+
+        total = middle_rows[lax.rem(c, 2)] + RESIDUAL * moe_sum[share_rows(c), :]
+        output_ref[share_rows(c), :] = total.astype(jnp.bfloat16)
+
+    line_start, line_step, line_end = line_stages(n, [moe_ref], [moe_sum], line, done)
     line_start()
+    fetch(jnp.int32(0)).start()
     blocks = length // ROWS
     units = heads * blocks
     taken = 0
@@ -950,7 +992,7 @@
 
 
 def attend_backward(
-    n, branch, out_w, query, key, value, attended, logsum, query_w, key_w, value_w, tables, opening, tokens, moe,
+    n, branch, out_w, query, key, value, attended, logsum, query_w, key_w, value_w, tables, opening, tokens, moe, middle,
     heads, group, name,
 ):
     length, width = branch.shape
@@ -964,11 +1006,14 @@
             jax.ShapeDtypeStruct((length, wide + 256), bf16),
             jax.ShapeDtypeStruct((length, width), f32),
             jax.ShapeDtypeStruct((1, width), f32),
-            jax.ShapeDtypeStruct((length, width), f32),
+            jax.ShapeDtypeStruct((length, width), bf16),
         ],
-        in_specs=[full] * 16,
+        in_specs=[full] * 16 + [pl.BlockSpec(memory_space=pl.ANY)],
         out_specs=[full] * 4,
         scratch_shapes=[
+            pltpu.VMEM((length, width), f32),
+            pltpu.VMEM((2, length // STEPS, width), f32),
+            pltpu.SemaphoreType.DMA((2,)),
             pltpu.VMEM((4, length, 128), bf16),
             pltpu.VMEM((4, length, 128), bf16),
             pltpu.VMEM((tiles, length, 128), bf16),
@@ -979,14 +1024,14 @@
         ]
         + line_scratch([moe]),
         compiler_params=pltpu.CompilerParams(
-            collective_id=name, has_side_effects=True, vmem_limit_bytes=62 << 20
+            collective_id=name, has_side_effects=True, vmem_limit_bytes=63 << 20
         ),
         cost_estimate=pl.CostEstimate(
             flops=12 * 10**9, bytes_accessed=30 * 10**6, transcendentals=5 * 10**6
         ),
     )(
         branch, out_w, query, key, value, attended, logsum, query_w, key_w, value_w, *tables,
-        opening.reshape(1, length), tokens, moe,
+        opening.reshape(1, length), tokens, moe, middle,
     )
 
 
@@ -1265,43 +1310,33 @@
         attended_all, out_all, tokens, ffn_gain, router_w, pad_columns(chosen.astype(jnp.float32))
     )
     gate_rows = jnp.transpose(lax.dynamic_slice_in_dim(gate_probs, first_expert, experts_local, 1))
-    numbers = (max(1, experts_local // 10), max(1, 3 * experts_local // 10))
-    numbers += (experts_local - sum(numbers),)
+    numbers = (max(1, experts_local // 10),)
+    numbers += (experts_local - numbers[0],)
     (grads_first,), sums = expert_stage(
         parts, 0, numbers[:1], counts, places_in, gate_rows, normed_two_b, cotangent,
         gate_weight, up_weight, down_weight, None,
     )
     shards_first = lax.psum_scatter(grads_first, "dp", scatter_dimension=2, tiled=True)
-    (grads_middle, grads_last), sums_last = expert_stage(
+    (grads_last,), sums_last = expert_stage(
         parts, numbers[0], numbers[1:], counts, places_in, gate_rows, normed_two_b, cotangent,
         gate_weight, up_weight, down_weight, sums,
     )
-    shards_first, grads_middle = lax.optimization_barrier((shards_first, grads_middle))
-    shards_middle = lax.psum_scatter(grads_middle, "dp", scatter_dimension=2, tiled=True)
     moe_part, grad_normed_part, unused = sums_last
-    grad_gates_local = jnp.concatenate([sums[2], sums_last[2]], 0)
+    shards_first, grads_last, grad_normed_part = lax.optimization_barrier(
+        (shards_first, grads_last, grad_normed_part)
+    )
+    shards_last = lax.psum_scatter(grads_last, "dp", scatter_dimension=2, tiled=True)
+    grad_gates_local = jnp.concatenate([sums[2], sums_last[2]], 0).reshape(experts_local, length)
     grad_gates_part = lax.dynamic_update_slice_in_dim(
-        jnp.zeros((experts_all, length), jnp.float32),
-        grad_gates_local.reshape(experts_local, length),
-        first_expert,
-        0,
-    ).reshape(-1, 128)
-    grad_gates_part = jnp.pad(grad_gates_part, ((0, GATE_ROWS - grad_gates_part.shape[0]), (0, 0)))
-    shards_first, grad_normed_part = lax.optimization_barrier((shards_first, grad_normed_part))
-    grad_normed_sum, gates_sum = line_sum(grad_normed_part, grad_gates_part, ring, 2)
-    grad_gates = gates_sum[: experts_all * length // 128].reshape(experts_all, length)
+        jnp.zeros(gate_probs.shape, jnp.float32), jnp.transpose(grad_gates_local), first_expert, 1
+    )
     grad_middle, grad_branch_b, grad_logits_b, grad_ffn_gain = turn_middle(
-        grad_normed_sum, grad_gates, gate_probs, middle, cotangent, ffn_gain, router_w
-    )
-    shards_middle, grads_last, grad_branch_b = lax.optimization_barrier(
-        (shards_middle, grads_last, grad_branch_b)
-    )
-    shards_last = lax.psum_scatter(grads_last, "dp", scatter_dimension=2, tiled=True)
-    grads_wide, grad_normed_local, first_gain, moe_out = attend_backward(
+        ring, grad_normed_part, grad_gates_part, gate_probs, middle, cotangent, ffn_gain, router_w, 2
+    )
+    grads_wide, grad_normed_local, first_gain, output = attend_backward(
         ring, grad_branch_b, out_w, queries, keys, values, attended, logsum,
-        query_w, key_w, value_w, tables, opening, tokens, moe_part, heads_local, group_size, 3,
-    )
-    output = (middle + RESIDUAL * moe_out).astype(jnp.bfloat16)
+        query_w, key_w, value_w, tables, opening, tokens, moe_part, middle, heads_local, group_size, 3,
+    )
     wide_q, wide_k = heads_local * HEAD, kv_local * HEAD
     grad_normed, *small = finish(
         ring, parts, grad_normed_local, normed_b, grads_wide, grad_branch_b, attended, normed_two_b,
@@ -1315,9 +1350,8 @@
     grad_tokens = grad_middle + recip_one * (scaled - unit_one * inner)
     shards_last, grad_tokens = lax.optimization_barrier((shards_last, grad_tokens))
     grads_placed = place_shards(parts, shards_first, 0, experts_local, None)
-    grads_placed = place_shards(parts, shards_middle, numbers[0], experts_local, grads_placed)
     grad_gate, grad_up, grad_down = place_shards(
-        parts, shards_last, numbers[0] + numbers[1], experts_local, grads_placed
+        parts, shards_last, numbers[0], experts_local, grads_placed
     )
     return (
         output,

time: 919 us -> 894 us (0.973)
  Pallas kernels: 837 us -> 825 us
    pallas_call x1, Pallas kernels: 188 us -> 176 us  [finish(): pl.pallas_call(functools.partial(finish_kernel, n, parts), out_shape=[jax...]
    pallas_call x2 -> x1, Pallas kernels: 170 us -> 179 us  [turn_middle(): pl.pallas_call(functools.partial(turn_kernel, n), out_shape=[jax.ShapeDty...]
    unnamed x85 -> x75, local copies, waits for them, and re-layouts: 24.2 us -> 20.6 us
  transfers between devices with their start and end apart: 5 -> 4, of which waited for: 1 -> 1; matrix products, arithmetic and copies ran while one was open for 3% -> 3% of each run, Pallas kernels for 87% -> 87%
where the time goes in v6:
time: 894 us; the launch traced here: 884 us
  Pallas kernels  825 us (92%)
  local copies, waits for them, and re-layouts  26.7 us (3%)
  other arithmetic  16.9 us (2%)
  between operations  14.5 us (2%)
    pallas_call x1, Pallas kernels, attend_backward(): pl.pallas_call(functools.partial(attend_backward_kernel, n, heads, group)...  186 us
    pallas_call x1, Pallas kernels, turn_middle(): pl.pallas_call(functools.partial(turn_kernel, n), out_shape=[jax.ShapeDty...  179 us
    pallas_call x1, Pallas kernels, finish(): pl.pallas_call(functools.partial(finish_kernel, n, parts), out_shape=[jax...  176 us
    pallas_call x2, Pallas kernels, expert_stage(): pl.pallas_call(functools.partial(expert_kernel, parts, first, numbers, ch...  129 us
    pallas_call x1, Pallas kernels, line_gather(): pl.pallas_call(functools.partial(line_gather_kernel, n), out_shape=jax.Sh...  104 us
    pallas_call x1, Pallas kernels, attend_forward(): pl.pallas_call(functools.partial(attend_forward_kernel, heads, group), ou...  21.1 us
    unnamed x75, local copies, waits for them, and re-layouts  20.6 us
  transfers between devices with their start and end apart: 4, of which 1 were waited for; matrix products, arithmetic and copies ran while one was open for 3% of the time, Pallas kernels for 87%

profile of v6, /device:TPU:8, one launch (start us, length us, event | category | flops | bytes accessed | tf_op | source)
XLA Modules:
  0.0 884.2 jit_solution(12689988739363797479)
XLA Ops:
  7.3 2.1 shard_map.229
  10.2 1.3 convert_reduce_fusion
  11.8 1.9 multiply_sine_fusion
  13.7 1.3 pad_maximum_fusion.2
  15.1 21.1 %shard_map.230 = (bf16[1024,1536]{1,0:T(8,128)(2,1)}, bf16[3,1024,128]{2,1,0:T(8,128)(2,1)S(1)}, bf16[1024,128]{1,0:T(8,128)(2,1)S(1)}, bf16[1024,128]{1,0:T(8,1...) custom-call(bf16[1024,1536]{1,0:T(8,128)(2,1)} %tokens_ref.5, f32[1,1536]{1,0:T(1,128)S(1)} %reshape.86.gain_ref, ...), custom_call_target="tpu_custom_call" | custom-call | flops 8000000000 | bytes 12000000 | tf_op jit(solution)/shard_map/pallas_call | solution.py:804
  38.6 0.9 copy-done.12
  44.1 104.0 %shard_map.231.attended_ref = bf16[1024,1536]{1,0:T(8,128)(2,1)S(1)} custom-call(bf16[1024,384]{1,0:T(8,128)(2,1)S(1)} %get-tuple-element.59.x_ref.attended_ref), custom_call_target="tpu_custom_call" | custom-call | bytes 25165824 | tf_op jit(solution)/shard_map/pallas_call | solution.py:521
  148.1 1.7 copy-done.2
  149.8 13.3 %shard_map.232 = (f32[1024,1536]{1,0:T(8,128)}, bf16[1024,1536]{1,0:T(8,128)(2,1)S(1)}, f32[1024,128]{1,0:T(8,128)S(1)}) custom-call(bf16[1024,1536]{1,0:T(8,128)(2,1)} %copy-done.2, f32[8,4,48,1536]{3,2,1,0:T(8,128)} %bitcast.19, bf16[1024,1536]{1,0:T(8,128)(2,1)} %tokens_ref.5, f32[1,1536]{1,0:T(1,128)S(1)} %reshape.87.gain_ref, ...), custom_call_target="tpu_custom_call" | custom-call | flops 4831838208 | bytes 25000000 | tf_op jit(solution)/shard_map/pallas_call | solution.py:589
  163.1 1.7 copy-done
  166.4 27.2 %shard_map.233 = (f32[1,3,1536,512]{3,2,1,0:T(8,128)}, f32[1024,1536]{1,0:T(8,128)}, f32[1024,1536]{1,0:T(8,128)}, f32[1,1,1024]{2,1,0:T(1,128)}) custom-call(s32[10]{0:T(128)} %get-tuple-element.165.count_ref, s32[10,1,1024]{2,1,0:T(1,128)} %reshape.85.place_ref, f32[10,1,1024]{2,1,0:T(1,128)} %reshape.88.gate_ref, bf16[1024,1536]{1,0:T(8,128)(2,1)} %copy-done, ...), custom_call_target="tpu_custom_call" | custom-call | flops 8000000000 | bytes 14000000 | tf_op jit(solution)/shard_map/pallas_call | solution.py:403
  193.6 102.2 %shard_map.234 = (f32[9,3,1536,512]{3,2,1,0:T(8,128)}, f32[1024,1536]{1,0:T(8,128)}, f32[1024,1536]{1,0:T(8,128)}, f32[9,1,1024]{2,1,0:T(1,128)}) custom-call(s32[10]{0:T(128)} %get-tuple-element.165.count_ref, s32[10,1,1024]{2,1,0:T(1,128)} %reshape.85.place_ref, f32[10,1,1024]{2,1,0:T(1,128)} %reshape.88.gate_ref, bf16[1024,1536]{1,0:T(8,128)(2,1)} %copy-done, ...), custom_call_target="tpu_custom_call" | custom-call | flops 71999995904 | bytes 126000000 | tf_op jit(solution)/shard_map/pallas_call | solution.py:403
  296.0 1.8 copy-done.16
  298.8 3.1 dynamic_update_slice.3.gates_part_ref
  302.7 179.5 %shard_map.235 = (f32[1024,1536]{1,0:T(8,128)}, bf16[1024,1536]{1,0:T(8,128)(2,1)}, bf16[1024,128]{1,0:T(8,128)(2,1)}, f32[1,1536]{1,0:T(1,128)}) custom-call(f32[1024,1536]{1,0:T(8,128)} %get-tuple-element.68.part_ref, f32[1024,128]{1,0:T(8,128)} %copy-done.20, f32[1024,128]{1,0:T(8,128)} %copy-done.3, f32[1024,1536]{1,0:T(8,128)} %get-tuple-element.71.middle_ref, ...), custom_call_target="tpu_custom_call" | custom-call | flops 62914560 | bytes 60000000 | tf_op jit(solution)/shard_map/pallas_call | solution.py:665
  482.2 185.7 %shard_map.236 = (bf16[1024,640]{1,0:T(8,128)(2,1)}, f32[1024,1536]{1,0:T(8,128)}, f32[1,1536]{1,0:T(1,128)}, bf16[1024,1536]{1,0:T(8,128)(2,1)}) custom-call(bf16[1024,1536]{1,0:T(8,128)(2,1)} %get-tuple-element.72.branch_ref, bf16[384,1536]{1,0:T(8,128)(2,1)} %out_w.1, bf16[3,1024,128]{2,1,0:T(8,128)(2,1)} %copy-done.12, bf16[1024,128]{1,0:T(8,128)(2,1)} %copy-done.13, ...), custom_call_target="tpu_custom_call" | custom-call | flops 12000000000 | bytes 30000000 | tf_op jit(solution)/shard_map/pallas_call | solution.py:1003
  667.9 176.1 %shard_map.237 = (f32[1024,1536]{1,0:T(8,128)}, f32[192,384]{1,0:T(8,128)}, f32[192,128]{1,0:T(8,128)}, f32[192,128]{1,0:T(8,128)}, f32[384,192]{1,0:T(8,128)}, ...) custom-call(f32[1024,1536]{1,0:T(8,128)} %get-tuple-element.81.local_ref, ...), custom_call_target="tpu_custom_call" | custom-call | flops 3623878656 | bytes 50000000 | tf_op jit(solution)/shard_map/pallas_call | solution.py:1200
  844.0 1.7 copy.68
  845.8 1.9 copy.67
  847.6 2.3 shard_map.238
  849.9 5.0 fusion.2
  855.4 5.5 fusion.5
  860.9 11.7 %shard_map.239 = (f32[10,192,512]{2,1,0:T(8,128)}, f32[10,192,512]{2,1,0:T(8,128)}, f32[10,64,1536]{2,1,0:T(8,128)}) custom-call(f32[9,3,192,512]{3,2,1,0:T(8,128)} %reduce-scatter.5.cloned.1.call-done.shards_ref, f32[10,192,512]{2,1,0:T(8,128)} %get-tuple-element.98.refs_0_, ...), custom_call_target="tpu_custom_call", output_to_operand_aliasing={{0}: (1, {}), {1}: (2, {}), {2}: (3, {})} | custom-call | bytes 21233664 | tf_op jit(solution)/shard_map/pallas_call | solution.py:1248
  872.7 1.7 copy.86
  (104 shorter events, 15.2 us)
Async XLA Ops:
  7.2 7.8 copy-start.11
  7.2 7.8 copy-start.10
  7.2 7.8 copy-start.9
  7.2 34.1 %all-gather.5.cloned.1.call-start = ((), (), s32[]{:S(2)}) async-start(), calls=%async_computation.4 | async-start | bytes 1474560 | tf_op jit(solution)/shard_map/all_gather | solution.py:556
  9.4 140.3 %all-gather.7.cloned.1.call-start = ((), (), s32[]{:S(2)}) async-start(), calls=%async_computation.5 | async-start | bytes 10616832 | tf_op jit(solution)/shard_map/all_gather | solution.py:1304
  11.5 24.7 %copy-start.27 = (s32[1024]{0:T(1024)}, s32[1024]{0:T(1024)S(1)}, u32[]{:S(2)}) copy-start(s32[1024]{0:T(1024)S(1)} %convert_reduce_fusion) | copy-start | bytes 12292
  15.0 26.4 %copy-start.29 = (f32[1536]{0:T(1024)S(1)}, f32[1536]{0:T(1024)}, u32[]{:S(2)}) copy-start(f32[1536]{0:T(1024)} %param.23) | copy-start | bytes 18436
  15.0 26.4 %copy-start.22 = (s32[1024,8]{0,1:T(8,128)S(1)}, s32[1024,8]{0,1:T(8,128)}, u32[]{:S(2)}) copy-start(s32[1024,8]{0,1:T(8,128)} %param.17) | copy-start | bytes 98308
  15.0 28.6 %copy-start.23 = (bf16[1536,40]{0,1:T(8,128)(2,1)S(1)}, bf16[1536,40]{0,1:T(8,128)(2,1)}, u32[]{:S(2)}) copy-start(bf16[1536,40]{0,1:T(8,128)(2,1)} %param.24) | copy-start | bytes 368644
  40.9 122.2 %copy-start.1 = (bf16[1024,384]{1,0:T(8,128)(2,1)}, bf16[1024,384]{1,0:T(8,128)(2,1)S(1)}, u32[]{:S(2)}) copy-start(bf16[1024,384]{1,0:T(8,128)(2,1)S(1)} %get-tuple-element.59.x_ref.attended_ref) | copy-start | bytes 2359300
  40.9 122.2 %copy-start.15 = (f32[6,1,1024]{2,1,0:T(1,128)}, f32[6,1,1024]{2,1,0:T(1,128)S(1)}, u32[]{:S(2)}) copy-start(f32[6,1,1024]{2,1,0:T(1,128)S(1)} %get-tuple-element.76.logsum_ref) | copy-start | bytes 73732
  41.4 254.5 %reduce-scatter.3.cloned.1.call-start = ((), (), s32[]{:S(2)}) async-start(), calls=%async_computation.2 | async-start | bytes 10616832 | tf_op jit(solution)/shard_map/reduce_scatter | solution.py:1319
  41.4 121.6 %copy-start.8 = (f32[1,1536]{1,0:T(1,128)}, f32[1,1536]{1,0:T(1,128)S(1)}, u32[]{:S(2)}) copy-start(f32[1,1536]{1,0:T(1,128)S(1)} %reshape.87.gain_ref) | copy-start | bytes 18436
  44.0 119.1 %copy-start.4 = (bf16[1536,128]{1,0:T(8,128)(2,1)}, bf16[1536,128]{1,0:T(8,128)(2,1)S(1)}, u32[]{:S(2)}) copy-start(bf16[1536,128]{1,0:T(8,128)(2,1)S(1)} %pad.10.router_ref) | copy-start | bytes 1179652
  193.6 667.4 %reduce-scatter.5.cloned.1.call-start = ((), (), s32[]{:S(2)}) async-start(), calls=%async_computation.3 | async-start | bytes 95551488 | tf_op jit(solution)/shard_map/reduce_scatter | solution.py:1328
  295.9 2.6 copy-start.28
  295.9 2.6 copy-start.30
  667.9 182.0 %copy-start.26 = (f32[1536]{0:T(1024)S(1)}, f32[1536]{0:T(1024)}, u32[]{:S(2)}) copy-start(f32[1536]{0:T(1024)} %param.18) | copy-start | bytes 18436
  844.0 11.0 %copy-start.17 = (bf16[1024,1536]{1,0:T(8,128)(2,1)S(1)}, bf16[1024,1536]{1,0:T(8,128)(2,1)}, u32[]{:S(2)}) copy-start(bf16[1024,1536]{1,0:T(8,128)(2,1)} %tokens_ref.5) | copy-start | bytes 9437188
  849.9 5.5 copy-start.18
  860.9 11.8 %copy-start.19 = (bf16[1024,1536]{1,0:T(8,128)(2,1)S(1)}, bf16[1024,1536]{1,0:T(8,128)(2,1)}, u32[]{:S(2)}) copy-start(bf16[1024,1536]{1,0:T(8,128)(2,1)} %get-tuple-element.184) | copy-start | bytes 9437188
  872.7 3.0 copy-start.25
  872.7 3.6 copy-start.24
  872.7 4.3 copy-start.31
  (13 other events, 15.5 us)
Sparse Core Ops, SparseCore 0:
  10.2 31.0 all-gather.4
  43.2 58.4 all-gather.6
  193.7 75.6 reduce-scatter.2
  296.1 488.1 reduce-scatter.4

commit v7 on v6

--- a/solution.py
+++ b/solution.py
@@ -79,7 +79,7 @@
 LAG = 2
 
 
-def line_stages(n, xs, outs, scratch, done=None):
+def line_stages(n, xs, outs, scratch, done=None, whole=0):
     count = len(xs)
     lows, highs = scratch[:count], scratch[count : 2 * count]
     low_recv, high_recv, total_recv, up_send, low_send, high_send = scratch[2 * count :]
@@ -108,26 +108,49 @@
         rows = ref.shape[0] // STEPS
         return ref.at[pl.ds(pl.multiple_of(c * rows, rows), rows), :]
 
-    def copies(sources, targets, c, send, recv, to):
+    cut = count - whole
+
+    def copies(sources, targets, c, send, recv, to, uncut):
         return [
             pltpu.make_async_remote_copy(
-                src_ref=piece(source, c),
-                dst_ref=piece(target, c),
+                src_ref=source if uncut else piece(source, c),
+                dst_ref=target if uncut else piece(target, c),
                 send_sem=send.at[i, c],
                 recv_sem=recv.at[i, c],
                 device_id={"tensor": to},
                 device_id_type=MESH,
             )
             for i, (source, target) in enumerate(zip(sources, targets))
+            if (i >= cut) == uncut
         ]
 
+    def each(sources, targets, c, send, recv, to, act):
+        for copy in copies(sources, targets, c, send, recv, to, False):
+            act(copy)
+        if whole:
+
+            @pl.when(c == 0)
+            def _():
+                for copy in copies(sources, targets, 0, send, recv, to, True):
+                    act(copy)
+
     def start(sources, targets, c, send, recv, to):
-        for copy in copies(sources, targets, c, send, recv, to):
-            copy.start()
+        each(sources, targets, c, send, recv, to, lambda copy: copy.start())
 
     def arrived(targets, c, send, recv):
-        for copy in copies(targets, targets, c, send, recv, me):
-            copy.wait_recv()
+        each(targets, targets, c, send, recv, me, lambda copy: copy.wait_recv())
+
+    def add(c, terms, targets):
+        for i, target in enumerate(targets):
+            if i < cut:
+                piece(target, c)[...] = functools.reduce(
+                    jnp.add, [piece(term[i], c)[...] for term in terms]
+                )
+            else:
+
+                @pl.when(c == 0)
+                def _():
+                    target[...] = functools.reduce(jnp.add, [term[i][...] for term in terms])
 
     def reduce_step(c):
         for side, inner, held, recv, to in (
@@ -138,8 +161,7 @@
             @pl.when(side & inner)
             def _():
                 arrived(held, c, up_send, recv)
-                for x, h in zip(xs, held):
-                    piece(h, c)[...] += piece(x, c)[...]
+                add(c, (held, xs), held)
                 start(held, held, c, up_send, recv, to)
 
             @pl.when(side & jnp.logical_not(inner))
@@ -151,11 +173,7 @@
             arrived(lows, c, up_send, low_recv)
             if root < n - 1:
                 arrived(highs, c, up_send, high_recv)
-            for x, low, high, out in zip(xs, lows, highs, outs):
-                total = piece(x, c)[...] + piece(low, c)[...]
-                if root < n - 1:
-                    total += piece(high, c)[...]
-                piece(out, c)[...] = total
+            add(c, (xs, lows, highs) if root < n - 1 else (xs, lows), outs)
             start(outs, outs, c, low_send, total_recv, me - 1)
             if root < n - 1:
                 start(outs, outs, c, high_send, total_recv, me + 1)
@@ -204,8 +222,7 @@
 
                 @pl.when(condition)
                 def _():
-                    for copy in copies(xs, lows, c, send, low_recv, me):
-                        copy.wait_send()
+                    each(xs, lows, c, send, low_recv, me, lambda copy: copy.wait_send())
 
             return carry
 
@@ -627,12 +644,22 @@
     logits_out,
     gain_out,
     summed_ref,
+    gates_rows_ref,
     grad_gates_ref,
     *line,
 ):
-    rows = part_ref.shape[0] // STEPS
+    length = part_ref.shape[0]
+    rows = length // STEPS
 
     def done(c):
+        @pl.when(c == 0)
+        def _():
+            experts = gates_rows_ref.shape[0]
+            empty = jnp.zeros((grad_gates_ref.shape[1] - experts, length), jnp.float32)
+            grad_gates_ref[...] = jnp.transpose(
+                jnp.concatenate([gates_rows_ref[...], empty], 0)
+            )
+
         own = pl.ds(pl.multiple_of(c * rows, rows), rows)
         gates, grad_gates = gates_ref[own, :], grad_gates_ref[own, :]
         weighted = jnp.sum(gates * grad_gates, axis=1, keepdims=True)
@@ -650,7 +677,7 @@
         branch_out[own, :] = (RESIDUAL * total).astype(jnp.bfloat16)
 
     begin, step, finish = line_stages(
-        n, [part_ref, gates_part_ref], [summed_ref, grad_gates_ref], line, done
+        n, [part_ref, gates_part_ref], [summed_ref, gates_rows_ref], line, done, 1
     )
     begin()
     gain_out[...] = jnp.zeros_like(gain_out)
@@ -672,7 +699,11 @@
         ],
         in_specs=[full] * 7,
         out_specs=[full] * 4,
-        scratch_shapes=[pltpu.VMEM(part.shape, f32), pltpu.VMEM(gates.shape, f32)]
+        scratch_shapes=[
+            pltpu.VMEM(part.shape, f32),
+            pltpu.VMEM(gates_part.shape, f32),
+            pltpu.VMEM(gates.shape, f32),
+        ]
         + line_scratch([part, gates_part]),
         compiler_params=pltpu.CompilerParams(
             collective_id=name, has_side_effects=True, vmem_limit_bytes=58 << 20
@@ -681,6 +712,31 @@
             flops=40 * length * width, bytes_accessed=60 * 10**6, transcendentals=0
         ),
     )(part, gates_part, gates, middle, cotangent, gain.reshape(1, width), router)
+
+
+def last_kernel(summed_ref, tokens_ref, middle_ref, gain_ref, out_ref):
+    hidden = tokens_ref[...].astype(jnp.float32)
+    recip = lax.rsqrt(jnp.mean(hidden * hidden, axis=1, keepdims=True) + EPSILON)
+    unit = hidden * recip
+    scaled = summed_ref[...] * gain_ref[...]
+    inner = jnp.mean(scaled * unit, axis=1, keepdims=True)
+    out_ref[...] = middle_ref[...] + recip * (scaled - unit * inner)
+
+
+def leave_first(summed, tokens, grad_middle, gain):
+    length, width = tokens.shape
+    rows = pl.BlockSpec((BLOCK // 2, width), lambda i: (i, 0))
+    return pl.pallas_call(
+        last_kernel,
+        out_shape=jax.ShapeDtypeStruct((length, width), jnp.float32),
+        grid=(2 * length // BLOCK,),
+        in_specs=[rows, rows, rows, pl.BlockSpec((1, width), lambda i: (0, 0))],
+        out_specs=rows,
+        compiler_params=pltpu.CompilerParams(vmem_limit_bytes=16 << 20),
+        cost_estimate=pl.CostEstimate(
+            flops=10 * length * width, bytes_accessed=14 * length * width, transcendentals=0
+        ),
+    )(summed, tokens, grad_middle, gain.reshape(1, width))
 
 
 SPAN = 768
@@ -1136,7 +1192,7 @@
                 )
         return made
 
-    stops = [6, 28, 18, 2]
+    stops = [6] + [42] * (levels > 1) + [4, 0, 0]
     for level in range(levels):
         for copy in copies(level):
             copy.start()
@@ -1168,8 +1224,8 @@
     query_out[...] = kept[:, : query_out.shape[1]]
     key_out[...] = kept[:, wide - 256 : wide - 256 + key_out.shape[1]]
     value_out[...] = kept[:, wide - 128 : wide - 128 + value_out.shape[1]]
-    branch_out[...] = jnp.transpose(kept[:, wide : wide + attended_wide])[: branch_out.shape[0]]
-    router_out[...] = gains_ref[0][:, : router_out.shape[1]]
+    branch_out[...] = kept[:, wide : wide + branch_out.shape[1]]
+    router_out[...] = jnp.transpose(gains_ref[0])[: router_out.shape[0]]
     run_line(done, 2 * STEPS)
     total = gains_ref[0]
     for ahead, copy in enumerate(gain_copies, 1):
@@ -1195,8 +1251,8 @@
     levels = parts.bit_length() - 1
     own = width // parts
     f32 = jnp.float32
-    shapes = [(length, width), (own, wide_q), (own, wide_k), (own, wide_k), (wide_q, own)]
-    shapes += [(own, experts), (1, own), (1, own)]
+    shapes = [(length, width), (own, wide_q), (own, wide_k), (own, wide_k), (own, wide_q)]
+    shapes += [(experts, own), (1, own), (1, own)]
     return pl.pallas_call(
         functools.partial(finish_kernel, n, parts),
         out_shape=[jax.ShapeDtypeStruct(shape, f32) for shape in shapes],
@@ -1288,7 +1344,6 @@
     tables = rope_tables(opening, HEAD)
     query_w, key_w, value_w = (pad_columns(w) for w in (query_weight, key_weight, value_weight))
     out_w = jnp.transpose(pad_columns(jnp.transpose(out_weight)))
-    hidden_in = tokens.astype(jnp.float32)
     ways, out_rows = gather_out_weight(out_weight, parts)
     normed_b, queries, keys, values, attended, logsum = attend_forward(
         tokens, attn_gain, query_w, key_w, value_w, tables, opening, heads_local, group_size
@@ -1328,7 +1383,7 @@
     shards_last = lax.psum_scatter(grads_last, "dp", scatter_dimension=2, tiled=True)
     grad_gates_local = jnp.concatenate([sums[2], sums_last[2]], 0).reshape(experts_local, length)
     grad_gates_part = lax.dynamic_update_slice_in_dim(
-        jnp.zeros(gate_probs.shape, jnp.float32), jnp.transpose(grad_gates_local), first_expert, 1
+        jnp.zeros((experts_all, length), jnp.float32), grad_gates_local, first_expert, 0
     )
     grad_middle, grad_branch_b, grad_logits_b, grad_ffn_gain = turn_middle(
         ring, grad_normed_part, grad_gates_part, gate_probs, middle, cotangent, ffn_gain, router_w, 2
@@ -1338,18 +1393,15 @@
         query_w, key_w, value_w, tables, opening, tokens, moe_part, middle, heads_local, group_size, 3,
     )
     wide_q, wide_k = heads_local * HEAD, kv_local * HEAD
+    grads_placed = place_shards(parts, shards_first, 0, experts_local, None)
+    grads_placed, grads_wide = lax.optimization_barrier((grads_placed, grads_wide))
     grad_normed, *small = finish(
         ring, parts, grad_normed_local, normed_b, grads_wide, grad_branch_b, attended, normed_two_b,
         grad_logits_b, grad_ffn_gain, first_gain, wide_q, wide_k, experts_all, 4,
     )
     grad_query, grad_key, grad_value, grad_out, grad_router, grad_ffn_gain, grad_attn_gain = small
-    recip_one = lax.rsqrt(jnp.mean(hidden_in * hidden_in, axis=-1, keepdims=True) + EPSILON)
-    unit_one = hidden_in * recip_one
-    scaled = grad_normed * attn_gain
-    inner = jnp.mean(scaled * unit_one, axis=-1, keepdims=True)
-    grad_tokens = grad_middle + recip_one * (scaled - unit_one * inner)
+    grad_tokens = leave_first(grad_normed, tokens, grad_middle, attn_gain)
     shards_last, grad_tokens = lax.optimization_barrier((shards_last, grad_tokens))
-    grads_placed = place_shards(parts, shards_first, 0, experts_local, None)
     grad_gate, grad_up, grad_down = place_shards(
         parts, shards_last, numbers[0], experts_local, grads_placed
     )
@@ -1360,9 +1412,9 @@
         grad_query,
         grad_key,
         grad_value,
-        grad_out,
+        jnp.transpose(grad_out),
         grad_ffn_gain.reshape(-1),
-        grad_router,
+        jnp.transpose(grad_router),
         grad_gate,
         grad_up,
         grad_down,

time: 894 us -> 880 us (0.984)
  other arithmetic: 16.9 us -> 5.66 us
    pallas_call x2, Pallas kernels: 129 us -> 114 us  [expert_stage(): pl.pallas_call(functools.partial(expert_kernel, parts, first, numbers, ch...]
    pallas_call x1, Pallas kernels: 176 us -> 185 us  [finish(): pl.pallas_call(functools.partial(finish_kernel, n, parts), out_shape=[jax...]
    unnamed x75 -> x77, local copies, waits for them, and re-layouts: 20.6 us -> 23.3 us
  transfers between devices with their start and end apart: 4 -> 4, of which waited for: 1 -> 1; matrix products, arithmetic and copies ran while one was open for 3% -> 1% of each run, Pallas kernels for 87% -> 89%
where the time goes in v7:
time: 880 us; the launch traced here: 869 us
  Pallas kernels  822 us (93%)
  local copies, waits for them, and re-layouts  26.6 us (3%)
  between operations  14.4 us (2%)
    pallas_call x1, Pallas kernels, finish(): pl.pallas_call(functools.partial(finish_kernel, n, parts), out_shape=[jax...  185 us
    pallas_call x1, Pallas kernels, attend_backward(): pl.pallas_call(functools.partial(attend_backward_kernel, n, heads, group)...  181 us
    pallas_call x1, Pallas kernels, turn_middle(): pl.pallas_call(functools.partial(turn_kernel, n), out_shape=[jax.ShapeDty...  181 us
    pallas_call x2, Pallas kernels, expert_stage(): pl.pallas_call(functools.partial(expert_kernel, parts, first, numbers, ch...  114 us
    pallas_call x1, Pallas kernels, line_gather(): pl.pallas_call(functools.partial(line_gather_kernel, n), out_shape=jax.Sh...  104 us
    unnamed x77, local copies, waits for them, and re-layouts  23.3 us
    pallas_call x1, Pallas kernels, attend_forward(): pl.pallas_call(functools.partial(attend_forward_kernel, heads, group), ou...  21.1 us
  transfers between devices with their start and end apart: 4, of which 1 were waited for; matrix products, arithmetic and copies ran while one was open for 1% of the time, Pallas kernels for 89%

profile of v7, /device:TPU:8, one launch (start us, length us, event | category | flops | bytes accessed | tf_op | source)
XLA Modules:
  0.0 869.3 jit_solution(17430540133541787569)
XLA Ops:
  7.3 2.1 shard_map.229
  10.2 1.3 convert_reduce_fusion
  11.8 1.9 multiply_sine_fusion
  13.7 1.3 pad_maximum_fusion.2
  15.1 21.1 %shard_map.230 = (bf16[1024,1536]{1,0:T(8,128)(2,1)}, bf16[3,1024,128]{2,1,0:T(8,128)(2,1)S(1)}, bf16[1024,128]{1,0:T(8,128)(2,1)S(1)}, bf16[1024,128]{1,0:T(8,1...) custom-call(bf16[1024,1536]{1,0:T(8,128)(2,1)} %tokens_ref.7, f32[1,1536]{1,0:T(1,128)S(1)} %reshape.74.gain_ref, ...), custom_call_target="tpu_custom_call" | custom-call | flops 8000000000 | bytes 12000000 | tf_op jit(solution)/shard_map/pallas_call | solution.py:860
  37.0 0.8 copy-done.9
  38.6 0.9 copy-done.15
  41.5 0.9 convert_reduce_fusion.2
  44.1 104.0 %shard_map.231.attended_ref = bf16[1024,1536]{1,0:T(8,128)(2,1)S(1)} custom-call(bf16[1024,384]{1,0:T(8,128)(2,1)S(1)} %get-tuple-element.63.x_ref.attended_ref), custom_call_target="tpu_custom_call" | custom-call | bytes 25165824 | tf_op jit(solution)/shard_map/pallas_call | solution.py:538
  148.1 1.7 copy-done.5
  149.8 13.3 %shard_map.232 = (f32[1024,1536]{1,0:T(8,128)}, bf16[1024,1536]{1,0:T(8,128)(2,1)S(1)}, f32[1024,128]{1,0:T(8,128)S(1)}) custom-call(bf16[1024,1536]{1,0:T(8,128)(2,1)} %copy-done.5, f32[8,4,48,1536]{3,2,1,0:T(8,128)} %bitcast.23, bf16[1024,1536]{1,0:T(8,128)(2,1)} %tokens_ref.7, f32[1,1536]{1,0:T(1,128)S(1)} %reshape.75.gain_ref, ...), custom_call_target="tpu_custom_call" | custom-call | flops 4831838208 | bytes 25000000 | tf_op jit(solution)/shard_map/pallas_call | solution.py:606
  163.1 1.6 copy-done
  165.6 22.3 %shard_map.233 = (f32[1,3,1536,512]{3,2,1,0:T(8,128)}, f32[1024,1536]{1,0:T(8,128)}, f32[1024,1536]{1,0:T(8,128)}, f32[1,1,1024]{2,1,0:T(1,128)}) custom-call(s32[10]{0:T(128)} %get-tuple-element.113.count_ref, s32[10,1,1024]{2,1,0:T(1,128)} %reshape.73.place_ref, f32[10,1,1024]{2,1,0:T(1,128)} %reshape.76.gate_ref, bf16[1024,1536]{1,0:T(8,128)(2,1)} %copy-done, ...), custom_call_target="tpu_custom_call" | custom-call | flops 8000000000 | bytes 14000000 | tf_op jit(solution)/shard_map/pallas_call | solution.py:420
  188.0 92.0 %shard_map.234 = (f32[9,3,1536,512]{3,2,1,0:T(8,128)}, f32[1024,1536]{1,0:T(8,128)}, f32[1024,1536]{1,0:T(8,128)}, f32[9,1,1024]{2,1,0:T(1,128)}) custom-call(s32[10]{0:T(128)} %get-tuple-element.113.count_ref, s32[10,1,1024]{2,1,0:T(1,128)} %reshape.73.place_ref, f32[10,1,1024]{2,1,0:T(1,128)} %reshape.76.gate_ref, bf16[1024,1536]{1,0:T(8,128)(2,1)} %copy-done, ...), custom_call_target="tpu_custom_call" | custom-call | flops 71999995904 | bytes 126000000 | tf_op jit(solution)/shard_map/pallas_call | solution.py:420
  282.1 180.8 %shard_map.235 = (f32[1024,1536]{1,0:T(8,128)}, bf16[1024,1536]{1,0:T(8,128)(2,1)}, bf16[1024,128]{1,0:T(8,128)(2,1)}, f32[1,1536]{1,0:T(1,128)}) custom-call(f32[1024,1536]{1,0:T(8,128)} %get-tuple-element.72.part_ref, f32[40,1024]{1,0:T(8,128)} %copy-done.20, f32[1024,128]{1,0:T(8,128)} %copy-done.6, f32[1024,1536]{1,0:T(8,128)} %get-tuple-element.75.middle_ref, ...), custom_call_target="tpu_custom_call" | custom-call | flops 62914560 | bytes 60000000 | tf_op jit(solution)/shard_map/pallas_call | solution.py:692
  462.9 181.2 %shard_map.236 = (bf16[1024,640]{1,0:T(8,128)(2,1)}, f32[1024,1536]{1,0:T(8,128)}, f32[1,1536]{1,0:T(1,128)}, bf16[1024,1536]{1,0:T(8,128)(2,1)}) custom-call(bf16[1024,1536]{1,0:T(8,128)(2,1)} %get-tuple-element.76.branch_ref, bf16[384,1536]{1,0:T(8,128)(2,1)} %out_w.1, bf16[3,1024,128]{2,1,0:T(8,128)(2,1)} %copy-done.15, bf16[1024,128]{1,0:T(8,128)(2,1)} %copy-done.16, ...), custom_call_target="tpu_custom_call" | custom-call | flops 12000000000 | bytes 30000000 | tf_op jit(solution)/shard_map/pallas_call | solution.py:1059
  644.1 2.3 shard_map.237
  646.4 185.4 %shard_map.238 = (f32[1024,1536]{1,0:T(8,128)}, f32[192,384]{1,0:T(8,128)}, f32[192,128]{1,0:T(8,128)}, f32[192,128]{1,0:T(8,128)}, f32[192,384]{1,0:T(8,128)}, ...) custom-call(f32[1024,1536]{1,0:T(8,128)} %get-tuple-element.84.local_ref, ...), custom_call_target="tpu_custom_call" | custom-call | flops 3623878656 | bytes 50000000 | tf_op jit(solution)/shard_map/pallas_call | solution.py:1256
  831.8 2.8 copy-done.1
  834.6 2.8 copy-done.2
  837.4 1.9 copy-done.4
  839.3 5.4 shard_map.239
  844.6 11.7 %shard_map.240 = (f32[10,192,512]{2,1,0:T(8,128)}, f32[10,192,512]{2,1,0:T(8,128)}, f32[10,64,1536]{2,1,0:T(8,128)}) custom-call(f32[9,3,192,512]{3,2,1,0:T(8,128)} %reduce-scatter.5.cloned.1.call-done.shards_ref, f32[10,192,512]{2,1,0:T(8,128)} %get-tuple-element.106.refs_0_, ...), custom_call_target="tpu_custom_call", output_to_operand_aliasing={{0}: (1, {}), {1}: (2, {}), {2}: (3, {})} | custom-call | bytes 21233664 | tf_op jit(solution)/shard_map/pallas_call | solution.py:1304
  856.4 1.7 copy.81
  (102 shorter events, 13.8 us)
Async XLA Ops:
  7.2 7.8 copy-start.14
  7.2 7.8 copy-start.13
  7.2 7.8 copy-start.12
  7.2 34.1 %all-gather.5.cloned.1.call-start = ((), (), s32[]{:S(2)}) async-start(), calls=%async_computation.4 | async-start | bytes 1474560 | tf_op jit(solution)/shard_map/all_gather | solution.py:573
  9.4 140.3 %all-gather.7.cloned.1.call-start = ((), (), s32[]{:S(2)}) async-start(), calls=%async_computation.5 | async-start | bytes 10616832 | tf_op jit(solution)/shard_map/all_gather | solution.py:1359
  11.5 24.7 %copy-start.28 = (s32[1024]{0:T(1024)}, s32[1024]{0:T(1024)S(1)}, u32[]{:S(2)}) copy-start(s32[1024]{0:T(1024)S(1)} %convert_reduce_fusion) | copy-start | bytes 12292
  15.0 26.4 %copy-start.30 = (f32[1536]{0:T(1024)S(1)}, f32[1536]{0:T(1024)}, u32[]{:S(2)}) copy-start(f32[1536]{0:T(1024)} %param.23) | copy-start | bytes 18436
  15.0 26.4 %copy-start.23 = (s32[1024,8]{0,1:T(8,128)S(1)}, s32[1024,8]{0,1:T(8,128)}, u32[]{:S(2)}) copy-start(s32[1024,8]{0,1:T(8,128)} %param.17) | copy-start | bytes 98308
  15.0 28.6 %copy-start.24 = (bf16[1536,40]{0,1:T(8,128)(2,1)S(1)}, bf16[1536,40]{0,1:T(8,128)(2,1)}, u32[]{:S(2)}) copy-start(bf16[1536,40]{0,1:T(8,128)(2,1)} %param.24) | copy-start | bytes 368644
  40.9 107.2 %copy-start.3 = (bf16[1024,384]{1,0:T(8,128)(2,1)}, bf16[1024,384]{1,0:T(8,128)(2,1)S(1)}, u32[]{:S(2)}) copy-start(bf16[1024,384]{1,0:T(8,128)(2,1)S(1)} %get-tuple-element.63.x_ref.attended_ref) | copy-start | bytes 2359300
  40.9 107.2 %copy-start.18 = (f32[6,1,1024]{2,1,0:T(1,128)}, f32[6,1,1024]{2,1,0:T(1,128)S(1)}, u32[]{:S(2)}) copy-start(f32[6,1,1024]{2,1,0:T(1,128)S(1)} %get-tuple-element.80.logsum_ref) | copy-start | bytes 73732
  41.3 238.7 %reduce-scatter.3.cloned.1.call-start = ((), (), s32[]{:S(2)}) async-start(), calls=%async_computation.2 | async-start | bytes 10616832 | tf_op jit(solution)/shard_map/reduce_scatter | solution.py:1374
  41.4 108.3 %copy-start.11 = (f32[1,1536]{1,0:T(1,128)}, f32[1,1536]{1,0:T(1,128)S(1)}, u32[]{:S(2)}) copy-start(f32[1,1536]{1,0:T(1,128)S(1)} %reshape.75.gain_ref) | copy-start | bytes 18436
  44.0 119.1 %copy-start.7 = (bf16[1536,128]{1,0:T(8,128)(2,1)}, bf16[1536,128]{1,0:T(8,128)(2,1)S(1)}, u32[]{:S(2)}) copy-start(bf16[1536,128]{1,0:T(8,128)(2,1)S(1)} %pad.10.router_ref) | copy-start | bytes 1179652
  164.7 23.2 %copy-start.6 = (f32[1024,128]{1,0:T(8,128)}, f32[1024,128]{1,0:T(8,128)S(1)}, u32[]{:S(2)}) copy-start(f32[1024,128]{1,0:T(8,128)S(1)} %get-tuple-element.65.gates_ref) | copy-start | bytes 1572868
  187.9 656.7 %reduce-scatter.5.cloned.1.call-start = ((), (), s32[]{:S(2)}) async-start(), calls=%async_computation.3 | async-start | bytes 95551488 | tf_op jit(solution)/shard_map/reduce_scatter | solution.py:1383
  831.8 2.8 copy-start.1
  834.6 2.8 copy-start.2
  844.6 11.8 %copy-start.19 = (bf16[1024,1536]{1,0:T(8,128)(2,1)S(1)}, bf16[1024,1536]{1,0:T(8,128)(2,1)}, u32[]{:S(2)}) copy-start(bf16[1024,1536]{1,0:T(8,128)(2,1)} %get-tuple-element.132) | copy-start | bytes 9437188
  856.4 3.0 copy-start.26
  856.4 3.6 copy-start.25
  856.4 4.3 copy-start.21
  856.4 5.0 copy-start.32
  856.4 5.5 copy-start.27
  (14 other events, 16.1 us)
Sparse Core Ops, SparseCore 0:
  10.2 31.0 all-gather.4
  43.2 58.4 all-gather.6
  188.1 82.7 reduce-scatter.2
  280.2 507.2 reduce-scatter.4

commit v8 on v7

--- a/solution.py
+++ b/solution.py
@@ -253,8 +253,8 @@
     *refs,
 ):
     if chained:
-        moe_in, back_in = refs[:2]
-        refs = refs[2:]
+        moe_in, back_in, early_in = refs[:3]
+        refs = refs[3:]
     grads_out, refs = refs[: len(numbers)], refs[len(numbers) :]
     moe_out, back_out, gates_out = refs[:3]
     rows_ref, grads_ref, active_ref, gate_in_ref, up_in_ref, weights_ref, sems, out_sems = refs[3:]
@@ -276,11 +276,14 @@
     if chained:
         copy_moe = pltpu.make_async_copy(moe_in, moe_out, sems.at[0])
         copy_back = pltpu.make_async_copy(back_in, back_out, sems.at[1])
+        early = early_in.shape[0]
+        copy_early = pltpu.make_async_copy(early_in, grads_out[0].at[:early], sems.at[2])
 
         @pl.when(expert == 0)
         def _():
             copy_moe.start()
             copy_back.start()
+            copy_early.start()
 
     else:
 
@@ -324,6 +327,7 @@
         def _():
             copy_moe.wait()
             copy_back.wait()
+            copy_early.wait()
 
     def leave(rows):
         column = jnp.transpose(jnp.broadcast_to(place_ref[0], (128, length)))
@@ -341,16 +345,13 @@
 
     by_size(leave)
 
-    def copies(target, number):
-        return [
-            pltpu.make_async_copy(weights_ref.at[kind], target.at[number, kind], out_sems.at[kind])
-            for kind in range(3)
-        ]
+    def copy_out(target, at, kind):
+        return pltpu.make_async_copy(weights_ref.at[kind], target.at[at], out_sems.at[kind])
 
     @pl.when(expert > 0)
     def _():
-        for copy in copies(grads_out[0], 0):
-            copy.wait()
+        for kind in range(3):
+            copy_out(grads_out[0], 0, kind).wait()
 
     def weigh(rows):
         grads = left_inner(
@@ -369,24 +370,24 @@
                 ]
 
     by_size(weigh)
-    start = 0
-    for target, number in zip(grads_out, numbers):
-
-        @pl.when((expert >= start) & (expert < start + number))
-        def _():
-            for copy in copies(target, expert - start):
-                copy.start()
-
-        start += number
+    for kind in range(3):
+        start = -early_in.shape[0] if chained else 0
+        for target, number in zip(grads_out, numbers):
+            at = 3 * expert + kind - start
+
+            @pl.when((at >= 0) & (at < number))
+            def _():
+                copy_out(target, at, kind).start()
+
+            start += number
 
     @pl.when(expert == pl.num_programs(0) - 1)
     def _():
-        for copy in copies(grads_out[0], 0):
-            copy.wait()
-
-
-def expert_stage(parts, first, numbers, counts, places, gate_rows, normed_b, grad_b, gate_w, up_w, down_w, sums):
-    number = sum(numbers)
+        for kind in range(3):
+            copy_out(grads_out[0], 0, kind).wait()
+
+
+def expert_stage(parts, first, number, numbers, counts, places, gate_rows, normed_b, grad_b, gate_w, up_w, down_w, sums):
     length, width = normed_b.shape
     hidden = gate_w.shape[2]
     experts = places.shape[0]
@@ -415,11 +416,11 @@
         down_w,
     ]
     if chained:
-        in_specs += [pl.BlockSpec(memory_space=pl.ANY)] * 2
-        args += [sums[0], sums[1]]
+        in_specs += [pl.BlockSpec(memory_space=pl.ANY)] * 3
+        args += list(sums)
     results = pl.pallas_call(
         functools.partial(expert_kernel, parts, first, numbers, chained),
-        out_shape=[jax.ShapeDtypeStruct((some, 3, width, hidden), f32) for some in numbers]
+        out_shape=[jax.ShapeDtypeStruct((some, width, hidden), f32) for some in numbers]
         + [
             jax.ShapeDtypeStruct((length, width), f32),
             jax.ShapeDtypeStruct((length, width), f32),
@@ -442,7 +443,7 @@
                 pltpu.VMEM((CAP, hidden), bf16),
                 pltpu.VMEM((CAP, hidden), bf16),
                 pltpu.VMEM((3, width, hidden), f32),
-                pltpu.SemaphoreType.DMA((2,)),
+                pltpu.SemaphoreType.DMA((3,)),
                 pltpu.SemaphoreType.DMA((3,)),
             ],
         ),
@@ -714,7 +715,8 @@
     )(part, gates_part, gates, middle, cotangent, gain.reshape(1, width), router)
 
 
-def last_kernel(summed_ref, tokens_ref, middle_ref, gain_ref, out_ref):
+def last_kernel(count, summed_ref, tokens_ref, middle_ref, gain_ref, *refs):
+    smalls, out_ref, small_outs = refs[:count], refs[count], refs[count + 1 :]
     hidden = tokens_ref[...].astype(jnp.float32)
     recip = lax.rsqrt(jnp.mean(hidden * hidden, axis=1, keepdims=True) + EPSILON)
     unit = hidden * recip
@@ -722,21 +724,29 @@
     inner = jnp.mean(scaled * unit, axis=1, keepdims=True)
     out_ref[...] = middle_ref[...] + recip * (scaled - unit * inner)
 
-
-def leave_first(summed, tokens, grad_middle, gain):
+    @pl.when(pl.program_id(0) == 0)
+    def _():
+        for small, out in zip(smalls, small_outs):
+            out[...] = small[...]
+
+
+def leave_first(summed, tokens, grad_middle, gain, smalls):
     length, width = tokens.shape
     rows = pl.BlockSpec((BLOCK // 2, width), lambda i: (i, 0))
+    whole = lambda shape: pl.BlockSpec(shape, lambda i: (0, 0))
+    f32 = jnp.float32
     return pl.pallas_call(
-        last_kernel,
-        out_shape=jax.ShapeDtypeStruct((length, width), jnp.float32),
+        functools.partial(last_kernel, len(smalls)),
+        out_shape=[jax.ShapeDtypeStruct((length, width), f32)]
+        + [jax.ShapeDtypeStruct(small.shape, f32) for small in smalls],
         grid=(2 * length // BLOCK,),
-        in_specs=[rows, rows, rows, pl.BlockSpec((1, width), lambda i: (0, 0))],
-        out_specs=rows,
-        compiler_params=pltpu.CompilerParams(vmem_limit_bytes=16 << 20),
+        in_specs=[rows, rows, rows, whole((1, width))] + [whole(small.shape) for small in smalls],
+        out_specs=[rows] + [whole(small.shape) for small in smalls],
+        compiler_params=pltpu.CompilerParams(vmem_limit_bytes=60 << 20),
         cost_estimate=pl.CostEstimate(
             flops=10 * length * width, bytes_accessed=14 * length * width, transcendentals=0
         ),
-    )(summed, tokens, grad_middle, gain.reshape(1, width))
+    )(summed, tokens, grad_middle, gain.reshape(1, width), *smalls)
 
 
 SPAN = 768
@@ -1042,7 +1052,7 @@
         recip = lax.rsqrt(jnp.mean(hidden * hidden, axis=1, keepdims=True) + EPSILON)
         gain_sum += jnp.sum(normed * (hidden * recip), axis=0, keepdims=True)
         run_line(2)
-    gain_out[...] = gain_sum
+    gain_out[...] = jnp.broadcast_to(gain_sum, gain_out.shape)
     run_line(2 * STEPS)
     line_end()
 
@@ -1061,7 +1071,7 @@
         out_shape=[
             jax.ShapeDtypeStruct((length, wide + 256), bf16),
             jax.ShapeDtypeStruct((length, width), f32),
-            jax.ShapeDtypeStruct((1, width), f32),
+            jax.ShapeDtypeStruct((8, width), f32),
             jax.ShapeDtypeStruct((length, width), bf16),
         ],
         in_specs=[full] * 16 + [pl.BlockSpec(memory_space=pl.ANY)],
@@ -1134,7 +1144,24 @@
     def run_line(first, last):
         lax.fori_loop(first, last, line_step, 0)
 
+    gain_copies = [
+        pltpu.make_async_remote_copy(
+            src_ref=first_gain_ref,
+            dst_ref=gains_ref.at[ahead],
+            send_sem=gain_send.at[ahead],
+            recv_sem=gain_recv.at[ahead],
+            device_id={"tensor": lax.rem(mine + ahead, n)},
+            device_id_type=MESH,
+        )
+        for ahead in range(1, n)
+    ]
+    for copy in gain_copies:
+        copy.start()
     run_line(0, 2)
+    first_gain = first_gain_ref[:1]
+    for ahead, copy in enumerate(gain_copies, 1):
+        copy.wait_recv()
+        first_gain = first_gain + gains_ref[ahead, :1]
     pieces = 4
     block = width // pieces
     for piece in range(pieces):
@@ -1144,13 +1171,13 @@
             branch_ref[:, rows], attended_ref[...]
         )
         gain = jnp.transpose(jnp.broadcast_to(gain_ref[:, rows], (128, block)))
-        first_gain = jnp.transpose(jnp.broadcast_to(first_gain_ref[:, rows], (128, block)))
+        own_gain = jnp.transpose(jnp.broadcast_to(first_gain[:, rows], (128, block)))
         lanes = lax.broadcasted_iota(jnp.int32, (block, 128), 1)
         weights_ref[rows, wide + attended_wide :] = jnp.where(
             lanes == 127,
             gain,
             jnp.where(
-                lanes == 126, first_gain, left_inner(normed_two_ref[:, rows], logits_ref[...])
+                lanes == 126, own_gain, left_inner(normed_two_ref[:, rows], logits_ref[...])
             ),
         )
         run_line(2 + 2 * piece, 4 + 2 * piece)
@@ -1206,33 +1233,16 @@
                 target = shard(number, lanes)
                 target[...] += held[level][i, :, lanes]
     everything = slice(0, columns)
-    gains_ref[0] = shard(me, slice(wide + attended_wide, columns))[...]
-    gain_copies = [
-        pltpu.make_async_remote_copy(
-            src_ref=gains_ref.at[0],
-            dst_ref=gains_ref.at[ahead],
-            send_sem=gain_send.at[ahead],
-            recv_sem=gain_recv.at[ahead],
-            device_id={"tensor": lax.rem(mine + ahead, n)},
-            device_id_type=MESH,
-        )
-        for ahead in range(1, n)
-    ]
-    for copy in gain_copies:
-        copy.start()
+    run_line(done, 2 * STEPS)
     kept = shard(me, everything)
+    tail = jnp.transpose(kept[:, wide + attended_wide :])
     query_out[...] = kept[:, : query_out.shape[1]]
     key_out[...] = kept[:, wide - 256 : wide - 256 + key_out.shape[1]]
     value_out[...] = kept[:, wide - 128 : wide - 128 + value_out.shape[1]]
     branch_out[...] = kept[:, wide : wide + branch_out.shape[1]]
-    router_out[...] = jnp.transpose(gains_ref[0])[: router_out.shape[0]]
-    run_line(done, 2 * STEPS)
-    total = gains_ref[0]
-    for ahead, copy in enumerate(gain_copies, 1):
-        copy.wait_recv()
-        total = total + gains_ref[ahead]
-    gain_out[...] = jnp.transpose(gains_ref[0])[127:]
-    first_gain_out[...] = jnp.transpose(total)[126:127]
+    router_out[...] = tail[: router_out.shape[0]]
+    gain_out[...] = tail[127:]
+    first_gain_out[...] = tail[126:127]
     for level in range(levels):
         for copy in copies(level):
             copy.wait_send()
@@ -1260,7 +1270,7 @@
         out_specs=[full] * 8,
         scratch_shapes=[
             pltpu.VMEM((width, columns), f32),
-            pltpu.VMEM((n, own, 128), f32),
+            pltpu.VMEM((n, 8, width), f32),
             pltpu.SemaphoreType.DMA((n,)),
             pltpu.SemaphoreType.DMA((n,)),
         ]
@@ -1279,37 +1289,51 @@
     )
 
 
-def place_kernel(shards_ref, *refs):
-    gate_out, up_out, down_out = refs[-3:]
-    gate_out[0] = shards_ref[0, 0]
-    up_out[0] = shards_ref[0, 1]
-    rows, hidden = down_out.shape[1], shards_ref.shape[3]
+def place_kernel(count, *refs):
+    shards, (gate_out, up_out, down_out) = refs[:count], refs[-3:]
+    gate, up, down = shards[-3:]
+    gate_out[...] = gate[...]
+    if count > 3:
+
+        @pl.when(pl.program_id(0) == 0)
+        def _():
+            gate_out[...] = shards[0][...]
+
+    up_out[...] = up[...]
+    rows, hidden = down_out.shape[1], down.shape[2]
     for piece in range(down_out.shape[2] // hidden):
-        down_out[0, :, piece * hidden : (piece + 1) * hidden] = shards_ref[
-            0, 2, piece * rows : (piece + 1) * rows, :
+        down_out[0, :, piece * hidden : (piece + 1) * hidden] = down[
+            0, piece * rows : (piece + 1) * rows, :
         ]
 
 
-def place_shards(parts, shards, first, experts, before):
-    number, unused, rows, hidden = shards.shape
-    down_rows = hidden // parts
-    width = rows * parts
-    shapes = [(experts, rows, hidden), (experts, rows, hidden), (experts, down_rows, width)]
+def place_shards(parts, first_shards, shards, experts, before):
+    unused, rows, hidden = first_shards.shape
+    shapes = [(experts, rows, hidden), (experts, rows, hidden)]
+    shapes += [(experts, hidden // parts, rows * parts)]
+    first = 0 if before is None else 1
     spec = lambda shape: pl.BlockSpec((1,) + shape[1:], lambda e: (first + e, 0, 0))
-    args, extra, aliases = [shards], [], {}
-    if before is not None:
-        args += list(before)
-        extra = [pl.BlockSpec(memory_space=pl.ANY)] * 3
-        aliases = {1: 0, 2: 1, 3: 2}
+    one = lambda at: pl.BlockSpec((1, rows, hidden), lambda e: (at(e), 0, 0))
+    if before is None:
+        args = [first_shards] * 3
+        in_specs = [one(lambda e: 0), one(lambda e: 1), one(lambda e: 2)]
+        aliases = {}
+    else:
+        args = [first_shards] + [shards] * 3 + list(before)
+        in_specs = [one(lambda e: 3), one(lambda e: jnp.maximum(3 * e - 1, 0))]
+        in_specs += [one(lambda e: 3 * e), one(lambda e: 3 * e + 1)]
+        in_specs += [pl.BlockSpec(memory_space=pl.ANY)] * 3
+        aliases = {4: 0, 5: 1, 6: 2}
     return pl.pallas_call(
-        place_kernel,
+        functools.partial(place_kernel, 3 if before is None else 4),
         out_shape=[jax.ShapeDtypeStruct(shape, jnp.float32) for shape in shapes],
-        grid=(number,),
-        in_specs=[pl.BlockSpec((1, 3, rows, hidden), lambda e: (e, 0, 0, 0))] + extra,
+        grid=(1 if before is None else experts - 1,),
+        in_specs=in_specs,
         out_specs=[spec(shape) for shape in shapes],
         input_output_aliases=aliases,
+        compiler_params=pltpu.CompilerParams(vmem_limit_bytes=60 << 20),
         cost_estimate=pl.CostEstimate(
-            flops=0, bytes_accessed=8 * shards.size, transcendentals=0
+            flops=0, bytes_accessed=8 * 3 * rows * hidden * experts, transcendentals=0
         ),
     )(*args)
 
@@ -1365,22 +1389,20 @@
         attended_all, out_all, tokens, ffn_gain, router_w, pad_columns(chosen.astype(jnp.float32))
     )
     gate_rows = jnp.transpose(lax.dynamic_slice_in_dim(gate_probs, first_expert, experts_local, 1))
-    numbers = (max(1, experts_local // 10),)
-    numbers += (experts_local - numbers[0],)
-    (grads_first,), sums = expert_stage(
-        parts, 0, numbers[:1], counts, places_in, gate_rows, normed_two_b, cotangent,
+    (grads_first, grads_next), sums = expert_stage(
+        parts, 0, 2, (4, 2), counts, places_in, gate_rows, normed_two_b, cotangent,
         gate_weight, up_weight, down_weight, None,
     )
-    shards_first = lax.psum_scatter(grads_first, "dp", scatter_dimension=2, tiled=True)
+    shards_first = lax.psum_scatter(grads_first, "dp", scatter_dimension=1, tiled=True)
     (grads_last,), sums_last = expert_stage(
-        parts, numbers[0], numbers[1:], counts, places_in, gate_rows, normed_two_b, cotangent,
-        gate_weight, up_weight, down_weight, sums,
+        parts, 2, experts_local - 2, (3 * experts_local - 4,), counts, places_in, gate_rows,
+        normed_two_b, cotangent, gate_weight, up_weight, down_weight, (sums[0], sums[1], grads_next),
     )
     moe_part, grad_normed_part, unused = sums_last
     shards_first, grads_last, grad_normed_part = lax.optimization_barrier(
         (shards_first, grads_last, grad_normed_part)
     )
-    shards_last = lax.psum_scatter(grads_last, "dp", scatter_dimension=2, tiled=True)
+    shards_last = lax.psum_scatter(grads_last, "dp", scatter_dimension=1, tiled=True)
     grad_gates_local = jnp.concatenate([sums[2], sums_last[2]], 0).reshape(experts_local, length)
     grad_gates_part = lax.dynamic_update_slice_in_dim(
         jnp.zeros((experts_all, length), jnp.float32), grad_gates_local, first_expert, 0
@@ -1393,17 +1415,17 @@
         query_w, key_w, value_w, tables, opening, tokens, moe_part, middle, heads_local, group_size, 3,
     )
     wide_q, wide_k = heads_local * HEAD, kv_local * HEAD
-    grads_placed = place_shards(parts, shards_first, 0, experts_local, None)
+    grads_placed = place_shards(parts, shards_first, None, experts_local, None)
     grads_placed, grads_wide = lax.optimization_barrier((grads_placed, grads_wide))
     grad_normed, *small = finish(
         ring, parts, grad_normed_local, normed_b, grads_wide, grad_branch_b, attended, normed_two_b,
         grad_logits_b, grad_ffn_gain, first_gain, wide_q, wide_k, experts_all, 4,
     )
+    grad_tokens, *small = leave_first(grad_normed, tokens, grad_middle, attn_gain, small)
     grad_query, grad_key, grad_value, grad_out, grad_router, grad_ffn_gain, grad_attn_gain = small
-    grad_tokens = leave_first(grad_normed, tokens, grad_middle, attn_gain)
     shards_last, grad_tokens = lax.optimization_barrier((shards_last, grad_tokens))
     grad_gate, grad_up, grad_down = place_shards(
-        parts, shards_last, numbers[0], experts_local, grads_placed
+        parts, shards_first, shards_last, experts_local, grads_placed
     )
     return (
         output,

time: 880 us -> 1080 us (1.23)
  Pallas kernels: 822 us -> 1040 us
  local copies, waits for them, and re-layouts: 26.6 us -> 14.7 us
    pallas_call x2, Pallas kernels: 114 us -> 332 us  [expert_stage(): pl.pallas_call(functools.partial(expert_kernel, parts, first, numbers, ch...]
    pallas_call x1, Pallas kernels: 185 us -> 172 us  [finish(): pl.pallas_call(functools.partial(finish_kernel, n, parts), out_shape=[jax...]
    unnamed x77 -> x52, local copies, waits for them, and re-layouts: 23.3 us -> 11.3 us
  transfers between devices with their start and end apart: 4 -> 4, of which waited for: 1 -> 1; matrix products, arithmetic and copies ran while one was open for 1% -> 1% of each run, Pallas kernels for 89% -> 88%
where the time goes in v8:
time: 1080 us; the launch traced here: 1070 us
  Pallas kernels  1040 us (96%)
  local copies, waits for them, and re-layouts  14.7 us (1%)
  between operations  14.4 us (1%)
    pallas_call x2, Pallas kernels, expert_stage(): pl.pallas_call(functools.partial(expert_kernel, parts, first, numbers, ch...  332 us
    pallas_call x1, Pallas kernels, turn_middle(): pl.pallas_call(functools.partial(turn_kernel, n), out_shape=[jax.ShapeDty...  184 us
    pallas_call x1, Pallas kernels, attend_backward(): pl.pallas_call(functools.partial(attend_backward_kernel, n, heads, group)...  181 us
    pallas_call x1, Pallas kernels, finish(): pl.pallas_call(functools.partial(finish_kernel, n, parts), out_shape=[jax...  172 us
    pallas_call x1, Pallas kernels, line_gather(): pl.pallas_call(functools.partial(line_gather_kernel, n), out_shape=jax.Sh...  104 us
  transfers between devices with their start and end apart: 4, of which 1 were waited for; matrix products, arithmetic and copies ran while one was open for 1% of the time, Pallas kernels for 88%

profile of v8, /device:TPU:8, one launch (start us, length us, event | category | flops | bytes accessed | tf_op | source)
XLA Modules:
  0.0 1070.9 jit_solution(3907413311336730054)
XLA Ops:
  7.3 2.1 shard_map.229
  10.2 1.3 convert_reduce_fusion
  11.8 1.9 multiply_sine_fusion
  13.7 1.3 pad_maximum_fusion.2
  15.1 21.1 %shard_map.230 = (bf16[1024,1536]{1,0:T(8,128)(2,1)}, bf16[3,1024,128]{2,1,0:T(8,128)(2,1)S(1)}, bf16[1024,128]{1,0:T(8,128)(2,1)S(1)}, bf16[1024,128]{1,0:T(8,1...) custom-call(bf16[1024,1536]{1,0:T(8,128)(2,1)} %tokens_ref.7, f32[1,1536]{1,0:T(1,128)S(1)} %reshape.74.gain_ref, ...), custom_call_target="tpu_custom_call" | custom-call | flops 8000000000 | bytes 12000000 | tf_op jit(solution)/shard_map/pallas_call | solution.py:870
  36.2 0.8 copy-done.5
  37.0 0.8 copy-done.6
  37.8 0.8 copy-done.7
  38.6 0.9 copy-done.13
  40.2 0.7 copy-done.15
  41.4 0.9 convert_reduce_fusion.2
  44.1 104.0 %shard_map.231.attended_ref = bf16[1024,1536]{1,0:T(8,128)(2,1)S(1)} custom-call(bf16[1024,384]{1,0:T(8,128)(2,1)S(1)} %get-tuple-element.72.x_ref.attended_ref), custom_call_target="tpu_custom_call" | custom-call | bytes 25165824 | tf_op jit(solution)/shard_map/pallas_call | solution.py:539
  148.1 1.7 copy-done.2
  149.8 13.3 %shard_map.232 = (f32[1024,1536]{1,0:T(8,128)}, bf16[1024,1536]{1,0:T(8,128)(2,1)S(1)}, f32[1024,128]{1,0:T(8,128)S(1)}) custom-call(bf16[1024,1536]{1,0:T(8,128)(2,1)} %copy-done.2, f32[8,4,48,1536]{3,2,1,0:T(8,128)} %bitcast.17, bf16[1024,1536]{1,0:T(8,128)(2,1)} %tokens_ref.7, f32[1,1536]{1,0:T(1,128)S(1)} %reshape.75.gain_ref, ...), custom_call_target="tpu_custom_call" | custom-call | flops 4831838208 | bytes 25000000 | tf_op jit(solution)/shard_map/pallas_call | solution.py:607
  163.0 1.7 copy-done.1
  165.6 64.5 %shard_map.233 = (f32[4,1536,512]{2,1,0:T(8,128)}, f32[2,1536,512]{2,1,0:T(8,128)}, f32[1024,1536]{1,0:T(8,128)}, f32[1024,1536]{1,0:T(8,128)}, f32[2,1,1024]{2,1,0:T(1,128)}) custom-call(s32[10]{0:T(128)} %get-tuple-element.131.count_ref, s32[10,1,1024]{2,1,0:T(1,128)} %reshape.73.place_ref, f32[10,1,1024]{2,1,0:T(1,128)} %reshape.76.gate_ref, ...), custom_call_target="tpu_custom_call" | custom-call | flops 16000000000 | bytes 28000000 | tf_op jit(solution)/shard_map/pallas_call | solution.py:421
  230.2 267.9 %shard_map.234 = (f32[26,1536,512]{2,1,0:T(8,128)}, f32[1024,1536]{1,0:T(8,128)}, f32[1024,1536]{1,0:T(8,128)}, f32[8,1,1024]{2,1,0:T(1,128)}) custom-call(s32[10]{0:T(128)} %get-tuple-element.131.count_ref, s32[10,1,1024]{2,1,0:T(1,128)} %reshape.73.place_ref, f32[10,1,1024]{2,1,0:T(1,128)} %reshape.76.gate_ref, bf16[1024,1536]{1,0:T(8,128)(2,1)} %copy-done.1, ...), custom_call_target="tpu_custom_call" | custom-call | flops 64000000000 | bytes 112000000 | tf_op jit(solution)/shard_map/pallas_call | solution.py:421
  500.2 183.8 %shard_map.235 = (f32[1024,1536]{1,0:T(8,128)}, bf16[1024,1536]{1,0:T(8,128)(2,1)}, bf16[1024,128]{1,0:T(8,128)(2,1)}, f32[1,1536]{1,0:T(1,128)}) custom-call(f32[1024,1536]{1,0:T(8,128)} %get-tuple-element.82.part_ref, f32[40,1024]{1,0:T(8,128)} %copy-done.18, f32[1024,128]{1,0:T(8,128)} %copy-done.3, f32[1024,1536]{1,0:T(8,128)} %get-tuple-element.85.middle_ref, ...), custom_call_target="tpu_custom_call" | custom-call | flops 62914560 | bytes 60000000 | tf_op jit(solution)/shard_map/pallas_call | solution.py:693
  684.0 181.4 %shard_map.236 = (bf16[1024,640]{1,0:T(8,128)(2,1)}, f32[1024,1536]{1,0:T(8,128)}, f32[8,1536]{1,0:T(8,128)}, bf16[1024,1536]{1,0:T(8,128)(2,1)}) custom-call(bf16[1024,1536]{1,0:T(8,128)(2,1)} %get-tuple-element.86.branch_ref, bf16[384,1536]{1,0:T(8,128)(2,1)} %out_w.1, bf16[3,1024,128]{2,1,0:T(8,128)(2,1)} %copy-done.13, bf16[1024,128]{1,0:T(8,128)(2,1)} %copy-done.14, ...), custom_call_target="tpu_custom_call" | custom-call | flops 12000000000 | bytes 30000000 | tf_op jit(solution)/shard_map/pallas_call | solution.py:1069
  865.3 2.3 shard_map.237
  867.6 171.7 %shard_map.238 = (f32[1024,1536]{1,0:T(8,128)}, f32[192,384]{1,0:T(8,128)}, f32[192,128]{1,0:T(8,128)}, f32[192,128]{1,0:T(8,128)}, f32[192,384]{1,0:T(8,128)}, ...) custom-call(f32[1024,1536]{1,0:T(8,128)} %get-tuple-element.94.local_ref, ...), custom_call_target="tpu_custom_call" | custom-call | flops 3623878656 | bytes 50000000 | tf_op jit(solution)/shard_map/pallas_call | solution.py:1266
  1039.3 11.4 %shard_map.239 = (f32[1024,1536]{1,0:T(8,128)}, f32[192,384]{1,0:T(8,128)}, f32[192,128]{1,0:T(8,128)}, f32[192,128]{1,0:T(8,128)}, f32[192,384]{1,0:T(8,128)}, ...) custom-call(f32[1024,1536]{1,0:T(8,128)} %get-tuple-element.105.summed_ref, bf16[1024,1536]{1,0:T(8,128)(2,1)} %tokens_ref.7, ...), custom_call_target="tpu_custom_call" | custom-call | flops 15728640 | bytes 22020096 | tf_op jit(solution)/shard_map/pallas_call | solution.py:738
  1050.8 11.7 %shard_map.240 = (f32[10,192,512]{2,1,0:T(8,128)}, f32[10,192,512]{2,1,0:T(8,128)}, f32[10,64,1536]{2,1,0:T(8,128)}) custom-call(f32[4,192,512]{2,1,0:T(8,128)} %reduce-scatter.3.cloned.1.call-done.refs_0_.refs_1_.refs_2_, ...), custom_call_target="tpu_custom_call", output_to_operand_aliasing={{0}: (4, {}), {1}: (5, {}), {2}: (6, {})} | custom-call | bytes 23592960 | tf_op jit(solution)/shard_map/pallas_call | solution.py:1327
  1062.5 1.7 copy.74
  (78 shorter events, 7.0 us)
Async XLA Ops:
  7.2 7.8 copy-start.10
  7.2 7.8 copy-start.11
  7.2 7.8 copy-start.12
  7.2 34.1 %all-gather.5.cloned.1.call-start = ((), (), s32[]{:S(2)}) async-start(), calls=%async_computation.4 | async-start | bytes 1474560 | tf_op jit(solution)/shard_map/all_gather | solution.py:574
  9.4 140.4 %all-gather.7.cloned.1.call-start = ((), (), s32[]{:S(2)}) async-start(), calls=%async_computation.5 | async-start | bytes 10616832 | tf_op jit(solution)/shard_map/all_gather | solution.py:1383
  10.2 26.0 %copy-start.8 = (f32[1,1536]{1,0:T(1,128)}, f32[1,1536]{1,0:T(1,128)S(1)}, u32[]{:S(2)}) copy-start(f32[1,1536]{1,0:T(1,128)S(1)} %reshape.74.gain_ref) | copy-start | bytes 18436
  11.5 24.7 %copy-start.21 = (s32[1024]{0:T(1024)}, s32[1024]{0:T(1024)S(1)}, u32[]{:S(2)}) copy-start(s32[1024]{0:T(1024)S(1)} %convert_reduce_fusion) | copy-start | bytes 12292
  15.0 26.4 %copy-start.19 = (s32[1024,8]{0,1:T(8,128)S(1)}, s32[1024,8]{0,1:T(8,128)}, u32[]{:S(2)}) copy-start(s32[1024,8]{0,1:T(8,128)} %param.17) | copy-start | bytes 98308
  15.0 28.2 %copy-start.23 = (f32[1536]{0:T(1024)S(1)}, f32[1536]{0:T(1024)}, u32[]{:S(2)}) copy-start(f32[1536]{0:T(1024)} %param.23) | copy-start | bytes 18436
  15.1 28.2 %copy-start.20 = (bf16[1536,40]{0,1:T(8,128)(2,1)S(1)}, bf16[1536,40]{0,1:T(8,128)(2,1)}, u32[]{:S(2)}) copy-start(bf16[1536,40]{0,1:T(8,128)(2,1)} %param.24) | copy-start | bytes 368644
  36.2 0.8 copy-start.5
  37.0 0.8 copy-start.6
  37.8 0.8 copy-start.7
  38.6 0.9 copy-start.13
  40.9 107.2 %copy-start = (bf16[1024,384]{1,0:T(8,128)(2,1)}, bf16[1024,384]{1,0:T(8,128)(2,1)S(1)}, u32[]{:S(2)}) copy-start(bf16[1024,384]{1,0:T(8,128)(2,1)S(1)} %get-tuple-element.72.x_ref.attended_ref) | copy-start | bytes 2359300
  40.9 107.2 %copy-start.16 = (f32[6,1,1024]{2,1,0:T(1,128)}, f32[6,1,1024]{2,1,0:T(1,128)S(1)}, u32[]{:S(2)}) copy-start(f32[6,1,1024]{2,1,0:T(1,128)S(1)} %get-tuple-element.90.logsum_ref) | copy-start | bytes 73732
  41.4 456.8 %reduce-scatter.3.cloned.1.call-start = ((), (), s32[]{:S(2)}) async-start(), calls=%async_computation.2 | async-start | bytes 14155776 | tf_op jit(solution)/shard_map/reduce_scatter | solution.py:1396
  43.3 119.7 %copy-start.9 = (f32[1,1536]{1,0:T(1,128)}, f32[1,1536]{1,0:T(1,128)S(1)}, u32[]{:S(2)}) copy-start(f32[1,1536]{1,0:T(1,128)S(1)} %reshape.75.gain_ref) | copy-start | bytes 18436
  44.0 119.1 %copy-start.4 = (bf16[1536,128]{1,0:T(8,128)(2,1)}, bf16[1536,128]{1,0:T(8,128)(2,1)S(1)}, u32[]{:S(2)}) copy-start(bf16[1536,128]{1,0:T(8,128)(2,1)S(1)} %pad.10.router_ref) | copy-start | bytes 1179652
  148.1 1.7 copy-start.2
  163.0 1.7 copy-start.1
  164.7 65.4 %copy-start.3 = (f32[1024,128]{1,0:T(8,128)}, f32[1024,128]{1,0:T(8,128)S(1)}, u32[]{:S(2)}) copy-start(f32[1024,128]{1,0:T(8,128)S(1)} %get-tuple-element.74.gates_ref) | copy-start | bytes 1572868
  230.1 820.7 %reduce-scatter.5.cloned.1.call-start = ((), (), s32[]{:S(2)}) async-start(), calls=%async_computation.3 | async-start | bytes 92012544 | tf_op jit(solution)/shard_map/reduce_scatter | solution.py:1405
  1050.8 11.7 %copy-start.17 = (bf16[1024,1536]{1,0:T(8,128)(2,1)S(1)}, bf16[1024,1536]{1,0:T(8,128)(2,1)}, u32[]{:S(2)}) copy-start(bf16[1024,1536]{1,0:T(8,128)(2,1)} %get-tuple-element.150) | copy-start | bytes 9437188
  (5 other events, 3.6 us)
Sparse Core Ops, SparseCore 0:
  10.2 31.0 all-gather.4
  43.2 58.4 all-gather.6
  230.2 98.5 reduce-scatter.2
  498.3 480.1 reduce-scatter.4

commit v9 on v7

--- a/solution.py
+++ b/solution.py
@@ -570,7 +570,8 @@
         in_specs=[full],
         out_specs=full,
     )(out_weight)
-    return ways, lax.all_gather(own, "tensor")
+    gathered = lax.all_gather(own, ("dp", "tensor") if ways > 1 else "tensor")
+    return gathered.reshape(ways, -1, rows // ways, width)
 
 
 def middle_kernel(
@@ -622,7 +623,7 @@
         out_specs=[rows(width), rows(width), rows(experts)],
         scratch_shapes=[pltpu.VMEM((attended.shape[1], width), jnp.bfloat16)],
         compiler_params=pltpu.CompilerParams(
-            dimension_semantics=("arbitrary",), vmem_limit_bytes=48 << 20
+            dimension_semantics=("arbitrary",), vmem_limit_bytes=62 << 20
         ),
         cost_estimate=pl.CostEstimate(
             flops=2 * length * width * width, bytes_accessed=25 * 10**6, transcendentals=0
@@ -714,7 +715,8 @@
     )(part, gates_part, gates, middle, cotangent, gain.reshape(1, width), router)
 
 
-def last_kernel(summed_ref, tokens_ref, middle_ref, gain_ref, out_ref):
+def last_kernel(count, summed_ref, tokens_ref, middle_ref, gain_ref, *refs):
+    smalls, out_ref, small_outs = refs[:count], refs[count], refs[count + 1 :]
     hidden = tokens_ref[...].astype(jnp.float32)
     recip = lax.rsqrt(jnp.mean(hidden * hidden, axis=1, keepdims=True) + EPSILON)
     unit = hidden * recip
@@ -722,21 +724,29 @@
     inner = jnp.mean(scaled * unit, axis=1, keepdims=True)
     out_ref[...] = middle_ref[...] + recip * (scaled - unit * inner)
 
-
-def leave_first(summed, tokens, grad_middle, gain):
+    @pl.when(pl.program_id(0) == 0)
+    def _():
+        for small, out in zip(smalls, small_outs):
+            out[...] = small[...]
+
+
+def leave_first(summed, tokens, grad_middle, gain, smalls):
     length, width = tokens.shape
     rows = pl.BlockSpec((BLOCK // 2, width), lambda i: (i, 0))
+    whole = lambda shape: pl.BlockSpec(shape, lambda i: (0, 0))
+    f32 = jnp.float32
     return pl.pallas_call(
-        last_kernel,
-        out_shape=jax.ShapeDtypeStruct((length, width), jnp.float32),
+        functools.partial(last_kernel, len(smalls)),
+        out_shape=[jax.ShapeDtypeStruct((length, width), f32)]
+        + [jax.ShapeDtypeStruct(small.shape, f32) for small in smalls],
         grid=(2 * length // BLOCK,),
-        in_specs=[rows, rows, rows, pl.BlockSpec((1, width), lambda i: (0, 0))],
-        out_specs=rows,
-        compiler_params=pltpu.CompilerParams(vmem_limit_bytes=16 << 20),
+        in_specs=[rows, rows, rows, whole((1, width))] + [whole(small.shape) for small in smalls],
+        out_specs=[rows] + [whole(small.shape) for small in smalls],
+        compiler_params=pltpu.CompilerParams(vmem_limit_bytes=60 << 20),
         cost_estimate=pl.CostEstimate(
             flops=10 * length * width, bytes_accessed=14 * length * width, transcendentals=0
         ),
-    )(summed, tokens, grad_middle, gain.reshape(1, width))
+    )(summed, tokens, grad_middle, gain.reshape(1, width), *smalls)
 
 
 SPAN = 768
@@ -874,7 +884,7 @@
             pltpu.VMEM((4, length, 128), bf16),
             pltpu.VMEM((tiles, length, 128), f32),
         ],
-        compiler_params=pltpu.CompilerParams(vmem_limit_bytes=48 << 20),
+        compiler_params=pltpu.CompilerParams(vmem_limit_bytes=62 << 20),
         cost_estimate=pl.CostEstimate(
             flops=8 * 10**9, bytes_accessed=12 * 10**6, transcendentals=5 * 10**6
         ),
@@ -1042,7 +1052,7 @@
         recip = lax.rsqrt(jnp.mean(hidden * hidden, axis=1, keepdims=True) + EPSILON)
         gain_sum += jnp.sum(normed * (hidden * recip), axis=0, keepdims=True)
         run_line(2)
-    gain_out[...] = gain_sum
+    gain_out[...] = jnp.broadcast_to(gain_sum, gain_out.shape)
     run_line(2 * STEPS)
     line_end()
 
@@ -1061,7 +1071,7 @@
         out_shape=[
             jax.ShapeDtypeStruct((length, wide + 256), bf16),
             jax.ShapeDtypeStruct((length, width), f32),
-            jax.ShapeDtypeStruct((1, width), f32),
+            jax.ShapeDtypeStruct((8, width), f32),
             jax.ShapeDtypeStruct((length, width), bf16),
         ],
         in_specs=[full] * 16 + [pl.BlockSpec(memory_space=pl.ANY)],
@@ -1134,7 +1144,24 @@
     def run_line(first, last):
         lax.fori_loop(first, last, line_step, 0)
 
+    gain_copies = [
+        pltpu.make_async_remote_copy(
+            src_ref=first_gain_ref,
+            dst_ref=gains_ref.at[ahead],
+            send_sem=gain_send.at[ahead],
+            recv_sem=gain_recv.at[ahead],
+            device_id={"tensor": lax.rem(mine + ahead, n)},
+            device_id_type=MESH,
+        )
+        for ahead in range(1, n)
+    ]
+    for copy in gain_copies:
+        copy.start()
     run_line(0, 2)
+    first_gain = first_gain_ref[:1]
+    for ahead, copy in enumerate(gain_copies, 1):
+        copy.wait_recv()
+        first_gain = first_gain + gains_ref[ahead, :1]
     pieces = 4
     block = width // pieces
     for piece in range(pieces):
@@ -1144,13 +1171,13 @@
             branch_ref[:, rows], attended_ref[...]
         )
         gain = jnp.transpose(jnp.broadcast_to(gain_ref[:, rows], (128, block)))
-        first_gain = jnp.transpose(jnp.broadcast_to(first_gain_ref[:, rows], (128, block)))
+        own_gain = jnp.transpose(jnp.broadcast_to(first_gain[:, rows], (128, block)))
         lanes = lax.broadcasted_iota(jnp.int32, (block, 128), 1)
         weights_ref[rows, wide + attended_wide :] = jnp.where(
             lanes == 127,
             gain,
             jnp.where(
-                lanes == 126, first_gain, left_inner(normed_two_ref[:, rows], logits_ref[...])
+                lanes == 126, own_gain, left_inner(normed_two_ref[:, rows], logits_ref[...])
             ),
         )
         run_line(2 + 2 * piece, 4 + 2 * piece)
@@ -1206,33 +1233,16 @@
                 target = shard(number, lanes)
                 target[...] += held[level][i, :, lanes]
     everything = slice(0, columns)
-    gains_ref[0] = shard(me, slice(wide + attended_wide, columns))[...]
-    gain_copies = [
-        pltpu.make_async_remote_copy(
-            src_ref=gains_ref.at[0],
-            dst_ref=gains_ref.at[ahead],
-            send_sem=gain_send.at[ahead],
-            recv_sem=gain_recv.at[ahead],
-            device_id={"tensor": lax.rem(mine + ahead, n)},
-            device_id_type=MESH,
-        )
-        for ahead in range(1, n)
-    ]
-    for copy in gain_copies:
-        copy.start()
+    run_line(done, 2 * STEPS)
     kept = shard(me, everything)
+    tail = jnp.transpose(kept[:, wide + attended_wide :])
     query_out[...] = kept[:, : query_out.shape[1]]
     key_out[...] = kept[:, wide - 256 : wide - 256 + key_out.shape[1]]
     value_out[...] = kept[:, wide - 128 : wide - 128 + value_out.shape[1]]
     branch_out[...] = kept[:, wide : wide + branch_out.shape[1]]
-    router_out[...] = jnp.transpose(gains_ref[0])[: router_out.shape[0]]
-    run_line(done, 2 * STEPS)
-    total = gains_ref[0]
-    for ahead, copy in enumerate(gain_copies, 1):
-        copy.wait_recv()
-        total = total + gains_ref[ahead]
-    gain_out[...] = jnp.transpose(gains_ref[0])[127:]
-    first_gain_out[...] = jnp.transpose(total)[126:127]
+    router_out[...] = tail[: router_out.shape[0]]
+    gain_out[...] = tail[127:]
+    first_gain_out[...] = tail[126:127]
     for level in range(levels):
         for copy in copies(level):
             copy.wait_send()
@@ -1260,7 +1270,7 @@
         out_specs=[full] * 8,
         scratch_shapes=[
             pltpu.VMEM((width, columns), f32),
-            pltpu.VMEM((n, own, 128), f32),
+            pltpu.VMEM((n, 8, width), f32),
             pltpu.SemaphoreType.DMA((n,)),
             pltpu.SemaphoreType.DMA((n,)),
         ]
@@ -1308,6 +1318,7 @@
         in_specs=[pl.BlockSpec((1, 3, rows, hidden), lambda e: (e, 0, 0, 0))] + extra,
         out_specs=[spec(shape) for shape in shapes],
         input_output_aliases=aliases,
+        compiler_params=pltpu.CompilerParams(vmem_limit_bytes=60 << 20),
         cost_estimate=pl.CostEstimate(
             flops=0, bytes_accessed=8 * shards.size, transcendentals=0
         ),
@@ -1344,7 +1355,7 @@
     tables = rope_tables(opening, HEAD)
     query_w, key_w, value_w = (pad_columns(w) for w in (query_weight, key_weight, value_weight))
     out_w = jnp.transpose(pad_columns(jnp.transpose(out_weight)))
-    ways, out_rows = gather_out_weight(out_weight, parts)
+    out_all = gather_out_weight(out_weight, parts)
     normed_b, queries, keys, values, attended, logsum = attend_forward(
         tokens, attn_gain, query_w, key_w, value_w, tables, opening, heads_local, group_size
     )
@@ -1355,8 +1366,6 @@
     picked = jnp.sum((routes[None, :, :] == local_ids[:, None, None]).astype(jnp.int32), axis=2)
     places_in = slot_places(picked)
     counts = jnp.sum(picked, axis=1)
-    out_rows, attended = lax.optimization_barrier((out_rows, attended))
-    out_all = lax.all_gather(out_rows, "dp") if ways > 1 else out_rows[None]
     attended_all = line_gather(attended, ring, 1)
     attended_all = attended_all.reshape(length, ring, attended.shape[1])
     attended_all = attended_all[:, :, : heads_local * HEAD].reshape(length, -1)
@@ -1399,8 +1408,8 @@
         ring, parts, grad_normed_local, normed_b, grads_wide, grad_branch_b, attended, normed_two_b,
         grad_logits_b, grad_ffn_gain, first_gain, wide_q, wide_k, experts_all, 4,
     )
+    grad_tokens, *small = leave_first(grad_normed, tokens, grad_middle, attn_gain, small)
     grad_query, grad_key, grad_value, grad_out, grad_router, grad_ffn_gain, grad_attn_gain = small
-    grad_tokens = leave_first(grad_normed, tokens, grad_middle, attn_gain)
     shards_last, grad_tokens = lax.optimization_barrier((shards_last, grad_tokens))
     grad_gate, grad_up, grad_down = place_shards(
         parts, shards_last, numbers[0], experts_local, grads_placed

time: 880 us -> 910 us (1.034)
  Pallas kernels: 822 us -> 860 us
  local copies, waits for them, and re-layouts: 26.6 us -> 14.8 us
    pallas_call x1, Pallas kernels: 104 us -> 135 us  [line_gather(): pl.pallas_call(functools.partial(line_gather_kernel, n), out_shape=jax.Sh...]
    unnamed x77 -> x18, local copies, waits for them, and re-layouts: 23.3 us -> 6.99 us
    pallas_call x1, Pallas kernels: 185 us -> 170 us  [finish(): pl.pallas_call(functools.partial(finish_kernel, n, parts), out_shape=[jax...]
  transfers between devices with their start and end apart: 4 -> 3, of which waited for: 1 -> 0; matrix products, arithmetic and copies ran while one was open for 1% -> 2% of each run, Pallas kernels for 89% -> 90%
where the time goes in v9:
time: 910 us; the launch traced here: 899 us
  Pallas kernels  860 us (95%)
  local copies, waits for them, and re-layouts  14.8 us (2%)
  between operations  14.2 us (2%)
    pallas_call x1, Pallas kernels, turn_middle(): pl.pallas_call(functools.partial(turn_kernel, n), out_shape=[jax.ShapeDty...  188 us
    pallas_call x1, Pallas kernels, attend_backward(): pl.pallas_call(functools.partial(attend_backward_kernel, n, heads, group)...  181 us
    pallas_call x1, Pallas kernels, finish(): pl.pallas_call(functools.partial(finish_kernel, n, parts), out_shape=[jax...  170 us
    pallas_call x1, Pallas kernels, line_gather(): pl.pallas_call(functools.partial(line_gather_kernel, n), out_shape=jax.Sh...  135 us
    pallas_call x2, Pallas kernels, expert_stage(): pl.pallas_call(functools.partial(expert_kernel, parts, first, numbers, ch...  122 us
    pallas_call x1, Pallas kernels, attend_forward(): pl.pallas_call(functools.partial(attend_forward_kernel, heads, group), ou...  22.9 us
  transfers between devices with their start and end apart: 3, of which 0 were waited for; matrix products, arithmetic and copies ran while one was open for 2% of the time, Pallas kernels for 90%

profile of v9, /device:TPU:8, one launch (start us, length us, event | category | flops | bytes accessed | tf_op | source)
XLA Modules:
  0.0 898.8 jit_solution(8678318716167346769)
XLA Ops:
  7.2 2.0 shard_map.231
  9.3 1.3 reshape.77.gain_ref
  10.6 1.3 reshape.79.gain_ref
  11.9 1.6 convert_reduce_fusion.2
  15.6 1.1 copy.49
  17.3 1.0 copy.48.opening_ref
  18.4 1.9 multiply_sine_fusion
  20.3 1.3 pad_maximum_fusion.cosine_ref
  21.6 1.9 pad_maximum_fusion.2
  23.5 22.9 %shard_map.229 = (bf16[1024,1536]{1,0:T(8,128)(2,1)}, bf16[3,1024,128]{2,1,0:T(8,128)(2,1)}, bf16[1024,128]{1,0:T(8,128)(2,1)}, bf16[1024,128]{1,0:T(8,128)(2,1)...) custom-call(bf16[1024,1536]{1,0:T(8,128)(2,1)} %tokens_ref.7, f32[1,1536]{1,0:T(1,128)} %reshape.77.gain_ref, ...), custom_call_target="tpu_custom_call" | custom-call | flops 8000000000 | bytes 12000000 | tf_op jit(solution)/shard_map/pallas_call | solution.py:870
  46.4 1.1 copy-done
  47.5 134.8 %shard_map.230.attended_ref = bf16[1024,1536]{1,0:T(8,128)(2,1)S(1)} custom-call(bf16[1024,384]{1,0:T(8,128)(2,1)S(1)} %copy-done), custom_call_target="tpu_custom_call" | custom-call | bytes 25165824 | tf_op jit(solution)/shard_map/pallas_call | solution.py:538
  182.3 1.7 copy-done.1
  185.7 13.9 %shard_map.232 = (f32[1024,1536]{1,0:T(8,128)}, bf16[1024,1536]{1,0:T(8,128)(2,1)}, f32[1024,128]{1,0:T(8,128)}) custom-call(bf16[1024,1536]{1,0:T(8,128)(2,1)} %copy-done.1, f32[8,4,48,1536]{3,2,1,0:T(8,128)} %bitcast.17, bf16[1024,1536]{1,0:T(8,128)(2,1)} %tokens_ref.7, f32[1,1536]{1,0:T(1,128)} %reshape.79.gain_ref, bf16[1536,128]{1,0:T(8,128)(2,1)} %pad.10.router_ref, ...), custom_call_target="tpu_custom_call" | custom-call | flops 4831838208 | bytes 25000000 | tf_op jit(solution)/shard_map/pallas_call | solution.py:607
  199.6 1.2 copy.52
  201.5 24.4 %shard_map.233 = (f32[1,3,1536,512]{3,2,1,0:T(8,128)}, f32[1024,1536]{1,0:T(8,128)}, f32[1024,1536]{1,0:T(8,128)}, f32[1,1,1024]{2,1,0:T(1,128)}) custom-call(s32[10]{0:T(128)} %get-tuple-element.125.count_ref, s32[10,1,1024]{2,1,0:T(1,128)} %reshape.76.place_ref, f32[10,1,1024]{2,1,0:T(1,128)} %reshape.80.gate_ref, ...), custom_call_target="tpu_custom_call" | custom-call | flops 8000000000 | bytes 14000000 | tf_op jit(solution)/shard_map/pallas_call | solution.py:420
  226.0 97.8 %shard_map.234 = (f32[9,3,1536,512]{3,2,1,0:T(8,128)}, f32[1024,1536]{1,0:T(8,128)}, f32[1024,1536]{1,0:T(8,128)}, f32[9,1,1024]{2,1,0:T(1,128)}) custom-call(s32[10]{0:T(128)} %get-tuple-element.125.count_ref, s32[10,1,1024]{2,1,0:T(1,128)} %reshape.76.place_ref, f32[10,1,1024]{2,1,0:T(1,128)} %reshape.80.gate_ref, ...), custom_call_target="tpu_custom_call" | custom-call | flops 71999995904 | bytes 126000000 | tf_op jit(solution)/shard_map/pallas_call | solution.py:420
  325.9 187.9 %shard_map.235 = (f32[1024,1536]{1,0:T(8,128)}, bf16[1024,1536]{1,0:T(8,128)(2,1)}, bf16[1024,128]{1,0:T(8,128)(2,1)}, f32[1,1536]{1,0:T(1,128)}) custom-call(f32[1024,1536]{1,0:T(8,128)} %get-tuple-element.76.part_ref, f32[40,1024]{1,0:T(8,128)} %copy-done.3, f32[1024,128]{1,0:T(8,128)} %get-tuple-element.69.gates_ref, ...), custom_call_target="tpu_custom_call" | custom-call | flops 62914560 | bytes 60000000 | tf_op jit(solution)/shard_map/pallas_call | solution.py:693
  513.8 181.0 %shard_map.236 = (bf16[1024,640]{1,0:T(8,128)(2,1)}, f32[1024,1536]{1,0:T(8,128)}, f32[8,1536]{1,0:T(8,128)}, bf16[1024,1536]{1,0:T(8,128)(2,1)}) custom-call(bf16[1024,1536]{1,0:T(8,128)(2,1)} %get-tuple-element.80.branch_ref, bf16[384,1536]{1,0:T(8,128)(2,1)} %out_w.1, bf16[3,1024,128]{2,1,0:T(8,128)(2,1)} %get-tuple-element.81.query_ref, ...), custom_call_target="tpu_custom_call" | custom-call | flops 12000000000 | bytes 30000000 | tf_op jit(solution)/shard_map/pallas_call | solution.py:1069
  694.8 2.5 shard_map.237
  697.3 169.8 %shard_map.238 = (f32[1024,1536]{1,0:T(8,128)}, f32[192,384]{1,0:T(8,128)}, f32[192,128]{1,0:T(8,128)}, f32[192,128]{1,0:T(8,128)}, f32[192,384]{1,0:T(8,128)}, ...) custom-call(f32[1024,1536]{1,0:T(8,128)} %get-tuple-element.88.local_ref, ...), custom_call_target="tpu_custom_call" | custom-call | flops 3623878656 | bytes 50000000 | tf_op jit(solution)/shard_map/pallas_call | solution.py:1266
  867.1 11.5 %shard_map.239 = (f32[1024,1536]{1,0:T(8,128)}, f32[192,384]{1,0:T(8,128)}, f32[192,128]{1,0:T(8,128)}, f32[192,128]{1,0:T(8,128)}, f32[192,384]{1,0:T(8,128)}, ...) custom-call(f32[1024,1536]{1,0:T(8,128)} %get-tuple-element.99.summed_ref, bf16[1024,1536]{1,0:T(8,128)(2,1)} %tokens_ref.7, ...), custom_call_target="tpu_custom_call" | custom-call | flops 15728640 | bytes 22020096 | tf_op jit(solution)/shard_map/pallas_call | solution.py:738
  878.7 11.7 %shard_map.240 = (f32[10,192,512]{2,1,0:T(8,128)}, f32[10,192,512]{2,1,0:T(8,128)}, f32[10,64,1536]{2,1,0:T(8,128)}) custom-call(f32[9,3,192,512]{3,2,1,0:T(8,128)} %reduce-scatter.5.cloned.1.call-done.shards_ref, f32[10,192,512]{2,1,0:T(8,128)} %get-tuple-element.118.refs_0_, ...), custom_call_target="tpu_custom_call", output_to_operand_aliasing={{0}: (1, {}), {1}: (2, {}), {2}: (3, {})} | custom-call | bytes 21233664 | tf_op jit(solution)/shard_map/pallas_call | solution.py:1314
  890.4 1.7 copy.67
  (41 shorter events, 7.3 us)
Async XLA Ops:
  7.2 9.6 %copy-start.6 = (s32[1,1024]{1,0:T(1,128)S(1)}, s32[1,1024]{1,0:T(1,128)}, u32[]{:S(2)}) copy-start(s32[1,1024]{1,0:T(1,128)} %param.16) | copy-start | bytes 12292
  7.2 178.5 %all-gather.3.cloned.1.call-start = ((), (), s32[]{:S(2)}) async-start(), calls=%async_computation.4 | async-start | bytes 9732096 | tf_op jit(solution)/shard_map/all_gather | solution.py:573
  9.3 314.6 %reduce-scatter.3.cloned.1.call-start = ((), (), s32[]{:S(2)}) async-start(), calls=%async_computation.2 | async-start | bytes 10616832 | tf_op jit(solution)/shard_map/reduce_scatter | solution.py:1383
  17.3 29.0 %copy-start.4 = (s32[1024]{0:T(1024)}, s32[1024]{0:T(1024)S(1)}, u32[]{:S(2)}) copy-start(s32[1024]{0:T(1024)S(1)} %convert_reduce_fusion) | copy-start | bytes 12292
  46.3 1.1 copy-start
  182.3 1.7 copy-start.1
  225.9 652.8 %reduce-scatter.5.cloned.1.call-start = ((), (), s32[]{:S(2)}) async-start(), calls=%async_computation.3 | async-start | bytes 95551488 | tf_op jit(solution)/shard_map/reduce_scatter | solution.py:1392
  323.9 0.8 copy-start.5
  323.9 0.8 copy-start.7
  325.2 0.7 copy-start.3
  878.7 11.7 %copy-start.2 = (bf16[1024,1536]{1,0:T(8,128)(2,1)S(1)}, bf16[1024,1536]{1,0:T(8,128)(2,1)}, u32[]{:S(2)}) copy-start(bf16[1024,1536]{1,0:T(8,128)(2,1)} %get-tuple-element.143) | copy-start | bytes 9437188
Sparse Core Ops, SparseCore 0:
  11.4 105.1 all-gather.2
  226.1 79.3 reduce-scatter.2
  324.0 502.3 reduce-scatter.4

commit v10 on v9

--- a/solution.py
+++ b/solution.py
@@ -342,9 +342,15 @@
     by_size(leave)
 
     def copies(target, number):
+        rows = width // 4
         return [
-            pltpu.make_async_copy(weights_ref.at[kind], target.at[number, kind], out_sems.at[kind])
+            pltpu.make_async_copy(
+                weights_ref.at[kind, pl.ds(piece * rows, rows), :],
+                target.at[number, kind, pl.ds(piece * rows, rows), :],
+                out_sems.at[kind, piece],
+            )
             for kind in range(3)
+            for piece in range(4)
         ]
 
     @pl.when(expert > 0)
@@ -443,7 +449,7 @@
                 pltpu.VMEM((CAP, hidden), bf16),
                 pltpu.VMEM((3, width, hidden), f32),
                 pltpu.SemaphoreType.DMA((2,)),
-                pltpu.SemaphoreType.DMA((3,)),
+                pltpu.SemaphoreType.DMA((3, 4)),
             ],
         ),
         compiler_params=pltpu.CompilerParams(
@@ -570,8 +576,7 @@
         in_specs=[full],
         out_specs=full,
     )(out_weight)
-    gathered = lax.all_gather(own, ("dp", "tensor") if ways > 1 else "tensor")
-    return gathered.reshape(ways, -1, rows // ways, width)
+    return ways, lax.all_gather(own, "tensor")
 
 
 def middle_kernel(
@@ -623,7 +628,7 @@
         out_specs=[rows(width), rows(width), rows(experts)],
         scratch_shapes=[pltpu.VMEM((attended.shape[1], width), jnp.bfloat16)],
         compiler_params=pltpu.CompilerParams(
-            dimension_semantics=("arbitrary",), vmem_limit_bytes=62 << 20
+            dimension_semantics=("arbitrary",), vmem_limit_bytes=48 << 20
         ),
         cost_estimate=pl.CostEstimate(
             flops=2 * length * width * width, bytes_accessed=25 * 10**6, transcendentals=0
@@ -884,7 +889,7 @@
             pltpu.VMEM((4, length, 128), bf16),
             pltpu.VMEM((tiles, length, 128), f32),
         ],
-        compiler_params=pltpu.CompilerParams(vmem_limit_bytes=62 << 20),
+        compiler_params=pltpu.CompilerParams(vmem_limit_bytes=48 << 20),
         cost_estimate=pl.CostEstimate(
             flops=8 * 10**9, bytes_accessed=12 * 10**6, transcendentals=5 * 10**6
         ),
@@ -1355,7 +1360,7 @@
     tables = rope_tables(opening, HEAD)
     query_w, key_w, value_w = (pad_columns(w) for w in (query_weight, key_weight, value_weight))
     out_w = jnp.transpose(pad_columns(jnp.transpose(out_weight)))
-    out_all = gather_out_weight(out_weight, parts)
+    ways, out_rows = gather_out_weight(out_weight, parts)
     normed_b, queries, keys, values, attended, logsum = attend_forward(
         tokens, attn_gain, query_w, key_w, value_w, tables, opening, heads_local, group_size
     )
@@ -1366,6 +1371,8 @@
     picked = jnp.sum((routes[None, :, :] == local_ids[:, None, None]).astype(jnp.int32), axis=2)
     places_in = slot_places(picked)
     counts = jnp.sum(picked, axis=1)
+    out_rows, attended = lax.optimization_barrier((out_rows, attended))
+    out_all = lax.all_gather(out_rows, "dp") if ways > 1 else out_rows[None]
     attended_all = line_gather(attended, ring, 1)
     attended_all = attended_all.reshape(length, ring, attended.shape[1])
     attended_all = attended_all[:, :, : heads_local * HEAD].reshape(length, -1)

time: 910 us -> 863 us (0.948)
  Pallas kernels: 860 us -> 818 us
    pallas_call x1, Pallas kernels: 135 us -> 104 us  [line_gather(): pl.pallas_call(functools.partial(line_gather_kernel, n), out_shape=jax.Sh...]
  transfers between devices with their start and end apart: 3 -> 4, of which waited for: 0 -> 1; matrix products, arithmetic and copies ran while one was open for 2% -> 1% of each run, Pallas kernels for 90% -> 90%
where the time goes in v10:
time: 863 us; the launch traced here: 854 us
  Pallas kernels  818 us (95%)
  local copies, waits for them, and re-layouts  14.6 us (2%)
  between operations  14.4 us (2%)
    pallas_call x1, Pallas kernels, turn_middle(): pl.pallas_call(functools.partial(turn_kernel, n), out_shape=[jax.ShapeDty...  185 us
    pallas_call x1, Pallas kernels, attend_backward(): pl.pallas_call(functools.partial(attend_backward_kernel, n, heads, group)...  182 us
    pallas_call x1, Pallas kernels, finish(): pl.pallas_call(functools.partial(finish_kernel, n, parts), out_shape=[jax...  169 us
    pallas_call x2, Pallas kernels, expert_stage(): pl.pallas_call(functools.partial(expert_kernel, parts, first, numbers, ch...  117 us
    pallas_call x1, Pallas kernels, line_gather(): pl.pallas_call(functools.partial(line_gather_kernel, n), out_shape=jax.Sh...  104 us
    pallas_call x1, Pallas kernels, attend_forward(): pl.pallas_call(functools.partial(attend_forward_kernel, heads, group), ou...  21.1 us
  transfers between devices with their start and end apart: 4, of which 1 were waited for; matrix products, arithmetic and copies ran while one was open for 1% of the time, Pallas kernels for 90%

profile of v10, /device:TPU:8, one launch (start us, length us, event | category | flops | bytes accessed | tf_op | source)
XLA Modules:
  0.0 854.1 jit_solution(2000402452664530306)
XLA Ops:
  7.3 2.1 shard_map.229
  10.2 1.3 convert_reduce_fusion
  11.8 1.9 multiply_sine_fusion
  13.7 1.3 pad_maximum_fusion.2
  15.1 21.1 %shard_map.230 = (bf16[1024,1536]{1,0:T(8,128)(2,1)}, bf16[3,1024,128]{2,1,0:T(8,128)(2,1)S(1)}, bf16[1024,128]{1,0:T(8,128)(2,1)S(1)}, bf16[1024,128]{1,0:T(8,1...) custom-call(bf16[1024,1536]{1,0:T(8,128)(2,1)} %tokens_ref.7, f32[1,1536]{1,0:T(1,128)S(1)} %reshape.74.gain_ref, ...), custom_call_target="tpu_custom_call" | custom-call | flops 8000000000 | bytes 12000000 | tf_op jit(solution)/shard_map/pallas_call | solution.py:875
  36.2 0.8 copy-done.5
  37.0 0.8 copy-done.6
  37.8 0.8 copy-done.7
  38.6 0.9 copy-done.13
  41.5 0.9 convert_reduce_fusion.2
  44.1 104.0 %shard_map.231.attended_ref = bf16[1024,1536]{1,0:T(8,128)(2,1)S(1)} custom-call(bf16[1024,384]{1,0:T(8,128)(2,1)S(1)} %get-tuple-element.71.x_ref.attended_ref), custom_call_target="tpu_custom_call" | custom-call | bytes 25165824 | tf_op jit(solution)/shard_map/pallas_call | solution.py:544
  148.1 1.7 copy-done.2
  149.8 13.3 %shard_map.232 = (f32[1024,1536]{1,0:T(8,128)}, bf16[1024,1536]{1,0:T(8,128)(2,1)S(1)}, f32[1024,128]{1,0:T(8,128)S(1)}) custom-call(bf16[1024,1536]{1,0:T(8,128)(2,1)} %copy-done.2, f32[8,4,48,1536]{3,2,1,0:T(8,128)} %bitcast.19, bf16[1024,1536]{1,0:T(8,128)(2,1)} %tokens_ref.7, f32[1,1536]{1,0:T(1,128)S(1)} %reshape.75.gain_ref, ...), custom_call_target="tpu_custom_call" | custom-call | flops 4831838208 | bytes 25000000 | tf_op jit(solution)/shard_map/pallas_call | solution.py:612
  163.1 1.6 copy-done
  165.6 22.4 %shard_map.233 = (f32[1,3,1536,512]{3,2,1,0:T(8,128)}, f32[1024,1536]{1,0:T(8,128)}, f32[1024,1536]{1,0:T(8,128)}, f32[1,1,1024]{2,1,0:T(1,128)}) custom-call(s32[10]{0:T(128)} %get-tuple-element.129.count_ref, s32[10,1,1024]{2,1,0:T(1,128)} %reshape.73.place_ref, f32[10,1,1024]{2,1,0:T(1,128)} %reshape.76.gate_ref, bf16[1024,1536]{1,0:T(8,128)(2,1)} %copy-done, ...), custom_call_target="tpu_custom_call" | custom-call | flops 8000000000 | bytes 14000000 | tf_op jit(solution)/shard_map/pallas_call | solution.py:426
  188.0 94.9 %shard_map.234 = (f32[9,3,1536,512]{3,2,1,0:T(8,128)}, f32[1024,1536]{1,0:T(8,128)}, f32[1024,1536]{1,0:T(8,128)}, f32[9,1,1024]{2,1,0:T(1,128)}) custom-call(s32[10]{0:T(128)} %get-tuple-element.129.count_ref, s32[10,1,1024]{2,1,0:T(1,128)} %reshape.73.place_ref, f32[10,1,1024]{2,1,0:T(1,128)} %reshape.76.gate_ref, bf16[1024,1536]{1,0:T(8,128)(2,1)} %copy-done, ...), custom_call_target="tpu_custom_call" | custom-call | flops 71999995904 | bytes 126000000 | tf_op jit(solution)/shard_map/pallas_call | solution.py:426
  283.0 0.7 copy-done.22
  285.0 184.7 %shard_map.235 = (f32[1024,1536]{1,0:T(8,128)}, bf16[1024,1536]{1,0:T(8,128)(2,1)}, bf16[1024,128]{1,0:T(8,128)(2,1)}, f32[1,1536]{1,0:T(1,128)}) custom-call(f32[1024,1536]{1,0:T(8,128)} %get-tuple-element.80.part_ref, f32[40,1024]{1,0:T(8,128)} %copy-done.18, f32[1024,128]{1,0:T(8,128)} %copy-done.3, f32[1024,1536]{1,0:T(8,128)} %get-tuple-element.83.middle_ref, ...), custom_call_target="tpu_custom_call" | custom-call | flops 62914560 | bytes 60000000 | tf_op jit(solution)/shard_map/pallas_call | solution.py:698
  469.7 181.8 %shard_map.236 = (bf16[1024,640]{1,0:T(8,128)(2,1)}, f32[1024,1536]{1,0:T(8,128)}, f32[8,1536]{1,0:T(8,128)}, bf16[1024,1536]{1,0:T(8,128)(2,1)}) custom-call(bf16[1024,1536]{1,0:T(8,128)(2,1)} %get-tuple-element.84.branch_ref, bf16[384,1536]{1,0:T(8,128)(2,1)} %out_w.1, bf16[3,1024,128]{2,1,0:T(8,128)(2,1)} %copy-done.13, bf16[1024,128]{1,0:T(8,128)(2,1)} %copy-done.14, ...), custom_call_target="tpu_custom_call" | custom-call | flops 12000000000 | bytes 30000000 | tf_op jit(solution)/shard_map/pallas_call | solution.py:1074
  651.5 2.3 shard_map.237
  653.9 168.6 %shard_map.238 = (f32[1024,1536]{1,0:T(8,128)}, f32[192,384]{1,0:T(8,128)}, f32[192,128]{1,0:T(8,128)}, f32[192,128]{1,0:T(8,128)}, f32[192,384]{1,0:T(8,128)}, ...) custom-call(f32[1024,1536]{1,0:T(8,128)} %get-tuple-element.92.local_ref, ...), custom_call_target="tpu_custom_call" | custom-call | flops 3623878656 | bytes 50000000 | tf_op jit(solution)/shard_map/pallas_call | solution.py:1271
  822.5 11.4 %shard_map.239 = (f32[1024,1536]{1,0:T(8,128)}, f32[192,384]{1,0:T(8,128)}, f32[192,128]{1,0:T(8,128)}, f32[192,128]{1,0:T(8,128)}, f32[192,384]{1,0:T(8,128)}, ...) custom-call(f32[1024,1536]{1,0:T(8,128)} %get-tuple-element.103.summed_ref, bf16[1024,1536]{1,0:T(8,128)(2,1)} %tokens_ref.7, ...), custom_call_target="tpu_custom_call" | custom-call | flops 15728640 | bytes 22020096 | tf_op jit(solution)/shard_map/pallas_call | solution.py:743
  834.0 11.7 %shard_map.240 = (f32[10,192,512]{2,1,0:T(8,128)}, f32[10,192,512]{2,1,0:T(8,128)}, f32[10,64,1536]{2,1,0:T(8,128)}) custom-call(f32[9,3,192,512]{3,2,1,0:T(8,128)} %reduce-scatter.5.cloned.1.call-done.shards_ref, f32[10,192,512]{2,1,0:T(8,128)} %get-tuple-element.122.refs_0_, ...), custom_call_target="tpu_custom_call", output_to_operand_aliasing={{0}: (1, {}), {1}: (2, {}), {2}: (3, {})} | custom-call | bytes 21233664 | tf_op jit(solution)/shard_map/pallas_call | solution.py:1319
  845.7 1.7 copy.74
  (77 shorter events, 7.0 us)
Async XLA Ops:
  7.2 7.8 copy-start.12
  7.2 7.8 copy-start.11
  7.2 7.8 copy-start.10
  7.2 34.1 %all-gather.5.cloned.1.call-start = ((), (), s32[]{:S(2)}) async-start(), calls=%async_computation.4 | async-start | bytes 1474560 | tf_op jit(solution)/shard_map/all_gather | solution.py:579
  9.4 140.4 %all-gather.7.cloned.1.call-start = ((), (), s32[]{:S(2)}) async-start(), calls=%async_computation.5 | async-start | bytes 10616832 | tf_op jit(solution)/shard_map/all_gather | solution.py:1375
  10.2 26.0 %copy-start.8 = (f32[1,1536]{1,0:T(1,128)}, f32[1,1536]{1,0:T(1,128)S(1)}, u32[]{:S(2)}) copy-start(f32[1,1536]{1,0:T(1,128)S(1)} %reshape.74.gain_ref) | copy-start | bytes 18436
  11.5 24.7 %copy-start.21 = (s32[1024]{0:T(1024)}, s32[1024]{0:T(1024)S(1)}, u32[]{:S(2)}) copy-start(s32[1024]{0:T(1024)S(1)} %convert_reduce_fusion) | copy-start | bytes 12292
  15.0 26.4 %copy-start.23 = (f32[1536]{0:T(1024)S(1)}, f32[1536]{0:T(1024)}, u32[]{:S(2)}) copy-start(f32[1536]{0:T(1024)} %param.23) | copy-start | bytes 18436
  15.0 26.4 %copy-start.19 = (s32[1024,8]{0,1:T(8,128)S(1)}, s32[1024,8]{0,1:T(8,128)}, u32[]{:S(2)}) copy-start(s32[1024,8]{0,1:T(8,128)} %param.17) | copy-start | bytes 98308
  15.1 28.6 %copy-start.20 = (bf16[1536,40]{0,1:T(8,128)(2,1)S(1)}, bf16[1536,40]{0,1:T(8,128)(2,1)}, u32[]{:S(2)}) copy-start(bf16[1536,40]{0,1:T(8,128)(2,1)} %param.24) | copy-start | bytes 368644
  36.2 0.8 copy-start.5
  37.0 0.8 copy-start.6
  37.8 0.8 copy-start.7
  38.6 0.9 copy-start.13
  40.9 107.2 %copy-start.1 = (bf16[1024,384]{1,0:T(8,128)(2,1)}, bf16[1024,384]{1,0:T(8,128)(2,1)S(1)}, u32[]{:S(2)}) copy-start(bf16[1024,384]{1,0:T(8,128)(2,1)S(1)} %get-tuple-element.71.x_ref.attended_ref) | copy-start | bytes 2359300
  40.9 107.2 %copy-start.16 = (f32[6,1,1024]{2,1,0:T(1,128)}, f32[6,1,1024]{2,1,0:T(1,128)S(1)}, u32[]{:S(2)}) copy-start(f32[6,1,1024]{2,1,0:T(1,128)S(1)} %get-tuple-element.88.logsum_ref) | copy-start | bytes 73732
  41.4 241.6 %reduce-scatter.3.cloned.1.call-start = ((), (), s32[]{:S(2)}) async-start(), calls=%async_computation.2 | async-start | bytes 10616832 | tf_op jit(solution)/shard_map/reduce_scatter | solution.py:1390
  41.4 108.3 %copy-start.9 = (f32[1,1536]{1,0:T(1,128)}, f32[1,1536]{1,0:T(1,128)S(1)}, u32[]{:S(2)}) copy-start(f32[1,1536]{1,0:T(1,128)S(1)} %reshape.75.gain_ref) | copy-start | bytes 18436
  44.0 119.1 %copy-start.4 = (bf16[1536,128]{1,0:T(8,128)(2,1)}, bf16[1536,128]{1,0:T(8,128)(2,1)S(1)}, u32[]{:S(2)}) copy-start(bf16[1536,128]{1,0:T(8,128)(2,1)S(1)} %pad.10.router_ref) | copy-start | bytes 1179652
  148.1 1.7 copy-start.2
  163.1 1.6 copy-start
  164.7 23.2 %copy-start.3 = (f32[1024,128]{1,0:T(8,128)}, f32[1024,128]{1,0:T(8,128)S(1)}, u32[]{:S(2)}) copy-start(f32[1024,128]{1,0:T(8,128)S(1)} %get-tuple-element.73.gates_ref) | copy-start | bytes 1572868
  188.0 646.0 %reduce-scatter.5.cloned.1.call-start = ((), (), s32[]{:S(2)}) async-start(), calls=%async_computation.3 | async-start | bytes 95551488 | tf_op jit(solution)/shard_map/reduce_scatter | solution.py:1399
  833.9 11.7 %copy-start.17 = (bf16[1024,1536]{1,0:T(8,128)(2,1)S(1)}, bf16[1024,1536]{1,0:T(8,128)(2,1)}, u32[]{:S(2)}) copy-start(bf16[1024,1536]{1,0:T(8,128)(2,1)} %get-tuple-element.148) | copy-start | bytes 9437188
  (5 other events, 3.6 us)
Sparse Core Ops, SparseCore 0:
  10.2 31.0 all-gather.4
  43.2 58.4 all-gather.6
  188.1 82.7 reduce-scatter.2
  283.1 505.9 reduce-scatter.4

commit v11 on v10

--- a/solution.py
+++ b/solution.py
@@ -256,8 +256,9 @@
         moe_in, back_in = refs[:2]
         refs = refs[2:]
     grads_out, refs = refs[: len(numbers)], refs[len(numbers) :]
-    moe_out, back_out, gates_out = refs[:3]
-    rows_ref, grads_ref, active_ref, gate_in_ref, up_in_ref, weights_ref, sems, out_sems = refs[3:]
+    moe_final, back_final, gates_out = refs[:3]
+    moe_out, back_out, rows_ref, grads_ref, active_ref, gate_in_ref, up_in_ref, weights_ref = refs[3:11]
+    sems, out_sems = refs[11:]
     expert = pl.program_id(0)
     filled = count_ref[first + expert]
     length, width = normed_ref.shape
@@ -273,14 +274,25 @@
             pl.when(fits)(functools.partial(run, rows))
             low = rows
 
+    def sum_copies(sources, targets):
+        rows = length // 4
+        return [
+            pltpu.make_async_copy(
+                source.at[pl.ds(piece * rows, rows), :],
+                target.at[pl.ds(piece * rows, rows), :],
+                sems.at[i, piece],
+            )
+            for i, (source, target) in enumerate(zip(sources, targets))
+            for piece in range(4)
+        ]
+
     if chained:
-        copy_moe = pltpu.make_async_copy(moe_in, moe_out, sems.at[0])
-        copy_back = pltpu.make_async_copy(back_in, back_out, sems.at[1])
+        entering = sum_copies((moe_in, back_in), (moe_out, back_out))
 
         @pl.when(expert == 0)
         def _():
-            copy_moe.start()
-            copy_back.start()
+            for copy in entering:
+                copy.start()
 
     else:
 
@@ -322,8 +334,8 @@
 
         @pl.when(expert == 0)
         def _():
-            copy_moe.wait()
-            copy_back.wait()
+            for copy in entering:
+                copy.wait()
 
     def leave(rows):
         column = jnp.transpose(jnp.broadcast_to(place_ref[0], (128, length)))
@@ -340,9 +352,16 @@
         )
 
     by_size(leave)
+    leaving = sum_copies((moe_out, back_out), (moe_final, back_final))
+    last = expert == pl.num_programs(0) - 1
+
+    @pl.when(last)
+    def _():
+        for copy in leaving:
+            copy.start()
 
     def copies(target, number):
-        rows = width // 4
+        rows = width // 8
         return [
             pltpu.make_async_copy(
                 weights_ref.at[kind, pl.ds(piece * rows, rows), :],
@@ -350,7 +369,7 @@
                 out_sems.at[kind, piece],
             )
             for kind in range(3)
-            for piece in range(4)
+            for piece in range(8)
         ]
 
     @pl.when(expert > 0)
@@ -385,9 +404,9 @@
 
         start += number
 
-    @pl.when(expert == pl.num_programs(0) - 1)
+    @pl.when(last)
     def _():
-        for copy in copies(grads_out[0], 0):
+        for copy in copies(grads_out[0], 0) + leaving:
             copy.wait()
 
 
@@ -437,19 +456,21 @@
             in_specs=in_specs,
             out_specs=[pl.BlockSpec(memory_space=pl.ANY)] * len(numbers)
             + [
-                pl.BlockSpec((length, width), whole, pipeline_mode=once),
-                pl.BlockSpec((length, width), whole, pipeline_mode=once),
+                pl.BlockSpec(memory_space=pl.ANY),
+                pl.BlockSpec(memory_space=pl.ANY),
                 pl.BlockSpec((1, 1, length), lambda e, c: (e, 0, 0)),
             ],
             scratch_shapes=[
+                pltpu.VMEM((length, width), f32),
+                pltpu.VMEM((length, width), f32),
                 pltpu.VMEM((CAP, width), bf16),
                 pltpu.VMEM((CAP, width), bf16),
                 pltpu.VMEM((CAP, hidden), bf16),
                 pltpu.VMEM((CAP, hidden), bf16),
                 pltpu.VMEM((CAP, hidden), bf16),
                 pltpu.VMEM((3, width, hidden), f32),
-                pltpu.SemaphoreType.DMA((2,)),
-                pltpu.SemaphoreType.DMA((3, 4)),
+                pltpu.SemaphoreType.DMA((2, 4)),
+                pltpu.SemaphoreType.DMA((3, 8)),
             ],
         ),
         compiler_params=pltpu.CompilerParams(
@@ -737,14 +758,14 @@
 
 def leave_first(summed, tokens, grad_middle, gain, smalls):
     length, width = tokens.shape
-    rows = pl.BlockSpec((BLOCK // 2, width), lambda i: (i, 0))
+    rows = pl.BlockSpec((BLOCK, width), lambda i: (i, 0))
     whole = lambda shape: pl.BlockSpec(shape, lambda i: (0, 0))
     f32 = jnp.float32
     return pl.pallas_call(
         functools.partial(last_kernel, len(smalls)),
         out_shape=[jax.ShapeDtypeStruct((length, width), f32)]
         + [jax.ShapeDtypeStruct(small.shape, f32) for small in smalls],
-        grid=(2 * length // BLOCK,),
+        grid=(length // BLOCK,),
         in_specs=[rows, rows, rows, whole((1, width))] + [whole(small.shape) for small in smalls],
         out_specs=[rows] + [whole(small.shape) for small in smalls],
         compiler_params=pltpu.CompilerParams(vmem_limit_bytes=60 << 20),
@@ -1294,14 +1315,14 @@
     )
 
 
-def place_kernel(shards_ref, *refs):
+def place_kernel(gate_ref, up_ref, down_ref, *refs):
     gate_out, up_out, down_out = refs[-3:]
-    gate_out[0] = shards_ref[0, 0]
-    up_out[0] = shards_ref[0, 1]
-    rows, hidden = down_out.shape[1], shards_ref.shape[3]
+    gate_out[0] = gate_ref[0, 0]
+    up_out[0] = up_ref[0, 0]
+    rows, hidden = down_out.shape[1], down_ref.shape[3]
     for piece in range(down_out.shape[2] // hidden):
-        down_out[0, :, piece * hidden : (piece + 1) * hidden] = shards_ref[
-            0, 2, piece * rows : (piece + 1) * rows, :
+        down_out[0, :, piece * hidden : (piece + 1) * hidden] = down_ref[
+            0, 0, piece * rows : (piece + 1) * rows, :
         ]
 
 
@@ -1311,16 +1332,17 @@
     width = rows * parts
     shapes = [(experts, rows, hidden), (experts, rows, hidden), (experts, down_rows, width)]
     spec = lambda shape: pl.BlockSpec((1,) + shape[1:], lambda e: (first + e, 0, 0))
-    args, extra, aliases = [shards], [], {}
+    one = lambda kind: pl.BlockSpec((1, 1, rows, hidden), lambda e: (e, kind, 0, 0))
+    args, extra, aliases = [shards] * 3, [], {}
     if before is not None:
         args += list(before)
         extra = [pl.BlockSpec(memory_space=pl.ANY)] * 3
-        aliases = {1: 0, 2: 1, 3: 2}
+        aliases = {3: 0, 4: 1, 5: 2}
     return pl.pallas_call(
         place_kernel,
         out_shape=[jax.ShapeDtypeStruct(shape, jnp.float32) for shape in shapes],
         grid=(number,),
-        in_specs=[pl.BlockSpec((1, 3, rows, hidden), lambda e: (e, 0, 0, 0))] + extra,
+        in_specs=[one(kind) for kind in range(3)] + extra,
         out_specs=[spec(shape) for shape in shapes],
         input_output_aliases=aliases,
         compiler_params=pltpu.CompilerParams(vmem_limit_bytes=60 << 20),

time: 863 us -> 860 us (level)
  no operation moved by 1% of the time
where the time goes in v11:
time: 860 us; the launch traced here: 851 us
  Pallas kernels  815 us (95%)
  local copies, waits for them, and re-layouts  14.6 us (2%)
  between operations  14.4 us (2%)
    pallas_call x1, Pallas kernels, attend_backward(): pl.pallas_call(functools.partial(attend_backward_kernel, n, heads, group)...  181 us
    pallas_call x1, Pallas kernels, turn_middle(): pl.pallas_call(functools.partial(turn_kernel, n), out_shape=[jax.ShapeDty...  179 us
    pallas_call x1, Pallas kernels, finish(): pl.pallas_call(functools.partial(finish_kernel, n, parts), out_shape=[jax...  175 us
    pallas_call x2, Pallas kernels, expert_stage(): pl.pallas_call(functools.partial(expert_kernel, parts, first, numbers, ch...  115 us
    pallas_call x1, Pallas kernels, line_gather(): pl.pallas_call(functools.partial(line_gather_kernel, n), out_shape=jax.Sh...  104 us
    pallas_call x1, Pallas kernels, attend_forward(): pl.pallas_call(functools.partial(attend_forward_kernel, heads, group), ou...  21.1 us
  transfers between devices with their start and end apart: 4, of which 1 were waited for; matrix products, arithmetic and copies ran while one was open for 1% of the time, Pallas kernels for 90%

profile of v11, /device:TPU:8, one launch (start us, length us, event | category | flops | bytes accessed | tf_op | source)
XLA Modules:
  0.0 850.8 jit_solution(17265927184266202437)
XLA Ops:
  7.3 2.1 shard_map.229
  10.2 1.3 convert_reduce_fusion
  11.8 1.9 multiply_sine_fusion
  13.7 1.3 pad_maximum_fusion.2
  15.1 21.1 %shard_map.230 = (bf16[1024,1536]{1,0:T(8,128)(2,1)}, bf16[3,1024,128]{2,1,0:T(8,128)(2,1)S(1)}, bf16[1024,128]{1,0:T(8,128)(2,1)S(1)}, bf16[1024,128]{1,0:T(8,1...) custom-call(bf16[1024,1536]{1,0:T(8,128)(2,1)} %tokens_ref.7, f32[1,1536]{1,0:T(1,128)S(1)} %reshape.74.gain_ref, ...), custom_call_target="tpu_custom_call" | custom-call | flops 8000000000 | bytes 12000000 | tf_op jit(solution)/shard_map/pallas_call | solution.py:896
  36.2 0.8 copy-done.5
  37.0 0.8 copy-done.6
  37.8 0.8 copy-done.7
  38.6 0.9 copy-done.13
  41.5 0.9 convert_reduce_fusion.2
  44.1 104.0 %shard_map.231.attended_ref = bf16[1024,1536]{1,0:T(8,128)(2,1)S(1)} custom-call(bf16[1024,384]{1,0:T(8,128)(2,1)S(1)} %get-tuple-element.71.x_ref.attended_ref), custom_call_target="tpu_custom_call" | custom-call | bytes 25165824 | tf_op jit(solution)/shard_map/pallas_call | solution.py:565
  148.1 1.7 copy-done.2
  149.8 13.3 %shard_map.232 = (f32[1024,1536]{1,0:T(8,128)}, bf16[1024,1536]{1,0:T(8,128)(2,1)S(1)}, f32[1024,128]{1,0:T(8,128)S(1)}) custom-call(bf16[1024,1536]{1,0:T(8,128)(2,1)} %copy-done.2, f32[8,4,48,1536]{3,2,1,0:T(8,128)} %bitcast.19, bf16[1024,1536]{1,0:T(8,128)(2,1)} %tokens_ref.7, f32[1,1536]{1,0:T(1,128)S(1)} %reshape.75.gain_ref, ...), custom_call_target="tpu_custom_call" | custom-call | flops 4831838208 | bytes 25000000 | tf_op jit(solution)/shard_map/pallas_call | solution.py:633
  163.1 1.6 copy-done
  165.6 21.0 %shard_map.233 = (f32[1,3,1536,512]{3,2,1,0:T(8,128)}, f32[1024,1536]{1,0:T(8,128)}, f32[1024,1536]{1,0:T(8,128)}, f32[1,1,1024]{2,1,0:T(1,128)}) custom-call(s32[10]{0:T(128)} %get-tuple-element.129.count_ref, s32[10,1,1024]{2,1,0:T(1,128)} %reshape.73.place_ref, f32[10,1,1024]{2,1,0:T(1,128)} %reshape.76.gate_ref, bf16[1024,1536]{1,0:T(8,128)(2,1)} %copy-done, ...), custom_call_target="tpu_custom_call" | custom-call | flops 8000000000 | bytes 14000000 | tf_op jit(solution)/shard_map/pallas_call | solution.py:445
  186.6 94.4 %shard_map.234 = (f32[9,3,1536,512]{3,2,1,0:T(8,128)}, f32[1024,1536]{1,0:T(8,128)}, f32[1024,1536]{1,0:T(8,128)}, f32[9,1,1024]{2,1,0:T(1,128)}) custom-call(s32[10]{0:T(128)} %get-tuple-element.129.count_ref, s32[10,1,1024]{2,1,0:T(1,128)} %reshape.73.place_ref, f32[10,1,1024]{2,1,0:T(1,128)} %reshape.76.gate_ref, bf16[1024,1536]{1,0:T(8,128)(2,1)} %copy-done, ...), custom_call_target="tpu_custom_call" | custom-call | flops 71999995904 | bytes 126000000 | tf_op jit(solution)/shard_map/pallas_call | solution.py:445
  281.1 0.7 copy-done.22
  283.1 178.5 %shard_map.235 = (f32[1024,1536]{1,0:T(8,128)}, bf16[1024,1536]{1,0:T(8,128)(2,1)}, bf16[1024,128]{1,0:T(8,128)(2,1)}, f32[1,1536]{1,0:T(1,128)}) custom-call(f32[1024,1536]{1,0:T(8,128)} %get-tuple-element.80.part_ref, f32[40,1024]{1,0:T(8,128)} %copy-done.18, f32[1024,128]{1,0:T(8,128)} %copy-done.3, f32[1024,1536]{1,0:T(8,128)} %get-tuple-element.83.middle_ref, ...), custom_call_target="tpu_custom_call" | custom-call | flops 62914560 | bytes 60000000 | tf_op jit(solution)/shard_map/pallas_call | solution.py:719
  461.7 181.5 %shard_map.236 = (bf16[1024,640]{1,0:T(8,128)(2,1)}, f32[1024,1536]{1,0:T(8,128)}, f32[8,1536]{1,0:T(8,128)}, bf16[1024,1536]{1,0:T(8,128)(2,1)}) custom-call(bf16[1024,1536]{1,0:T(8,128)(2,1)} %get-tuple-element.84.branch_ref, bf16[384,1536]{1,0:T(8,128)(2,1)} %out_w.1, bf16[3,1024,128]{2,1,0:T(8,128)(2,1)} %copy-done.13, bf16[1024,128]{1,0:T(8,128)(2,1)} %copy-done.14, ...), custom_call_target="tpu_custom_call" | custom-call | flops 12000000000 | bytes 30000000 | tf_op jit(solution)/shard_map/pallas_call | solution.py:1095
  643.2 2.3 shard_map.237
  645.4 175.4 %shard_map.238 = (f32[1024,1536]{1,0:T(8,128)}, f32[192,384]{1,0:T(8,128)}, f32[192,128]{1,0:T(8,128)}, f32[192,128]{1,0:T(8,128)}, f32[192,384]{1,0:T(8,128)}, ...) custom-call(f32[1024,1536]{1,0:T(8,128)} %get-tuple-element.92.local_ref, ...), custom_call_target="tpu_custom_call" | custom-call | flops 3623878656 | bytes 50000000 | tf_op jit(solution)/shard_map/pallas_call | solution.py:1292
  820.8 9.9 %shard_map.239 = (f32[1024,1536]{1,0:T(8,128)}, f32[192,384]{1,0:T(8,128)}, f32[192,128]{1,0:T(8,128)}, f32[192,128]{1,0:T(8,128)}, f32[192,384]{1,0:T(8,128)}, ...) custom-call(f32[1024,1536]{1,0:T(8,128)} %get-tuple-element.103.summed_ref, bf16[1024,1536]{1,0:T(8,128)(2,1)} %tokens_ref.7, ...), custom_call_target="tpu_custom_call" | custom-call | flops 15728640 | bytes 22020096 | tf_op jit(solution)/shard_map/pallas_call | solution.py:764
  830.8 11.6 %shard_map.240 = (f32[10,192,512]{2,1,0:T(8,128)}, f32[10,192,512]{2,1,0:T(8,128)}, f32[10,64,1536]{2,1,0:T(8,128)}) custom-call(f32[9,3,192,512]{3,2,1,0:T(8,128)} %reduce-scatter.5.cloned.1.call-done.gate_ref.up_ref.down_ref, ...), custom_call_target="tpu_custom_call", output_to_operand_aliasing={{0}: (3, {}), {1}: (4, {}), {2}: (5, {})} | custom-call | bytes 21233664 | tf_op jit(solution)/shard_map/pallas_call | solution.py:1341
  842.4 1.7 copy.74
  (77 shorter events, 7.0 us)
Async XLA Ops:
  7.2 7.8 copy-start.12
  7.2 7.8 copy-start.11
  7.2 7.8 copy-start.10
  7.2 34.1 %all-gather.5.cloned.1.call-start = ((), (), s32[]{:S(2)}) async-start(), calls=%async_computation.4 | async-start | bytes 1474560 | tf_op jit(solution)/shard_map/all_gather | solution.py:600
  9.4 140.4 %all-gather.7.cloned.1.call-start = ((), (), s32[]{:S(2)}) async-start(), calls=%async_computation.5 | async-start | bytes 10616832 | tf_op jit(solution)/shard_map/all_gather | solution.py:1397
  10.2 26.0 %copy-start.8 = (f32[1,1536]{1,0:T(1,128)}, f32[1,1536]{1,0:T(1,128)S(1)}, u32[]{:S(2)}) copy-start(f32[1,1536]{1,0:T(1,128)S(1)} %reshape.74.gain_ref) | copy-start | bytes 18436
  11.5 24.7 %copy-start.21 = (s32[1024]{0:T(1024)}, s32[1024]{0:T(1024)S(1)}, u32[]{:S(2)}) copy-start(s32[1024]{0:T(1024)S(1)} %convert_reduce_fusion) | copy-start | bytes 12292
  15.0 26.4 %copy-start.23 = (f32[1536]{0:T(1024)S(1)}, f32[1536]{0:T(1024)}, u32[]{:S(2)}) copy-start(f32[1536]{0:T(1024)} %param.23) | copy-start | bytes 18436
  15.0 26.4 %copy-start.19 = (s32[1024,8]{0,1:T(8,128)S(1)}, s32[1024,8]{0,1:T(8,128)}, u32[]{:S(2)}) copy-start(s32[1024,8]{0,1:T(8,128)} %param.17) | copy-start | bytes 98308
  15.1 28.6 %copy-start.20 = (bf16[1536,40]{0,1:T(8,128)(2,1)S(1)}, bf16[1536,40]{0,1:T(8,128)(2,1)}, u32[]{:S(2)}) copy-start(bf16[1536,40]{0,1:T(8,128)(2,1)} %param.24) | copy-start | bytes 368644
  36.2 0.8 copy-start.5
  37.0 0.8 copy-start.6
  37.8 0.8 copy-start.7
  38.6 0.9 copy-start.13
  40.9 107.2 %copy-start.1 = (bf16[1024,384]{1,0:T(8,128)(2,1)}, bf16[1024,384]{1,0:T(8,128)(2,1)S(1)}, u32[]{:S(2)}) copy-start(bf16[1024,384]{1,0:T(8,128)(2,1)S(1)} %get-tuple-element.71.x_ref.attended_ref) | copy-start | bytes 2359300
  40.9 107.2 %copy-start.16 = (f32[6,1,1024]{2,1,0:T(1,128)}, f32[6,1,1024]{2,1,0:T(1,128)S(1)}, u32[]{:S(2)}) copy-start(f32[6,1,1024]{2,1,0:T(1,128)S(1)} %get-tuple-element.88.logsum_ref) | copy-start | bytes 73732
  41.4 239.7 %reduce-scatter.3.cloned.1.call-start = ((), (), s32[]{:S(2)}) async-start(), calls=%async_computation.2 | async-start | bytes 10616832 | tf_op jit(solution)/shard_map/reduce_scatter | solution.py:1412
  41.4 108.3 %copy-start.9 = (f32[1,1536]{1,0:T(1,128)}, f32[1,1536]{1,0:T(1,128)S(1)}, u32[]{:S(2)}) copy-start(f32[1,1536]{1,0:T(1,128)S(1)} %reshape.75.gain_ref) | copy-start | bytes 18436
  44.0 119.1 %copy-start.4 = (bf16[1536,128]{1,0:T(8,128)(2,1)}, bf16[1536,128]{1,0:T(8,128)(2,1)S(1)}, u32[]{:S(2)}) copy-start(bf16[1536,128]{1,0:T(8,128)(2,1)S(1)} %pad.10.router_ref) | copy-start | bytes 1179652
  148.1 1.7 copy-start.2
  163.1 1.6 copy-start
  164.7 21.9 %copy-start.3 = (f32[1024,128]{1,0:T(8,128)}, f32[1024,128]{1,0:T(8,128)S(1)}, u32[]{:S(2)}) copy-start(f32[1024,128]{1,0:T(8,128)S(1)} %get-tuple-element.73.gates_ref) | copy-start | bytes 1572868
  186.6 644.2 %reduce-scatter.5.cloned.1.call-start = ((), (), s32[]{:S(2)}) async-start(), calls=%async_computation.3 | async-start | bytes 95551488 | tf_op jit(solution)/shard_map/reduce_scatter | solution.py:1421
  830.8 11.6 %copy-start.17 = (bf16[1024,1536]{1,0:T(8,128)(2,1)S(1)}, bf16[1024,1536]{1,0:T(8,128)(2,1)}, u32[]{:S(2)}) copy-start(bf16[1024,1536]{1,0:T(8,128)(2,1)} %get-tuple-element.148) | copy-start | bytes 9437188
  (5 other events, 3.6 us)
Sparse Core Ops, SparseCore 0:
  10.2 31.0 all-gather.4
  43.2 58.4 all-gather.6
  186.7 82.4 reduce-scatter.2
  281.2 503.3 reduce-scatter.4

commit v12 on v11

--- a/solution.py
+++ b/solution.py
@@ -361,7 +361,7 @@
             copy.start()
 
     def copies(target, number):
-        rows = width // 8
+        rows = width // 4
         return [
             pltpu.make_async_copy(
                 weights_ref.at[kind, pl.ds(piece * rows, rows), :],
@@ -369,7 +369,7 @@
                 out_sems.at[kind, piece],
             )
             for kind in range(3)
-            for piece in range(8)
+            for piece in range(4)
         ]
 
     @pl.when(expert > 0)
@@ -470,7 +470,7 @@
                 pltpu.VMEM((CAP, hidden), bf16),
                 pltpu.VMEM((3, width, hidden), f32),
                 pltpu.SemaphoreType.DMA((2, 4)),
-                pltpu.SemaphoreType.DMA((3, 8)),
+                pltpu.SemaphoreType.DMA((3, 4)),
             ],
         ),
         compiler_params=pltpu.CompilerParams(
@@ -861,28 +861,32 @@
     blocks = length // ROWS
     tiles_ref[...] = jnp.zeros_like(tiles_ref)
 
-    def unit(step, carry):
-        head, block = step // blocks, step % blocks
-        tile, half = head // 2, head % 2
-        pair = 2 * (head // group) + half
-        first, low = window(block)
-        rows = pl.ds(pl.multiple_of(first, ROWS), ROWS)
-        span = pl.ds(pl.multiple_of(low, ROWS), SPAN)
-        scores = right_inner(query_out[tile, rows, :], key_pairs[pair, span, :])
-        columns = low + lax.broadcasted_iota(jnp.int32, (ROWS, SPAN), 1)
-        own = first + lax.broadcasted_iota(jnp.int32, (ROWS, SPAN), 0)
-        allowed = (columns >= opening_ref[rows, :]) & (columns <= own)
-        raised = jnp.where(allowed, jnp.exp(ATTN_SCALE * scores), 0.0)
-        total = jnp.sum(raised, axis=1, keepdims=True)
-        product = jnp.dot(
-            raised.astype(jnp.bfloat16), value_pairs[pair, span, :], preferred_element_type=jnp.float32
-        )
-        tiles_ref[tile, rows, :] += product / total
-        wide = jnp.broadcast_to(jnp.log(total), (ROWS, 128))
-        logsum_out[head, :, rows] = jnp.transpose(wide)[:1]
-        return carry
-
-    lax.fori_loop(0, heads * blocks, unit, 0)
+    for block in range(blocks):
+        first = block * ROWS
+        low = max(first + ROWS - SPAN, 0)
+        rows, span = slice(first, first + ROWS), slice(low, first + ROWS)
+        shape = (ROWS, first + ROWS - low)
+        columns = low + lax.broadcasted_iota(jnp.int32, shape, 1)
+        own = first + lax.broadcasted_iota(jnp.int32, shape, 0)
+
+        def unit(head, carry):
+            tile, half = head // 2, head % 2
+            pair = 2 * (head // group) + half
+            scores = right_inner(query_out[tile, rows, :], key_pairs[pair, span, :])
+            allowed = (columns >= opening_ref[rows, :]) & (columns <= own)
+            raised = jnp.where(allowed, jnp.exp(ATTN_SCALE * scores), 0.0)
+            total = jnp.sum(raised, axis=1, keepdims=True)
+            product = jnp.dot(
+                raised.astype(jnp.bfloat16),
+                value_pairs[pair, span, :],
+                preferred_element_type=jnp.float32,
+            )
+            tiles_ref[tile, rows, :] += product / total
+            wide = jnp.broadcast_to(jnp.log(total), (ROWS, 128))
+            logsum_out[head, :, rows] = jnp.transpose(wide)[:1]
+            return carry
+
+        lax.fori_loop(0, heads, unit, 0)
     for tile in range(tiles):
         attended_out[:, tile * 128 : (tile + 1) * 128] = tiles_ref[tile].astype(jnp.bfloat16)
 

time: 860 us -> 864 us (level)
  no operation moved by 1% of the time
where the time goes in v12:
time: 864 us; the launch traced here: 855 us
  Pallas kernels  818 us (95%)
  local copies, waits for them, and re-layouts  14.6 us (2%)
  between operations  14.4 us (2%)
    pallas_call x1, Pallas kernels, turn_middle(): pl.pallas_call(functools.partial(turn_kernel, n), out_shape=[jax.ShapeDty...  182 us
    pallas_call x1, Pallas kernels, attend_backward(): pl.pallas_call(functools.partial(attend_backward_kernel, n, heads, group)...  177 us
    pallas_call x1, Pallas kernels, finish(): pl.pallas_call(functools.partial(finish_kernel, n, parts), out_shape=[jax...  176 us
    pallas_call x2, Pallas kernels, expert_stage(): pl.pallas_call(functools.partial(expert_kernel, parts, first, numbers, ch...  120 us
    pallas_call x1, Pallas kernels, line_gather(): pl.pallas_call(functools.partial(line_gather_kernel, n), out_shape=jax.Sh...  104 us
    pallas_call x1, Pallas kernels, attend_forward(): pl.pallas_call(functools.partial(attend_forward_kernel, heads, group), ou...  19.1 us
  transfers between devices with their start and end apart: 4, of which 1 were waited for; matrix products, arithmetic and copies ran while one was open for 1% of the time, Pallas kernels for 90%

profile of v12, /device:TPU:8, one launch (start us, length us, event | category | flops | bytes accessed | tf_op | source)
XLA Modules:
  0.0 855.4 jit_solution(9857896122783216567)
XLA Ops:
  7.3 2.1 shard_map.229
  10.2 1.3 convert_reduce_fusion
  11.8 1.9 multiply_sine_fusion
  13.7 1.3 pad_maximum_fusion.2
  15.1 19.1 %shard_map.230 = (bf16[1024,1536]{1,0:T(8,128)(2,1)}, bf16[3,1024,128]{2,1,0:T(8,128)(2,1)S(1)}, bf16[1024,128]{1,0:T(8,128)(2,1)S(1)}, bf16[1024,128]{1,0:T(8,1...) custom-call(bf16[1024,1536]{1,0:T(8,128)(2,1)} %tokens_ref.7, f32[1,1536]{1,0:T(1,128)S(1)} %reshape.74.gain_ref, ...), custom_call_target="tpu_custom_call" | custom-call | flops 8000000000 | bytes 12000000 | tf_op jit(solution)/shard_map/pallas_call | solution.py:900
  34.1 0.8 copy-done.5
  35.0 0.8 copy-done.6
  35.8 0.8 copy-done.7
  36.5 0.9 copy-done.13
  38.8 2.5 all-gather.5.cloned.1.call-done
  41.5 0.9 convert_reduce_fusion.2
  44.1 103.9 %shard_map.231.attended_ref = bf16[1024,1536]{1,0:T(8,128)(2,1)S(1)} custom-call(bf16[1024,384]{1,0:T(8,128)(2,1)S(1)} %get-tuple-element.71.x_ref.attended_ref), custom_call_target="tpu_custom_call" | custom-call | bytes 25165824 | tf_op jit(solution)/shard_map/pallas_call | solution.py:565
  148.1 1.7 copy-done.2
  149.8 13.3 %shard_map.232 = (f32[1024,1536]{1,0:T(8,128)}, bf16[1024,1536]{1,0:T(8,128)(2,1)S(1)}, f32[1024,128]{1,0:T(8,128)S(1)}) custom-call(bf16[1024,1536]{1,0:T(8,128)(2,1)} %copy-done.2, f32[8,4,48,1536]{3,2,1,0:T(8,128)} %bitcast.19, bf16[1024,1536]{1,0:T(8,128)(2,1)} %tokens_ref.7, f32[1,1536]{1,0:T(1,128)S(1)} %reshape.75.gain_ref, ...), custom_call_target="tpu_custom_call" | custom-call | flops 4831838208 | bytes 25000000 | tf_op jit(solution)/shard_map/pallas_call | solution.py:633
  163.0 1.6 copy-done
  165.5 20.6 %shard_map.233 = (f32[1,3,1536,512]{3,2,1,0:T(8,128)}, f32[1024,1536]{1,0:T(8,128)}, f32[1024,1536]{1,0:T(8,128)}, f32[1,1,1024]{2,1,0:T(1,128)}) custom-call(s32[10]{0:T(128)} %get-tuple-element.129.count_ref, s32[10,1,1024]{2,1,0:T(1,128)} %reshape.73.place_ref, f32[10,1,1024]{2,1,0:T(1,128)} %reshape.76.gate_ref, bf16[1024,1536]{1,0:T(8,128)(2,1)} %copy-done, ...), custom_call_target="tpu_custom_call" | custom-call | flops 8000000000 | bytes 14000000 | tf_op jit(solution)/shard_map/pallas_call | solution.py:445
  186.3 99.6 %shard_map.234 = (f32[9,3,1536,512]{3,2,1,0:T(8,128)}, f32[1024,1536]{1,0:T(8,128)}, f32[1024,1536]{1,0:T(8,128)}, f32[9,1,1024]{2,1,0:T(1,128)}) custom-call(s32[10]{0:T(128)} %get-tuple-element.129.count_ref, s32[10,1,1024]{2,1,0:T(1,128)} %reshape.73.place_ref, f32[10,1,1024]{2,1,0:T(1,128)} %reshape.76.gate_ref, bf16[1024,1536]{1,0:T(8,128)(2,1)} %copy-done, ...), custom_call_target="tpu_custom_call" | custom-call | flops 71999995904 | bytes 126000000 | tf_op jit(solution)/shard_map/pallas_call | solution.py:445
  288.0 182.3 %shard_map.235 = (f32[1024,1536]{1,0:T(8,128)}, bf16[1024,1536]{1,0:T(8,128)(2,1)}, bf16[1024,128]{1,0:T(8,128)(2,1)}, f32[1,1536]{1,0:T(1,128)}) custom-call(f32[1024,1536]{1,0:T(8,128)} %get-tuple-element.80.part_ref, f32[40,1024]{1,0:T(8,128)} %copy-done.18, f32[1024,128]{1,0:T(8,128)} %copy-done.3, f32[1024,1536]{1,0:T(8,128)} %get-tuple-element.83.middle_ref, ...), custom_call_target="tpu_custom_call" | custom-call | flops 62914560 | bytes 60000000 | tf_op jit(solution)/shard_map/pallas_call | solution.py:719
  470.3 177.1 %shard_map.236 = (bf16[1024,640]{1,0:T(8,128)(2,1)}, f32[1024,1536]{1,0:T(8,128)}, f32[8,1536]{1,0:T(8,128)}, bf16[1024,1536]{1,0:T(8,128)(2,1)}) custom-call(bf16[1024,1536]{1,0:T(8,128)(2,1)} %get-tuple-element.84.branch_ref, bf16[384,1536]{1,0:T(8,128)(2,1)} %out_w.1, bf16[3,1024,128]{2,1,0:T(8,128)(2,1)} %copy-done.13, bf16[1024,128]{1,0:T(8,128)(2,1)} %copy-done.14, ...), custom_call_target="tpu_custom_call" | custom-call | flops 12000000000 | bytes 30000000 | tf_op jit(solution)/shard_map/pallas_call | solution.py:1099
  647.4 2.3 shard_map.237
  649.7 175.7 %shard_map.238 = (f32[1024,1536]{1,0:T(8,128)}, f32[192,384]{1,0:T(8,128)}, f32[192,128]{1,0:T(8,128)}, f32[192,128]{1,0:T(8,128)}, f32[192,384]{1,0:T(8,128)}, ...) custom-call(f32[1024,1536]{1,0:T(8,128)} %get-tuple-element.92.local_ref, ...), custom_call_target="tpu_custom_call" | custom-call | flops 3623878656 | bytes 50000000 | tf_op jit(solution)/shard_map/pallas_call | solution.py:1296
  825.4 9.9 %shard_map.239 = (f32[1024,1536]{1,0:T(8,128)}, f32[192,384]{1,0:T(8,128)}, f32[192,128]{1,0:T(8,128)}, f32[192,128]{1,0:T(8,128)}, f32[192,384]{1,0:T(8,128)}, ...) custom-call(f32[1024,1536]{1,0:T(8,128)} %get-tuple-element.103.summed_ref, bf16[1024,1536]{1,0:T(8,128)(2,1)} %tokens_ref.7, ...), custom_call_target="tpu_custom_call" | custom-call | flops 15728640 | bytes 22020096 | tf_op jit(solution)/shard_map/pallas_call | solution.py:764
  835.4 11.6 %shard_map.240 = (f32[10,192,512]{2,1,0:T(8,128)}, f32[10,192,512]{2,1,0:T(8,128)}, f32[10,64,1536]{2,1,0:T(8,128)}) custom-call(f32[9,3,192,512]{3,2,1,0:T(8,128)} %reduce-scatter.5.cloned.1.call-done.gate_ref.up_ref.down_ref, ...), custom_call_target="tpu_custom_call", output_to_operand_aliasing={{0}: (3, {}), {1}: (4, {}), {2}: (5, {})} | custom-call | bytes 21233664 | tf_op jit(solution)/shard_map/pallas_call | solution.py:1345
  846.9 1.7 copy.74
  (77 shorter events, 7.3 us)
Async XLA Ops:
  7.2 7.8 copy-start.12
  7.2 7.8 copy-start.11
  7.2 7.8 copy-start.10
  7.2 34.1 %all-gather.5.cloned.1.call-start = ((), (), s32[]{:S(2)}) async-start(), calls=%async_computation.4 | async-start | bytes 1474560 | tf_op jit(solution)/shard_map/all_gather | solution.py:600
  9.4 140.3 %all-gather.7.cloned.1.call-start = ((), (), s32[]{:S(2)}) async-start(), calls=%async_computation.5 | async-start | bytes 10616832 | tf_op jit(solution)/shard_map/all_gather | solution.py:1401
  10.2 24.0 %copy-start.8 = (f32[1,1536]{1,0:T(1,128)}, f32[1,1536]{1,0:T(1,128)S(1)}, u32[]{:S(2)}) copy-start(f32[1,1536]{1,0:T(1,128)S(1)} %reshape.74.gain_ref) | copy-start | bytes 18436
  11.5 22.6 %copy-start.21 = (s32[1024]{0:T(1024)}, s32[1024]{0:T(1024)S(1)}, u32[]{:S(2)}) copy-start(s32[1024]{0:T(1024)S(1)} %convert_reduce_fusion) | copy-start | bytes 12292
  15.0 26.4 %copy-start.23 = (f32[1536]{0:T(1024)S(1)}, f32[1536]{0:T(1024)}, u32[]{:S(2)}) copy-start(f32[1536]{0:T(1024)} %param.23) | copy-start | bytes 18436
  15.0 26.4 %copy-start.19 = (s32[1024,8]{0,1:T(8,128)S(1)}, s32[1024,8]{0,1:T(8,128)}, u32[]{:S(2)}) copy-start(s32[1024,8]{0,1:T(8,128)} %param.17) | copy-start | bytes 98308
  15.1 28.6 %copy-start.20 = (bf16[1536,40]{0,1:T(8,128)(2,1)S(1)}, bf16[1536,40]{0,1:T(8,128)(2,1)}, u32[]{:S(2)}) copy-start(bf16[1536,40]{0,1:T(8,128)(2,1)} %param.24) | copy-start | bytes 368644
  34.1 0.8 copy-start.5
  35.0 0.8 copy-start.6
  35.8 0.8 copy-start.7
  36.5 0.9 copy-start.13
  38.8 109.2 %copy-start.1 = (bf16[1024,384]{1,0:T(8,128)(2,1)}, bf16[1024,384]{1,0:T(8,128)(2,1)S(1)}, u32[]{:S(2)}) copy-start(bf16[1024,384]{1,0:T(8,128)(2,1)S(1)} %get-tuple-element.71.x_ref.attended_ref) | copy-start | bytes 2359300
  38.8 109.2 %copy-start.16 = (f32[6,1,1024]{2,1,0:T(1,128)}, f32[6,1,1024]{2,1,0:T(1,128)S(1)}, u32[]{:S(2)}) copy-start(f32[6,1,1024]{2,1,0:T(1,128)S(1)} %get-tuple-element.88.logsum_ref) | copy-start | bytes 73732
  41.4 244.5 %reduce-scatter.3.cloned.1.call-start = ((), (), s32[]{:S(2)}) async-start(), calls=%async_computation.2 | async-start | bytes 10616832 | tf_op jit(solution)/shard_map/reduce_scatter | solution.py:1416
  41.4 108.3 %copy-start.9 = (f32[1,1536]{1,0:T(1,128)}, f32[1,1536]{1,0:T(1,128)S(1)}, u32[]{:S(2)}) copy-start(f32[1,1536]{1,0:T(1,128)S(1)} %reshape.75.gain_ref) | copy-start | bytes 18436
  44.0 119.1 %copy-start.4 = (bf16[1536,128]{1,0:T(8,128)(2,1)}, bf16[1536,128]{1,0:T(8,128)(2,1)S(1)}, u32[]{:S(2)}) copy-start(bf16[1536,128]{1,0:T(8,128)(2,1)S(1)} %pad.10.router_ref) | copy-start | bytes 1179652
  148.1 1.7 copy-start.2
  163.0 1.6 copy-start
  164.7 21.5 %copy-start.3 = (f32[1024,128]{1,0:T(8,128)}, f32[1024,128]{1,0:T(8,128)S(1)}, u32[]{:S(2)}) copy-start(f32[1024,128]{1,0:T(8,128)S(1)} %get-tuple-element.73.gates_ref) | copy-start | bytes 1572868
  186.2 649.1 %reduce-scatter.5.cloned.1.call-start = ((), (), s32[]{:S(2)}) async-start(), calls=%async_computation.3 | async-start | bytes 95551488 | tf_op jit(solution)/shard_map/reduce_scatter | solution.py:1425
  835.4 11.6 %copy-start.17 = (bf16[1024,1536]{1,0:T(8,128)(2,1)S(1)}, bf16[1024,1536]{1,0:T(8,128)(2,1)}, u32[]{:S(2)}) copy-start(bf16[1024,1536]{1,0:T(8,128)(2,1)} %get-tuple-element.148) | copy-start | bytes 9437188
  (5 other events, 3.6 us)
Sparse Core Ops, SparseCore 0:
  10.2 31.0 all-gather.4
  43.2 58.4 all-gather.6
  186.3 81.7 reduce-scatter.2
  286.1 504.0 reduce-scatter.4

commit v13 on v12

--- a/solution.py
+++ b/solution.py
@@ -1397,14 +1397,17 @@
     picked = jnp.sum((routes[None, :, :] == local_ids[:, None, None]).astype(jnp.int32), axis=2)
     places_in = slot_places(picked)
     counts = jnp.sum(picked, axis=1)
-    out_rows, attended = lax.optimization_barrier((out_rows, attended))
+    chosen = pad_columns(chosen.astype(jnp.float32))
+    out_rows, attended, chosen, places_in, counts = lax.optimization_barrier(
+        (out_rows, attended, chosen, places_in, counts)
+    )
     out_all = lax.all_gather(out_rows, "dp") if ways > 1 else out_rows[None]
     attended_all = line_gather(attended, ring, 1)
     attended_all = attended_all.reshape(length, ring, attended.shape[1])
     attended_all = attended_all[:, :, : heads_local * HEAD].reshape(length, -1)
     router_w = pad_columns(router_weight)
     middle, normed_two_b, gate_probs = enter_middle(
-        attended_all, out_all, tokens, ffn_gain, router_w, pad_columns(chosen.astype(jnp.float32))
+        attended_all, out_all, tokens, ffn_gain, router_w, chosen
     )
     gate_rows = jnp.transpose(lax.dynamic_slice_in_dim(gate_probs, first_expert, experts_local, 1))
     numbers = (max(1, experts_local // 10),)

time: 864 us -> 864 us (level)
  transfers between devices with their start and end apart: 4 -> 4, of which waited for: 1 -> 0; matrix products, arithmetic and copies ran while one was open for 1% -> 1% of each run, Pallas kernels for 90% -> 90%
where the time goes in v13:
time: 864 us; the launch traced here: 857 us
  Pallas kernels  820 us (95%)
  local copies, waits for them, and re-layouts  15.1 us (2%)
  between operations  14.4 us (2%)
    pallas_call x1, Pallas kernels, turn_middle(): pl.pallas_call(functools.partial(turn_kernel, n), out_shape=[jax.ShapeDty...  185 us
    pallas_call x1, Pallas kernels, attend_backward(): pl.pallas_call(functools.partial(attend_backward_kernel, n, heads, group)...  183 us
    pallas_call x1, Pallas kernels, finish(): pl.pallas_call(functools.partial(finish_kernel, n, parts), out_shape=[jax...  174 us
    pallas_call x2, Pallas kernels, expert_stage(): pl.pallas_call(functools.partial(expert_kernel, parts, first, numbers, ch...  116 us
    pallas_call x1, Pallas kernels, line_gather(): pl.pallas_call(functools.partial(line_gather_kernel, n), out_shape=jax.Sh...  104 us
    pallas_call x1, Pallas kernels, attend_forward(): pl.pallas_call(functools.partial(attend_forward_kernel, heads, group), ou...  19.2 us
  transfers between devices with their start and end apart: 4, of which 0 were waited for; matrix products, arithmetic and copies ran while one was open for 1% of the time, Pallas kernels for 90%

profile of v13, /device:TPU:8, one launch (start us, length us, event | category | flops | bytes accessed | tf_op | source)
XLA Modules:
  0.0 857.5 jit_solution(17249378389103737595)
XLA Ops:
  7.2 2.0 shard_map.229
  9.3 1.3 convert_reduce_fusion
  10.7 0.9 convert_reduce_fusion.1
  11.6 1.6 convert_reduce_fusion.2
  14.5 1.9 multiply_sine_fusion
  16.5 1.3 pad_maximum_fusion.2
  18.8 19.2 %shard_map.230 = (bf16[1024,1536]{1,0:T(8,128)(2,1)}, bf16[3,1024,128]{2,1,0:T(8,128)(2,1)S(1)}, bf16[1024,128]{1,0:T(8,128)(2,1)S(1)}, bf16[1024,128]{1,0:T(8,1...) custom-call(bf16[1024,1536]{1,0:T(8,128)(2,1)} %tokens_ref.7, f32[1,1536]{1,0:T(1,128)S(1)} %reshape.73.gain_ref, ...), custom_call_target="tpu_custom_call" | custom-call | flops 8000000000 | bytes 12000000 | tf_op jit(solution)/shard_map/pallas_call | solution.py:900
  38.0 0.8 copy-done.7
  38.8 0.9 copy-done.13
  42.8 104.4 %shard_map.231.attended_ref = bf16[1024,1536]{1,0:T(8,128)(2,1)S(1)} custom-call(bf16[1024,384]{1,0:T(8,128)(2,1)S(1)} %get-tuple-element.76.x_ref.attended_ref), custom_call_target="tpu_custom_call" | custom-call | bytes 25165824 | tf_op jit(solution)/shard_map/pallas_call | solution.py:565
  147.2 1.7 copy-done.2
  148.9 13.3 %shard_map.232 = (f32[1024,1536]{1,0:T(8,128)}, bf16[1024,1536]{1,0:T(8,128)(2,1)S(1)}, f32[1024,128]{1,0:T(8,128)S(1)}) custom-call(bf16[1024,1536]{1,0:T(8,128)(2,1)} %copy-done.2, f32[8,4,48,1536]{3,2,1,0:T(8,128)} %bitcast.19, bf16[1024,1536]{1,0:T(8,128)(2,1)} %tokens_ref.7, f32[1,1536]{1,0:T(1,128)S(1)} %reshape.75.gain_ref, ...), custom_call_target="tpu_custom_call" | custom-call | flops 4831838208 | bytes 25000000 | tf_op jit(solution)/shard_map/pallas_call | solution.py:633
  162.2 1.6 copy-done
  163.8 0.8 copy-done.3
  165.5 20.6 %shard_map.233 = (f32[1,3,1536,512]{3,2,1,0:T(8,128)}, f32[1024,1536]{1,0:T(8,128)}, f32[1024,1536]{1,0:T(8,128)}, f32[1,1,1024]{2,1,0:T(1,128)}) custom-call(s32[10]{0:T(128)} %get-tuple-element.74.count_ref, s32[10,1,1024]{2,1,0:T(1,128)} %reshape.74.place_ref, f32[10,1,1024]{2,1,0:T(1,128)} %reshape.76.gate_ref, bf16[1024,1536]{1,0:T(8,128)(2,1)} %copy-done, ...), custom_call_target="tpu_custom_call" | custom-call | flops 8000000000 | bytes 14000000 | tf_op jit(solution)/shard_map/pallas_call | solution.py:445
  186.2 95.0 %shard_map.234 = (f32[9,3,1536,512]{3,2,1,0:T(8,128)}, f32[1024,1536]{1,0:T(8,128)}, f32[1024,1536]{1,0:T(8,128)}, f32[9,1,1024]{2,1,0:T(1,128)}) custom-call(s32[10]{0:T(128)} %get-tuple-element.74.count_ref, s32[10,1,1024]{2,1,0:T(1,128)} %reshape.74.place_ref, f32[10,1,1024]{2,1,0:T(1,128)} %reshape.76.gate_ref, bf16[1024,1536]{1,0:T(8,128)(2,1)} %copy-done, ...), custom_call_target="tpu_custom_call" | custom-call | flops 71999995904 | bytes 126000000 | tf_op jit(solution)/shard_map/pallas_call | solution.py:445
  281.2 0.7 copy-done.21
  283.3 184.5 %shard_map.235 = (f32[1024,1536]{1,0:T(8,128)}, bf16[1024,1536]{1,0:T(8,128)(2,1)}, bf16[1024,128]{1,0:T(8,128)(2,1)}, f32[1,1536]{1,0:T(1,128)}) custom-call(f32[1024,1536]{1,0:T(8,128)} %get-tuple-element.86.part_ref, f32[40,1024]{1,0:T(8,128)} %copy-done.18, f32[1024,128]{1,0:T(8,128)} %copy-done.3, f32[1024,1536]{1,0:T(8,128)} %get-tuple-element.89.middle_ref, ...), custom_call_target="tpu_custom_call" | custom-call | flops 62914560 | bytes 60000000 | tf_op jit(solution)/shard_map/pallas_call | solution.py:719
  467.8 183.1 %shard_map.236 = (bf16[1024,640]{1,0:T(8,128)(2,1)}, f32[1024,1536]{1,0:T(8,128)}, f32[8,1536]{1,0:T(8,128)}, bf16[1024,1536]{1,0:T(8,128)(2,1)}) custom-call(bf16[1024,1536]{1,0:T(8,128)(2,1)} %get-tuple-element.90.branch_ref, bf16[384,1536]{1,0:T(8,128)(2,1)} %out_w.1, bf16[3,1024,128]{2,1,0:T(8,128)(2,1)} %copy-done.13, bf16[1024,128]{1,0:T(8,128)(2,1)} %copy-done.14, ...), custom_call_target="tpu_custom_call" | custom-call | flops 12000000000 | bytes 30000000 | tf_op jit(solution)/shard_map/pallas_call | solution.py:1099
  650.9 2.3 shard_map.237
  653.1 174.3 %shard_map.238 = (f32[1024,1536]{1,0:T(8,128)}, f32[192,384]{1,0:T(8,128)}, f32[192,128]{1,0:T(8,128)}, f32[192,128]{1,0:T(8,128)}, f32[192,384]{1,0:T(8,128)}, ...) custom-call(f32[1024,1536]{1,0:T(8,128)} %get-tuple-element.98.local_ref, ...), custom_call_target="tpu_custom_call" | custom-call | flops 3623878656 | bytes 50000000 | tf_op jit(solution)/shard_map/pallas_call | solution.py:1296
  827.5 9.9 %shard_map.239 = (f32[1024,1536]{1,0:T(8,128)}, f32[192,384]{1,0:T(8,128)}, f32[192,128]{1,0:T(8,128)}, f32[192,128]{1,0:T(8,128)}, f32[192,384]{1,0:T(8,128)}, ...) custom-call(f32[1024,1536]{1,0:T(8,128)} %get-tuple-element.109.summed_ref, bf16[1024,1536]{1,0:T(8,128)(2,1)} %tokens_ref.7, ...), custom_call_target="tpu_custom_call" | custom-call | flops 15728640 | bytes 22020096 | tf_op jit(solution)/shard_map/pallas_call | solution.py:764
  837.5 11.6 %shard_map.240 = (f32[10,192,512]{2,1,0:T(8,128)}, f32[10,192,512]{2,1,0:T(8,128)}, f32[10,64,1536]{2,1,0:T(8,128)}) custom-call(f32[9,3,192,512]{3,2,1,0:T(8,128)} %reduce-scatter.5.cloned.1.call-done.gate_ref.up_ref.down_ref, ...), custom_call_target="tpu_custom_call", output_to_operand_aliasing={{0}: (3, {}), {1}: (4, {}), {2}: (5, {})} | custom-call | bytes 21233664 | tf_op jit(solution)/shard_map/pallas_call | solution.py:1345
  849.0 1.7 copy.74
  (75 shorter events, 7.7 us)
Async XLA Ops:
  7.2 34.5 %all-gather.5.cloned.1.call-start = ((), (), s32[]{:S(2)}) async-start(), calls=%async_computation.4 | async-start | bytes 1474560 | tf_op jit(solution)/shard_map/all_gather | solution.py:600
  9.3 139.6 %all-gather.7.cloned.1.call-start = ((), (), s32[]{:S(2)}) async-start(), calls=%async_computation.5 | async-start | bytes 10616832 | tf_op jit(solution)/shard_map/all_gather | solution.py:1404
  10.6 7.1 copy-start.20
  14.2 3.9 copy-start.8
  14.4 4.3 copy-start.10
  14.4 4.3 copy-start.11
  14.4 4.3 copy-start.12
  17.8 0.8 copy-start.5
  17.8 1.0 copy-start.6
  18.8 23.0 %copy-start.22 = (f32[1536]{0:T(1024)S(1)}, f32[1536]{0:T(1024)}, u32[]{:S(2)}) copy-start(f32[1536]{0:T(1024)} %param.23) | copy-start | bytes 18436
  18.8 23.0 %copy-start.19 = (bf16[1536,40]{0,1:T(8,128)(2,1)S(1)}, bf16[1536,40]{0,1:T(8,128)(2,1)}, u32[]{:S(2)}) copy-start(bf16[1536,40]{0,1:T(8,128)(2,1)} %param.24) | copy-start | bytes 368644
  38.0 0.8 copy-start.7
  38.8 0.9 copy-start.13
  41.6 120.5 %copy-start.1 = (bf16[1024,384]{1,0:T(8,128)(2,1)}, bf16[1024,384]{1,0:T(8,128)(2,1)S(1)}, u32[]{:S(2)}) copy-start(bf16[1024,384]{1,0:T(8,128)(2,1)S(1)} %get-tuple-element.76.x_ref.attended_ref) | copy-start | bytes 2359300
  41.7 239.5 %reduce-scatter.3.cloned.1.call-start = ((), (), s32[]{:S(2)}) async-start(), calls=%async_computation.2 | async-start | bytes 10616832 | tf_op jit(solution)/shard_map/reduce_scatter | solution.py:1419
  41.8 120.4 %copy-start.9 = (f32[1,1536]{1,0:T(1,128)}, f32[1,1536]{1,0:T(1,128)S(1)}, u32[]{:S(2)}) copy-start(f32[1,1536]{1,0:T(1,128)S(1)} %reshape.75.gain_ref) | copy-start | bytes 18436
  42.1 120.1 %copy-start.4 = (bf16[1536,128]{1,0:T(8,128)(2,1)}, bf16[1536,128]{1,0:T(8,128)(2,1)S(1)}, u32[]{:S(2)}) copy-start(bf16[1536,128]{1,0:T(8,128)(2,1)S(1)} %pad.13.router_ref) | copy-start | bytes 1179652
  147.2 1.7 copy-start.2
  162.2 1.6 copy-start
  163.8 0.8 copy-start.3
  186.1 651.3 %reduce-scatter.5.cloned.1.call-start = ((), (), s32[]{:S(2)}) async-start(), calls=%async_computation.3 | async-start | bytes 95551488 | tf_op jit(solution)/shard_map/reduce_scatter | solution.py:1428
  281.2 0.8 copy-start.21
  281.2 0.8 copy-start.23
  837.4 11.6 %copy-start.17 = (bf16[1024,1536]{1,0:T(8,128)(2,1)S(1)}, bf16[1024,1536]{1,0:T(8,128)(2,1)}, u32[]{:S(2)}) copy-start(bf16[1024,1536]{1,0:T(8,128)(2,1)} %get-tuple-element.154) | copy-start | bytes 9437188
  (4 other events, 2.7 us)
Sparse Core Ops, SparseCore 0:
  10.2 31.0 all-gather.4
  43.2 58.5 all-gather.6
  186.2 83.4 reduce-scatter.2
  281.4 508.9 reduce-scatter.4
